TPU v7x, 32 devices: a whole 2x2x4 slice. The times are simulated.
32 devices in a mesh: req: 8 (over y, x, core), tp: 4 (over z).
Axes of the slice: x: 2, y: 2, z: 4, core: 2. Of those that a mesh axis runs over, the one named last changes fastest.
Arguments:
- suffix_heads: bfloat16 [4096, 3, 2048], P('req', None, 'tp')
- prefix_cache: bfloat16 [4096, 2, 2048], P('req', None, 'tp'), may hold values from -6 to 6
- lengths: int32 [8, 8], P('req'), may hold values from 1 to 128, 512 in all within a row
- groups: int32 [8, 8], P('req'), may hold values from 0 to 3
- owners: int32 [4, 2], replicated, may hold values from 0 to 7, as said below
- out_weight: bfloat16 [2048, 4096], P('tp'), may hold values from -3 to 3
Outputs:
- attention_out: bfloat16 [4096, 4096], P('req', 'tp')
Inputs may be any that keep to these rules, and one draw needn't show every extreme that they name: `lengths`: each row sums to 512; the largest length in every row is exactly 128. `owners`: all entries are distinct; the first and the last index of req are always among them.
All inputs are finite; a program needn't handle non-finite values.
Results may differ from a plain program's by a relative error of at most 0.012.
Values may be sent and summed in bfloat16 or wider, within the bound.
No kernel may reach another device: no remote copies, remote signals or barrier semaphores. Data moves between devices by JAX's collectives and lax.ppermute only.
A program may use at most 64 MiB of HBM per device.

v0:
```python
import jax
import jax.numpy as jnp
from jax import lax
from jax.sharding import PartitionSpec as P

HD = 256
ROT = 64
BLK = 512
OWNERS = 2
GROUPS = 4


NEG_FILL = -1e30
ROPE_BASE = 10000.0


def from_root(x, axis, root):
    mine = lax.axis_index(axis) == root
    return lax.psum(jnp.where(mine, x, jnp.zeros_like(x)), axis)


def token_layout(length_row, group_row, row_count):
    span_end = jnp.cumsum(length_row)
    starts = span_end - length_row
    row_ids = jnp.arange(row_count, dtype=jnp.int32)
    member = (
        (row_ids[:, None] >= starts[None, :]) & (row_ids[:, None] < span_end[None, :])
    ).astype(jnp.int32)
    request = jnp.sum(member * jnp.arange(length_row.shape[0], dtype=jnp.int32)[None, :], axis=1)
    first_row = jnp.sum(member * starts[None, :], axis=1)
    tok_group = jnp.sum(member * group_row[None, :], axis=1)
    return (row_ids, request, row_ids - first_row, tok_group)


def rotary(heads_in, positions):
    inverse = ROPE_BASE ** (-2.0 * jnp.arange(ROT // 2, dtype=jnp.float32) / ROT)
    angles = positions.astype(jnp.float32)[:, None] * inverse[None, :]
    sines = jnp.repeat(jnp.sin(angles), 2, axis=1)[:, None, :]
    cosines = jnp.repeat(jnp.cos(angles), 2, axis=1)[:, None, :]
    leading = heads_in[..., :ROT]
    even_part = leading[..., 0::2]
    odd_part = leading[..., 1::2]
    turned = jnp.stack((-odd_part, even_part), axis=-1).reshape(leading.shape)
    return jnp.concatenate((leading * cosines + turned * sines, heads_in[..., ROT:]), axis=-1)


def joint_attention(queries, keys_new, values_new, causal, shared, visible):
    heads_here = queries.shape[1]
    prefix_keys = shared[:, 0].reshape(shared.shape[0], heads_here, HD)
    prefix_values = shared[:, 1].reshape(shared.shape[0], heads_here, HD)
    score_scale = HD ** (-0.5)

    def one_head(items):
        query_h, key_h, value_h, pkey_h, pvalue_h = items
        local_scores = (
            lax.dot_general(
                query_h, key_h, (((1,), (1,)), ((), ())), preferred_element_type=jnp.float32
            )
            * score_scale
        )
        local_scores = jnp.where(causal, local_scores, NEG_FILL)
        prefix_scores = (
            lax.dot_general(
                query_h, pkey_h, (((1,), (1,)), ((), ())), preferred_element_type=jnp.float32
            )
            * score_scale
        )
        prefix_scores = jnp.where(visible, prefix_scores, NEG_FILL)
        peak = jnp.maximum(
            jnp.max(local_scores, axis=1, keepdims=True),
            jnp.max(prefix_scores, axis=1, keepdims=True),
        )
        local_exp = jnp.exp(local_scores - peak)
        prefix_exp = jnp.exp(prefix_scores - peak)
        weight_sum = jnp.sum(local_exp, axis=1, keepdims=True) + jnp.sum(
            prefix_exp, axis=1, keepdims=True
        )
        weighted = jnp.dot(
            local_exp.astype(jnp.bfloat16), value_h, preferred_element_type=jnp.float32
        )
        weighted = weighted + jnp.dot(
            prefix_exp.astype(jnp.bfloat16), pvalue_h, preferred_element_type=jnp.float32
        )
        return weighted / weight_sum

    per_head = lax.map(
        one_head,
        (
            jnp.swapaxes(queries, 0, 1),
            jnp.swapaxes(keys_new, 0, 1),
            jnp.swapaxes(values_new, 0, 1),
            jnp.swapaxes(prefix_keys, 0, 1),
            jnp.swapaxes(prefix_values, 0, 1),
        ),
    )
    return jnp.swapaxes(per_head, 0, 1)


def per_device(suffix_heads, prefix_cache, lengths, groups, owners, out_weight):
    row_count = suffix_heads.shape[0]
    local_feat = suffix_heads.shape[2]
    local_heads = local_feat // HD
    slot_count = GROUPS * OWNERS
    row_ids, request, offsets, tok_group = token_layout(lengths[0], groups[0], row_count)
    positions = OWNERS * BLK + offsets
    split_heads = suffix_heads.reshape(row_count, 3, local_heads, HD)
    queries = rotary(split_heads[:, 0].astype(jnp.float32), positions).astype(jnp.bfloat16)
    keys_new = rotary(split_heads[:, 1].astype(jnp.float32), positions).astype(jnp.bfloat16)
    values_new = split_heads[:, 2]
    causal = (request[:, None] == request[None, :]) & (row_ids[None, :] <= row_ids[:, None])
    key_group = jnp.arange(slot_count * BLK, dtype=jnp.int32) // (OWNERS * BLK)
    visible_all = tok_group[:, None] == key_group[None, :]
    received = []
    for slot_index in range(slot_count):
        root = owners[slot_index // OWNERS, slot_index % OWNERS]
        received.append(from_root(prefix_cache, "req", root))
    shared = jnp.concatenate(received, axis=0)
    attended = joint_attention(queries, keys_new, values_new, causal, shared, visible_all)
    attended = attended.astype(jnp.bfloat16).reshape(row_count, local_feat)
    partial_out = jnp.dot(attended, out_weight, preferred_element_type=jnp.float32)
    return lax.psum_scatter(partial_out.astype(jnp.bfloat16), "tp", scatter_dimension=1, tiled=True)


def solution(mesh):
    placed = (
        P("req", None, "tp"),
        P("req", None, "tp"),
        P("req", None),
        P("req", None),
        P(),
        P("tp", None),
    )
    return jax.shard_map(
        per_device, mesh=mesh, in_specs=placed, out_specs=P("req", "tp"), check_vma=False
    )
```

profile of v0, /device:TPU:0, one launch (start us, length us, event | category | flops | bytes accessed | tf_op | source)
XLA Modules:
  0.0 266.2 jit_solution(17296798090594078986)
XLA Ops:
  6.5 1.6 fusion.45
  13.1 2.5 copy.31
  15.6 3.4 %broadcast_select_fusion = (bf16[512,2,512]{0,2,1:T(8,128)(2,1)}, bf16[512,2,512]{0,2,1:T(8,128)(2,1)}, bf16[512,2,512]{0,2,1:T(8,128)(2,1)}, bf16[512,2,512]{0,...) fusion(bf16[512,2,512]{0,2,1:T(8,128)(2,1)S(1)} %copy.31, ...), kind=kLoop, calls=%fused_computation.37 | loop fusion | flops 4194304 | bytes 9437192 | tf_op jit(solution)/shard_map/jit(_where)/select_n | solution.py:19
  19.1 0.7 copy.26
  19.8 0.9 slice_bitcast_fusion
  21.1 0.2 copy.27
  21.4 0.2 copy.29
  21.6 0.2 reduce-window.4
  21.9 0.3 multiply_cosine_fusion
  22.8 128.2 %all-reduce.3.cloned.1.call-done = (bf16[512,2,512]{0,2,1:T(8,128)(2,1)}, bf16[512,2,512]{0,2,1:T(8,128)(2,1)}, bf16[512,2,512]{0,2,1:T(8,128)(2,1)}, bf16[512,2...) async-done(((bf16[512,2,512]{0,2,1:T(8,128)(2,1)}, ...) | async-done | bytes 8388624 | tf_op jit(solution)/shard_map/psum | solution.py:19
  151.0 1.5 constant_dynamic-update-slice_fusion.8
  152.5 1.4 constant_dynamic-update-slice_fusion.7
  153.9 1.3 constant_dynamic-update-slice_fusion.6
  155.3 1.3 constant_dynamic-update-slice_fusion.5
  157.2 3.7 %fusion.44 = (bf16[4096,1,512]{0,2,1:T(8,128)(2,1)}, bf16[4096,1,512]{0,2,1:T(8,128)(2,1)}) fusion(bf16[4096,2,512]{0,2,1:T(8,128)(2,1)S(1)} %constant_dynamic-update-slice_fusion.1), kind=kLoop, calls=%fused_computation.91 | loop fusion | bytes 16777216 | tf_op jit(solution)/shard_map/slice | solution.py:50
  160.9 14.8 %while.11 = (s32[]{:T(128)}, bf16[2,512,256]{1,2,0:T(8,128)(2,1)S(1)}, bf16[2,512,256]{1,2,0:T(8,128)(2,1)S(1)}, bf16[2,512,256]{1,2,0:T(8,128)(2,1)S(1)}, bf16[...) while((s32[]{:T(128)}, ...), condition=%wide.region_17.18_spmd.clone, body=%wide.region_12.17_spmd.clone.sunk | while | flops 2435709952 | bytes 52746388 | solution.py:86
  160.9 3.3 %fusion.62 = (f32[512]{0:T(512)S(1)}, f32[512,4096]{1,0:T(8,128)S(1)}) fusion(bf16[2,4096,256]{1,2,0:T(8,128)(2,1)} %get-tuple-element.256, s32[]{:T(128)} %get-tuple-element.241, bf16[2,512,256]{1,2,0:T(8,128)(2,1)S(1)} %get-tuple-element.254, s32[4096]{0:T(1024)S(1)} %get-tuple-element.260, s32[512]{0:T(512)S(1)} %get-tuple-element.261), kind=kOutput, calls=%fused_computation.90.clone.1 | convolution fusion | flops 1082129920 | bytes 10769408 | tf_op jit(solution)/shard_map/while/body/eval_jaxpr/dot_general | solution.py:63
  164.2 0.4 fusion.63
  164.6 1.3 fusion.66
  165.9 0.2 fusion.65
  166.1 0.3 copy-done
  166.4 1.4 fusion.64
  167.7 0.4 fusion.67
  168.3 3.3 %fusion.62 = (f32[512]{0:T(512)S(1)}, f32[512,4096]{1,0:T(8,128)S(1)}) fusion(bf16[2,4096,256]{1,2,0:T(8,128)(2,1)} %get-tuple-element.256, s32[]{:T(128)} %get-tuple-element.241, bf16[2,512,256]{1,2,0:T(8,128)(2,1)S(1)} %get-tuple-element.254, s32[4096]{0:T(1024)S(1)} %get-tuple-element.260, s32[512]{0:T(512)S(1)} %get-tuple-element.261), kind=kOutput, calls=%fused_computation.90.clone.1 | convolution fusion | flops 1082129920 | bytes 10769408 | tf_op jit(solution)/shard_map/while/body/eval_jaxpr/dot_general | solution.py:63
  171.6 0.4 fusion.63
  172.0 1.3 fusion.66
  173.3 0.2 fusion.65
  173.5 0.3 copy-done
  173.8 1.4 fusion.64
  175.2 0.4 fusion.67
  175.7 6.5 %convolution_convert_fusion = bf16[512,4096]{1,0:T(8,128)(2,1)} fusion(bf16[512,512]{0,1:T(8,128)(2,1)S(1)} %bitcast.105, bf16[512,4096]{1,0:T(8,128)(2,1)} %param.13), kind=kOutput, calls=%fused_computation.36 | convolution fusion | flops 2149580800 | bytes 8912896 | tf_op jit(solution)/shard_map/dot_general | solution.py:120
  182.2 77.2 %reduce-scatter.2.cloned.1.call-done = bf16[512,1024]{1,0:T(8,128)(2,1)} async-done(((bf16[512,4096]{1,0:T(8,128)(2,1)}), bf16[512,1024]{1,0:T(8,128)(2,1)}) %reduce-scatter.2.cloned.1.call-update) | async-done | bytes 1048592 | tf_op jit(solution)/shard_map/reduce_scatter | solution.py:121
  (58 shorter events, 1.9 us)
Async XLA Ops:
  6.5 144.4 %all-reduce.3.cloned.1.call-start = ((), (), s32[]{:S(2)}) async-start(), calls=%async_computation.2 | async-start | bytes 16777216 | tf_op jit(solution)/shard_map/psum | solution.py:19
  15.6 3.5 %copy-start.1 = (bf16[512,3,512]{2,0,1:T(8,128)(2,1)S(1)}, bf16[512,3,512]{2,0,1:T(8,128)(2,1)}, u32[]{:S(2)}) copy-start(bf16[512,3,512]{2,0,1:T(8,128)(2,1)} %param.8) | copy-start | bytes 4718596
  19.0 2.6 copy-start.8
  19.0 2.8 %copy-start.7 = (s32[1,8]{1,0:T(1,128)S(1)}, s32[1,8]{1,0:T(1,128)}, u32[]{:S(2)}) copy-start(s32[1,8]{1,0:T(1,128)} %param.11) | copy-start | bytes 100
  19.0 240.4 %reduce-scatter.2.cloned.1.call-start = ((), (), s32[]{:S(2)}) async-start(), calls=%async_computation.1 | async-start | bytes 5242880 | tf_op jit(solution)/shard_map/reduce_scatter | solution.py:121
  151.0 5.6 %copy-start.5 = (bf16[512,2,512]{0,2,1:T(8,128)(2,1)S(1)}, bf16[512,2,512]{0,2,1:T(8,128)(2,1)}, u32[]{:S(2)}) copy-start(bf16[512,2,512]{0,2,1:T(8,128)(2,1)} %get-tuple-element.126) | copy-start | bytes 3145732
  151.0 5.8 %copy-start.4 = (bf16[512,2,512]{0,2,1:T(8,128)(2,1)S(1)}, bf16[512,2,512]{0,2,1:T(8,128)(2,1)}, u32[]{:S(2)}) copy-start(bf16[512,2,512]{0,2,1:T(8,128)(2,1)} %get-tuple-element.127) | copy-start | bytes 3145732
  151.0 5.9 %copy-start.3 = (bf16[512,2,512]{0,2,1:T(8,128)(2,1)S(1)}, bf16[512,2,512]{0,2,1:T(8,128)(2,1)}, u32[]{:S(2)}) copy-start(bf16[512,2,512]{0,2,1:T(8,128)(2,1)} %get-tuple-element.128) | copy-start | bytes 3145732
  151.0 6.1 %copy-start.2 = (bf16[512,2,512]{0,2,1:T(8,128)(2,1)S(1)}, bf16[512,2,512]{0,2,1:T(8,128)(2,1)}, u32[]{:S(2)}) copy-start(bf16[512,2,512]{0,2,1:T(8,128)(2,1)} %get-tuple-element.129) | copy-start | bytes 3145732
  157.2 3.8 %copy-start.6 = (bf16[2,512,256]{1,2,0:T(8,128)(2,1)S(1)}, bf16[2,512,256]{1,2,0:T(8,128)(2,1)}, u32[]{:S(2)}) copy-start(bf16[2,512,256]{1,2,0:T(8,128)(2,1)} %get-tuple-element.235) | copy-start | bytes 1572868
  164.2 2.2 copy-start
  171.6 2.2 copy-start
Sparse Core Ops, SparseCore 0:
  19.1 131.7 all-reduce.2
  182.4 77.0 reduce-scatter.1
where the time goes:
time: 267 us; the launch traced here: 266 us
  waiting for transfers between devices  205 us (77%)
  between operations  18.7 us (7%)
  local copies, waits for them, and re-layouts  17.4 us (7%)
  matrix products  17.3 us (6%)
  other arithmetic  7.3 us (3%)
    psum x1, waiting for transfers between devices, from_root(): return lax.psum(jnp.where(mine, x, jnp.zeros_like(x)), axis)  128 us
    reduce_scatter x1, waiting for transfers between devices, per_device(): lax.psum_scatter(partial_out.astype(jnp.bfloat16), 'tp', scatter_dimensio...  77.2 us
    unnamed x25, local copies, waits for them, and re-layouts  9.15 us
    dot_general x2, matrix products, one_head(): lax.dot_general(query_h, pkey_h, (((1,), (1,)), ((), ())), preferred_elem...  6.51 us
    dot_general x1, matrix products, per_device(): jnp.dot(attended, out_weight, preferred_element_type=jnp.float32)  6.49 us
  transfers between devices with their start and end apart: 2, of which 2 were waited for; matrix products, arithmetic and copies ran while one was open for 1% of the time, Pallas kernels for 0%

commit v1 on v0

v1 whole, which is shorter than its diff:
```python
import functools
import jax
import jax.numpy as jnp
from jax import lax
from jax.experimental import pallas as pl
from jax.experimental.pallas import tpu as pltpu
from jax.sharding import PartitionSpec as P

HD = 256
ROT = 64
BLK = 512
OWNERS = 2
GROUPS = 4
SLOTS = GROUPS * OWNERS
MOST = 128

NEG_FILL = -1e30
ROPE_BASE = 10000.0
LOG2E = 1.4426950408889634
SCALE = HD ** (-0.5)

VMEM = pl.BlockSpec(memory_space=pltpu.VMEM)
SMEM = pl.BlockSpec(memory_space=pltpu.SMEM)
ANY = pl.BlockSpec(memory_space=pl.ANY)


def from_root(x, axis, root):
    mine = lax.axis_index(axis) == root
    return lax.psum(jnp.where(mine, x, jnp.zeros_like(x)), axis)


def token_layout(length_row, group_row, row_count):
    span_end = jnp.cumsum(length_row)
    starts = span_end - length_row
    row_ids = jnp.arange(row_count, dtype=jnp.int32)
    member = (
        (row_ids[:, None] >= starts[None, :]) & (row_ids[:, None] < span_end[None, :])
    ).astype(jnp.int32)
    first_row = jnp.sum(member * starts[None, :], axis=1)
    tok_group = jnp.sum(member * group_row[None, :], axis=1)
    return row_ids, first_row, tok_group


def rope_tables(positions):
    inverse = ROPE_BASE ** (-2.0 * jnp.arange(ROT // 2, dtype=jnp.float32) / ROT)
    inverse = jnp.concatenate([jnp.repeat(inverse, 2), jnp.zeros((128 - ROT,), jnp.float32)])
    angles = positions.astype(jnp.float32)[:, None] * inverse[None, :]
    sign = jnp.where(jnp.arange(128) % 2 == 0, -1.0, 1.0).astype(jnp.float32)
    return jnp.cos(angles), jnp.sin(angles) * sign[None, :]


def prep_kernel(x_ref, cos_ref, sin_ref, o_ref):
    rows = x_ref.shape[0]
    lane = lax.broadcasted_iota(jnp.int32, (rows, 128), 1)
    even = (lane % 2) == 0
    cos = cos_ref[...]
    sin = sin_ref[...]
    for i in range(x_ref.shape[1] // HD):
        x = x_ref[:, i * HD : i * HD + 128].astype(jnp.float32)
        swapped = jnp.where(even, pltpu.roll(x, 127, 1), pltpu.roll(x, 1, 1))
        o_ref[i, :, 0:128] = (x * cos + swapped * sin).astype(jnp.bfloat16)
        o_ref[i, :, 128:HD] = x_ref[:, i * HD + 128 : (i + 1) * HD]


def rotate(x, cos, sin):
    rows = x.shape[0]
    return pl.pallas_call(
        prep_kernel,
        out_shape=jax.ShapeDtypeStruct((x.shape[1] // HD, rows, HD), jnp.bfloat16),
        in_specs=[VMEM] * 3,
        out_specs=VMEM,
        name="rotate",
    )(x, cos, sin)


RB = 128


def attn_kernel(head, heads, pos_ref, qk_ref, v_ref, first_ref, grp_ref, *rest):
    pieces_k = rest[:SLOTS]
    pieces_v = rest[SLOTS : 2 * SLOTS]
    o_ref, ks, vs, sems = rest[2 * SLOTS :]
    rows = o_ref.shape[0]
    copies_k = []
    copies_v = []
    for d in range(SLOTS):
        copies_k.append(pltpu.make_async_copy(pieces_k[d], ks.at[pos_ref[d]], sems.at[0, d]))
        copies_v.append(pltpu.make_async_copy(pieces_v[d], vs.at[pos_ref[d]], sems.at[1, d]))
    for c in copies_k + copies_v:
        c.start()
    for c in copies_k:
        c.wait()
    for c in copies_v:
        c.wait()
    factor = SCALE * LOG2E
    half = 256
    nb = rows // RB
    for b in range(nb):
        r0 = b * RB
        q = qk_ref[head, r0 : r0 + RB, :]
        grp = jnp.broadcast_to(grp_ref[r0 : r0 + RB, :], (RB, half))
        scores = []
        for o in range(OWNERS):
            for j in range(BLK // half):
                acc = None
                for g in range(GROUPS):
                    s = lax.dot_general(
                        q,
                        ks[g * OWNERS + o, j * half : (j + 1) * half, :],
                        (((1,), (1,)), ((), ())),
                        preferred_element_type=jnp.float32,
                    )
                    acc = s if acc is None else jnp.where(grp == g, s, acc)
                scores.append(acc)
        lo = max(0, r0 - MOST)
        width = r0 + RB - lo
        local = lax.dot_general(
            q,
            qk_ref[heads + head, lo : r0 + RB, :],
            (((1,), (1,)), ((), ())),
            preferred_element_type=jnp.float32,
        )
        row = r0 + lax.broadcasted_iota(jnp.int32, (RB, width), 0)
        key = lo + lax.broadcasted_iota(jnp.int32, (RB, width), 1)
        seen = (key <= row) & (key >= jnp.broadcast_to(first_ref[r0 : r0 + RB, :], (RB, width)))
        local = jnp.where(seen, local, NEG_FILL)
        top = jnp.max(local, axis=1, keepdims=True)
        whole = scores[0]
        for s in scores[1:]:
            whole = jnp.maximum(whole, s)
        top = jnp.maximum(top, jnp.max(whole, axis=1, keepdims=True))
        e_local = jnp.exp2((local - top) * factor)
        den = jnp.sum(e_local, axis=1, keepdims=True)
        out = jnp.dot(
            e_local.astype(jnp.bfloat16), v_ref[lo : r0 + RB, :], preferred_element_type=jnp.float32
        )
        total = None
        i = 0
        for o in range(OWNERS):
            for j in range(BLK // half):
                e = jnp.exp2((scores[i] - top) * factor)
                i += 1
                total = e if total is None else total + e
                for g in range(GROUPS):
                    w = jnp.where(grp == g, e, 0.0).astype(jnp.bfloat16)
                    out = out + jnp.dot(
                        w,
                        vs[g * OWNERS + o, j * half : (j + 1) * half, :],
                        preferred_element_type=jnp.float32,
                    )
        den = den + jnp.sum(total, axis=1, keepdims=True)
        o_ref[r0 : r0 + RB, :] = (out / den).astype(jnp.bfloat16)


def attend(head, heads, place, qk, v, first, grp, keys, values):
    rows = qk.shape[1]
    return pl.pallas_call(
        functools.partial(attn_kernel, head, heads),
        out_shape=jax.ShapeDtypeStruct((rows, HD), jnp.bfloat16),
        in_specs=[SMEM, VMEM, VMEM, VMEM, VMEM] + [ANY] * (2 * SLOTS),
        out_specs=VMEM,
        scratch_shapes=[
            pltpu.VMEM((SLOTS, BLK, HD), jnp.bfloat16),
            pltpu.VMEM((SLOTS, BLK, HD), jnp.bfloat16),
            pltpu.SemaphoreType.DMA((2, SLOTS)),
        ],
        compiler_params=pltpu.CompilerParams(vmem_limit_bytes=32 << 20),
        name=f"attend{head}",
    )(place, qk, v, first, grp, *keys, *values)


def proj_kernel(parts, where_ref, *refs):
    n_att = 2 * parts
    att = refs[:n_att]
    w_ref = refs[n_att]
    pieces = refs[n_att + 1 : n_att + 1 + 16]
    o_ref, own, far, sems = refs[n_att + 17 :]
    cols = o_ref.shape[1]
    z = where_ref[0]
    chip = where_ref[1]
    core = where_ref[2]
    copies = [
        pltpu.make_async_copy(
            w_ref.at[:, pl.ds(pl.multiple_of(z * cols, cols), cols)], own, sems.at[16]
        )
    ]
    for d in range(8):
        head = lax.bitwise_xor(core, d & 1)
        block = lax.bitwise_xor(chip, d >> 1)
        for s in range(2):
            copies.append(
                pltpu.make_async_copy(
                    pieces[2 * d + s],
                    far.at[
                        :,
                        head,
                        s * 128 : (s + 1) * 128,
                        pl.ds(pl.multiple_of(block * HD, HD), HD),
                    ],
                    sems.at[2 * d + s],
                )
            )
    for c in copies:
        c.start()
    for c in copies:
        c.wait()
    rows = o_ref.shape[0]
    for n in range(cols // HD):
        c0 = n * HD
        acc = jnp.zeros((rows, HD), jnp.float32)
        for m in range(parts):
            for h in range(2):
                if m == 0:
                    w = own[h * HD : (h + 1) * HD, c0 : c0 + HD]
                else:
                    w = far[m - 1, h, :, c0 : c0 + HD]
                acc = acc + jnp.dot(att[2 * m + h][...], w, preferred_element_type=jnp.float32)
        o_ref[:, c0 : c0 + HD] = acc.astype(jnp.bfloat16)


def project(where, att, w, pieces, cols):
    rows = att[0].shape[0]
    parts = len(att) // 2
    return pl.pallas_call(
        functools.partial(proj_kernel, parts),
        out_shape=jax.ShapeDtypeStruct((rows, cols), jnp.bfloat16),
        in_specs=[SMEM] + [VMEM] * len(att) + [ANY] * (1 + len(pieces)),
        out_specs=VMEM,
        scratch_shapes=[
            pltpu.VMEM((w.shape[0], cols), jnp.bfloat16),
            pltpu.VMEM((parts - 1, 2, HD, cols), jnp.bfloat16),
            pltpu.SemaphoreType.DMA((17,)),
        ],
        compiler_params=pltpu.CompilerParams(vmem_limit_bytes=32 << 20),
        name="project",
    )(where, *att, w, *pieces)


def swap(x, axis, mask, size):
    return lax.ppermute(x, axis, [(i, i ^ mask) for i in range(size)])


def after(x, *deps):
    return lax.optimization_barrier((x,) + deps)[0]


def spread_pair(a, b):
    x = functools.partial(swap, axis="req", mask=2, size=8)
    y = functools.partial(swap, axis="req", mask=4, size=8)
    c = functools.partial(swap, axis="req", mask=1, size=8)
    ax = x(a)
    by = y(b)
    ay = y(a)
    bx = x(b)
    axy = y(ax)
    bxy = x(by)
    return (
        [a, c(a), ax, c(ax), ay, c(ay), axy, c(axy)],
        [b, c(b), bx, c(bx), by, c(by), bxy, c(bxy)],
    )


def per_device(req_size, tp_size, suffix_heads, prefix_cache, lengths, groups, owners, out_weight):
    row_count = suffix_heads.shape[0]
    local_feat = suffix_heads.shape[2]
    heads = local_feat // HD
    row_ids, first, tok_group = token_layout(lengths[0], groups[0], row_count)
    positions = OWNERS * BLK + row_ids - first
    cos, sin = rope_tables(positions)
    first = first[:, None]
    grp = tok_group[:, None]
    me = lax.axis_index("req")
    z = lax.axis_index("tp")
    split = req_size == 8 and tp_size == 4 and heads == 2
    flat_owner = owners.reshape(-1)

    if split:
        cols = out_weight.shape[1] // tp_size
        pieces = []
        for m in range(1, tp_size):
            piece = lax.dynamic_slice(
                out_weight,
                ((me % 2) * HD, (z ^ m) * cols + (me // 2) * HD),
                (HD, HD),
            )
            pieces.append(swap(piece, "tp", m, tp_size))
        place = jnp.sum(
            jnp.where(
                flat_owner[None, :] == (me ^ jnp.arange(SLOTS, dtype=jnp.int32))[:, None],
                jnp.arange(SLOTS, dtype=jnp.int32)[None, :],
                0,
            ),
            axis=1,
        ).astype(jnp.int32)
        keys = []
        values = []
        for h in range(heads):
            k = prefix_cache[:, 0, h * HD : (h + 1) * HD]
            v = prefix_cache[:, 1, h * HD : (h + 1) * HD]
            if h:
                k, v = lax.optimization_barrier((k, v, keys[-1][6], values[-1][6]))[:2]
            ks, vs = spread_pair(k, v)
            keys.append(ks)
            values.append(vs)
    else:
        place = jnp.arange(SLOTS, dtype=jnp.int32)
        received = [from_root(prefix_cache, "req", flat_owner[i]) for i in range(SLOTS)]
        keys = [[s[:, 0, h * HD : (h + 1) * HD] for s in received] for h in range(heads)]
        values = [[s[:, 1, h * HD : (h + 1) * HD] for s in received] for h in range(heads)]

    qk = rotate(
        jnp.concatenate([suffix_heads[:, 0], suffix_heads[:, 1]], axis=1), cos, sin
    )
    attended = []
    for h in range(heads):
        v = suffix_heads[:, 2, h * HD : (h + 1) * HD]
        attended.append(
            attend(h, heads, place, qk, v, first, grp, keys[h], values[h])
        )

    if split:
        last = (keys[-1][6], values[-1][6])
        stacked = jnp.stack(pieces)
        low, high = lax.optimization_barrier((stacked[:, :128], stacked[:, 128:]) + last)[:2]
        low, high = spread_pair(low, high)
        tiles = []
        for d in range(8):
            tiles += [low[d], high[d]]
        att = list(attended)
        for m in range(1, tp_size):
            for h in range(heads):
                att.append(swap(attended[h], "tp", m, tp_size))
        where = jnp.stack([z, me // 2, me % 2]).astype(jnp.int32)
        return project(where, att, out_weight, tiles, cols)
    partial_out = jnp.dot(
        jnp.concatenate(attended, axis=1), out_weight, preferred_element_type=jnp.float32
    )
    return lax.psum_scatter(partial_out.astype(jnp.bfloat16), "tp", scatter_dimension=1, tiled=True)


def solution(mesh):
    placed = (
        P("req", None, "tp"),
        P("req", None, "tp"),
        P("req", None),
        P("req", None),
        P(),
        P("tp", None),
    )
    return jax.shard_map(
        functools.partial(per_device, mesh.shape["req"], mesh.shape["tp"]),
        mesh=mesh,
        in_specs=placed,
        out_specs=P("req", "tp"),
        check_vma=False,
    )
```

time: 267 us -> 162 us (0.61)
  waiting for transfers between devices: 205 us -> 67.7 us
  starting transfers between devices: 0.04 us -> 37.2 us
  Pallas kernels: 0 us -> 22.8 us
  between operations: 18.7 us -> 0.47 us
  matrix products: 17.3 us -> 0 us
  local copies, waits for them, and re-layouts: 17.4 us -> 24.1 us
    psum x1 -> x0, waiting for transfers between devices: 128 us -> none  [from_root(): return lax.psum(jnp.where(mine, x, jnp.zeros_like(x)), axis)]
    reduce_scatter x1 -> x0, waiting for transfers between devices: 77.2 us -> none  [per_device(): lax.psum_scatter(partial_out.astype(jnp.bfloat16), 'tp', scatter_dimensio...]
    ppermute x0 -> x51, waiting for transfers between devices: none -> 67.7 us  [swap(): return lax.ppermute(x, axis, [(i, i ^ mask) for i in range(size)])]
    ppermute x0 -> x51, starting transfers between devices: none -> 37.2 us  [swap(): return lax.ppermute(x, axis, [(i, i ^ mask) for i in range(size)])]
    pallas_call x0 -> x4, Pallas kernels: none -> 22.8 us  [the longest x2 15.3 us: attend(): pl.pallas_call(functools.partial(attn_kernel, head, heads), out_shape=jax...]
    dot_general x9 -> x0, matrix products: 17.3 us -> none  [the longest x2 6.51 us: one_head(): lax.dot_general(query_h, pkey_h, (((1,), (1,)), ((), ())), preferred_elem...]
    unnamed x25 -> x73, local copies, waits for them, and re-layouts: 9.15 us -> 16.2 us
    select_n x2 -> x1, other arithmetic: 3.39 us -> 0.57 us  [rope_tables(): sign = jnp.where(jnp.arange(128) % 2 == 0, -1.0, 1.0).astype(jnp.float32)]
  transfers between devices with their start and end apart: 2 -> 51, of which waited for: 2 -> 14; matrix products, arithmetic and copies ran while one was open for 1% -> 8% of each run, Pallas kernels for 0% -> 11%
where the time goes in v1:
time: 162 us; the launch traced here: 160 us
  waiting for transfers between devices  67.7 us (42%)
  starting transfers between devices  37.2 us (23%)
  local copies, waits for them, and re-layouts  24.1 us (15%)
  Pallas kernels  22.8 us (14%)
  other arithmetic  7.65 us (5%)
    ppermute x51, waiting for transfers between devices, swap(): return lax.ppermute(x, axis, [(i, i ^ mask) for i in range(size)])  67.7 us
    ppermute x51, starting transfers between devices, swap(): return lax.ppermute(x, axis, [(i, i ^ mask) for i in range(size)])  37.2 us
    unnamed x73, local copies, waits for them, and re-layouts  16.2 us
    pallas_call x2, Pallas kernels, attend(): pl.pallas_call(functools.partial(attn_kernel, head, heads), out_shape=jax...  15.3 us
    pallas_call x1, Pallas kernels, project(): pl.pallas_call(functools.partial(proj_kernel, parts), out_shape=jax.Shape...  4.63 us
  transfers between devices with their start and end apart: 51, of which 14 were waited for; matrix products, arithmetic and copies ran while one was open for 8% of the time, Pallas kernels for 11%

profile of v1, /device:TPU:0, one launch (start us, length us, event | category | flops | bytes accessed | tf_op | source)
XLA Modules:
  0.0 159.8 jit_solution(11723127456742900153)
XLA Ops:
  0.0 3.2 %fusion.4 = (bf16[512,1,256]{2,1,0:T(2,128)(2,1)S(1)}, bf16[512,1,256]{2,1,0:T(2,128)(2,1)S(1)}, bf16[512,1,256]{2,1,0:T(2,128)(2,1)S(1)}, bf16[512,1,256]{2,1,0:T(2,128)(2,1)S(1)}) fusion(bf16[512,2,512]{2,1,0:T(2,128)(2,1)} %param.7), kind=kLoop, calls=%fused_computation.28 | loop fusion | bytes 2097152 | tf_op jit(solution)/shard_map/slice | solution.py:299
  3.7 2.6 %collective-permute-start.1 = (bf16[512,256]{1,0:T(8,128)(2,1)S(1)}, bf16[512,256]{1,0:T(8,128)(2,1)S(1)}, u32[]{:S(2)}, u32[]{:S(2)}) collective-permute-start(bf16[512,256]{1,0:T(8,128)(2,1)S(1)} %bitcast.36), channel_id=1, source_target_pairs={{0,8},{4,12},{8,0},{12,4},{16,24},{20,28},{24,16},{28,20},{1,9},{5... | collective-permute-start | bytes 786440 | tf_op jit(solution)/shard_map/ppermute | solution.py:240
  6.3 1.5 collective-permute-start.3
  7.8 1.8 %fusion.3 = (bf16[256,256]{1,0:T(8,128)(2,1)}, bf16[256,256]{1,0:T(8,128)(2,1)S(1)}, bf16[256,256]{1,0:T(8,128)(2,1)}) fusion(bf16[512,4096]{1,0:T(8,128)(2,1)} %refs_8_.1, s32[]{:T(128)S(6)} %select_n.61, s32[]{:T(128)S(6)} %select_n.62, s32[]{:T(128)S(6)} %select_n.63, s32[]{:T(128)S(6)} %select_n.64), kind=kLoop, calls=%fused_computation.27 | loop fusion | bytes 786448 | tf_op jit(solution)/shard_map/dynamic_slice | solution.py:281
  9.6 3.6 %collective-permute-start.36 = (bf16[256,256]{1,0:T(8,128)(2,1)}, bf16[256,256]{1,0:T(8,128)(2,1)S(1)}, u32[]{:S(2)}, u32[]{:S(2)}) collective-permute-start(bf16[256,256]{1,0:T(8,128)(2,1)} %get-tuple-element.17), channel_id=1, source_target_pairs={{0,3},{1,2},{2,1},{3,0},{4,7},{5,6},{6,5},{7,4},{8,11},{9,10},{10,... | collective-permute-start | bytes 393224 | tf_op jit(solution)/shard_map/ppermute | solution.py:240
  14.9 3.2 %collective-permute-done.36 = bf16[256,256]{1,0:T(8,128)(2,1)S(1)} collective-permute-done((bf16[256,256]{1,0:T(8,128)(2,1)}, bf16[256,256]{1,0:T(8,128)(2,1)S(1)}, u32[]{:S(2)}, u32[]{:S(2)}) %collective-permute-start.36) | collective-permute-done | bytes 131104 | tf_op jit(solution)/shard_map/ppermute | solution.py:240
  18.6 6.0 %collective-permute-done.35 = bf16[256,256]{1,0:T(8,128)(2,1)S(1)} collective-permute-done((bf16[256,256]{1,0:T(8,128)(2,1)S(1)}, bf16[256,256]{1,0:T(8,128)(2,1)S(1)}, u32[]{:S(2)}, u32[]{:S(2)}) %collective-permute-start.35) | collective-permute-done | bytes 131104 | tf_op jit(solution)/shard_map/ppermute | solution.py:240
  25.3 4.3 %collective-permute-done.34 = bf16[256,256]{1,0:T(8,128)(2,1)S(1)} collective-permute-done((bf16[256,256]{1,0:T(8,128)(2,1)S(1)}, bf16[256,256]{1,0:T(8,128)(2,1)S(1)}, u32[]{:S(2)}, u32[]{:S(2)}) %collective-permute-start.34) | collective-permute-done | bytes 131104 | tf_op jit(solution)/shard_map/ppermute | solution.py:240
  30.8 1.6 collective-permute-start.12
  34.2 4.5 %collective-permute-done.8.rest_10_ = bf16[512,256]{1,0:T(8,128)(2,1)S(1)} collective-permute-done((bf16[512,256]{1,0:T(8,128)(2,1)S(1)}, bf16[512,256]{1,0:T(8,128)(2,1)S(1)}, u32[]{:S(2)}, u32[]{:S(2)}) %collective-permute-start.8) | collective-permute-done | bytes 262176 | tf_op jit(solution)/shard_map/ppermute | solution.py:240
  40.7 3.2 %collective-permute-done.12.rest_14_ = bf16[512,256]{1,0:T(8,128)(2,1)S(1)} collective-permute-done((bf16[512,256]{1,0:T(8,128)(2,1)S(1)}, bf16[512,256]{1,0:T(8,128)(2,1)S(1)}, u32[]{:S(2)}, u32[]{:S(2)}) %collective-permute-start.12) | collective-permute-done | bytes 262176 | tf_op jit(solution)/shard_map/ppermute | solution.py:240
  50.0 1.6 collective-permute-start.24
  51.6 2.5 %fusion = (f32[512,128]{1,0:T(8,128)}, f32[512,128]{1,0:T(8,128)}) fusion(f32[128]{0:T(128)} %compare_select_fusion, f32[128]{0:T(128)S(1)} %concatenate.7, f32[512]{0:T(512)} %subtract_convert_fusion), kind=kLoop, calls=%fused_computation.6 | loop fusion | flops 131072 | bytes 527360 | tf_op jit(solution)/shard_map/mul | solution.py:49
  54.1 1.5 collective-permute-start.22
  55.6 1.9 %collective-permute-done.17.rest_4_ = bf16[512,256]{1,0:T(8,128)(2,1)} collective-permute-done((bf16[512,256]{1,0:T(8,128)(2,1)S(1)}, bf16[512,256]{1,0:T(8,128)(2,1)}, u32[]{:S(2)}, u32[]{:S(2)}) %collective-permute-start.17) | collective-permute-done | bytes 262176 | tf_op jit(solution)/shard_map/ppermute | solution.py:240
  57.5 2.3 %pad_maximum_fusion.x_ref = bf16[512,1024]{1,0:T(8,128)(2,1)} fusion(bf16[512,512]{1,0:T(8,128)(2,1)} %get-tuple-element.21, bf16[512,512]{1,0:T(8,128)(2,1)} %get-tuple-element.20), kind=kLoop, calls=%fused_computation | loop fusion | flops 2097152 | bytes 2097152 | tf_op jit(solution)/shard_map/concatenate | solution.py:312
  61.9 1.5 collective-permute-start.26
  64.4 2.9 %rotate.1.qk_ref = bf16[4,512,256]{2,1,0:T(8,128)(2,1)} custom-call(bf16[512,1024]{1,0:T(8,128)(2,1)} %pad_maximum_fusion.x_ref, f32[512,128]{1,0:T(8,128)} %get-tuple-element.29.cos_ref, f32[512,128]{1,0:T(8,128)} %get-tuple-element.28.sin_ref), custom_call_target="tpu_custom_call" | custom-call | tf_op jit(solution)/shard_map/rotate/pallas_call | solution.py:67
  77.3 7.4 %attend0.1.refs_0_ = bf16[512,256]{1,0:T(8,128)(2,1)S(1)} custom-call(s32[8]{0:T(128)S(1)} %select_reduce_fusion.2.pos_ref, bf16[4,512,256]{2,1,0:T(8,128)(2,1)S(1)} %copy-done, bf16[512,256]{1,0:T(8,128)(2,1)S(1)} %get-tuple-element.19.v_ref, s32[512,1]{1,0:T(8,128)S(1)} %copy.24.first_ref, s32[512,1]{1,0:T(8,128)S(1)} %copy.25.grp_ref, ...), custom_call_target="tpu_custom_call" | custom-call | tf_op jit(solution)/shard_map/attend0/pallas_call | solution.py:157
  85.4 3.0 %collective-permute-start.30 = (bf16[512,256]{1,0:T(8,128)(2,1)S(1)}, bf16[512,256]{1,0:T(8,128)(2,1)S(1)}, u32[]{:S(2)}, u32[]{:S(2)}) collective-permute-start(bf16[512,256]{1,0:T(8,128)(2,1)S(1)} %attend0.1.refs_0_), channel_id=1, source_target_pairs={{0,2},{1,3},{2,0},{3,1},{4,6},{5,7},{6,4},{7,5},{8,10},{9,11},{10,... | collective-permute-start | bytes 786440 | tf_op jit(solution)/shard_map/ppermute | solution.py:240
  90.4 5.2 %collective-permute-done.28.refs_2_ = bf16[512,256]{1,0:T(8,128)(2,1)S(1)} collective-permute-done((bf16[512,256]{1,0:T(8,128)(2,1)S(1)}, bf16[512,256]{1,0:T(8,128)(2,1)S(1)}, u32[]{:S(2)}, u32[]{:S(2)}) %collective-permute-start.28) | collective-permute-done | bytes 262176 | tf_op jit(solution)/shard_map/ppermute | solution.py:240
  96.1 10.6 %collective-permute-done.30.refs_4_ = bf16[512,256]{1,0:T(8,128)(2,1)S(1)} collective-permute-done((bf16[512,256]{1,0:T(8,128)(2,1)S(1)}, bf16[512,256]{1,0:T(8,128)(2,1)S(1)}, u32[]{:S(2)}, u32[]{:S(2)}) %collective-permute-start.30) | collective-permute-done | bytes 262176 | tf_op jit(solution)/shard_map/ppermute | solution.py:240
  109.4 3.1 %collective-permute-done.40.refs_14_ = bf16[3,128,256]{2,1,0:T(8,128)(2,1)S(1)} collective-permute-done((bf16[3,128,256]{2,1,0:T(8,128)(2,1)S(1)}, bf16[3,128,256]{2,1,0:T(8,128)(2,1)S(1)}, u32[]{:S(2)}, u32[]{:S(2)}) %collective-permute-start.40) | collective-permute-done | bytes 196640 | tf_op jit(solution)/shard_map/ppermute | solution.py:240
  112.6 2.5 %collective-permute-done.43.refs_17_ = bf16[3,128,256]{2,1,0:T(8,128)(2,1)S(1)} collective-permute-done((bf16[3,128,256]{2,1,0:T(8,128)(2,1)S(1)}, bf16[3,128,256]{2,1,0:T(8,128)(2,1)S(1)}, u32[]{:S(2)}, u32[]{:S(2)}) %collective-permute-start.43) | collective-permute-done | bytes 196640 | tf_op jit(solution)/shard_map/ppermute | solution.py:240
  115.1 3.7 %collective-permute-done.44.refs_18_ = bf16[3,128,256]{2,1,0:T(8,128)(2,1)S(1)} collective-permute-done((bf16[3,128,256]{2,1,0:T(8,128)(2,1)S(1)}, bf16[3,128,256]{2,1,0:T(8,128)(2,1)S(1)}, u32[]{:S(2)}, u32[]{:S(2)}) %collective-permute-start.44) | collective-permute-done | bytes 196640 | tf_op jit(solution)/shard_map/ppermute | solution.py:240
  120.1 1.5 collective-permute-start.48
  121.6 7.9 %attend1.1.refs_1_ = bf16[512,256]{1,0:T(8,128)(2,1)S(1)} custom-call(s32[8]{0:T(128)S(1)} %select_reduce_fusion.2.pos_ref, bf16[4,512,256]{2,1,0:T(8,128)(2,1)S(1)} %copy-done, bf16[512,256]{1,0:T(8,128)(2,1)S(1)} %get-tuple-element.18.v_ref, s32[512,1]{1,0:T(8,128)S(1)} %copy.24.first_ref, s32[512,1]{1,0:T(8,128)S(1)} %copy.25.grp_ref, ...), custom_call_target="tpu_custom_call" | custom-call | tf_op jit(solution)/shard_map/attend1/pallas_call | solution.py:157
  129.5 4.2 %collective-permute-start.29 = (bf16[512,256]{1,0:T(8,128)(2,1)S(1)}, bf16[512,256]{1,0:T(8,128)(2,1)S(1)}, u32[]{:S(2)}, u32[]{:S(2)}) collective-permute-start(bf16[512,256]{1,0:T(8,128)(2,1)S(1)} %attend1.1.refs_1_), channel_id=1, source_target_pairs={{0,1},{1,0},{2,3},{3,2},{4,5},{5,4},{6,7},{7,6},{8,9},{9,8},{10,11... | collective-permute-start | bytes 786440 | tf_op jit(solution)/shard_map/ppermute | solution.py:240
  134.6 1.5 collective-permute-start.33
  136.7 7.6 %collective-permute-done.29.refs_3_ = bf16[512,256]{1,0:T(8,128)(2,1)S(1)} collective-permute-done((bf16[512,256]{1,0:T(8,128)(2,1)S(1)}, bf16[512,256]{1,0:T(8,128)(2,1)S(1)}, u32[]{:S(2)}, u32[]{:S(2)}) %collective-permute-start.29) | collective-permute-done | bytes 262176 | tf_op jit(solution)/shard_map/ppermute | solution.py:240
  144.2 10.8 %collective-permute-done.31.refs_5_ = bf16[512,256]{1,0:T(8,128)(2,1)S(1)} collective-permute-done((bf16[512,256]{1,0:T(8,128)(2,1)S(1)}, bf16[512,256]{1,0:T(8,128)(2,1)S(1)}, u32[]{:S(2)}, u32[]{:S(2)}) %collective-permute-start.31) | collective-permute-done | bytes 262176 | tf_op jit(solution)/shard_map/ppermute | solution.py:240
  155.0 4.6 %project.1 = bf16[512,1024]{1,0:T(8,128)(2,1)} custom-call(s32[3]{0:T(128)S(1)} %pad_add_fusion.where_ref, bf16[512,256]{1,0:T(8,128)(2,1)S(1)} %attend0.1.refs_0_, bf16[512,256]{1,0:T(8,128)(2,1)S(1)} %attend1.1.refs_1_, bf16[512,256]{1,0:T(8,128)(2,1)S(1)} %collective-permute-done.28.refs_2_, bf16[512,256]{1,0:T(8,128)(2,1)S(1)} %collective-permute-done.29.refs_3_, ...), custom_call_target="tpu_custom_call" | custom-call | tf_op jit(solution)/shard_map/project/pallas_call | solution.py:224
  (171 shorter events, 36.2 us)
Async XLA Ops:
  3.2 26.3 %collective-permute-start = (bf16[512,256]{1,0:T(8,128)(2,1)S(1)}, bf16[512,256]{1,0:T(8,128)(2,1)S(1)}, u32[]{:S(2)}, u32[]{:S(2)}) collective-permute-start(bf16[512,256]{1,0:T(8,128)(2,1)S(1)} %bitcast.35), channel_id=1, source_target_pairs={{0,4},{4,0},{8,12},{12,8},{16,20},{20,16},{24,28},{28,24},{1,5},{5... | collective-permute-start | bytes 786440 | tf_op jit(solution)/shard_map/ppermute | solution.py:240
  3.7 26.4 %collective-permute-start.1 = (bf16[512,256]{1,0:T(8,128)(2,1)S(1)}, bf16[512,256]{1,0:T(8,128)(2,1)S(1)}, u32[]{:S(2)}, u32[]{:S(2)}) collective-permute-start(bf16[512,256]{1,0:T(8,128)(2,1)S(1)} %bitcast.36), channel_id=1, source_target_pairs={{0,8},{4,12},{8,0},{12,4},{16,24},{20,28},{24,16},{28,20},{1,9},{5... | collective-permute-start | bytes 786440 | tf_op jit(solution)/shard_map/ppermute | solution.py:240
  6.3 24.0 %collective-permute-start.3 = (bf16[512,256]{1,0:T(8,128)(2,1)S(1)}, bf16[512,256]{1,0:T(8,128)(2,1)S(1)}, u32[]{:S(2)}, u32[]{:S(2)}) collective-permute-start(bf16[512,256]{1,0:T(8,128)(2,1)S(1)} %bitcast.37), channel_id=1, source_target_pairs={{0,16},{4,20},{8,24},{12,28},{16,0},{20,4},{24,8},{28,12},{1,17},{... | collective-permute-start | bytes 786440 | tf_op jit(solution)/shard_map/ppermute | solution.py:240
  13.2 11.3 %collective-permute-start.35 = (bf16[256,256]{1,0:T(8,128)(2,1)S(1)}, bf16[256,256]{1,0:T(8,128)(2,1)S(1)}, u32[]{:S(2)}, u32[]{:S(2)}) collective-permute-start(bf16[256,256]{1,0:T(8,128)(2,1)S(1)} %get-tuple-element.16), channel_id=1, source_target_pairs={{0,2},{1,3},{2,0},{3,1},{4,6},{5,7},{6,4},{7,5},{8,10},{9,11},{10,... | collective-permute-start | bytes 393224 | tf_op jit(solution)/shard_map/ppermute | solution.py:240
  18.0 12.8 %collective-permute-start.10 = (bf16[512,256]{1,0:T(8,128)(2,1)S(1)}, bf16[512,256]{1,0:T(8,128)(2,1)S(1)}, u32[]{:S(2)}, u32[]{:S(2)}) collective-permute-start(bf16[512,256]{1,0:T(8,128)(2,1)S(1)} %bitcast.39), channel_id=1, source_target_pairs={{0,16},{4,20},{8,24},{12,28},{16,0},{20,4},{24,8},{28,12},{1,17},{... | collective-permute-start | bytes 786440 | tf_op jit(solution)/shard_map/ppermute | solution.py:240
  30.3 10.4 %collective-permute-start.5 = (bf16[512,256]{1,0:T(8,128)(2,1)S(1)}, bf16[512,256]{1,0:T(8,128)(2,1)S(1)}, u32[]{:S(2)}, u32[]{:S(2)}) collective-permute-start(bf16[512,256]{1,0:T(8,128)(2,1)S(1)} %collective-permute-done.1.rest_2_), channel_id=1, source_target_pairs={{0,16},{4,20},{8,24},{12,28},{16,0},{20,4},{24,8},{28,12},{1,17},{... | collective-permute-start | bytes 786440 | tf_op jit(solution)/shard_map/ppermute | solution.py:240
  30.8 13.0 %collective-permute-start.12 = (bf16[512,256]{1,0:T(8,128)(2,1)S(1)}, bf16[512,256]{1,0:T(8,128)(2,1)S(1)}, u32[]{:S(2)}, u32[]{:S(2)}) collective-permute-start(bf16[512,256]{1,0:T(8,128)(2,1)S(1)} %collective-permute-done.10.rest_12_), channel_id=1, source_target_pairs={{0,8},{4,12},{8,0},{12,4},{16,24},{20,28},{24,16},{28,20},{1,9},{5... | collective-permute-start | bytes 786440 | tf_op jit(solution)/shard_map/ppermute | solution.py:240
  34.2 13.3 %collective-permute-start.11 = (bf16[512,256]{1,0:T(8,128)(2,1)S(1)}, bf16[512,256]{1,0:T(8,128)(2,1)S(1)}, u32[]{:S(2)}, u32[]{:S(2)}) collective-permute-start(bf16[512,256]{1,0:T(8,128)(2,1)S(1)} %collective-permute-done.10.rest_12_), channel_id=1, source_target_pairs={{0,4},{4,0},{8,12},{12,8},{16,20},{20,16},{24,28},{28,24},{1,5},{5... | collective-permute-start | bytes 786440 | tf_op jit(solution)/shard_map/ppermute | solution.py:240
  50.0 11.9 %collective-permute-start.24 = (bf16[512,256]{1,0:T(8,128)(2,1)S(1)}, bf16[512,256]{1,0:T(8,128)(2,1)}, u32[]{:S(2)}, u32[]{:S(2)}) collective-permute-start(bf16[512,256]{1,0:T(8,128)(2,1)S(1)} %get-tuple-element.10.rest_8_), channel_id=1, source_target_pairs={{0,16},{4,20},{8,24},{12,28},{16,0},{20,4},{24,8},{28,12},{1,17},{... | collective-permute-start | bytes 786440 | tf_op jit(solution)/shard_map/ppermute | solution.py:240
  54.1 30.5 %collective-permute-start.22 = (bf16[512,256]{1,0:T(8,128)(2,1)S(1)}, bf16[512,256]{1,0:T(8,128)(2,1)}, u32[]{:S(2)}, u32[]{:S(2)}) collective-permute-start(bf16[512,256]{1,0:T(8,128)(2,1)S(1)} %get-tuple-element.10.rest_8_), channel_id=1, source_target_pairs={{0,8},{4,12},{8,0},{12,4},{16,24},{20,28},{24,16},{28,20},{1,9},{5... | collective-permute-start | bytes 786440 | tf_op jit(solution)/shard_map/ppermute | solution.py:240
  55.6 29.1 %collective-permute-start.16 = (bf16[512,256]{1,0:T(8,128)(2,1)S(1)}, bf16[512,256]{1,0:T(8,128)(2,1)}, u32[]{:S(2)}, u32[]{:S(2)}) collective-permute-start(bf16[512,256]{1,0:T(8,128)(2,1)S(1)} %collective-permute-done.15.rest_2_), channel_id=1, source_target_pairs={{0,4},{4,0},{8,12},{12,8},{16,20},{20,16},{24,28},{28,24},{1,5},{5... | collective-permute-start | bytes 786440 | tf_op jit(solution)/shard_map/ppermute | solution.py:240
  57.5 27.3 %collective-permute-start.18 = (bf16[512,256]{1,0:T(8,128)(2,1)}, bf16[512,256]{1,0:T(8,128)(2,1)}, u32[]{:S(2)}, u32[]{:S(2)}) collective-permute-start(bf16[512,256]{1,0:T(8,128)(2,1)} %collective-permute-done.17.rest_4_), channel_id=1, source_target_pairs={{0,4},{4,0},{8,12},{12,8},{16,20},{20,16},{24,28},{28,24},{1,5},{5... | collective-permute-start | bytes 786440 | tf_op jit(solution)/shard_map/ppermute | solution.py:240
  60.5 24.8 %collective-permute-start.19 = (bf16[512,256]{1,0:T(8,128)(2,1)S(1)}, bf16[512,256]{1,0:T(8,128)(2,1)}, u32[]{:S(2)}, u32[]{:S(2)}) collective-permute-start(bf16[512,256]{1,0:T(8,128)(2,1)S(1)} %collective-permute-done.15.rest_2_), channel_id=1, source_target_pairs={{0,16},{4,20},{8,24},{12,28},{16,0},{20,4},{24,8},{28,12},{1,17},{... | collective-permute-start | bytes 786440 | tf_op jit(solution)/shard_map/ppermute | solution.py:240
  61.9 26.5 %collective-permute-start.26 = (bf16[512,256]{1,0:T(8,128)(2,1)}, bf16[512,256]{1,0:T(8,128)(2,1)}, u32[]{:S(2)}, u32[]{:S(2)}) collective-permute-start(bf16[512,256]{1,0:T(8,128)(2,1)} %collective-permute-done.24.rest_12_), channel_id=1, source_target_pairs={{0,8},{4,12},{8,0},{12,4},{16,24},{20,28},{24,16},{28,20},{1,9},{5... | collective-permute-start | bytes 786440 | tf_op jit(solution)/shard_map/ppermute | solution.py:240
  84.6 11.0 %collective-permute-start.28 = (bf16[512,256]{1,0:T(8,128)(2,1)S(1)}, bf16[512,256]{1,0:T(8,128)(2,1)S(1)}, u32[]{:S(2)}, u32[]{:S(2)}) collective-permute-start(bf16[512,256]{1,0:T(8,128)(2,1)S(1)} %attend0.1.refs_0_), channel_id=1, source_target_pairs={{0,1},{1,0},{2,3},{3,2},{4,5},{5,4},{6,7},{7,6},{8,9},{9,8},{10,11... | collective-permute-start | bytes 786440 | tf_op jit(solution)/shard_map/ppermute | solution.py:240
  85.4 21.4 %collective-permute-start.30 = (bf16[512,256]{1,0:T(8,128)(2,1)S(1)}, bf16[512,256]{1,0:T(8,128)(2,1)S(1)}, u32[]{:S(2)}, u32[]{:S(2)}) collective-permute-start(bf16[512,256]{1,0:T(8,128)(2,1)S(1)} %attend0.1.refs_0_), channel_id=1, source_target_pairs={{0,2},{1,3},{2,0},{3,1},{4,6},{5,7},{6,4},{7,5},{8,10},{9,11},{10,... | collective-permute-start | bytes 786440 | tf_op jit(solution)/shard_map/ppermute | solution.py:240
  88.4 18.9 %collective-permute-start.32 = (bf16[512,256]{1,0:T(8,128)(2,1)S(1)}, bf16[512,256]{1,0:T(8,128)(2,1)S(1)}, u32[]{:S(2)}, u32[]{:S(2)}) collective-permute-start(bf16[512,256]{1,0:T(8,128)(2,1)S(1)} %attend0.1.refs_0_), channel_id=1, source_target_pairs={{0,3},{1,2},{2,1},{3,0},{4,7},{5,6},{6,5},{7,4},{8,11},{9,10},{10,... | collective-permute-start | bytes 786440 | tf_op jit(solution)/shard_map/ppermute | solution.py:240
  89.8 17.5 %collective-permute-start.37 = (bf16[3,128,256]{2,1,0:T(8,128)(2,1)S(1)}, bf16[3,128,256]{2,1,0:T(8,128)(2,1)S(1)}, u32[]{:S(2)}, u32[]{:S(2)}) collective-permute-start(bf16[3,128,256]{2,1,0:T(8,128)(2,1)S(1)} %get-tuple-element.11.refs_9_), channel_id=1, source_target_pairs={{0,4},{4,0},{8,12},{12,8},{16,20},{20,16},{24,28},{28,24},{1,5},{5... | collective-permute-start | bytes 589832 | tf_op jit(solution)/shard_map/ppermute | solution.py:240
  89.9 18.2 %collective-permute-start.38 = (bf16[3,128,256]{2,1,0:T(8,128)(2,1)S(1)}, bf16[3,128,256]{2,1,0:T(8,128)(2,1)S(1)}, u32[]{:S(2)}, u32[]{:S(2)}) collective-permute-start(bf16[3,128,256]{2,1,0:T(8,128)(2,1)S(1)} %get-tuple-element.12.refs_10_), channel_id=1, source_target_pairs={{0,4},{4,0},{8,12},{12,8},{16,20},{20,16},{24,28},{28,24},{1,5},{5... | collective-permute-start | bytes 589832 | tf_op jit(solution)/shard_map/ppermute | solution.py:240
  95.6 13.8 %collective-permute-start.39 = (bf16[3,128,256]{2,1,0:T(8,128)(2,1)S(1)}, bf16[3,128,256]{2,1,0:T(8,128)(2,1)S(1)}, u32[]{:S(2)}, u32[]{:S(2)}) collective-permute-start(bf16[3,128,256]{2,1,0:T(8,128)(2,1)S(1)} %get-tuple-element.11.refs_9_), channel_id=1, source_target_pairs={{0,8},{4,12},{8,0},{12,4},{16,24},{20,28},{24,16},{28,20},{1,9},{5... | collective-permute-start | bytes 589832 | tf_op jit(solution)/shard_map/ppermute | solution.py:240
  107.3 11.5 %collective-permute-start.20 = (bf16[512,256]{1,0:T(8,128)(2,1)}, bf16[512,256]{1,0:T(8,128)(2,1)S(1)}, u32[]{:S(2)}, u32[]{:S(2)}) collective-permute-start(bf16[512,256]{1,0:T(8,128)(2,1)} %collective-permute-done.19.rest_6_), channel_id=1, source_target_pairs={{0,4},{4,0},{8,12},{12,8},{16,20},{20,16},{24,28},{28,24},{1,5},{5... | collective-permute-start | bytes 786440 | tf_op jit(solution)/shard_map/ppermute | solution.py:240
  108.1 10.8 %collective-permute-start.44 = (bf16[3,128,256]{2,1,0:T(8,128)(2,1)S(1)}, bf16[3,128,256]{2,1,0:T(8,128)(2,1)S(1)}, u32[]{:S(2)}, u32[]{:S(2)}) collective-permute-start(bf16[3,128,256]{2,1,0:T(8,128)(2,1)S(1)} %get-tuple-element.12.refs_10_), channel_id=1, source_target_pairs={{0,16},{4,20},{8,24},{12,28},{16,0},{20,4},{24,8},{28,12},{1,17},{... | collective-permute-start | bytes 589832 | tf_op jit(solution)/shard_map/ppermute | solution.py:240
  115.1 14.4 %collective-permute-start.42 = (bf16[3,128,256]{2,1,0:T(8,128)(2,1)S(1)}, bf16[3,128,256]{2,1,0:T(8,128)(2,1)S(1)}, u32[]{:S(2)}, u32[]{:S(2)}) collective-permute-start(bf16[3,128,256]{2,1,0:T(8,128)(2,1)S(1)} %collective-permute-done.40.refs_14_), channel_id=1, source_target_pairs={{0,4},{4,0},{8,12},{12,8},{16,20},{20,16},{24,28},{28,24},{1,5},{5... | collective-permute-start | bytes 589832 | tf_op jit(solution)/shard_map/ppermute | solution.py:240
  118.9 14.8 %collective-permute-start.45 = (bf16[3,128,256]{2,1,0:T(8,128)(2,1)S(1)}, bf16[3,128,256]{2,1,0:T(8,128)(2,1)S(1)}, u32[]{:S(2)}, u32[]{:S(2)}) collective-permute-start(bf16[3,128,256]{2,1,0:T(8,128)(2,1)S(1)} %collective-permute-done.43.refs_17_), channel_id=1, source_target_pairs={{0,4},{4,0},{8,12},{12,8},{16,20},{20,16},{24,28},{28,24},{1,5},{5... | collective-permute-start | bytes 589832 | tf_op jit(solution)/shard_map/ppermute | solution.py:240
  118.9 15.8 %collective-permute-start.46 = (bf16[3,128,256]{2,1,0:T(8,128)(2,1)S(1)}, bf16[3,128,256]{2,1,0:T(8,128)(2,1)S(1)}, u32[]{:S(2)}, u32[]{:S(2)}) collective-permute-start(bf16[3,128,256]{2,1,0:T(8,128)(2,1)S(1)} %collective-permute-done.44.refs_18_), channel_id=1, source_target_pairs={{0,4},{4,0},{8,12},{12,8},{16,20},{20,16},{24,28},{28,24},{1,5},{5... | collective-permute-start | bytes 589832 | tf_op jit(solution)/shard_map/ppermute | solution.py:240
  119.4 16.7 %collective-permute-start.47 = (bf16[3,128,256]{2,1,0:T(8,128)(2,1)S(1)}, bf16[3,128,256]{2,1,0:T(8,128)(2,1)S(1)}, u32[]{:S(2)}, u32[]{:S(2)}) collective-permute-start(bf16[3,128,256]{2,1,0:T(8,128)(2,1)S(1)} %collective-permute-done.39.refs_13_), channel_id=1, source_target_pairs={{0,16},{4,20},{8,24},{12,28},{16,0},{20,4},{24,8},{28,12},{1,17},{... | collective-permute-start | bytes 589832 | tf_op jit(solution)/shard_map/ppermute | solution.py:240
  120.1 16.0 %collective-permute-start.48 = (bf16[3,128,256]{2,1,0:T(8,128)(2,1)S(1)}, bf16[3,128,256]{2,1,0:T(8,128)(2,1)S(1)}, u32[]{:S(2)}, u32[]{:S(2)}) collective-permute-start(bf16[3,128,256]{2,1,0:T(8,128)(2,1)S(1)} %collective-permute-done.44.refs_18_), channel_id=1, source_target_pairs={{0,8},{4,12},{8,0},{12,4},{16,24},{20,28},{24,16},{28,20},{1,9},{5... | collective-permute-start | bytes 589832 | tf_op jit(solution)/shard_map/ppermute | solution.py:240
  129.5 14.8 %collective-permute-start.29 = (bf16[512,256]{1,0:T(8,128)(2,1)S(1)}, bf16[512,256]{1,0:T(8,128)(2,1)S(1)}, u32[]{:S(2)}, u32[]{:S(2)}) collective-permute-start(bf16[512,256]{1,0:T(8,128)(2,1)S(1)} %attend1.1.refs_1_), channel_id=1, source_target_pairs={{0,1},{1,0},{2,3},{3,2},{4,5},{5,4},{6,7},{7,6},{8,9},{9,8},{10,11... | collective-permute-start | bytes 786440 | tf_op jit(solution)/shard_map/ppermute | solution.py:240
  133.6 21.4 %collective-permute-start.31 = (bf16[512,256]{1,0:T(8,128)(2,1)S(1)}, bf16[512,256]{1,0:T(8,128)(2,1)S(1)}, u32[]{:S(2)}, u32[]{:S(2)}) collective-permute-start(bf16[512,256]{1,0:T(8,128)(2,1)S(1)} %attend1.1.refs_1_), channel_id=1, source_target_pairs={{0,2},{1,3},{2,0},{3,1},{4,6},{5,7},{6,4},{7,5},{8,10},{9,11},{10,... | collective-permute-start | bytes 786440 | tf_op jit(solution)/shard_map/ppermute | solution.py:240
  134.6 20.4 %collective-permute-start.33 = (bf16[512,256]{1,0:T(8,128)(2,1)S(1)}, bf16[512,256]{1,0:T(8,128)(2,1)S(1)}, u32[]{:S(2)}, u32[]{:S(2)}) collective-permute-start(bf16[512,256]{1,0:T(8,128)(2,1)S(1)} %attend1.1.refs_1_), channel_id=1, source_target_pairs={{0,3},{1,2},{2,1},{3,0},{4,7},{5,6},{6,5},{7,4},{8,11},{9,10},{10,... | collective-permute-start | bytes 786440 | tf_op jit(solution)/shard_map/ppermute | solution.py:240
  136.1 18.9 %collective-permute-start.49 = (bf16[3,128,256]{2,1,0:T(8,128)(2,1)S(1)}, bf16[3,128,256]{2,1,0:T(8,128)(2,1)S(1)}, u32[]{:S(2)}, u32[]{:S(2)}) collective-permute-start(bf16[3,128,256]{2,1,0:T(8,128)(2,1)S(1)} %collective-permute-done.47.refs_21_), channel_id=1, source_target_pairs={{0,4},{4,0},{8,12},{12,8},{16,20},{20,16},{24,28},{28,24},{1,5},{5... | collective-permute-start | bytes 589832 | tf_op jit(solution)/shard_map/ppermute | solution.py:240
  136.1 18.9 %collective-permute-start.50 = (bf16[3,128,256]{2,1,0:T(8,128)(2,1)S(1)}, bf16[3,128,256]{2,1,0:T(8,128)(2,1)S(1)}, u32[]{:S(2)}, u32[]{:S(2)}) collective-permute-start(bf16[3,128,256]{2,1,0:T(8,128)(2,1)S(1)} %collective-permute-done.48.refs_22_), channel_id=1, source_target_pairs={{0,4},{4,0},{8,12},{12,8},{16,20},{20,16},{24,28},{28,24},{1,5},{5... | collective-permute-start | bytes 589832 | tf_op jit(solution)/shard_map/ppermute | solution.py:240
  (54 other events, 430.9 us)

commit v2 on v0

v2 whole, which is shorter than its diff:
```python
import functools
import jax
import jax.numpy as jnp
from jax import lax
from jax.experimental import pallas as pl
from jax.experimental.pallas import tpu as pltpu
from jax.sharding import PartitionSpec as P

HD = 256
ROT = 64
BLK = 512
OWNERS = 2
GROUPS = 4
SLOTS = GROUPS * OWNERS
MOST = 128
SEEN = OWNERS * BLK

NEG_FILL = -1e30
ROPE_BASE = 10000.0
FACTOR = HD ** (-0.5) * 1.4426950408889634

RB = 128
VCHUNKS = 2

VMEM = pl.BlockSpec(memory_space=pltpu.VMEM)
SMEM = pl.BlockSpec(memory_space=pltpu.SMEM)
HBM = pl.BlockSpec(memory_space=pltpu.HBM)


def from_root(x, axis, root):
    mine = lax.axis_index(axis) == root
    return lax.psum(jnp.where(mine, x, jnp.zeros_like(x)), axis)


def token_layout(length_row, group_row, row_count):
    span_end = jnp.cumsum(length_row)
    starts = span_end - length_row
    row_ids = jnp.arange(row_count, dtype=jnp.int32)
    member = (
        (row_ids[:, None] >= starts[None, :]) & (row_ids[:, None] < span_end[None, :])
    ).astype(jnp.int32)
    first_row = jnp.sum(member * starts[None, :], axis=1)
    tok_group = jnp.sum(member * group_row[None, :], axis=1)
    return row_ids, first_row, tok_group


def rope_tables(positions):
    inverse = ROPE_BASE ** (-2.0 * jnp.arange(ROT // 2, dtype=jnp.float32) / ROT)
    inverse = jnp.concatenate([jnp.repeat(inverse, 2), jnp.zeros((128 - ROT,), jnp.float32)])
    angles = positions.astype(jnp.float32)[:, None] * inverse[None, :]
    sign = jnp.where(jnp.arange(128) % 2 == 0, -1.0, 1.0).astype(jnp.float32)
    return jnp.cos(angles), jnp.sin(angles) * sign[None, :]


def prep_kernel(flip_ref, q_ref, k_ref, v_ref, cos_ref, sin_ref, *o_refs):
    rows = q_ref.shape[0]
    lane = lax.broadcasted_iota(jnp.int32, (rows, 128), 1)
    even = (lane % 2) == 0
    cos = cos_ref[...]
    sin = sin_ref[...]
    heads = len(o_refs)
    for i, o_ref in enumerate(o_refs):
        for flip in range(heads):

            @pl.when(flip_ref[0] == flip)
            def _():
                c0 = (i ^ flip) * HD
                for n, ref in enumerate((q_ref, k_ref)):
                    x = ref[:, c0 : c0 + 128].astype(jnp.float32)
                    swapped = jnp.where(even, pltpu.roll(x, 127, 1), pltpu.roll(x, 1, 1))
                    o_ref[n, :, 0:128] = (x * cos + swapped * sin).astype(jnp.bfloat16)
                    o_ref[n, :, 128:HD] = ref[:, c0 + 128 : c0 + HD]
                o_ref[2] = v_ref[:, c0 : c0 + HD]


def prepare(flip, q, k, v, cos, sin):
    rows, feat = q.shape
    heads = feat // HD
    return pl.pallas_call(
        prep_kernel,
        out_shape=[jax.ShapeDtypeStruct((3, rows, HD), jnp.bfloat16)] * heads,
        in_specs=[SMEM] + [VMEM] * 5,
        out_specs=[VMEM] * heads,
        compiler_params=pltpu.CompilerParams(vmem_limit_bytes=3 << 20),
        name="prepare",
    )(flip, q, k, v, cos, sin)


def fetch(pieces, members, place_ref, store, sems):
    copies = []
    for piece, member in zip(pieces, members):
        for j, d in enumerate(member):
            copies.append(
                pltpu.make_async_copy(piece.at[j], store.at[place_ref[d]], sems.at[d])
            )
    for c in copies:
        c.start()
    return copies


def score_kernel(nb, members, place_ref, here_ref, first_ref, grp_ref, *rest):
    sufs = rest[:nb]
    pieces = rest[nb : nb + len(members)]
    p_ref, near_ref, den_ref, ks, sc, sems = rest[nb + len(members) :]
    copies = fetch(pieces, members, place_ref, ks, sems)
    for c in copies:
        c.wait()
    half = 256
    for n in range(nb):
        rows = sufs[n].shape[1]
        for b in range(rows // RB):
            r0 = b * RB
            t0 = n * rows + r0
            blk = t0 // RB
            buf = blk % 2
            q = sufs[n][0, r0 : r0 + RB, :]
            grp = jnp.broadcast_to(grp_ref[t0 : t0 + RB, :], (RB, half))
            for g in range(GROUPS):

                @pl.when(here_ref[blk * GROUPS + g] > 0)
                def _():
                    for o in range(OWNERS):
                        for j in range(BLK // half):
                            s = lax.dot_general(
                                q,
                                ks[g * OWNERS + o, j * half : (j + 1) * half, :],
                                (((1,), (1,)), ((), ())),
                                preferred_element_type=jnp.float32,
                            )
                            c0 = o * BLK + j * half
                            sc[buf, :, c0 : c0 + half] = jnp.where(
                                grp == g, s, sc[buf, :, c0 : c0 + half]
                            )

            lo = max(0, r0 - MOST)
            width = r0 + RB - lo
            local = lax.dot_general(
                q,
                sufs[n][1, lo : r0 + RB, :],
                (((1,), (1,)), ((), ())),
                preferred_element_type=jnp.float32,
            )
            row = r0 + lax.broadcasted_iota(jnp.int32, (RB, width), 0)
            key = lo + lax.broadcasted_iota(jnp.int32, (RB, width), 1)
            start = jnp.broadcast_to(first_ref[t0 : t0 + RB, :], (RB, width))
            local = jnp.where((key <= row) & (key >= start), local, NEG_FILL)
            top = jnp.max(local, axis=1, keepdims=True)
            whole = sc[buf, :, 0:half]
            for c0 in range(half, SEEN, half):
                whole = jnp.maximum(whole, sc[buf, :, c0 : c0 + half])
            top = jnp.maximum(top, jnp.max(whole, axis=1, keepdims=True))
            e = jnp.exp2((local - top) * FACTOR)
            den = jnp.sum(e, axis=1, keepdims=True)
            near_ref[t0 : t0 + RB, 0:width] = e.astype(jnp.bfloat16)
            total = None
            for c0 in range(0, SEEN, half):
                e = jnp.exp2((sc[buf, :, c0 : c0 + half] - top) * FACTOR)
                p_ref[t0 : t0 + RB, c0 : c0 + half] = e.astype(jnp.bfloat16)
                total = e if total is None else total + e
            den = den + jnp.sum(total, axis=1, keepdims=True)
            den_ref[t0 : t0 + RB, :] = jnp.broadcast_to(den, (RB, 128))


def score(place, here, first, grp, sufs, pieces, members):
    rows = sum(s.shape[1] for s in sufs)
    return pl.pallas_call(
        functools.partial(score_kernel, len(sufs), members),
        out_shape=[
            jax.ShapeDtypeStruct((rows, SEEN), jnp.bfloat16),
            jax.ShapeDtypeStruct((rows, RB + MOST), jnp.bfloat16),
            jax.ShapeDtypeStruct((rows, 128), jnp.float32),
        ],
        in_specs=[SMEM, SMEM] + [VMEM] * (2 + len(sufs)) + [HBM] * len(pieces),
        out_specs=[VMEM] * 3,
        scratch_shapes=[
            pltpu.VMEM((SLOTS, BLK, HD), jnp.bfloat16),
            pltpu.VMEM((2, RB, SEEN), jnp.float32),
            pltpu.SemaphoreType.DMA((SLOTS,)),
        ],
        compiler_params=pltpu.CompilerParams(vmem_limit_bytes=5 << 20),
        name="score",
    )(place, here, first, grp, *sufs, *pieces)


def mix_kernel(nb, members, col, place_ref, here_ref, grp_ref, p_ref, near_ref, den_ref, *rest):
    sufs = rest[:nb]
    pieces = rest[nb : nb + len(members)]
    outs = rest[nb + len(members) : nb + len(members) + nb]
    vs, acc, sems = rest[nb + len(members) + nb :]
    width = outs[0].shape[1]
    copies = fetch(pieces, members, place_ref, vs, sems)
    for c in copies:
        c.wait()
    for n in range(nb):
        rows = outs[n].shape[0]
        for b in range(rows // RB):
            r0 = b * RB
            t0 = n * rows + r0
            blk = t0 // RB
            buf = blk % 2
            grp = jnp.broadcast_to(grp_ref[t0 : t0 + RB, :], (RB, width))
            for g in range(GROUPS):

                @pl.when(here_ref[blk * GROUPS + g] > 0)
                def _():
                    part = jnp.zeros((RB, width), jnp.float32)
                    for o in range(OWNERS):
                        part = part + jnp.dot(
                            p_ref[t0 : t0 + RB, o * BLK : (o + 1) * BLK],
                            vs[g * OWNERS + o],
                            preferred_element_type=jnp.float32,
                        )
                    acc[buf] = jnp.where(grp == g, part, acc[buf])

            lo = max(0, r0 - MOST)
            near = jnp.dot(
                near_ref[t0 : t0 + RB, 0 : r0 + RB - lo],
                sufs[n][2, lo : r0 + RB, col : col + width],
                preferred_element_type=jnp.float32,
            )
            den = den_ref[t0 : t0 + RB, :]
            if width > 128:
                den = jnp.concatenate([den] * (width // 128), axis=1)
            outs[n][r0 : r0 + RB, :] = ((near + acc[buf]) / den).astype(jnp.bfloat16)


def mix(col, width, place, here, grp, scored, sufs, pieces, members):
    rows = sufs[0].shape[1]
    nb = len(sufs)
    return pl.pallas_call(
        functools.partial(mix_kernel, nb, members, col),
        out_shape=[jax.ShapeDtypeStruct((rows, width), jnp.bfloat16)] * nb,
        in_specs=[SMEM, SMEM] + [VMEM] * (4 + nb) + [HBM] * len(pieces),
        out_specs=[VMEM] * nb,
        scratch_shapes=[
            pltpu.VMEM((SLOTS, BLK, width), jnp.bfloat16),
            pltpu.VMEM((2, RB, width), jnp.float32),
            pltpu.SemaphoreType.DMA((SLOTS,)),
        ],
        compiler_params=pltpu.CompilerParams(vmem_limit_bytes=3 << 20),
        name="mix",
    )(place, here, grp, *scored, *sufs, *pieces)


def proj_kernel(where_ref, *refs):
    n_att = VCHUNKS * 2 * 5
    att = refs[:n_att]
    w_ref, gathered, o_ref, own, far, sems = refs[n_att:]
    cols = o_ref.shape[1]
    rows = o_ref.shape[0]
    z = where_ref[0]
    core = where_ref[1]
    copies = []
    for h in range(2):
        copies.append(
            pltpu.make_async_copy(
                w_ref.at[
                    h * HD : (h + 1) * HD, pl.ds(pl.multiple_of(z * cols, cols), cols)
                ],
                own.at[h],
                sems.at[h],
            )
        )
    for r in range(8):
        copies.append(
            pltpu.make_async_copy(
                gathered.at[r],
                far.at[:, r & 1, :, (r >> 1) * HD : (r >> 1) * HD + HD],
                sems.at[2 + r],
            )
        )
    for c in copies:
        c.start()
    for c in copies:
        c.wait()
    for n in range(cols // HD):
        c0 = n * HD
        acc = jnp.zeros((rows, HD), jnp.float32)
        for h in range(2):
            head = lax.bitwise_xor(core, h)
            for m in range(4):
                part = []
                for i in range(VCHUNKS):
                    at = (i * 2 + h) * 5 + m
                    a = att[at][...]
                    if m == 3:
                        a = a + att[at + 1][...]
                    part.append(a)
                a = jnp.concatenate(part, axis=1)
                if m == 0:
                    w = own[head, :, c0 : c0 + HD]
                else:
                    w = far[m - 1, head, :, c0 : c0 + HD]
                acc = acc + jnp.dot(a, w, preferred_element_type=jnp.float32)
        o_ref[:, c0 : c0 + HD] = acc.astype(jnp.bfloat16)


def project(where, att, w, gathered, cols):
    rows = att[0].shape[0]
    return pl.pallas_call(
        proj_kernel,
        out_shape=jax.ShapeDtypeStruct((rows, cols), jnp.bfloat16),
        in_specs=[SMEM] + [VMEM] * len(att) + [HBM] * 2,
        out_specs=VMEM,
        scratch_shapes=[
            pltpu.VMEM((2, HD, cols), jnp.bfloat16),
            pltpu.VMEM((3, 2, HD, cols), jnp.bfloat16),
            pltpu.SemaphoreType.DMA((10,)),
        ],
        compiler_params=pltpu.CompilerParams(vmem_limit_bytes=7 << 20),
        name="project",
    )(where, *att, w, gathered)


def swap(x, axis, mask, size):
    return lax.ppermute(x, axis, [(i, i ^ mask) for i in range(size)])


def after(x, *deps):
    return lax.optimization_barrier((x,) + deps)[0]


over_x = functools.partial(swap, axis="req", mask=2, size=8)
over_y = functools.partial(swap, axis="req", mask=4, size=8)
over_core = functools.partial(swap, axis="req", mask=1, size=8)


def blocks_here(grp):
    blocks = grp.reshape(-1, RB)
    kinds = jnp.arange(GROUPS, dtype=jnp.int32)
    return jnp.any(blocks[:, None, :] == kinds[None, :, None], axis=2).astype(jnp.int32).reshape(-1)


def split_heads(suffix_heads, prefix_cache, lengths, groups, owners, out_weight):
    rows = suffix_heads.shape[0]
    me = lax.axis_index("req")
    z = lax.axis_index("tp")
    core = me % 2
    tp_size = 4
    first_head = core == 0

    k = prefix_cache[:, 0]
    v = prefix_cache[:, 1]
    k_own = jnp.where(first_head, k[:, :HD], k[:, HD:])
    k_other = jnp.where(first_head, k[:, HD:], k[:, :HD])
    ax = over_x(k_own)
    ay = over_y(k_own)
    k_pair = over_core(k_other)
    bx = over_x(k_pair)
    by = over_y(k_pair)
    axy = over_y(ax)
    bxy = over_x(by)
    k_pieces = [p[None] for p in (k_own, k_pair, ax, bx, ay, by, axy, bxy)]
    k_members = tuple((d,) for d in range(SLOTS))

    v_own = jnp.where(first_head, v[:, :HD], v[:, HD:])
    v_other = jnp.where(first_head, v[:, HD:], v[:, :HD])
    v_pair = over_core(after(v_other, ax, ay))
    width = HD // VCHUNKS
    v_pieces = []
    gate = (axy, bxy)
    for i in range(VCHUNKS):
        c0 = i * width
        both = jnp.stack([v_own[:, c0 : c0 + width], v_pair[:, c0 : c0 + width]])
        both = after(both, *gate)
        vx = over_x(both)
        vy = over_y(both)
        vxy0 = over_y(vx[0:1])
        vxy1 = over_x(vy[1:2])
        v_pieces.append((both, vx, vy, vxy0, vxy1))
        gate = (vx, vy)
    v_members = ((0, 1), (2, 3), (4, 5), (6,), (7,))

    cols = out_weight.shape[1] // tp_size
    pieces = [None] * 3
    gates = ((axy, bxy), (bx, by), (ax, ay))
    last = ()
    for m in (3, 2, 1):
        piece = lax.dynamic_slice(
            out_weight, (core * HD, (z ^ m) * cols + (me // 2) * HD), (HD, HD)
        )
        piece = after(piece, *gates[m - 1], *last)
        pieces[m - 1] = swap(piece, "tp", m, tp_size)
        last = (pieces[m - 1],)
    gathered = lax.all_gather(after(jnp.stack(pieces), v_pieces[0][1], v_pieces[0][2]), "req")

    flat_owner = owners.reshape(-1)
    place = jnp.sum(
        jnp.where(
            flat_owner[None, :] == (me ^ jnp.arange(SLOTS, dtype=jnp.int32))[:, None],
            jnp.arange(SLOTS, dtype=jnp.int32)[None, :],
            0,
        ),
        axis=1,
    ).astype(jnp.int32)

    table = jnp.concatenate([lengths, groups], axis=0)
    table_pair = over_core(table)
    row_ids, first, grp = token_layout(table[0], table[1], rows)
    _, first_pair, grp_pair = token_layout(table_pair[0], table_pair[1], rows)
    cos, sin = rope_tables(OWNERS * BLK + row_ids - first)
    first = jnp.concatenate([first, first_pair])
    grp = jnp.concatenate([grp, grp_pair])
    here = blocks_here(grp)
    first = first[:, None]
    grp = grp[:, None]
    mine, other = prepare(
        core[None].astype(jnp.int32),
        suffix_heads[:, 0],
        suffix_heads[:, 1],
        suffix_heads[:, 2],
        cos,
        sin,
    )
    sufs = [mine, over_core(other)]

    scored = score(place, here, first, grp, sufs, k_pieces, k_members)
    att = []
    for i in range(VCHUNKS):
        own, pair = mix(i * width, width, place, here, grp, scored, sufs, v_pieces[i], v_members)
        back = over_core(pair)
        for a in (own, back):
            one = swap(a, "tp", 1, tp_size)
            two = swap(a, "tp", 2, tp_size)
            three = lax.ppermute(a, "tp", [(1, 2), (2, 1)])
            forward = lax.ppermute(two, "tp", [(2, 3), (1, 0)])
            att += [a, one, two, three, forward]
    where = jnp.stack([z, core]).astype(jnp.int32)
    return project(where, att, out_weight, gathered, cols)


def whole_heads(suffix_heads, prefix_cache, lengths, groups, owners, out_weight):
    rows = suffix_heads.shape[0]
    heads = suffix_heads.shape[2] // HD
    flat_owner = owners.reshape(-1)
    received = [from_root(prefix_cache, "req", flat_owner[i]) for i in range(SLOTS)]
    row_ids, first, grp = token_layout(lengths[0], groups[0], rows)
    cos, sin = rope_tables(OWNERS * BLK + row_ids - first)
    place = jnp.arange(SLOTS, dtype=jnp.int32)
    here = blocks_here(grp)
    first = first[:, None]
    grp = grp[:, None]
    sufs = prepare(
        jnp.zeros((1,), jnp.int32),
        suffix_heads[:, 0],
        suffix_heads[:, 1],
        suffix_heads[:, 2],
        cos,
        sin,
    )
    members = tuple((d,) for d in range(SLOTS))
    attended = []
    for h in range(heads):
        keys = [s[None, :, 0, h * HD : (h + 1) * HD] for s in received]
        values = [s[None, :, 1, h * HD : (h + 1) * HD] for s in received]
        scored = score(place, here, first, grp, [sufs[h]], keys, members)
        attended += mix(0, HD, place, here, grp, scored, [sufs[h]], values, members)
    partial_out = jnp.dot(
        jnp.concatenate(attended, axis=1), out_weight, preferred_element_type=jnp.float32
    )
    return lax.psum_scatter(partial_out.astype(jnp.bfloat16), "tp", scatter_dimension=1, tiled=True)


def per_device(req_size, tp_size, *args):
    if req_size == 8 and tp_size == 4 and args[0].shape[2] == 2 * HD:
        return split_heads(*args)
    return whole_heads(*args)


def solution(mesh):
    placed = (
        P("req", None, "tp"),
        P("req", None, "tp"),
        P("req", None),
        P("req", None),
        P(),
        P("tp", None),
    )
    return jax.shard_map(
        functools.partial(per_device, mesh.shape["req"], mesh.shape["tp"]),
        mesh=mesh,
        in_specs=placed,
        out_specs=P("req", "tp"),
        check_vma=False,
    )
```

time: 267 us -> 151 us (0.57)
  waiting for transfers between devices: 205 us -> 31.8 us
  starting transfers between devices: 0.04 us -> 49.9 us
  Pallas kernels: 0 us -> 29.1 us
  matrix products: 17.3 us -> 0 us
  between operations: 18.7 us -> 13.9 us
  local copies, waits for them, and re-layouts: 17.4 us -> 21.9 us
  other arithmetic: 7.3 us -> 2.93 us
    psum x1 -> x0, waiting for transfers between devices: 128 us -> none  [from_root(): return lax.psum(jnp.where(mine, x, jnp.zeros_like(x)), axis)]
    reduce_scatter x1 -> x0, waiting for transfers between devices: 77.2 us -> none  [per_device(): lax.psum_scatter(partial_out.astype(jnp.bfloat16), 'tp', scatter_dimensio...]
    ppermute x0 -> x39, starting transfers between devices: none -> 49.9 us  [the longest x31 42.1 us: swap(): return lax.ppermute(x, axis, [(i, i ^ mask) for i in range(size)])]
    ppermute x0 -> x39, waiting for transfers between devices: none -> 31.8 us  [the longest x31 24.6 us: swap(): return lax.ppermute(x, axis, [(i, i ^ mask) for i in range(size)])]
    pallas_call x0 -> x5, Pallas kernels: none -> 29.1 us  [the longest x2 14 us: mix(): pl.pallas_call(functools.partial(mix_kernel, nb, members, col), out_shape...]
    dot_general x9 -> x0, matrix products: 17.3 us -> none  [the longest x2 6.51 us: one_head(): lax.dot_general(query_h, pkey_h, (((1,), (1,)), ((), ())), preferred_elem...]
    select_n x2 -> x3, other arithmetic: 3.39 us -> 0.08 us  [the longest x1 0.04 us: split_heads(): k_other = jnp.where(first_head, k[:, HD:], k[:, :HD])]
    reduce_sum x5 -> x3, other arithmetic: 3.06 us -> 0.37 us  [the longest x1 0.18 us: split_heads(): jnp.sum(jnp.where(flat_owner[None, :] == (me ^ jnp.arange(SLOTS, dtype=jn...]
  transfers between devices with their start and end apart: 2 -> 40, of which waited for: 2 -> 13; matrix products, arithmetic and copies ran while one was open for 1% -> 6% of each run, Pallas kernels for 0% -> 16%
where the time goes in v2:
time: 151 us; the launch traced here: 150 us
  starting transfers between devices  49.9 us (33%)
  waiting for transfers between devices  31.8 us (21%)
  Pallas kernels  29.1 us (19%)
  local copies, waits for them, and re-layouts  21.9 us (15%)
  between operations  13.9 us (9%)
  other arithmetic  2.93 us (2%)
    ppermute x31, starting transfers between devices, swap(): return lax.ppermute(x, axis, [(i, i ^ mask) for i in range(size)])  42.1 us
    ppermute x31, waiting for transfers between devices, swap(): return lax.ppermute(x, axis, [(i, i ^ mask) for i in range(size)])  24.6 us
    pallas_call x2, Pallas kernels, mix(): pl.pallas_call(functools.partial(mix_kernel, nb, members, col), out_shape...  14 us
    unnamed x47, local copies, waits for them, and re-layouts  11.6 us
    pallas_call x1, Pallas kernels, score(): pl.pallas_call(functools.partial(score_kernel, len(sufs), members), out_s...  9.08 us
    ppermute x4, waiting for transfers between devices, split_heads(): forward = lax.ppermute(two, 'tp', [(2, 3), (1, 0)])  7.19 us
    ppermute x4, starting transfers between devices, split_heads(): forward = lax.ppermute(two, 'tp', [(2, 3), (1, 0)])  5.13 us
    pallas_call x1, Pallas kernels, project(): pl.pallas_call(proj_kernel, out_shape=jax.ShapeDtypeStruct((rows, cols),...  4.49 us
  transfers between devices with their start and end apart: 40, of which 13 were waited for; matrix products, arithmetic and copies ran while one was open for 6% of the time, Pallas kernels for 16%

profile of v2, /device:TPU:0, one launch (start us, length us, event | category | flops | bytes accessed | tf_op | source)
XLA Modules:
  0.0 149.5 jit_solution(637960077069679709)
XLA Ops:
  6.5 3.4 %fusion.7 = (bf16[512,1,512]{2,1,0:T(2,128)(2,1)S(1)}, bf16[512,1,512]{2,1,0:T(2,128)(2,1)S(1)}) fusion(bf16[512,2,512]{2,1,0:T(2,128)(2,1)} %param.7), kind=kLoop, calls=%fused_computation.49 | loop fusion | bytes 2097152 | tf_op jit(solution)/shard_map/slice | solution.py:343
  10.3 3.0 %collective-permute-start.3 = (bf16[512,256]{1,0:T(8,128)(2,1)S(1)}, bf16[512,256]{1,0:T(8,128)(2,1)S(1)}, u32[]{:S(2)}, u32[]{:S(2)}) collective-permute-start(bf16[512,256]{1,0:T(8,128)(2,1)S(1)} %get-tuple-element.52), channel_id=1, source_target_pairs={{0,8},{4,12},{8,0},{12,4},{16,24},{20,28},{24,16},{28,20},{1,9},{5... | collective-permute-start | bytes 786440 | tf_op jit(solution)/shard_map/ppermute | solution.py:316
  13.3 1.5 %collective-permute-start.5 = (bf16[512,256]{1,0:T(8,128)(2,1)S(1)}, bf16[512,256]{1,0:T(8,128)(2,1)S(1)}, u32[]{:S(2)}, u32[]{:S(2)}) collective-permute-start(bf16[512,256]{1,0:T(8,128)(2,1)S(1)} %get-tuple-element.52), channel_id=1, source_target_pairs={{0,16},{4,20},{8,24},{12,28},{16,0},{20,4},{24,8},{28,12},{1,17},{... | collective-permute-start | bytes 786440 | tf_op jit(solution)/shard_map/ppermute | solution.py:316
  14.8 4.7 %collective-permute-done.3 = bf16[512,256]{1,0:T(8,128)(2,1)S(1)} collective-permute-done((bf16[512,256]{1,0:T(8,128)(2,1)S(1)}, bf16[512,256]{1,0:T(8,128)(2,1)S(1)}, u32[]{:S(2)}, u32[]{:S(2)}) %collective-permute-start.3) | collective-permute-done | bytes 262176 | tf_op jit(solution)/shard_map/ppermute | solution.py:316
  21.5 1.7 %collective-permute-start.6 = (bf16[512,256]{1,0:T(8,128)(2,1)S(1)}, bf16[512,256]{1,0:T(8,128)(2,1)S(1)}, u32[]{:S(2)}, u32[]{:S(2)}) collective-permute-start(bf16[512,256]{1,0:T(8,128)(2,1)S(1)} %collective-permute-done.2), channel_id=1, source_target_pairs={{0,16},{4,20},{8,24},{12,28},{16,0},{20,4},{24,8},{28,12},{1,17},{... | collective-permute-start | bytes 786440 | tf_op jit(solution)/shard_map/ppermute | solution.py:316
  24.2 3.7 %collective-permute-start.36 = (bf16[256,256]{1,0:T(8,128)(2,1)S(1)}, bf16[256,256]{1,0:T(8,128)(2,1)S(1)}, u32[]{:S(2)}, u32[]{:S(2)}) collective-permute-start(bf16[256,256]{1,0:T(8,128)(2,1)S(1)} %get-tuple-element.33), channel_id=1, source_target_pairs={{0,3},{1,2},{2,1},{3,0},{4,7},{5,6},{6,5},{7,4},{8,11},{9,10},{10,... | collective-permute-start | bytes 393224 | tf_op jit(solution)/shard_map/ppermute | solution.py:316
  28.5 3.1 %collective-permute-done.36 = bf16[256,256]{1,0:T(8,128)(2,1)S(1)} collective-permute-done((bf16[256,256]{1,0:T(8,128)(2,1)S(1)}, bf16[256,256]{1,0:T(8,128)(2,1)S(1)}, u32[]{:S(2)}, u32[]{:S(2)}) %collective-permute-start.36) | collective-permute-done | bytes 131104 | tf_op jit(solution)/shard_map/ppermute | solution.py:316
  31.6 3.5 %collective-permute-start.37 = (bf16[256,256]{1,0:T(8,128)(2,1)S(1)}, bf16[256,256]{1,0:T(8,128)(2,1)S(1)}, u32[]{:S(2)}, u32[]{:S(2)}) collective-permute-start(bf16[256,256]{1,0:T(8,128)(2,1)S(1)} %get-tuple-element.34), channel_id=1, source_target_pairs={{0,2},{1,3},{2,0},{3,1},{4,6},{5,7},{6,4},{7,5},{8,10},{9,11},{10,... | collective-permute-start | bytes 393224 | tf_op jit(solution)/shard_map/ppermute | solution.py:316
  35.1 1.5 collective-permute-start.8
  36.7 5.4 %collective-permute-done.8 = bf16[512,256]{1,0:T(8,128)(2,1)S(1)} collective-permute-done((bf16[512,256]{1,0:T(8,128)(2,1)S(1)}, bf16[512,256]{1,0:T(8,128)(2,1)S(1)}, u32[]{:S(2)}, u32[]{:S(2)}) %collective-permute-start.8) | collective-permute-done | bytes 262176 | tf_op jit(solution)/shard_map/ppermute | solution.py:316
  42.8 1.5 collective-permute-start.10
  45.4 3.9 %collective-permute-done.38 = bf16[256,256]{1,0:T(8,128)(2,1)S(1)} collective-permute-done((bf16[256,256]{1,0:T(8,128)(2,1)S(1)}, bf16[256,256]{1,0:T(8,128)(2,1)S(1)}, u32[]{:S(2)}, u32[]{:S(2)}) %collective-permute-start.38) | collective-permute-done | bytes 131104 | tf_op jit(solution)/shard_map/ppermute | solution.py:316
  52.3 1.5 slice_bitcast_fusion
  53.8 1.5 %prepare.1 = (bf16[3,512,256]{2,1,0:T(8,128)(2,1)S(1)}, bf16[3,512,256]{2,1,0:T(8,128)(2,1)}) custom-call(s32[1]{0:T(128)} %bitcast.1.flip_ref, bf16[512,512]{1,0:T(8,128)(2,1)S(1)} %get-tuple-element.45.q_ref, bf16[512,512]{1,0:T(8,128)(2,1)S(1)} %get-tuple-element.46.k_ref, bf16[512,512]{1,0:T(8,128)(2,1)S(1)} %get-tuple-element.44.v_ref, ...), custom_call_target="tpu_custom_call" | custom-call | tf_op jit(solution)/shard_map/prepare/pallas_call | solution.py:79
  60.6 1.5 collective-permute-start.13
  69.6 9.1 %score.1 = (bf16[1024,1024]{1,0:T(8,128)(2,1)S(1)}, bf16[1024,256]{1,0:T(8,128)(2,1)S(1)}, f32[1024,128]{1,0:T(8,128)S(1)}) custom-call(s32[8]{0:T(128)S(1)} %select_reduce_fusion.4.place_ref, s32[32]{0:T(128)S(1)} %reshape.59.here_ref, s32[1024,1]{1,0:T(8,128)S(1)} %copy.27.first_ref, s32[1024,1]{1,0:T(8,128)S(1)} %copy.30.grp_ref, ...), custom_call_target="tpu_custom_call" | custom-call | tf_op jit(solution)/shard_map/score/pallas_call | solution.py:166
  78.7 7.3 %mix.2 = (bf16[512,128]{1,0:T(8,128)(2,1)S(1)}, bf16[512,128]{1,0:T(8,128)(2,1)S(1)}) custom-call(s32[8]{0:T(128)S(1)} %select_reduce_fusion.4.place_ref, s32[32]{0:T(128)S(1)} %reshape.59.here_ref, s32[1024,1]{1,0:T(8,128)S(1)} %copy.30.grp_ref, bf16[1024,1024]{1,0:T(8,128)(2,1)S(1)} %get-tuple-element.23.p_ref, ...), custom_call_target="tpu_custom_call" | custom-call | tf_op jit(solution)/shard_map/mix/pallas_call | solution.py:230
  87.2 2.6 %collective-permute-start.25 = (bf16[1,512,128]{2,1,0:T(8,128)(2,1)S(1)}, bf16[1,512,128]{2,1,0:T(8,128)(2,1)S(1)}, u32[]{:S(2)}, u32[]{:S(2)}) collective-permute-start(bf16[1,512,128]{2,1,0:T(8,128)(2,1)S(1)} %slice.90), channel_id=1, source_target_pairs={{0,16},{4,20},{8,24},{12,28},{16,0},{20,4},{24,8},{28,12},{1,17},{... | collective-permute-start | bytes 393224 | tf_op jit(solution)/shard_map/ppermute | solution.py:316
  91.9 1.9 %collective-permute-start.14 = (bf16[512,128]{1,0:T(8,128)(2,1)S(1)}, bf16[512,128]{1,0:T(8,128)(2,1)S(1)}, u32[]{:S(2)}, u32[]{:S(2)}) collective-permute-start(bf16[512,128]{1,0:T(8,128)(2,1)S(1)} %get-tuple-element.28.refs_0_), channel_id=1, source_target_pairs={{0,1},{1,0},{2,3},{3,2},{4,5},{5,4},{6,7},{7,6},{8,9},{9,8},{10,11... | collective-permute-start | bytes 393224 | tf_op jit(solution)/shard_map/ppermute | solution.py:316
  94.9 2.4 %collective-permute-start.20 = (bf16[512,128]{1,0:T(8,128)(2,1)S(1)}, bf16[512,128]{1,0:T(8,128)(2,1)S(1)}, u32[]{:S(2)}, u32[]{:S(2)}) collective-permute-start(bf16[512,128]{1,0:T(8,128)(2,1)S(1)} %collective-permute-done.18.refs_5_), channel_id=1, source_target_pairs={{0,2},{1,3},{2,0},{3,1},{4,6},{5,7},{6,4},{7,5},{8,10},{9,11},{10,... | collective-permute-start | bytes 393224 | tf_op jit(solution)/shard_map/ppermute | solution.py:316
  98.6 2.7 %collective-permute-start.19 = (bf16[512,128]{1,0:T(8,128)(2,1)S(1)}, bf16[512,128]{1,0:T(8,128)(2,1)S(1)}, u32[]{:S(2)}, u32[]{:S(2)}) collective-permute-start(bf16[512,128]{1,0:T(8,128)(2,1)S(1)} %collective-permute-done.18.refs_5_), channel_id=1, source_target_pairs={{0,1},{1,0},{2,3},{3,2},{4,5},{5,4},{6,7},{7,6},{8,9},{9,8},{10,11... | collective-permute-start | bytes 393224 | tf_op jit(solution)/shard_map/ppermute | solution.py:316
  101.4 6.7 %mix.3 = (bf16[512,128]{1,0:T(8,128)(2,1)S(1)}, bf16[512,128]{1,0:T(8,128)(2,1)S(1)}) custom-call(s32[8]{0:T(128)S(1)} %select_reduce_fusion.4.place_ref, s32[32]{0:T(128)S(1)} %reshape.59.here_ref, s32[1024,1]{1,0:T(8,128)S(1)} %copy.30.grp_ref, bf16[1024,1024]{1,0:T(8,128)(2,1)S(1)} %get-tuple-element.23.p_ref, ...), custom_call_target="tpu_custom_call" | custom-call | tf_op jit(solution)/shard_map/mix/pallas_call | solution.py:230
  110.1 4.1 %collective-permute-start.28 = (bf16[512,128]{1,0:T(8,128)(2,1)S(1)}, bf16[512,128]{1,0:T(8,128)(2,1)S(1)}, u32[]{:S(2)}, u32[]{:S(2)}) collective-permute-start(bf16[512,128]{1,0:T(8,128)(2,1)S(1)} %get-tuple-element.31.refs_10_), channel_id=1, source_target_pairs={{0,2},{1,3},{2,0},{3,1},{4,6},{5,7},{6,4},{7,5},{8,10},{9,11},{10,... | collective-permute-start | bytes 393224 | tf_op jit(solution)/shard_map/ppermute | solution.py:316
  114.3 2.1 %collective-permute-start.33 = (bf16[512,128]{1,0:T(8,128)(2,1)S(1)}, bf16[512,128]{1,0:T(8,128)(2,1)S(1)}, u32[]{:S(2)}, u32[]{:S(2)}) collective-permute-start(bf16[512,128]{1,0:T(8,128)(2,1)S(1)} %collective-permute-done.31.refs_15_), channel_id=1, source_target_pairs={{0,2},{1,3},{2,0},{3,1},{4,6},{5,7},{6,4},{7,5},{8,10},{9,11},{10,... | collective-permute-start | bytes 393224 | tf_op jit(solution)/shard_map/ppermute | solution.py:316
  117.0 1.6 %collective-permute-done.22.refs_9_ = bf16[512,128]{1,0:T(8,128)(2,1)S(1)} collective-permute-done((bf16[512,128]{1,0:T(8,128)(2,1)S(1)}, bf16[512,128]{1,0:T(8,128)(2,1)S(1)}, u32[]{:S(2)}, u32[]{:S(2)}) %collective-permute-start.22) | collective-permute-done | bytes 131104 | tf_op jit(solution)/shard_map/ppermute | solution.py:426
  118.7 1.6 %collective-permute-start.32 = (bf16[512,128]{1,0:T(8,128)(2,1)S(1)}, bf16[512,128]{1,0:T(8,128)(2,1)S(1)}, u32[]{:S(2)}, u32[]{:S(2)}) collective-permute-start(bf16[512,128]{1,0:T(8,128)(2,1)S(1)} %collective-permute-done.31.refs_15_), channel_id=1, source_target_pairs={{0,1},{1,0},{2,3},{3,2},{4,5},{5,4},{6,7},{7,6},{8,9},{9,8},{10,11... | collective-permute-start | bytes 393224 | tf_op jit(solution)/shard_map/ppermute | solution.py:316
  125.0 2.2 %collective-permute-done.33.refs_17_ = bf16[512,128]{1,0:T(8,128)(2,1)S(1)} collective-permute-done((bf16[512,128]{1,0:T(8,128)(2,1)S(1)}, bf16[512,128]{1,0:T(8,128)(2,1)S(1)}, u32[]{:S(2)}, u32[]{:S(2)}) %collective-permute-start.33) | collective-permute-done | bytes 131104 | tf_op jit(solution)/shard_map/ppermute | solution.py:316
  128.5 2.7 %collective-permute-done.30.refs_14_ = bf16[512,128]{1,0:T(8,128)(2,1)S(1)} collective-permute-done((bf16[512,128]{1,0:T(8,128)(2,1)S(1)}, bf16[512,128]{1,0:T(8,128)(2,1)S(1)}, u32[]{:S(2)}, u32[]{:S(2)}) %collective-permute-start.30) | collective-permute-done | bytes 131104 | tf_op jit(solution)/shard_map/ppermute | solution.py:426
  131.2 2.8 %collective-permute-done.35.refs_19_ = bf16[512,128]{1,0:T(8,128)(2,1)S(1)} collective-permute-done((bf16[512,128]{1,0:T(8,128)(2,1)S(1)}, bf16[512,128]{1,0:T(8,128)(2,1)S(1)}, u32[]{:S(2)}, u32[]{:S(2)}) %collective-permute-start.35) | collective-permute-done | bytes 131104 | tf_op jit(solution)/shard_map/ppermute | solution.py:426
  134.1 2.2 %copy-done = bf16[512,4096]{1,0:T(8,128)(2,1)S(1)} copy-done((bf16[512,4096]{1,0:T(8,128)(2,1)S(1)}, bf16[512,4096]{1,0:T(8,128)(2,1)}, u32[]{:S(2)}) %copy-start) | copy-done | bytes 4194328
  136.3 1.9 %copy-done.1 = bf16[24,256,256]{2,1,0:T(8,128)(2,1)S(1)} copy-done((bf16[24,256,256]{2,1,0:T(8,128)(2,1)S(1)}, bf16[24,256,256]{2,1,0:T(8,128)(2,1)}, u32[]{:S(2)}) %copy-start.1) | copy-done | bytes 3145752
  138.2 4.5 %project.1 = bf16[512,1024]{1,0:T(8,128)(2,1)} custom-call(s32[2]{0:T(128)S(1)} %pad_add_fusion.3.where_ref, bf16[512,128]{1,0:T(8,128)(2,1)S(1)} %get-tuple-element.28.refs_0_, bf16[512,128]{1,0:T(8,128)(2,1)S(1)} %collective-permute-done.14.refs_1_, bf16[512,128]{1,0:T(8,128)(2,1)S(1)} %collective-permute-done.15.refs_2_, ...), custom_call_target="tpu_custom_call" | custom-call | tf_op jit(solution)/shard_map/project/pallas_call | solution.py:300
  (143 shorter events, 35.8 us)
Async XLA Ops:
  6.5 127.5 %all-gather.3.cloned.1.call-start = ((), (), s32[]{:S(2)}) async-start(), calls=%async_computation | async-start | bytes 3538944 | tf_op jit(solution)/shard_map/all_gather | solution.py:385
  10.3 9.3 %collective-permute-start.3 = (bf16[512,256]{1,0:T(8,128)(2,1)S(1)}, bf16[512,256]{1,0:T(8,128)(2,1)S(1)}, u32[]{:S(2)}, u32[]{:S(2)}) collective-permute-start(bf16[512,256]{1,0:T(8,128)(2,1)S(1)} %get-tuple-element.52), channel_id=1, source_target_pairs={{0,8},{4,12},{8,0},{12,4},{16,24},{20,28},{24,16},{28,20},{1,9},{5... | collective-permute-start | bytes 786440 | tf_op jit(solution)/shard_map/ppermute | solution.py:316
  13.3 7.8 %collective-permute-start.5 = (bf16[512,256]{1,0:T(8,128)(2,1)S(1)}, bf16[512,256]{1,0:T(8,128)(2,1)S(1)}, u32[]{:S(2)}, u32[]{:S(2)}) collective-permute-start(bf16[512,256]{1,0:T(8,128)(2,1)S(1)} %get-tuple-element.52), channel_id=1, source_target_pairs={{0,16},{4,20},{8,24},{12,28},{16,0},{20,4},{24,8},{28,12},{1,17},{... | collective-permute-start | bytes 786440 | tf_op jit(solution)/shard_map/ppermute | solution.py:316
  21.0 15.5 %collective-permute-start.9 = (bf16[512,256]{1,0:T(8,128)(2,1)S(1)}, bf16[512,256]{1,0:T(8,128)(2,1)S(1)}, u32[]{:S(2)}, u32[]{:S(2)}) collective-permute-start(bf16[512,256]{1,0:T(8,128)(2,1)S(1)} %get-tuple-element.26), channel_id=1, source_target_pairs={{0,4},{4,0},{8,12},{12,8},{16,20},{20,16},{24,28},{28,24},{1,5},{5... | collective-permute-start | bytes 786440 | tf_op jit(solution)/shard_map/ppermute | solution.py:316
  21.1 10.5 %collective-permute-start.4 = (bf16[512,256]{1,0:T(8,128)(2,1)S(1)}, bf16[512,256]{1,0:T(8,128)(2,1)S(1)}, u32[]{:S(2)}, u32[]{:S(2)}) collective-permute-start(bf16[512,256]{1,0:T(8,128)(2,1)S(1)} %collective-permute-done.2), channel_id=1, source_target_pairs={{0,8},{4,12},{8,0},{12,4},{16,24},{20,28},{24,16},{28,20},{1,9},{5... | collective-permute-start | bytes 786440 | tf_op jit(solution)/shard_map/ppermute | solution.py:316
  21.5 10.1 %collective-permute-start.6 = (bf16[512,256]{1,0:T(8,128)(2,1)S(1)}, bf16[512,256]{1,0:T(8,128)(2,1)S(1)}, u32[]{:S(2)}, u32[]{:S(2)}) collective-permute-start(bf16[512,256]{1,0:T(8,128)(2,1)S(1)} %collective-permute-done.2), channel_id=1, source_target_pairs={{0,16},{4,20},{8,24},{12,28},{16,0},{20,4},{24,8},{28,12},{1,17},{... | collective-permute-start | bytes 786440 | tf_op jit(solution)/shard_map/ppermute | solution.py:316
  24.2 7.3 %collective-permute-start.36 = (bf16[256,256]{1,0:T(8,128)(2,1)S(1)}, bf16[256,256]{1,0:T(8,128)(2,1)S(1)}, u32[]{:S(2)}, u32[]{:S(2)}) collective-permute-start(bf16[256,256]{1,0:T(8,128)(2,1)S(1)} %get-tuple-element.33), channel_id=1, source_target_pairs={{0,3},{1,2},{2,1},{3,0},{4,7},{5,6},{6,5},{7,4},{8,11},{9,10},{10,... | collective-permute-start | bytes 393224 | tf_op jit(solution)/shard_map/ppermute | solution.py:316
  27.9 8.7 %collective-permute-start.7 = (bf16[512,256]{1,0:T(8,128)(2,1)S(1)}, bf16[512,256]{1,0:T(8,128)(2,1)S(1)}, u32[]{:S(2)}, u32[]{:S(2)}) collective-permute-start(bf16[512,256]{1,0:T(8,128)(2,1)S(1)} %collective-permute-done.3), channel_id=1, source_target_pairs={{0,16},{4,20},{8,24},{12,28},{16,0},{20,4},{24,8},{28,12},{1,17},{... | collective-permute-start | bytes 786440 | tf_op jit(solution)/shard_map/ppermute | solution.py:316
  31.6 12.7 %collective-permute-start.37 = (bf16[256,256]{1,0:T(8,128)(2,1)S(1)}, bf16[256,256]{1,0:T(8,128)(2,1)S(1)}, u32[]{:S(2)}, u32[]{:S(2)}) collective-permute-start(bf16[256,256]{1,0:T(8,128)(2,1)S(1)} %get-tuple-element.34), channel_id=1, source_target_pairs={{0,2},{1,3},{2,0},{3,1},{4,6},{5,7},{6,4},{7,5},{8,10},{9,11},{10,... | collective-permute-start | bytes 393224 | tf_op jit(solution)/shard_map/ppermute | solution.py:316
  42.8 7.3 %collective-permute-start.10 = (bf16[2,512,128]{2,1,0:T(8,128)(2,1)S(1)}, bf16[2,512,128]{2,1,0:T(8,128)(2,1)S(1)}, u32[]{:S(2)}, u32[]{:S(2)}) collective-permute-start(bf16[2,512,128]{2,1,0:T(8,128)(2,1)S(1)} %pad_maximum_fusion.1.rest_2_), channel_id=1, source_target_pairs={{0,8},{4,12},{8,0},{12,4},{16,24},{20,28},{24,16},{28,20},{1,9},{5... | collective-permute-start | bytes 786440 | tf_op jit(solution)/shard_map/ppermute | solution.py:316
  55.4 7.5 %collective-permute-start.1 = (bf16[3,512,256]{2,1,0:T(8,128)(2,1)}, bf16[3,512,256]{2,1,0:T(8,128)(2,1)S(1)}, u32[]{:S(2)}, u32[]{:S(2)}) collective-permute-start(bf16[3,512,256]{2,1,0:T(8,128)(2,1)} %get-tuple-element.22), channel_id=1, source_target_pairs={{0,4},{4,0},{8,12},{12,8},{16,20},{20,16},{24,28},{28,24},{1,5},{5... | collective-permute-start | bytes 2359304 | tf_op jit(solution)/shard_map/ppermute | solution.py:316
  56.6 29.6 %collective-permute-start.23 = (bf16[2,512,128]{2,1,0:T(8,128)(2,1)S(1)}, bf16[2,512,128]{2,1,0:T(8,128)(2,1)}, u32[]{:S(2)}, u32[]{:S(2)}) collective-permute-start(bf16[2,512,128]{2,1,0:T(8,128)(2,1)S(1)} %pad_maximum_fusion.2.rest_2_), channel_id=1, source_target_pairs={{0,8},{4,12},{8,0},{12,4},{16,24},{20,28},{24,16},{28,20},{1,9},{5... | collective-permute-start | bytes 786440 | tf_op jit(solution)/shard_map/ppermute | solution.py:316
  57.2 32.5 %collective-permute-start.24 = (bf16[2,512,128]{2,1,0:T(8,128)(2,1)S(1)}, bf16[2,512,128]{2,1,0:T(8,128)(2,1)}, u32[]{:S(2)}, u32[]{:S(2)}) collective-permute-start(bf16[2,512,128]{2,1,0:T(8,128)(2,1)S(1)} %pad_maximum_fusion.2.rest_2_), channel_id=1, source_target_pairs={{0,16},{4,20},{8,24},{12,28},{16,0},{20,4},{24,8},{28,12},{1,17},{... | collective-permute-start | bytes 786440 | tf_op jit(solution)/shard_map/ppermute | solution.py:316
  59.3 19.4 %collective-permute-start.12 = (bf16[1,512,128]{2,1,0:T(8,128)(2,1)}, bf16[1,512,128]{2,1,0:T(8,128)(2,1)S(1)}, u32[]{:S(2)}, u32[]{:S(2)}) collective-permute-start(bf16[1,512,128]{2,1,0:T(8,128)(2,1)} %slice.86), channel_id=1, source_target_pairs={{0,16},{4,20},{8,24},{12,28},{16,0},{20,4},{24,8},{28,12},{1,17},{... | collective-permute-start | bytes 393224 | tf_op jit(solution)/shard_map/ppermute | solution.py:316
  60.6 18.1 %collective-permute-start.13 = (bf16[1,512,128]{2,1,0:T(8,128)(2,1)}, bf16[1,512,128]{2,1,0:T(8,128)(2,1)}, u32[]{:S(2)}, u32[]{:S(2)}) collective-permute-start(bf16[1,512,128]{2,1,0:T(8,128)(2,1)} %slice.87), channel_id=1, source_target_pairs={{0,8},{4,12},{8,0},{12,4},{16,24},{20,28},{24,16},{28,20},{1,9},{5... | collective-permute-start | bytes 393224 | tf_op jit(solution)/shard_map/ppermute | solution.py:316
  86.1 8.2 %collective-permute-start.15 = (bf16[512,128]{1,0:T(8,128)(2,1)S(1)}, bf16[512,128]{1,0:T(8,128)(2,1)S(1)}, u32[]{:S(2)}, u32[]{:S(2)}) collective-permute-start(bf16[512,128]{1,0:T(8,128)(2,1)S(1)} %get-tuple-element.28.refs_0_), channel_id=1, source_target_pairs={{0,2},{1,3},{2,0},{3,1},{4,6},{5,7},{6,4},{7,5},{8,10},{9,11},{10,... | collective-permute-start | bytes 393224 | tf_op jit(solution)/shard_map/ppermute | solution.py:316
  86.2 8.8 %collective-permute-start.18 = (bf16[512,128]{1,0:T(8,128)(2,1)S(1)}, bf16[512,128]{1,0:T(8,128)(2,1)S(1)}, u32[]{:S(2)}, u32[]{:S(2)}) collective-permute-start(bf16[512,128]{1,0:T(8,128)(2,1)S(1)} %get-tuple-element.29), channel_id=1, source_target_pairs={{0,4},{4,0},{8,12},{12,8},{16,20},{20,16},{24,28},{28,24},{1,5},{5... | collective-permute-start | bytes 393224 | tf_op jit(solution)/shard_map/ppermute | solution.py:316
  87.2 10.2 %collective-permute-start.25 = (bf16[1,512,128]{2,1,0:T(8,128)(2,1)S(1)}, bf16[1,512,128]{2,1,0:T(8,128)(2,1)S(1)}, u32[]{:S(2)}, u32[]{:S(2)}) collective-permute-start(bf16[1,512,128]{2,1,0:T(8,128)(2,1)S(1)} %slice.90), channel_id=1, source_target_pairs={{0,16},{4,20},{8,24},{12,28},{16,0},{20,4},{24,8},{28,12},{1,17},{... | collective-permute-start | bytes 393224 | tf_op jit(solution)/shard_map/ppermute | solution.py:316
  90.7 8.0 %collective-permute-start.26 = (bf16[1,512,128]{2,1,0:T(8,128)(2,1)S(1)}, bf16[1,512,128]{2,1,0:T(8,128)(2,1)S(1)}, u32[]{:S(2)}, u32[]{:S(2)}) collective-permute-start(bf16[1,512,128]{2,1,0:T(8,128)(2,1)S(1)} %slice.91), channel_id=1, source_target_pairs={{0,8},{4,12},{8,0},{12,4},{16,24},{20,28},{24,16},{28,20},{1,9},{5... | collective-permute-start | bytes 393224 | tf_op jit(solution)/shard_map/ppermute | solution.py:316
  91.9 16.2 %collective-permute-start.14 = (bf16[512,128]{1,0:T(8,128)(2,1)S(1)}, bf16[512,128]{1,0:T(8,128)(2,1)S(1)}, u32[]{:S(2)}, u32[]{:S(2)}) collective-permute-start(bf16[512,128]{1,0:T(8,128)(2,1)S(1)} %get-tuple-element.28.refs_0_), channel_id=1, source_target_pairs={{0,1},{1,0},{2,3},{3,2},{4,5},{5,4},{6,7},{7,6},{8,9},{9,8},{10,11... | collective-permute-start | bytes 393224 | tf_op jit(solution)/shard_map/ppermute | solution.py:316
  94.2 13.9 %collective-permute-start.16 = (bf16[512,128]{1,0:T(8,128)(2,1)S(1)}, bf16[512,128]{1,0:T(8,128)(2,1)S(1)}, u32[]{:S(2)}, u32[]{:S(2)}) collective-permute-start(bf16[512,128]{1,0:T(8,128)(2,1)S(1)} %get-tuple-element.28.refs_0_), channel_id=1, source_target_pairs={{1,2},{2,1},{5,6},{6,5},{9,10},{10,9},{13,14},{14,13},{17,18},{18,... | collective-permute-start | bytes 393224 | tf_op jit(solution)/shard_map/ppermute | solution.py:425
  94.9 13.9 %collective-permute-start.20 = (bf16[512,128]{1,0:T(8,128)(2,1)S(1)}, bf16[512,128]{1,0:T(8,128)(2,1)S(1)}, u32[]{:S(2)}, u32[]{:S(2)}) collective-permute-start(bf16[512,128]{1,0:T(8,128)(2,1)S(1)} %collective-permute-done.18.refs_5_), channel_id=1, source_target_pairs={{0,2},{1,3},{2,0},{3,1},{4,6},{5,7},{6,4},{7,5},{8,10},{9,11},{10,... | collective-permute-start | bytes 393224 | tf_op jit(solution)/shard_map/ppermute | solution.py:316
  97.3 12.8 %collective-permute-start.17 = (bf16[512,128]{1,0:T(8,128)(2,1)S(1)}, bf16[512,128]{1,0:T(8,128)(2,1)S(1)}, u32[]{:S(2)}, u32[]{:S(2)}) collective-permute-start(bf16[512,128]{1,0:T(8,128)(2,1)S(1)} %collective-permute-done.15.refs_2_), channel_id=1, source_target_pairs={{2,3},{1,0},{6,7},{5,4},{10,11},{9,8},{14,15},{13,12},{18,19},{17,... | collective-permute-start | bytes 393224 | tf_op jit(solution)/shard_map/ppermute | solution.py:426
  98.6 15.6 %collective-permute-start.19 = (bf16[512,128]{1,0:T(8,128)(2,1)S(1)}, bf16[512,128]{1,0:T(8,128)(2,1)S(1)}, u32[]{:S(2)}, u32[]{:S(2)}) collective-permute-start(bf16[512,128]{1,0:T(8,128)(2,1)S(1)} %collective-permute-done.18.refs_5_), channel_id=1, source_target_pairs={{0,1},{1,0},{2,3},{3,2},{4,5},{5,4},{6,7},{7,6},{8,9},{9,8},{10,11... | collective-permute-start | bytes 393224 | tf_op jit(solution)/shard_map/ppermute | solution.py:316
  108.1 8.2 %collective-permute-start.21 = (bf16[512,128]{1,0:T(8,128)(2,1)S(1)}, bf16[512,128]{1,0:T(8,128)(2,1)S(1)}, u32[]{:S(2)}, u32[]{:S(2)}) collective-permute-start(bf16[512,128]{1,0:T(8,128)(2,1)S(1)} %collective-permute-done.18.refs_5_), channel_id=1, source_target_pairs={{1,2},{2,1},{5,6},{6,5},{9,10},{10,9},{13,14},{14,13},{17,18},{18,... | collective-permute-start | bytes 393224 | tf_op jit(solution)/shard_map/ppermute | solution.py:425
  108.8 9.8 %collective-permute-start.22 = (bf16[512,128]{1,0:T(8,128)(2,1)S(1)}, bf16[512,128]{1,0:T(8,128)(2,1)S(1)}, u32[]{:S(2)}, u32[]{:S(2)}) collective-permute-start(bf16[512,128]{1,0:T(8,128)(2,1)S(1)} %collective-permute-done.20.refs_7_), channel_id=1, source_target_pairs={{2,3},{1,0},{6,7},{5,4},{10,11},{9,8},{14,15},{13,12},{18,19},{17,... | collective-permute-start | bytes 393224 | tf_op jit(solution)/shard_map/ppermute | solution.py:426
  110.1 11.4 %collective-permute-start.28 = (bf16[512,128]{1,0:T(8,128)(2,1)S(1)}, bf16[512,128]{1,0:T(8,128)(2,1)S(1)}, u32[]{:S(2)}, u32[]{:S(2)}) collective-permute-start(bf16[512,128]{1,0:T(8,128)(2,1)S(1)} %get-tuple-element.31.refs_10_), channel_id=1, source_target_pairs={{0,2},{1,3},{2,0},{3,1},{4,6},{5,7},{6,4},{7,5},{8,10},{9,11},{10,... | collective-permute-start | bytes 393224 | tf_op jit(solution)/shard_map/ppermute | solution.py:316
  114.3 10.0 %collective-permute-start.27 = (bf16[512,128]{1,0:T(8,128)(2,1)S(1)}, bf16[512,128]{1,0:T(8,128)(2,1)S(1)}, u32[]{:S(2)}, u32[]{:S(2)}) collective-permute-start(bf16[512,128]{1,0:T(8,128)(2,1)S(1)} %get-tuple-element.31.refs_10_), channel_id=1, source_target_pairs={{0,1},{1,0},{2,3},{3,2},{4,5},{5,4},{6,7},{7,6},{8,9},{9,8},{10,11... | collective-permute-start | bytes 393224 | tf_op jit(solution)/shard_map/ppermute | solution.py:316
  114.3 12.9 %collective-permute-start.33 = (bf16[512,128]{1,0:T(8,128)(2,1)S(1)}, bf16[512,128]{1,0:T(8,128)(2,1)S(1)}, u32[]{:S(2)}, u32[]{:S(2)}) collective-permute-start(bf16[512,128]{1,0:T(8,128)(2,1)S(1)} %collective-permute-done.31.refs_15_), channel_id=1, source_target_pairs={{0,2},{1,3},{2,0},{3,1},{4,6},{5,7},{6,4},{7,5},{8,10},{9,11},{10,... | collective-permute-start | bytes 393224 | tf_op jit(solution)/shard_map/ppermute | solution.py:316
  116.4 12.1 %collective-permute-start.29 = (bf16[512,128]{1,0:T(8,128)(2,1)S(1)}, bf16[512,128]{1,0:T(8,128)(2,1)S(1)}, u32[]{:S(2)}, u32[]{:S(2)}) collective-permute-start(bf16[512,128]{1,0:T(8,128)(2,1)S(1)} %get-tuple-element.31.refs_10_), channel_id=1, source_target_pairs={{1,2},{2,1},{5,6},{6,5},{9,10},{10,9},{13,14},{14,13},{17,18},{18,... | collective-permute-start | bytes 393224 | tf_op jit(solution)/shard_map/ppermute | solution.py:425
  118.7 12.6 %collective-permute-start.32 = (bf16[512,128]{1,0:T(8,128)(2,1)S(1)}, bf16[512,128]{1,0:T(8,128)(2,1)S(1)}, u32[]{:S(2)}, u32[]{:S(2)}) collective-permute-start(bf16[512,128]{1,0:T(8,128)(2,1)S(1)} %collective-permute-done.31.refs_15_), channel_id=1, source_target_pairs={{0,1},{1,0},{2,3},{3,2},{4,5},{5,4},{6,7},{7,6},{8,9},{9,8},{10,11... | collective-permute-start | bytes 393224 | tf_op jit(solution)/shard_map/ppermute | solution.py:316
  121.6 9.7 %collective-permute-start.30 = (bf16[512,128]{1,0:T(8,128)(2,1)S(1)}, bf16[512,128]{1,0:T(8,128)(2,1)S(1)}, u32[]{:S(2)}, u32[]{:S(2)}) collective-permute-start(bf16[512,128]{1,0:T(8,128)(2,1)S(1)} %collective-permute-done.28.refs_12_), channel_id=1, source_target_pairs={{2,3},{1,0},{6,7},{5,4},{10,11},{9,8},{14,15},{13,12},{18,19},{17,... | collective-permute-start | bytes 393224 | tf_op jit(solution)/shard_map/ppermute | solution.py:426
  (31 other events, 364.2 us)
Sparse Core Ops, SparseCore 0:
  50.8 34.6 all-gather.2

commit v3 on v0

v3 whole, which is shorter than its diff:
```python
import functools
import jax
import jax.numpy as jnp
import numpy as np
from jax import lax
from jax.experimental import pallas as pl
from jax.experimental.pallas import tpu as pltpu
from jax.sharding import PartitionSpec as P

HD = 256
ROT = 64
BLK = 512
OWNERS = 2
GROUPS = 4
SLOTS = GROUPS * OWNERS
MOST = 128
SEEN = OWNERS * BLK

NEG_FILL = -1e30
ROPE_BASE = 10000.0
FACTOR = HD ** (-0.5) * 1.4426950408889634

RB = 128

VMEM = pl.BlockSpec(memory_space=pltpu.VMEM)
SMEM = pl.BlockSpec(memory_space=pltpu.SMEM)


def from_root(x, axis, root):
    mine = lax.axis_index(axis) == root
    return lax.psum(jnp.where(mine, x, jnp.zeros_like(x)), axis)


def rope_table():
    inverse = np.float32(ROPE_BASE) ** (-2.0 * np.arange(ROT // 2, dtype=np.float32) / ROT)
    inverse = np.concatenate([np.repeat(inverse, 2), np.zeros(128 - ROT)]).astype(np.float32)
    angles = np.arange(SEEN, SEEN + MOST, dtype=np.float32)[:, None] * inverse[None, :]
    angles = angles.astype(np.float64)
    sign = np.where(np.arange(128) % 2 == 0, -1.0, 1.0)
    table = np.concatenate([np.cos(angles), np.sin(angles) * sign[None, :]], axis=1)
    return jnp.asarray(table.astype(np.float32))


def prep_kernel(spans, where_ref, *refs):
    tables = refs[:spans]
    q_ref, k_ref, v_ref, rope_ref = refs[spans : spans + 4]
    first_ref, grp_ref = refs[spans + 4 : spans + 6]
    o_refs = refs[spans + 6 :]
    rows = q_ref.shape[0]
    heads = len(o_refs)
    lane = lax.broadcasted_iota(jnp.int32, (RB, 128), 1)
    even = (lane % 2) == 0
    for n in range(spans):
        requests = tables[n].shape[1]
        for r0 in range(0, rows, RB):
            row = r0 + lax.broadcasted_iota(jnp.int32, (RB, 128), 0)
            start = jnp.int32(0)
            first = jnp.zeros((RB, 128), jnp.int32)
            grp = jnp.zeros((RB, 128), jnp.int32) + tables[n][1, 0]
            for r in range(1, requests):
                start = start + tables[n][0, r - 1]
                later = row >= start
                first = jnp.where(later, start, first)
                grp = jnp.where(later, tables[n][1, r], grp)
            first_ref[n * rows + r0 : n * rows + r0 + RB, :] = first
            grp_ref[n * rows + r0 : n * rows + r0 + RB, :] = grp
    for r0 in range(0, rows, RB):
        at = slice(r0, r0 + RB)
        row = r0 + lax.broadcasted_iota(jnp.int32, (RB, 128), 0)
        chosen = jnp.where(row - first_ref[at, :] == lane, 1.0, 0.0)
        turn = lax.dot_general(
            chosen,
            rope_ref[...],
            (((1,), (0,)), ((), ())),
            precision=lax.Precision.HIGHEST,
            preferred_element_type=jnp.float32,
        )
        cos = turn[:, :128]
        sin = turn[:, 128:]
        for i, o_ref in enumerate(o_refs):
            flip = where_ref[1] > 0
            for n, ref in enumerate((q_ref, k_ref)):
                x = ref[at, i * HD : (i + 1) * HD]
                if heads == 2:
                    x = jnp.where(flip, ref[at, (1 - i) * HD : (2 - i) * HD], x)
                y = x[:, :128].astype(jnp.float32)
                swapped = jnp.where(even, pltpu.roll(y, 127, 1), pltpu.roll(y, 1, 1))
                o_ref[n, at, 0:128] = (y * cos + swapped * sin).astype(jnp.bfloat16)
                o_ref[n, at, 128:HD] = x[:, 128:]
            v = v_ref[at, i * HD : (i + 1) * HD]
            if heads == 2:
                v = jnp.where(flip, v_ref[at, (1 - i) * HD : (2 - i) * HD], v)
            o_ref[2, at, :] = v


def prepare(where, tables, q, k, v):
    rows, feat = q.shape
    heads = feat // HD
    spans = len(tables)
    column = jax.ShapeDtypeStruct((spans * rows, 128), jnp.int32)
    return pl.pallas_call(
        functools.partial(prep_kernel, spans),
        out_shape=[column] * 2 + [jax.ShapeDtypeStruct((3, rows, HD), jnp.bfloat16)] * heads,
        in_specs=[SMEM] * (1 + spans) + [VMEM] * 4,
        out_specs=[VMEM] * (2 + heads),
        compiler_params=pltpu.CompilerParams(vmem_limit_bytes=4 << 20),
        name="prepare",
    )(where, *tables, q, k, v, rope_table())


def cut_kernel(where_ref, w_ref, own_ref, *rest):
    sends = rest[:-1]
    sems = rest[-1]
    z = where_ref[0]
    core = where_ref[1]
    side = where_ref[2]
    cols = own_ref.shape[1]
    high, width = sends[0].shape
    copies = []
    for m in range(1, 1 + len(sends)):
        at = lax.bitwise_xor(z, m) * cols + side * width
        copies.append(
            pltpu.make_async_copy(
                w_ref.at[
                    pl.ds(pl.multiple_of(core * high, high), high),
                    pl.ds(pl.multiple_of(at, width), width),
                ],
                sends[m - 1],
                sems.at[m],
            )
        )
    copies.append(
        pltpu.make_async_copy(
            w_ref.at[:, pl.ds(pl.multiple_of(z * cols, cols), cols)], own_ref, sems.at[0]
        )
    )
    for c in copies:
        c.start()
    for c in copies:
        c.wait()


def cut(where, w, tp_size):
    rows, cols = w.shape[0], w.shape[1] // tp_size
    return pl.pallas_call(
        cut_kernel,
        out_shape=[jax.ShapeDtypeStruct((rows, cols), w.dtype)]
        + [jax.ShapeDtypeStruct((rows // 2, cols // 2), w.dtype)] * (tp_size - 1),
        in_specs=[SMEM, pl.BlockSpec(memory_space=pl.ANY)],
        out_specs=[VMEM] * tp_size,
        scratch_shapes=[pltpu.SemaphoreType.DMA((tp_size,))],
        compiler_params=pltpu.CompilerParams(vmem_limit_bytes=1 << 20),
        name="cut",
    )(where, w)


def wide(x, width):
    return x if width == 128 else jnp.concatenate([x] * (width // 128), axis=1)


def score_kernel(nb, place_ref, first_ref, grp_ref, *rest):
    sufs = rest[:nb]
    pieces = rest[nb : nb + SLOTS]
    p_ref, near_ref, den_ref, sc = rest[nb + SLOTS :]
    half = 256
    for n in range(nb):
        rows = sufs[n].shape[1]
        for b in range(rows // RB):
            r0 = b * RB
            t0 = n * rows + r0
            buf = (t0 // RB) % 2
            q = sufs[n][0, r0 : r0 + RB, :]
            grp = wide(grp_ref[t0 : t0 + RB, :], half)
            for d in range(SLOTS):
                g = place_ref[d] // OWNERS
                o = place_ref[d] % OWNERS
                for j in range(BLK // half):
                    s = lax.dot_general(
                        q,
                        pieces[d][j * half : (j + 1) * half, :],
                        (((1,), (1,)), ((), ())),
                        preferred_element_type=jnp.float32,
                    )
                    at = pl.ds(pl.multiple_of(o * BLK + j * half, half), half)
                    sc[buf, :, at] = jnp.where(grp == g, s, sc[buf, :, at])
            lo = max(0, r0 - MOST)
            width = r0 + RB - lo
            local = lax.dot_general(
                q,
                sufs[n][1, lo : r0 + RB, :],
                (((1,), (1,)), ((), ())),
                preferred_element_type=jnp.float32,
            )
            row = r0 + lax.broadcasted_iota(jnp.int32, (RB, width), 0)
            key = lo + lax.broadcasted_iota(jnp.int32, (RB, width), 1)
            start = wide(first_ref[t0 : t0 + RB, :], width)
            local = jnp.where((key <= row) & (key >= start), local, NEG_FILL)
            top = jnp.max(local, axis=1, keepdims=True)
            whole = sc[buf, :, 0:half]
            for c0 in range(half, SEEN, half):
                whole = jnp.maximum(whole, sc[buf, :, c0 : c0 + half])
            top = jnp.maximum(top, jnp.max(whole, axis=1, keepdims=True))
            e = jnp.exp2((local - top) * FACTOR)
            den = jnp.sum(e, axis=1, keepdims=True)
            near_ref[t0 : t0 + RB, 0:width] = e.astype(jnp.bfloat16)
            total = None
            for c0 in range(0, SEEN, half):
                e = jnp.exp2((sc[buf, :, c0 : c0 + half] - top) * FACTOR)
                p_ref[t0 : t0 + RB, c0 : c0 + half] = e.astype(jnp.bfloat16)
                total = e if total is None else total + e
            den = den + jnp.sum(total, axis=1, keepdims=True)
            den_ref[t0 : t0 + RB, :] = jnp.broadcast_to(den, (RB, 128))


def score(place, first, grp, sufs, pieces):
    rows = sum(s.shape[1] for s in sufs)
    return pl.pallas_call(
        functools.partial(score_kernel, len(sufs)),
        out_shape=[
            jax.ShapeDtypeStruct((rows, SEEN), jnp.bfloat16),
            jax.ShapeDtypeStruct((rows, RB + MOST), jnp.bfloat16),
            jax.ShapeDtypeStruct((rows, 128), jnp.float32),
        ],
        in_specs=[SMEM] + [VMEM] * (2 + len(sufs) + SLOTS),
        out_specs=[VMEM] * 3,
        scratch_shapes=[pltpu.VMEM((2, RB, SEEN), jnp.float32)],
        compiler_params=pltpu.CompilerParams(vmem_limit_bytes=4 << 20),
        name="score",
    )(place, first, grp, *sufs, *pieces)


def mix_kernel(nb, col, place_ref, grp_ref, p_ref, near_ref, den_ref, *rest):
    sufs = rest[:nb]
    pieces = rest[nb : nb + SLOTS]
    outs = rest[nb + SLOTS :]
    width = outs[0].shape[1]
    for n in reversed(range(nb)):
        rows = outs[n].shape[0]
        for b in range(rows // RB):
            r0 = b * RB
            t0 = n * rows + r0
            grp = wide(grp_ref[t0 : t0 + RB, :], width)
            lo = max(0, r0 - MOST)
            acc = jnp.dot(
                near_ref[t0 : t0 + RB, 0 : r0 + RB - lo],
                sufs[n][2, lo : r0 + RB, col : col + width],
                preferred_element_type=jnp.float32,
            )
            for d in range(SLOTS):
                g = place_ref[d] // OWNERS
                o = place_ref[d] % OWNERS
                part = jnp.dot(
                    p_ref[t0 : t0 + RB, pl.ds(pl.multiple_of(o * BLK, BLK), BLK)],
                    pieces[d][...],
                    preferred_element_type=jnp.float32,
                )
                acc = acc + jnp.where(grp == g, part, 0.0)
            den = wide(den_ref[t0 : t0 + RB, :], width)
            outs[n][r0 : r0 + RB, :] = (acc / den).astype(jnp.bfloat16)


def mix(col, width, place, grp, scored, sufs, pieces):
    rows = sufs[0].shape[1]
    nb = len(sufs)
    return pl.pallas_call(
        functools.partial(mix_kernel, nb, col),
        out_shape=[jax.ShapeDtypeStruct((rows, width), jnp.bfloat16)] * nb,
        in_specs=[SMEM] + [VMEM] * (4 + nb + SLOTS),
        out_specs=[VMEM] * nb,
        compiler_params=pltpu.CompilerParams(vmem_limit_bytes=4 << 20),
        name="mix",
    )(place, grp, *scored, *sufs, *pieces)


def proj_kernel(where_ref, *refs):
    att = refs[:10]
    own = refs[10]
    far = refs[11:15]
    o_ref = refs[15]
    cols = o_ref.shape[1] // 2
    rows = o_ref.shape[0]
    core = where_ref[1]
    side = where_ref[2]
    tall = 256
    for r0 in range(0, rows, tall):
        for x in range(2):
            c0 = pl.multiple_of(lax.bitwise_xor(side, x) * cols, cols)
            acc = jnp.zeros((tall, cols), jnp.float32)
            for h in range(2):
                head = lax.bitwise_xor(core, h)
                for m in range(4):
                    a = att[h * 5 + m][r0 : r0 + tall, :]
                    if m == 3:
                        a = a + att[h * 5 + 4][r0 : r0 + tall, :]
                    if m == 0:
                        w = own[pl.ds(pl.multiple_of(head * HD, HD), HD), pl.ds(c0, cols)]
                    else:
                        w = far[2 * h + x][m - 1]
                    acc = acc + jnp.dot(a, w, preferred_element_type=jnp.float32)
            o_ref[r0 : r0 + tall, pl.ds(c0, cols)] = acc.astype(jnp.bfloat16)


def project(where, att, own, far):
    rows = att[0].shape[0]
    cols = own.shape[1]
    return pl.pallas_call(
        proj_kernel,
        out_shape=jax.ShapeDtypeStruct((rows, cols), jnp.bfloat16),
        in_specs=[SMEM] + [VMEM] * (len(att) + 1 + len(far)),
        out_specs=VMEM,
        compiler_params=pltpu.CompilerParams(vmem_limit_bytes=6 << 20),
        name="project",
    )(where, *att, own, *far)


def swap(x, axis, mask, size):
    return lax.ppermute(x, axis, [(i, i ^ mask) for i in range(size)])


def after(x, *deps):
    return lax.optimization_barrier((x,) + deps)[0]


over_x = functools.partial(swap, axis="req", mask=2, size=8)
over_y = functools.partial(swap, axis="req", mask=4, size=8)
over_core = functools.partial(swap, axis="req", mask=1, size=8)


def split_heads(suffix_heads, prefix_cache, lengths, groups, owners, out_weight):
    me = lax.axis_index("req")
    z = lax.axis_index("tp")
    core = me & 1
    side = (me >> 1) & 1
    where = jnp.stack([z, core, side]).astype(jnp.int32)
    place = jnp.sum(
        jnp.where(
            owners[None] == (me ^ jnp.arange(SLOTS, dtype=jnp.int32))[:, None, None],
            jnp.arange(SLOTS, dtype=jnp.int32).reshape(1, GROUPS, OWNERS),
            0,
        ),
        axis=(1, 2),
    ).astype(jnp.int32)
    tp_size = 4
    first_head = core == 0

    k = prefix_cache[:, 0]
    k_own = jnp.where(first_head, k[:, :HD], k[:, HD:])
    k_other = jnp.where(first_head, k[:, HD:], k[:, :HD])
    k_pair = over_core(k_other)
    ax = over_x(k_own)
    ay = over_y(k_own)
    bx = over_x(k_pair)
    by = over_y(k_pair)

    table = jnp.concatenate([lengths, groups], axis=0)
    table_pair = over_core(table)
    first, grp, mine, other = prepare(
        where, (table, table_pair), suffix_heads[:, 0], suffix_heads[:, 1], suffix_heads[:, 2]
    )
    axy = over_y(after(ax, mine))
    bxy = over_x(after(by, mine))
    sufs = [mine, over_core(other)]
    k_pieces = [k_own, k_pair, ax, bx, ay, by, axy, bxy]

    v = after(prefix_cache, k_own)[:, 1]
    v_own = jnp.where(first_head, v[:, :HD], v[:, HD:])
    v_other = jnp.where(first_head, v[:, HD:], v[:, :HD])
    v_pair = over_core(v_other)
    v_own, v_pair = lax.optimization_barrier((v_own, v_pair, ay, bx, axy, bxy))[:2]
    vax = over_x(v_own)
    vay = over_y(v_own)
    vbx = over_x(v_pair)
    vby = over_y(v_pair)

    w_own, *sends = cut(where, out_weight, tp_size)
    w_far = jnp.stack([swap(sends[m - 1], "tp", m, tp_size) for m in range(1, tp_size)])

    vaxy = over_y(after(vax, w_far))
    vbxy = over_x(after(vby, w_far))
    v_pieces = [v_own, v_pair, vax, vbx, vay, vby, vaxy, vbxy]

    w_x = over_x(after(w_far, vay, vbx, vaxy, vbxy))
    w_core = over_core(after(w_far, vay, vbx, vaxy, vbxy))
    w_core_x = over_core(w_x)

    scored = score(place, first, grp, sufs, k_pieces)
    own, pair = mix(0, HD, place, grp, scored, sufs, v_pieces)
    back = over_core(pair)
    att = []
    for a in (own, back):
        two = swap(a, "tp", 2, tp_size)
        three = lax.ppermute(a, "tp", [(1, 2), (2, 1)])
        one = swap(a, "tp", 1, tp_size)
        forward = lax.ppermute(two, "tp", [(2, 3), (1, 0)])
        att += [a, one, two, three, forward]
    return project(where, att, w_own, [w_far, w_x, w_core, w_core_x])


def whole_heads(suffix_heads, prefix_cache, lengths, groups, owners, out_weight):
    heads = suffix_heads.shape[2] // HD
    received = [
        from_root(prefix_cache, "req", owners[i // OWNERS, i % OWNERS]) for i in range(SLOTS)
    ]
    place = jnp.arange(SLOTS, dtype=jnp.int32)
    first, grp, *sufs = prepare(
        jnp.zeros((3,), jnp.int32),
        (jnp.concatenate([lengths, groups], axis=0),),
        suffix_heads[:, 0],
        suffix_heads[:, 1],
        suffix_heads[:, 2],
    )
    attended = []
    for h in range(heads):
        keys = [s[:, 0, h * HD : (h + 1) * HD] for s in received]
        values = [s[:, 1, h * HD : (h + 1) * HD] for s in received]
        scored = score(place, first, grp, [sufs[h]], keys)
        attended += mix(0, HD, place, grp, scored, [sufs[h]], values)
    partial_out = jnp.dot(
        jnp.concatenate(attended, axis=1), out_weight, preferred_element_type=jnp.float32
    )
    return lax.psum_scatter(partial_out.astype(jnp.bfloat16), "tp", scatter_dimension=1, tiled=True)


def per_device(req_size, tp_size, *args):
    if req_size == 8 and tp_size == 4 and args[0].shape[2] == 2 * HD:
        return split_heads(*args)
    return whole_heads(*args)


def solution(mesh):
    placed = (
        P("req", None, "tp"),
        P("req", None, "tp"),
        P("req", None),
        P("req", None),
        P(),
        P("tp", None),
    )
    return jax.shard_map(
        functools.partial(per_device, mesh.shape["req"], mesh.shape["tp"]),
        mesh=mesh,
        in_specs=placed,
        out_specs=P("req", "tp"),
        check_vma=False,
    )
```

time: 267 us -> 128 us (0.48)
  waiting for transfers between devices: 205 us -> 71.2 us
  starting transfers between devices: 0.04 us -> 32.8 us
  between operations: 18.7 us -> 0.19 us
  Pallas kernels: 0 us -> 18.5 us
  matrix products: 17.3 us -> 0 us
  local copies, waits for them, and re-layouts: 17.4 us -> 3.95 us
  other arithmetic: 7.3 us -> 1.06 us
    psum x1 -> x0, waiting for transfers between devices: 128 us -> none  [from_root(): return lax.psum(jnp.where(mine, x, jnp.zeros_like(x)), axis)]
    reduce_scatter x1 -> x0, waiting for transfers between devices: 77.2 us -> none  [per_device(): lax.psum_scatter(partial_out.astype(jnp.bfloat16), 'tp', scatter_dimensio...]
    ppermute x0 -> x31, waiting for transfers between devices: none -> 71.2 us  [the longest x27 61.3 us: swap(): return lax.ppermute(x, axis, [(i, i ^ mask) for i in range(size)])]
    ppermute x0 -> x31, starting transfers between devices: none -> 32.8 us  [the longest x27 28.9 us: swap(): return lax.ppermute(x, axis, [(i, i ^ mask) for i in range(size)])]
    pallas_call x0 -> x5, Pallas kernels: none -> 18.5 us  [the longest x1 8.06 us: score(): pl.pallas_call(functools.partial(score_kernel, len(sufs)), out_shape=[jax...]
    dot_general x9 -> x0, matrix products: 17.3 us -> none  [the longest x2 6.51 us: one_head(): lax.dot_general(query_h, pkey_h, (((1,), (1,)), ((), ())), preferred_elem...]
    slice x8 -> x0, local copies, waits for them, and re-layouts: 5.62 us -> none  [the longest x1 3.75 us: joint_attention(): prefix_values = shared[:, 1].reshape(shared.shape[0], heads_here, HD)]
    unnamed x25 -> x15, local copies, waits for them, and re-layouts: 9.15 us -> 3.65 us
  transfers between devices with their start and end apart: 2 -> 31, of which waited for: 2 -> 13; matrix products, arithmetic and copies ran while one was open for 1% -> 1% of each run, Pallas kernels for 0% -> 11%
where the time goes in v3:
time: 128 us
  waiting for transfers between devices  71.2 us (56%)
  starting transfers between devices  32.8 us (26%)
  Pallas kernels  18.5 us (14%)
  local copies, waits for them, and re-layouts  3.95 us (3%)
    ppermute x27, waiting for transfers between devices, swap(): return lax.ppermute(x, axis, [(i, i ^ mask) for i in range(size)])  61.3 us
    ppermute x27, starting transfers between devices, swap(): return lax.ppermute(x, axis, [(i, i ^ mask) for i in range(size)])  28.9 us
    ppermute x2, waiting for transfers between devices, split_heads(): forward = lax.ppermute(two, 'tp', [(2, 3), (1, 0)])  9.83 us
    pallas_call x1, Pallas kernels, score(): pl.pallas_call(functools.partial(score_kernel, len(sufs)), out_shape=[jax...  8.06 us
    pallas_call x1, Pallas kernels, project(): pl.pallas_call(proj_kernel, out_shape=jax.ShapeDtypeStruct((rows, cols),...  3.86 us
    pallas_call x1, Pallas kernels, mix(): pl.pallas_call(functools.partial(mix_kernel, nb, col), out_shape=[jax.Sha...  3.84 us
    unnamed x15, local copies, waits for them, and re-layouts  3.65 us
    ppermute x2, starting transfers between devices, split_heads(): forward = lax.ppermute(two, 'tp', [(2, 3), (1, 0)])  2.56 us
  transfers between devices with their start and end apart: 31, of which 13 were waited for; matrix products, arithmetic and copies ran while one was open for 1% of the time, Pallas kernels for 11%

profile of v3, /device:TPU:0, one launch (start us, length us, event | category | flops | bytes accessed | tf_op | source)
XLA Modules:
  0.0 127.6 jit_solution(14909817210739846274)
XLA Ops:
  0.0 1.4 %copy.15 = bf16[512,1,512]{2,0,1:T(8,128)(2,1)S(1)} copy(bf16[512,1,512]{2,1,0:T(2,128)(2,1)} %bitcast.18) | data formatting | bytes 1048576
  1.5 3.0 %collective-permute-start.5 = (bf16[512,256]{1,0:T(8,128)(2,1)S(1)}, bf16[512,256]{1,0:T(8,128)(2,1)S(1)}, u32[]{:S(2)}, u32[]{:S(2)}) collective-permute-start(bf16[512,256]{1,0:T(8,128)(2,1)S(1)} %get-tuple-element.53.rest_2_), channel_id=1, source_target_pairs={{0,16},{4,20},{8,24},{12,28},{16,0},{20,4},{24,8},{28,12},{1,17},{... | collective-permute-start | bytes 786440 | tf_op jit(solution)/shard_map/ppermute | solution.py:317
  4.5 1.5 %collective-permute-start.3 = (bf16[512,256]{1,0:T(8,128)(2,1)S(1)}, bf16[512,256]{1,0:T(8,128)(2,1)S(1)}, u32[]{:S(2)}, u32[]{:S(2)}) collective-permute-start(bf16[512,256]{1,0:T(8,128)(2,1)S(1)} %get-tuple-element.53.rest_2_), channel_id=1, source_target_pairs={{0,8},{4,12},{8,0},{12,4},{16,24},{20,28},{24,16},{28,20},{1,9},{5... | collective-permute-start | bytes 786440 | tf_op jit(solution)/shard_map/ppermute | solution.py:317
  6.9 0.7 broadcast_select_fusion
  8.6 1.8 %prepare.1 = (s32[1024,128]{1,0:T(8,128)S(1)}, s32[1024,128]{1,0:T(8,128)S(1)}, bf16[3,512,256]{2,1,0:T(8,128)(2,1)S(1)}, bf16[3,512,256]{2,1,0:T(8,128)(2,1)S(1)}) custom-call(s32[3]{0:T(128)S(1)} %pad_add_fusion.1.where_ref, s32[2,8]{1,0:T(2,128)S(1)} %pad_add_fusion.refs_0_, s32[2,8]{1,0:T(2,128)S(1)} %collective-permute-done.refs_1_, ...), custom_call_target="tpu_custom_call" | custom-call | tf_op jit(solution)/shard_map/prepare/pallas_call | solution.py:101
  10.4 3.2 %collective-permute-done.3.rest_4_ = bf16[512,256]{1,0:T(8,128)(2,1)S(1)} collective-permute-done((bf16[512,256]{1,0:T(8,128)(2,1)S(1)}, bf16[512,256]{1,0:T(8,128)(2,1)S(1)}, u32[]{:S(2)}, u32[]{:S(2)}) %collective-permute-start.3) | collective-permute-done | bytes 262176 | tf_op jit(solution)/shard_map/ppermute | solution.py:317
  13.6 3.4 %collective-permute-done.6.rest_7_ = bf16[512,256]{1,0:T(8,128)(2,1)S(1)} collective-permute-done((bf16[512,256]{1,0:T(8,128)(2,1)S(1)}, bf16[512,256]{1,0:T(8,128)(2,1)S(1)}, u32[]{:S(2)}, u32[]{:S(2)}) %collective-permute-start.6) | collective-permute-done | bytes 262176 | tf_op jit(solution)/shard_map/ppermute | solution.py:317
  16.9 2.4 %collective-permute-start.8 = (bf16[512,256]{1,0:T(8,128)(2,1)S(1)}, bf16[512,256]{1,0:T(8,128)(2,1)S(1)}, u32[]{:S(2)}, u32[]{:S(2)}) collective-permute-start(bf16[512,256]{1,0:T(8,128)(2,1)S(1)} %collective-permute-done.6.rest_7_), channel_id=1, source_target_pairs={{0,8},{4,12},{8,0},{12,4},{16,24},{20,28},{24,16},{28,20},{1,9},{5... | collective-permute-start | bytes 786440 | tf_op jit(solution)/shard_map/ppermute | solution.py:317
  19.3 2.2 %copy-done = bf16[512,4096]{1,0:T(8,128)(2,1)S(1)} copy-done((bf16[512,4096]{1,0:T(8,128)(2,1)S(1)}, bf16[512,4096]{1,0:T(8,128)(2,1)}, u32[]{:S(2)}) %copy-start) | copy-done | bytes 4194328
  21.5 1.0 cut.1
  22.5 1.6 %collective-permute-start.14 = (bf16[256,512]{1,0:T(8,128)(2,1)S(1)}, bf16[256,512]{1,0:T(8,128)(2,1)S(1)}, u32[]{:S(2)}, u32[]{:S(2)}) collective-permute-start(bf16[256,512]{1,0:T(8,128)(2,1)S(1)} %get-tuple-element.38), channel_id=1, source_target_pairs={{0,1},{1,0},{2,3},{3,2},{4,5},{5,4},{6,7},{7,6},{8,9},{9,8},{10,11... | collective-permute-start | bytes 786440 | tf_op jit(solution)/shard_map/ppermute | solution.py:317
  24.1 2.6 %collective-permute-start.15 = (bf16[256,512]{1,0:T(8,128)(2,1)S(1)}, bf16[256,512]{1,0:T(8,128)(2,1)S(1)}, u32[]{:S(2)}, u32[]{:S(2)}) collective-permute-start(bf16[256,512]{1,0:T(8,128)(2,1)S(1)} %get-tuple-element.39), channel_id=1, source_target_pairs={{0,2},{1,3},{2,0},{3,1},{4,6},{5,7},{6,4},{7,5},{8,10},{9,11},{10,... | collective-permute-start | bytes 786440 | tf_op jit(solution)/shard_map/ppermute | solution.py:317
  27.0 1.5 %collective-permute-start.13 = (bf16[512,256]{1,0:T(8,128)(2,1)}, bf16[512,256]{1,0:T(8,128)(2,1)S(1)}, u32[]{:S(2)}, u32[]{:S(2)}) collective-permute-start(bf16[512,256]{1,0:T(8,128)(2,1)} %collective-permute-done.9.rest_3_), channel_id=1, source_target_pairs={{0,16},{4,20},{8,24},{12,28},{16,0},{20,4},{24,8},{28,12},{1,17},{... | collective-permute-start | bytes 786440 | tf_op jit(solution)/shard_map/ppermute | solution.py:317
  29.0 2.9 %collective-permute-done.14 = bf16[256,512]{1,0:T(8,128)(2,1)S(1)} collective-permute-done((bf16[256,512]{1,0:T(8,128)(2,1)S(1)}, bf16[256,512]{1,0:T(8,128)(2,1)S(1)}, u32[]{:S(2)}, u32[]{:S(2)}) %collective-permute-start.14) | collective-permute-done | bytes 262176 | tf_op jit(solution)/shard_map/ppermute | solution.py:317
  31.9 12.7 %collective-permute-done.15 = bf16[256,512]{1,0:T(8,128)(2,1)S(1)} collective-permute-done((bf16[256,512]{1,0:T(8,128)(2,1)S(1)}, bf16[256,512]{1,0:T(8,128)(2,1)S(1)}, u32[]{:S(2)}, u32[]{:S(2)}) %collective-permute-start.15) | collective-permute-done | bytes 262176 | tf_op jit(solution)/shard_map/ppermute | solution.py:317
  44.7 1.6 %collective-permute-start.12 = (bf16[512,256]{1,0:T(8,128)(2,1)S(1)}, bf16[512,256]{1,0:T(8,128)(2,1)S(1)}, u32[]{:S(2)}, u32[]{:S(2)}) collective-permute-start(bf16[512,256]{1,0:T(8,128)(2,1)S(1)} %get-tuple-element.36.rest_2_), channel_id=1, source_target_pairs={{0,16},{4,20},{8,24},{12,28},{16,0},{20,4},{24,8},{28,12},{1,17},{... | collective-permute-start | bytes 786440 | tf_op jit(solution)/shard_map/ppermute | solution.py:317
  46.8 0.9 collective-permute-start.17
  47.7 1.1 collective-permute-start.18
  48.8 2.3 %collective-permute-done.12.rest_6_ = bf16[512,256]{1,0:T(8,128)(2,1)S(1)} collective-permute-done((bf16[512,256]{1,0:T(8,128)(2,1)S(1)}, bf16[512,256]{1,0:T(8,128)(2,1)S(1)}, u32[]{:S(2)}, u32[]{:S(2)}) %collective-permute-start.12) | collective-permute-done | bytes 262176 | tf_op jit(solution)/shard_map/ppermute | solution.py:317
  51.1 2.5 %collective-permute-done.11.rest_5_ = bf16[512,256]{1,0:T(8,128)(2,1)S(1)} collective-permute-done((bf16[512,256]{1,0:T(8,128)(2,1)}, bf16[512,256]{1,0:T(8,128)(2,1)S(1)}, u32[]{:S(2)}, u32[]{:S(2)}) %collective-permute-start.11) | collective-permute-done | bytes 262176 | tf_op jit(solution)/shard_map/ppermute | solution.py:317
  53.9 5.3 %collective-permute-done.18.rest_9_ = bf16[512,256]{1,0:T(8,128)(2,1)S(1)} collective-permute-done((bf16[512,256]{1,0:T(8,128)(2,1)S(1)}, bf16[512,256]{1,0:T(8,128)(2,1)S(1)}, u32[]{:S(2)}, u32[]{:S(2)}) %collective-permute-start.18) | collective-permute-done | bytes 262176 | tf_op jit(solution)/shard_map/ppermute | solution.py:317
  59.5 8.1 %score.1 = (bf16[1024,1024]{1,0:T(8,128)(2,1)S(1)}, bf16[1024,256]{1,0:T(8,128)(2,1)S(1)}, f32[1024,128]{1,0:T(8,128)S(1)}) custom-call(s32[8]{0:T(128)S(1)} %select_reduce_fusion.place_ref, s32[1024,128]{1,0:T(8,128)S(1)} %get-tuple-element.27.first_ref, s32[1024,128]{1,0:T(8,128)S(1)} %get-tuple-element.26.grp_ref, ...), custom_call_target="tpu_custom_call" | custom-call | tf_op jit(solution)/shard_map/score/pallas_call | solution.py:217
  67.6 3.8 %mix.1 = (bf16[512,256]{1,0:T(8,128)(2,1)S(1)}, bf16[512,256]{1,0:T(8,128)(2,1)S(1)}) custom-call(s32[8]{0:T(128)S(1)} %select_reduce_fusion.place_ref, s32[1024,128]{1,0:T(8,128)S(1)} %get-tuple-element.26.grp_ref, bf16[1024,1024]{1,0:T(8,128)(2,1)S(1)} %get-tuple-element.32.p_ref, bf16[1024,256]{1,0:T(8,128)(2,1)S(1)} %get-tuple-element.33.near_ref, ...), custom_call_target="tpu_custom_call" | custom-call | tf_op jit(solution)/shard_map/mix/pallas_call | solution.py:265
  72.2 5.5 %collective-permute-start.20 = (bf16[512,256]{1,0:T(8,128)(2,1)S(1)}, bf16[512,256]{1,0:T(8,128)(2,1)S(1)}, u32[]{:S(2)}, u32[]{:S(2)}) collective-permute-start(bf16[512,256]{1,0:T(8,128)(2,1)S(1)} %get-tuple-element.43.refs_0_), channel_id=1, source_target_pairs={{0,2},{1,3},{2,0},{3,1},{4,6},{5,7},{6,4},{7,5},{8,10},{9,11},{10,... | collective-permute-start | bytes 786440 | tf_op jit(solution)/shard_map/ppermute | solution.py:317
  79.4 16.6 %collective-permute-done.20.refs_2_ = bf16[512,256]{1,0:T(8,128)(2,1)S(1)} collective-permute-done((bf16[512,256]{1,0:T(8,128)(2,1)S(1)}, bf16[512,256]{1,0:T(8,128)(2,1)S(1)}, u32[]{:S(2)}, u32[]{:S(2)}) %collective-permute-start.20) | collective-permute-done | bytes 262176 | tf_op jit(solution)/shard_map/ppermute | solution.py:317
  96.0 3.3 %collective-permute-start.24 = (bf16[512,256]{1,0:T(8,128)(2,1)S(1)}, bf16[512,256]{1,0:T(8,128)(2,1)S(1)}, u32[]{:S(2)}, u32[]{:S(2)}) collective-permute-start(bf16[512,256]{1,0:T(8,128)(2,1)S(1)} %collective-permute-done.23.refs_5_), channel_id=1, source_target_pairs={{0,1},{1,0},{2,3},{3,2},{4,5},{5,4},{6,7},{7,6},{8,9},{9,8},{10,11... | collective-permute-start | bytes 786440 | tf_op jit(solution)/shard_map/ppermute | solution.py:317
  99.3 1.3 %collective-permute-start.22 = (bf16[512,256]{1,0:T(8,128)(2,1)S(1)}, bf16[512,256]{1,0:T(8,128)(2,1)S(1)}, u32[]{:S(2)}, u32[]{:S(2)}) collective-permute-start(bf16[512,256]{1,0:T(8,128)(2,1)S(1)} %collective-permute-done.20.refs_2_), channel_id=1, source_target_pairs={{2,3},{1,0},{6,7},{5,4},{10,11},{9,8},{14,15},{13,12},{18,19},{17,... | collective-permute-start | bytes 786440 | tf_op jit(solution)/shard_map/ppermute | solution.py:394
  100.6 12.1 %collective-permute-done.25.refs_7_ = bf16[512,256]{1,0:T(8,128)(2,1)S(1)} collective-permute-done((bf16[512,256]{1,0:T(8,128)(2,1)S(1)}, bf16[512,256]{1,0:T(8,128)(2,1)S(1)}, u32[]{:S(2)}, u32[]{:S(2)}) %collective-permute-start.25) | collective-permute-done | bytes 262176 | tf_op jit(solution)/shard_map/ppermute | solution.py:317
  112.6 1.3 %collective-permute-start.27 = (bf16[512,256]{1,0:T(8,128)(2,1)S(1)}, bf16[512,256]{1,0:T(8,128)(2,1)S(1)}, u32[]{:S(2)}, u32[]{:S(2)}) collective-permute-start(bf16[512,256]{1,0:T(8,128)(2,1)S(1)} %collective-permute-done.25.refs_7_), channel_id=1, source_target_pairs={{2,3},{1,0},{6,7},{5,4},{10,11},{9,8},{14,15},{13,12},{18,19},{17,... | collective-permute-start | bytes 786440 | tf_op jit(solution)/shard_map/ppermute | solution.py:394
  113.9 4.3 %collective-permute-done.22.refs_4_ = bf16[512,256]{1,0:T(8,128)(2,1)S(1)} collective-permute-done((bf16[512,256]{1,0:T(8,128)(2,1)S(1)}, bf16[512,256]{1,0:T(8,128)(2,1)S(1)}, u32[]{:S(2)}, u32[]{:S(2)}) %collective-permute-start.22) | collective-permute-done | bytes 262176 | tf_op jit(solution)/shard_map/ppermute | solution.py:394
  118.2 5.5 %collective-permute-done.27.refs_9_ = bf16[512,256]{1,0:T(8,128)(2,1)S(1)} collective-permute-done((bf16[512,256]{1,0:T(8,128)(2,1)S(1)}, bf16[512,256]{1,0:T(8,128)(2,1)S(1)}, u32[]{:S(2)}, u32[]{:S(2)}) %collective-permute-start.27) | collective-permute-done | bytes 262176 | tf_op jit(solution)/shard_map/ppermute | solution.py:394
  123.8 3.9 %project.1 = bf16[512,1024]{1,0:T(8,128)(2,1)} custom-call(s32[3]{0:T(128)S(1)} %pad_add_fusion.1.where_ref, bf16[512,256]{1,0:T(8,128)(2,1)S(1)} %get-tuple-element.43.refs_0_, bf16[512,256]{1,0:T(8,128)(2,1)S(1)} %collective-permute-done.19.refs_1_, bf16[512,256]{1,0:T(8,128)(2,1)S(1)} %collective-permute-done.20.refs_2_, ...), custom_call_target="tpu_custom_call" | custom-call | tf_op jit(solution)/shard_map/project/pallas_call | solution.py:306
  (61 shorter events, 6.2 us)
Async XLA Ops:
  1.5 21.0 %collective-permute-start.5 = (bf16[512,256]{1,0:T(8,128)(2,1)S(1)}, bf16[512,256]{1,0:T(8,128)(2,1)S(1)}, u32[]{:S(2)}, u32[]{:S(2)}) collective-permute-start(bf16[512,256]{1,0:T(8,128)(2,1)S(1)} %get-tuple-element.53.rest_2_), channel_id=1, source_target_pairs={{0,16},{4,20},{8,24},{12,28},{16,0},{20,4},{24,8},{28,12},{1,17},{... | collective-permute-start | bytes 786440 | tf_op jit(solution)/shard_map/ppermute | solution.py:317
  4.5 9.0 %collective-permute-start.3 = (bf16[512,256]{1,0:T(8,128)(2,1)S(1)}, bf16[512,256]{1,0:T(8,128)(2,1)S(1)}, u32[]{:S(2)}, u32[]{:S(2)}) collective-permute-start(bf16[512,256]{1,0:T(8,128)(2,1)S(1)} %get-tuple-element.53.rest_2_), channel_id=1, source_target_pairs={{0,8},{4,12},{8,0},{12,4},{16,24},{20,28},{24,16},{28,20},{1,9},{5... | collective-permute-start | bytes 786440 | tf_op jit(solution)/shard_map/ppermute | solution.py:317
  6.0 2.3 %collective-permute-start = (s32[2,8]{1,0:T(2,128)S(1)}, s32[2,8]{1,0:T(2,128)S(1)}, u32[]{:S(2)}, u32[]{:S(2)}) collective-permute-start(s32[2,8]{1,0:T(2,128)S(1)} %pad_add_fusion.refs_0_), channel_id=1, source_target_pairs={{0,4},{4,0},{8,12},{12,8},{16,20},{20,16},{24,28},{28,24},{1,5},{5... | collective-permute-start | bytes 200 | tf_op jit(solution)/shard_map/ppermute | solution.py:317
  6.1 1.6 %collective-permute-start.2 = (bf16[512,256]{1,0:T(8,128)(2,1)S(1)}, bf16[512,256]{1,0:T(8,128)(2,1)S(1)}, u32[]{:S(2)}, u32[]{:S(2)}) collective-permute-start(bf16[512,256]{1,0:T(8,128)(2,1)S(1)} %get-tuple-element.52), channel_id=1, source_target_pairs={{0,4},{4,0},{8,12},{12,8},{16,20},{20,16},{24,28},{28,24},{1,5},{5... | collective-permute-start | bytes 786440 | tf_op jit(solution)/shard_map/ppermute | solution.py:317
  7.6 16.5 %collective-permute-start.9 = (bf16[512,256]{1,0:T(8,128)(2,1)}, bf16[512,256]{1,0:T(8,128)(2,1)}, u32[]{:S(2)}, u32[]{:S(2)}) collective-permute-start(bf16[512,256]{1,0:T(8,128)(2,1)} %get-tuple-element.50), channel_id=1, source_target_pairs={{0,4},{4,0},{8,12},{12,8},{16,20},{20,16},{24,28},{28,24},{1,5},{5... | collective-permute-start | bytes 786440 | tf_op jit(solution)/shard_map/ppermute | solution.py:317
  7.8 9.1 %collective-permute-start.6 = (bf16[512,256]{1,0:T(8,128)(2,1)S(1)}, bf16[512,256]{1,0:T(8,128)(2,1)S(1)}, u32[]{:S(2)}, u32[]{:S(2)}) collective-permute-start(bf16[512,256]{1,0:T(8,128)(2,1)S(1)} %collective-permute-done.2.rest_3_), channel_id=1, source_target_pairs={{0,16},{4,20},{8,24},{12,28},{16,0},{20,4},{24,8},{28,12},{1,17},{... | collective-permute-start | bytes 786440 | tf_op jit(solution)/shard_map/ppermute | solution.py:317
  8.3 18.4 %collective-permute-start.4 = (bf16[512,256]{1,0:T(8,128)(2,1)S(1)}, bf16[512,256]{1,0:T(8,128)(2,1)S(1)}, u32[]{:S(2)}, u32[]{:S(2)}) collective-permute-start(bf16[512,256]{1,0:T(8,128)(2,1)S(1)} %collective-permute-done.2.rest_3_), channel_id=1, source_target_pairs={{0,8},{4,12},{8,0},{12,4},{16,24},{20,28},{24,16},{28,20},{1,9},{5... | collective-permute-start | bytes 786440 | tf_op jit(solution)/shard_map/ppermute | solution.py:317
  13.6 45.9 %copy-start.4 = (s32[4,2]{0,1:T(2,128)S(1)}, s32[4,2]{0,1:T(2,128)}, u32[]{:S(2)}) copy-start(s32[4,2]{0,1:T(2,128)} %param.11) | copy-start | bytes 100
  13.6 13.4 %collective-permute-start.7 = (bf16[512,256]{1,0:T(8,128)(2,1)S(1)}, bf16[512,256]{1,0:T(8,128)(2,1)S(1)}, u32[]{:S(2)}, u32[]{:S(2)}) collective-permute-start(bf16[512,256]{1,0:T(8,128)(2,1)S(1)} %collective-permute-done.3.rest_4_), channel_id=1, source_target_pairs={{0,16},{4,20},{8,24},{12,28},{16,0},{20,4},{24,8},{28,12},{1,17},{... | collective-permute-start | bytes 786440 | tf_op jit(solution)/shard_map/ppermute | solution.py:317
  16.9 10.0 %collective-permute-start.8 = (bf16[512,256]{1,0:T(8,128)(2,1)S(1)}, bf16[512,256]{1,0:T(8,128)(2,1)S(1)}, u32[]{:S(2)}, u32[]{:S(2)}) collective-permute-start(bf16[512,256]{1,0:T(8,128)(2,1)S(1)} %collective-permute-done.6.rest_7_), channel_id=1, source_target_pairs={{0,8},{4,12},{8,0},{12,4},{16,24},{20,28},{24,16},{28,20},{1,9},{5... | collective-permute-start | bytes 786440 | tf_op jit(solution)/shard_map/ppermute | solution.py:317
  22.5 9.4 %collective-permute-start.14 = (bf16[256,512]{1,0:T(8,128)(2,1)S(1)}, bf16[256,512]{1,0:T(8,128)(2,1)S(1)}, u32[]{:S(2)}, u32[]{:S(2)}) collective-permute-start(bf16[256,512]{1,0:T(8,128)(2,1)S(1)} %get-tuple-element.38), channel_id=1, source_target_pairs={{0,1},{1,0},{2,3},{3,2},{4,5},{5,4},{6,7},{7,6},{8,9},{9,8},{10,11... | collective-permute-start | bytes 786440 | tf_op jit(solution)/shard_map/ppermute | solution.py:317
  24.1 20.5 %collective-permute-start.15 = (bf16[256,512]{1,0:T(8,128)(2,1)S(1)}, bf16[256,512]{1,0:T(8,128)(2,1)S(1)}, u32[]{:S(2)}, u32[]{:S(2)}) collective-permute-start(bf16[256,512]{1,0:T(8,128)(2,1)S(1)} %get-tuple-element.39), channel_id=1, source_target_pairs={{0,2},{1,3},{2,0},{3,1},{4,6},{5,7},{6,4},{7,5},{8,10},{9,11},{10,... | collective-permute-start | bytes 786440 | tf_op jit(solution)/shard_map/ppermute | solution.py:317
  26.7 17.9 %collective-permute-start.16 = (bf16[256,512]{1,0:T(8,128)(2,1)S(1)}, bf16[256,512]{1,0:T(8,128)(2,1)S(1)}, u32[]{:S(2)}, u32[]{:S(2)}) collective-permute-start(bf16[256,512]{1,0:T(8,128)(2,1)S(1)} %get-tuple-element.40), channel_id=1, source_target_pairs={{0,3},{1,2},{2,1},{3,0},{4,7},{5,6},{6,5},{7,4},{8,11},{9,10},{10,... | collective-permute-start | bytes 786440 | tf_op jit(solution)/shard_map/ppermute | solution.py:317
  27.0 19.9 %collective-permute-start.13 = (bf16[512,256]{1,0:T(8,128)(2,1)}, bf16[512,256]{1,0:T(8,128)(2,1)S(1)}, u32[]{:S(2)}, u32[]{:S(2)}) collective-permute-start(bf16[512,256]{1,0:T(8,128)(2,1)} %collective-permute-done.9.rest_3_), channel_id=1, source_target_pairs={{0,16},{4,20},{8,24},{12,28},{16,0},{20,4},{24,8},{28,12},{1,17},{... | collective-permute-start | bytes 786440 | tf_op jit(solution)/shard_map/ppermute | solution.py:317
  28.5 18.3 %collective-permute-start.10 = (bf16[512,256]{1,0:T(8,128)(2,1)S(1)}, bf16[512,256]{1,0:T(8,128)(2,1)S(1)}, u32[]{:S(2)}, u32[]{:S(2)}) collective-permute-start(bf16[512,256]{1,0:T(8,128)(2,1)S(1)} %get-tuple-element.36.rest_2_), channel_id=1, source_target_pairs={{0,8},{4,12},{8,0},{12,4},{16,24},{20,28},{24,16},{28,20},{1,9},{5... | collective-permute-start | bytes 786440 | tf_op jit(solution)/shard_map/ppermute | solution.py:317
  44.7 6.4 %collective-permute-start.12 = (bf16[512,256]{1,0:T(8,128)(2,1)S(1)}, bf16[512,256]{1,0:T(8,128)(2,1)S(1)}, u32[]{:S(2)}, u32[]{:S(2)}) collective-permute-start(bf16[512,256]{1,0:T(8,128)(2,1)S(1)} %get-tuple-element.36.rest_2_), channel_id=1, source_target_pairs={{0,16},{4,20},{8,24},{12,28},{16,0},{20,4},{24,8},{28,12},{1,17},{... | collective-permute-start | bytes 786440 | tf_op jit(solution)/shard_map/ppermute | solution.py:317
  46.3 7.4 %collective-permute-start.11 = (bf16[512,256]{1,0:T(8,128)(2,1)}, bf16[512,256]{1,0:T(8,128)(2,1)S(1)}, u32[]{:S(2)}, u32[]{:S(2)}) collective-permute-start(bf16[512,256]{1,0:T(8,128)(2,1)} %collective-permute-done.9.rest_3_), channel_id=1, source_target_pairs={{0,8},{4,12},{8,0},{12,4},{16,24},{20,28},{24,16},{28,20},{1,9},{5... | collective-permute-start | bytes 786440 | tf_op jit(solution)/shard_map/ppermute | solution.py:317
  46.8 7.1 %collective-permute-start.17 = (bf16[512,256]{1,0:T(8,128)(2,1)S(1)}, bf16[512,256]{1,0:T(8,128)(2,1)S(1)}, u32[]{:S(2)}, u32[]{:S(2)}) collective-permute-start(bf16[512,256]{1,0:T(8,128)(2,1)S(1)} %collective-permute-done.10.rest_4_), channel_id=1, source_target_pairs={{0,16},{4,20},{8,24},{12,28},{16,0},{20,4},{24,8},{28,12},{1,17},{... | collective-permute-start | bytes 786440 | tf_op jit(solution)/shard_map/ppermute | solution.py:317
  47.7 11.5 %collective-permute-start.18 = (bf16[512,256]{1,0:T(8,128)(2,1)S(1)}, bf16[512,256]{1,0:T(8,128)(2,1)S(1)}, u32[]{:S(2)}, u32[]{:S(2)}) collective-permute-start(bf16[512,256]{1,0:T(8,128)(2,1)S(1)} %collective-permute-done.13.rest_7_), channel_id=1, source_target_pairs={{0,8},{4,12},{8,0},{12,4},{16,24},{20,28},{24,16},{28,20},{1,9},{5... | collective-permute-start | bytes 786440 | tf_op jit(solution)/shard_map/ppermute | solution.py:317
  48.8 10.7 %collective-permute-start.1 = (bf16[3,512,256]{2,1,0:T(8,128)(2,1)S(1)}, bf16[3,512,256]{2,1,0:T(8,128)(2,1)S(1)}, u32[]{:S(2)}, u32[]{:S(2)}) collective-permute-start(bf16[3,512,256]{2,1,0:T(8,128)(2,1)S(1)} %get-tuple-element.29), channel_id=1, source_target_pairs={{0,4},{4,0},{8,12},{12,8},{16,20},{20,16},{24,28},{28,24},{1,5},{5... | collective-permute-start | bytes 2359304 | tf_op jit(solution)/shard_map/ppermute | solution.py:317
  59.3 18.5 %collective-permute-start.28 = (bf16[3,256,512]{2,1,0:T(8,128)(2,1)S(1)}, bf16[3,256,512]{2,1,0:T(8,128)(2,1)S(1)}, u32[]{:S(2)}, u32[]{:S(2)}) collective-permute-start(bf16[3,256,512]{2,1,0:T(8,128)(2,1)S(1)} %pad_maximum_fusion.refs_11_), channel_id=1, source_target_pairs={{0,8},{4,12},{8,0},{12,4},{16,24},{20,28},{24,16},{28,20},{1,9},{5... | collective-permute-start | bytes 2359304 | tf_op jit(solution)/shard_map/ppermute | solution.py:317
  71.4 6.8 %collective-permute-start.23 = (bf16[512,256]{1,0:T(8,128)(2,1)S(1)}, bf16[512,256]{1,0:T(8,128)(2,1)S(1)}, u32[]{:S(2)}, u32[]{:S(2)}) collective-permute-start(bf16[512,256]{1,0:T(8,128)(2,1)S(1)} %get-tuple-element.44), channel_id=1, source_target_pairs={{0,4},{4,0},{8,12},{12,8},{16,20},{20,16},{24,28},{28,24},{1,5},{5... | collective-permute-start | bytes 786440 | tf_op jit(solution)/shard_map/ppermute | solution.py:317
  71.5 7.2 %collective-permute-start.21 = (bf16[512,256]{1,0:T(8,128)(2,1)S(1)}, bf16[512,256]{1,0:T(8,128)(2,1)S(1)}, u32[]{:S(2)}, u32[]{:S(2)}) collective-permute-start(bf16[512,256]{1,0:T(8,128)(2,1)S(1)} %get-tuple-element.43.refs_0_), channel_id=1, source_target_pairs={{1,2},{2,1},{5,6},{6,5},{9,10},{10,9},{13,14},{14,13},{17,18},{18,... | collective-permute-start | bytes 786440 | tf_op jit(solution)/shard_map/ppermute | solution.py:392
  72.2 23.8 %collective-permute-start.20 = (bf16[512,256]{1,0:T(8,128)(2,1)S(1)}, bf16[512,256]{1,0:T(8,128)(2,1)S(1)}, u32[]{:S(2)}, u32[]{:S(2)}) collective-permute-start(bf16[512,256]{1,0:T(8,128)(2,1)S(1)} %get-tuple-element.43.refs_0_), channel_id=1, source_target_pairs={{0,2},{1,3},{2,0},{3,1},{4,6},{5,7},{6,4},{7,5},{8,10},{9,11},{10,... | collective-permute-start | bytes 786440 | tf_op jit(solution)/shard_map/ppermute | solution.py:317
  77.7 46.1 %collective-permute-start.29 = (bf16[3,256,512]{2,1,0:T(8,128)(2,1)S(1)}, bf16[3,256,512]{2,1,0:T(8,128)(2,1)S(1)}, u32[]{:S(2)}, u32[]{:S(2)}) collective-permute-start(bf16[3,256,512]{2,1,0:T(8,128)(2,1)S(1)} %pad_maximum_fusion.refs_11_), channel_id=1, source_target_pairs={{0,4},{4,0},{8,12},{12,8},{16,20},{20,16},{24,28},{28,24},{1,5},{5... | collective-permute-start | bytes 2359304 | tf_op jit(solution)/shard_map/ppermute | solution.py:317
  77.8 46.0 %collective-permute-start.30 = (bf16[3,256,512]{2,1,0:T(8,128)(2,1)S(1)}, bf16[3,256,512]{2,1,0:T(8,128)(2,1)S(1)}, u32[]{:S(2)}, u32[]{:S(2)}) collective-permute-start(bf16[3,256,512]{2,1,0:T(8,128)(2,1)S(1)} %collective-permute-done.28.refs_12_), channel_id=1, source_target_pairs={{0,4},{4,0},{8,12},{12,8},{16,20},{20,16},{24,28},{28,24},{1,5},{5... | collective-permute-start | bytes 2359304 | tf_op jit(solution)/shard_map/ppermute | solution.py:317
  78.2 17.8 %collective-permute-start.19 = (bf16[512,256]{1,0:T(8,128)(2,1)S(1)}, bf16[512,256]{1,0:T(8,128)(2,1)S(1)}, u32[]{:S(2)}, u32[]{:S(2)}) collective-permute-start(bf16[512,256]{1,0:T(8,128)(2,1)S(1)} %get-tuple-element.43.refs_0_), channel_id=1, source_target_pairs={{0,1},{1,0},{2,3},{3,2},{4,5},{5,4},{6,7},{7,6},{8,9},{9,8},{10,11... | collective-permute-start | bytes 786440 | tf_op jit(solution)/shard_map/ppermute | solution.py:317
  78.7 20.6 %collective-permute-start.26 = (bf16[512,256]{1,0:T(8,128)(2,1)S(1)}, bf16[512,256]{1,0:T(8,128)(2,1)S(1)}, u32[]{:S(2)}, u32[]{:S(2)}) collective-permute-start(bf16[512,256]{1,0:T(8,128)(2,1)S(1)} %collective-permute-done.23.refs_5_), channel_id=1, source_target_pairs={{1,2},{2,1},{5,6},{6,5},{9,10},{10,9},{13,14},{14,13},{17,18},{18,... | collective-permute-start | bytes 786440 | tf_op jit(solution)/shard_map/ppermute | solution.py:392
  96.0 16.6 %collective-permute-start.25 = (bf16[512,256]{1,0:T(8,128)(2,1)S(1)}, bf16[512,256]{1,0:T(8,128)(2,1)S(1)}, u32[]{:S(2)}, u32[]{:S(2)}) collective-permute-start(bf16[512,256]{1,0:T(8,128)(2,1)S(1)} %collective-permute-done.23.refs_5_), channel_id=1, source_target_pairs={{0,2},{1,3},{2,0},{3,1},{4,6},{5,7},{6,4},{7,5},{8,10},{9,11},{10,... | collective-permute-start | bytes 786440 | tf_op jit(solution)/shard_map/ppermute | solution.py:317
  96.0 17.9 %collective-permute-start.24 = (bf16[512,256]{1,0:T(8,128)(2,1)S(1)}, bf16[512,256]{1,0:T(8,128)(2,1)S(1)}, u32[]{:S(2)}, u32[]{:S(2)}) collective-permute-start(bf16[512,256]{1,0:T(8,128)(2,1)S(1)} %collective-permute-done.23.refs_5_), channel_id=1, source_target_pairs={{0,1},{1,0},{2,3},{3,2},{4,5},{5,4},{6,7},{7,6},{8,9},{9,8},{10,11... | collective-permute-start | bytes 786440 | tf_op jit(solution)/shard_map/ppermute | solution.py:317
  99.3 19.0 %collective-permute-start.22 = (bf16[512,256]{1,0:T(8,128)(2,1)S(1)}, bf16[512,256]{1,0:T(8,128)(2,1)S(1)}, u32[]{:S(2)}, u32[]{:S(2)}) collective-permute-start(bf16[512,256]{1,0:T(8,128)(2,1)S(1)} %collective-permute-done.20.refs_2_), channel_id=1, source_target_pairs={{2,3},{1,0},{6,7},{5,4},{10,11},{9,8},{14,15},{13,12},{18,19},{17,... | collective-permute-start | bytes 786440 | tf_op jit(solution)/shard_map/ppermute | solution.py:394
  112.6 11.1 %collective-permute-start.27 = (bf16[512,256]{1,0:T(8,128)(2,1)S(1)}, bf16[512,256]{1,0:T(8,128)(2,1)S(1)}, u32[]{:S(2)}, u32[]{:S(2)}) collective-permute-start(bf16[512,256]{1,0:T(8,128)(2,1)S(1)} %collective-permute-done.25.refs_7_), channel_id=1, source_target_pairs={{2,3},{1,0},{6,7},{5,4},{10,11},{9,8},{14,15},{13,12},{18,19},{17,... | collective-permute-start | bytes 786440 | tf_op jit(solution)/shard_map/ppermute | solution.py:394
  (6 other events, 24.9 us)

commit v4 on v3

--- a/solution.py
+++ b/solution.py
@@ -108,60 +108,19 @@
     )(where, *tables, q, k, v, rope_table())
 
 
-def cut_kernel(where_ref, w_ref, own_ref, *rest):
-    sends = rest[:-1]
-    sems = rest[-1]
-    z = where_ref[0]
-    core = where_ref[1]
-    side = where_ref[2]
-    cols = own_ref.shape[1]
-    high, width = sends[0].shape
-    copies = []
-    for m in range(1, 1 + len(sends)):
-        at = lax.bitwise_xor(z, m) * cols + side * width
-        copies.append(
-            pltpu.make_async_copy(
-                w_ref.at[
-                    pl.ds(pl.multiple_of(core * high, high), high),
-                    pl.ds(pl.multiple_of(at, width), width),
-                ],
-                sends[m - 1],
-                sems.at[m],
-            )
-        )
-    copies.append(
-        pltpu.make_async_copy(
-            w_ref.at[:, pl.ds(pl.multiple_of(z * cols, cols), cols)], own_ref, sems.at[0]
-        )
-    )
-    for c in copies:
-        c.start()
-    for c in copies:
-        c.wait()
-
-
-def cut(where, w, tp_size):
-    rows, cols = w.shape[0], w.shape[1] // tp_size
-    return pl.pallas_call(
-        cut_kernel,
-        out_shape=[jax.ShapeDtypeStruct((rows, cols), w.dtype)]
-        + [jax.ShapeDtypeStruct((rows // 2, cols // 2), w.dtype)] * (tp_size - 1),
-        in_specs=[SMEM, pl.BlockSpec(memory_space=pl.ANY)],
-        out_specs=[VMEM] * tp_size,
-        scratch_shapes=[pltpu.SemaphoreType.DMA((tp_size,))],
-        compiler_params=pltpu.CompilerParams(vmem_limit_bytes=1 << 20),
-        name="cut",
-    )(where, w)
-
-
 def wide(x, width):
     return x if width == 128 else jnp.concatenate([x] * (width // 128), axis=1)
 
 
-def score_kernel(nb, place_ref, first_ref, grp_ref, *rest):
+def flatten(refs, counts):
+    return [ref.at[j] for ref, count in zip(refs, counts) for j in range(count)]
+
+
+def score_kernel(nb, counts, place_ref, first_ref, grp_ref, *rest):
     sufs = rest[:nb]
-    pieces = rest[nb : nb + SLOTS]
-    p_ref, near_ref, den_ref, sc = rest[nb + SLOTS :]
+    n_pieces = len(counts)
+    pieces = flatten(rest[nb : nb + n_pieces], counts)
+    p_ref, near_ref, den_ref, sc = rest[nb + n_pieces :]
     half = 256
     for n in range(nb):
         rows = sufs[n].shape[1]
@@ -215,13 +174,13 @@
 def score(place, first, grp, sufs, pieces):
     rows = sum(s.shape[1] for s in sufs)
     return pl.pallas_call(
-        functools.partial(score_kernel, len(sufs)),
+        functools.partial(score_kernel, len(sufs), tuple(p.shape[0] for p in pieces)),
         out_shape=[
             jax.ShapeDtypeStruct((rows, SEEN), jnp.bfloat16),
             jax.ShapeDtypeStruct((rows, RB + MOST), jnp.bfloat16),
             jax.ShapeDtypeStruct((rows, 128), jnp.float32),
         ],
-        in_specs=[SMEM] + [VMEM] * (2 + len(sufs) + SLOTS),
+        in_specs=[SMEM] + [VMEM] * (2 + len(sufs) + len(pieces)),
         out_specs=[VMEM] * 3,
         scratch_shapes=[pltpu.VMEM((2, RB, SEEN), jnp.float32)],
         compiler_params=pltpu.CompilerParams(vmem_limit_bytes=4 << 20),
@@ -229,10 +188,11 @@
     )(place, first, grp, *sufs, *pieces)
 
 
-def mix_kernel(nb, col, place_ref, grp_ref, p_ref, near_ref, den_ref, *rest):
+def mix_kernel(nb, counts, col, place_ref, grp_ref, p_ref, near_ref, den_ref, *rest):
     sufs = rest[:nb]
-    pieces = rest[nb : nb + SLOTS]
-    outs = rest[nb + SLOTS :]
+    n_pieces = len(counts)
+    pieces = flatten(rest[nb : nb + n_pieces], counts)
+    outs = rest[nb + n_pieces :]
     width = outs[0].shape[1]
     for n in reversed(range(nb)):
         rows = outs[n].shape[0]
@@ -263,9 +223,9 @@
     rows = sufs[0].shape[1]
     nb = len(sufs)
     return pl.pallas_call(
-        functools.partial(mix_kernel, nb, col),
+        functools.partial(mix_kernel, nb, tuple(p.shape[0] for p in pieces), col),
         out_shape=[jax.ShapeDtypeStruct((rows, width), jnp.bfloat16)] * nb,
-        in_specs=[SMEM] + [VMEM] * (4 + nb + SLOTS),
+        in_specs=[SMEM] + [VMEM] * (4 + nb + len(pieces)),
         out_specs=[VMEM] * nb,
         compiler_params=pltpu.CompilerParams(vmem_limit_bytes=4 << 20),
         name="mix",
@@ -343,54 +303,60 @@
     tp_size = 4
     first_head = core == 0
 
+    cols = out_weight.shape[1] // tp_size
+    z_u, core_u, side_u = (i.astype(jnp.uint32) for i in (z, core, side))
+    starts = [core_u * HD, z_u * cols]
+    starts += [(z_u ^ m) * cols + side_u * (cols // 2) for m in range(1, tp_size)]
+    first_head, *starts = lax.optimization_barrier((first_head, *starts))
+    sends = [
+        lax.dynamic_slice(out_weight, (starts[0], starts[1 + m]), (HD, cols // 2))
+        for m in range(1, tp_size)
+    ]
+    w_own = lax.dynamic_slice(
+        out_weight, (jnp.zeros_like(starts[0]), starts[1]), (out_weight.shape[0], cols)
+    )
+
     k = prefix_cache[:, 0]
     k_own = jnp.where(first_head, k[:, :HD], k[:, HD:])
     k_other = jnp.where(first_head, k[:, HD:], k[:, :HD])
-    k_pair = over_core(k_other)
-    ax = over_x(k_own)
-    ay = over_y(k_own)
-    bx = over_x(k_pair)
-    by = over_y(k_pair)
+    k_both = jnp.stack([k_own, over_core(k_other)])
+    kx = over_x(k_both)
+    ky = over_y(k_both)
+    w_one, w_two = (swap(sends[m - 1], "tp", m, tp_size) for m in (1, 2))
 
     table = jnp.concatenate([lengths, groups], axis=0)
     table_pair = over_core(table)
     first, grp, mine, other = prepare(
-        where, (table, table_pair), suffix_heads[:, 0], suffix_heads[:, 1], suffix_heads[:, 2]
-    )
-    axy = over_y(after(ax, mine))
-    bxy = over_x(after(by, mine))
+        after(where, k_both), (table, table_pair), suffix_heads[:, 0], suffix_heads[:, 1], suffix_heads[:, 2]
+    )
     sufs = [mine, over_core(other)]
-    k_pieces = [k_own, k_pair, ax, bx, ay, by, axy, bxy]
-
-    v = after(prefix_cache, k_own)[:, 1]
+    v = after(prefix_cache, k_both)[:, 1]
     v_own = jnp.where(first_head, v[:, :HD], v[:, HD:])
     v_other = jnp.where(first_head, v[:, HD:], v[:, :HD])
-    v_pair = over_core(v_other)
-    v_own, v_pair = lax.optimization_barrier((v_own, v_pair, ay, bx, axy, bxy))[:2]
-    vax = over_x(v_own)
-    vay = over_y(v_own)
-    vbx = over_x(v_pair)
-    vby = over_y(v_pair)
-
-    w_own, *sends = cut(where, out_weight, tp_size)
-    w_far = jnp.stack([swap(sends[m - 1], "tp", m, tp_size) for m in range(1, tp_size)])
-
-    vaxy = over_y(after(vax, w_far))
-    vbxy = over_x(after(vby, w_far))
-    v_pieces = [v_own, v_pair, vax, vbx, vay, vby, vaxy, vbxy]
-
-    w_x = over_x(after(w_far, vay, vbx, vaxy, vbxy))
-    w_core = over_core(after(w_far, vay, vbx, vaxy, vbxy))
+    v_both = jnp.stack([v_own, over_core(v_other)])
+
+    kxy = over_y(after(kx[0:1], mine, v_both, w_own))
+    kyx = over_x(after(ky[1:2], mine, v_both, w_own))
+    v_both = after(v_both, kxy, kyx, w_one, w_two, sufs[1])
+    vx = over_x(v_both)
+    vy = over_y(v_both)
+    w_three = swap(after(sends[2], w_two), "tp", 3, tp_size)
+    scored = score(place, first, grp, sufs, (k_both, kx, ky, kxy, kyx))
+    w_far = jnp.stack([after(w_one, scored[0]), w_two, w_three])
+    w_core = over_core(w_far)
+    vxy = over_y(after(vx[0:1], scored[0], w_far))
+    vyx = over_x(after(vy[1:2], scored[0], w_far))
+    own, pair = mix(0, HD, place, grp, scored, sufs, (v_both, vx, vy, vxy, vyx))
+    w_x = over_x(after(w_far, vxy, vyx))
     w_core_x = over_core(w_x)
 
-    scored = score(place, first, grp, sufs, k_pieces)
-    own, pair = mix(0, HD, place, grp, scored, sufs, v_pieces)
     back = over_core(pair)
+    two_own = swap(own, "tp", 2, tp_size)
+    two_back = swap(back, "tp", 2, tp_size)
     att = []
-    for a in (own, back):
-        two = swap(a, "tp", 2, tp_size)
-        three = lax.ppermute(a, "tp", [(1, 2), (2, 1)])
+    for a, two in ((own, two_own), (back, two_back)):
         one = swap(a, "tp", 1, tp_size)
+        three = lax.ppermute(after(a, two), "tp", [(1, 2), (2, 1)])
         forward = lax.ppermute(two, "tp", [(2, 3), (1, 0)])
         att += [a, one, two, three, forward]
     return project(where, att, w_own, [w_far, w_x, w_core, w_core_x])
@@ -411,8 +377,8 @@
     )
     attended = []
     for h in range(heads):
-        keys = [s[:, 0, h * HD : (h + 1) * HD] for s in received]
-        values = [s[:, 1, h * HD : (h + 1) * HD] for s in received]
+        keys = [s[None, :, 0, h * HD : (h + 1) * HD] for s in received]
+        values = [s[None, :, 1, h * HD : (h + 1) * HD] for s in received]
         scored = score(place, first, grp, [sufs[h]], keys)
         attended += mix(0, HD, place, grp, scored, [sufs[h]], values)
     partial_out = jnp.dot(

time: 128 us -> 109 us (0.85)
  waiting for transfers between devices: 71.2 us -> 49.6 us
  local copies, waits for them, and re-layouts: 3.95 us -> 6.73 us
    ppermute x27 -> x23, waiting for transfers between devices: 61.3 us -> 40.6 us  [swap(): return lax.ppermute(x, axis, [(i, i ^ mask) for i in range(size)])]
    dynamic_slice x0 -> x2, local copies, waits for them, and re-layouts: none -> 3.54 us  [the longest x1 1.88 us: split_heads(): lax.dynamic_slice(out_weight, (jnp.zeros_like(starts[0]), starts[1]), (ou...]
    unnamed x15 -> x7, local copies, waits for them, and re-layouts: 3.65 us -> 1.46 us
    squeeze x1, local copies, waits for them, and re-layouts: 0.1 us -> 1.46 us  [split_heads(): suffix_heads[:, 2]]
    ppermute x27 -> x23, starting transfers between devices: 28.9 us -> 30.1 us  [swap(): return lax.ppermute(x, axis, [(i, i ^ mask) for i in range(size)])]
    pallas_call x3 -> x2, Pallas kernels: 12.9 us -> 11.7 us  [the longest x1 8.2 us: score(): pl.pallas_call(functools.partial(score_kernel, len(sufs), tuple((p.shape[...]
  transfers between devices with their start and end apart: 31 -> 27, of which waited for: 13 -> 11; matrix products, arithmetic and copies ran while one was open for 1% -> 6% of each run, Pallas kernels for 11% -> 12%
where the time goes in v4:
time: 109 us
  waiting for transfers between devices  49.6 us (46%)
  starting transfers between devices  34 us (31%)
  Pallas kernels  17.4 us (16%)
  local copies, waits for them, and re-layouts  6.73 us (6%)
  other arithmetic  1.12 us (1%)
    ppermute x23, waiting for transfers between devices, swap(): return lax.ppermute(x, axis, [(i, i ^ mask) for i in range(size)])  40.6 us
    ppermute x23, starting transfers between devices, swap(): return lax.ppermute(x, axis, [(i, i ^ mask) for i in range(size)])  30.1 us
    ppermute x2, waiting for transfers between devices, split_heads(): forward = lax.ppermute(two, 'tp', [(2, 3), (1, 0)])  8.97 us
    pallas_call x1, Pallas kernels, score(): pl.pallas_call(functools.partial(score_kernel, len(sufs), tuple((p.shape[...  8.2 us
    pallas_call x1, Pallas kernels, project(): pl.pallas_call(proj_kernel, out_shape=jax.ShapeDtypeStruct((rows, cols),...  3.86 us
    pallas_call x1, Pallas kernels, mix(): pl.pallas_call(functools.partial(mix_kernel, nb, tuple((p.shape[0] for p...  3.53 us
    ppermute x2, starting transfers between devices, split_heads(): forward = lax.ppermute(two, 'tp', [(2, 3), (1, 0)])  2.57 us
  transfers between devices with their start and end apart: 27, of which 11 were waited for; matrix products, arithmetic and copies ran while one was open for 6% of the time, Pallas kernels for 12%

profile of v4, /device:TPU:0, one launch (start us, length us, event | category | flops | bytes accessed | tf_op | source)
XLA Modules:
  0.0 109.1 jit_solution(3991406369667085237)
XLA Ops:
  0.0 1.4 %copy.15 = bf16[512,1,512]{2,0,1:T(8,128)(2,1)S(1)} copy(bf16[512,1,512]{2,1,0:T(2,128)(2,1)} %bitcast.24) | data formatting | bytes 1048576
  2.8 1.5 %slice_bitcast_fusion.1 = (bf16[512,512]{1,0:T(8,128)(2,1)S(1)}, bf16[512,512]{1,0:T(8,128)(2,1)S(1)}, bf16[512,512]{1,0:T(8,128)(2,1)S(1)}) fusion(bf16[512,3,512]{2,0,1:T(8,128)(2,1)} %param.7), kind=kLoop, calls=%fused_computation.5 | loop fusion | bytes 3145728 | tf_op jit(solution)/shard_map/squeeze | solution.py:330
  4.4 3.0 %collective-permute-start.3 = (bf16[2,512,256]{2,1,0:T(8,128)(2,1)S(1)}, bf16[2,512,256]{2,1,0:T(8,128)(2,1)S(1)}, u32[]{:S(2)}, u32[]{:S(2)}) collective-permute-start(bf16[2,512,256]{2,1,0:T(8,128)(2,1)S(1)} %pad_maximum_fusion.1.rest_2_), channel_id=1, source_target_pairs={{0,8},{4,12},{8,0},{12,4},{16,24},{20,28},{24,16},{28,20},{1,9},{5... | collective-permute-start | bytes 1572872 | tf_op jit(solution)/shard_map/ppermute | solution.py:277
  7.4 1.5 %collective-permute-start.4 = (bf16[2,512,256]{2,1,0:T(8,128)(2,1)S(1)}, bf16[2,512,256]{2,1,0:T(8,128)(2,1)S(1)}, u32[]{:S(2)}, u32[]{:S(2)}) collective-permute-start(bf16[2,512,256]{2,1,0:T(8,128)(2,1)S(1)} %pad_maximum_fusion.1.rest_2_), channel_id=1, source_target_pairs={{0,16},{4,20},{8,24},{12,28},{16,0},{20,4},{24,8},{28,12},{1,17},{... | collective-permute-start | bytes 1572872 | tf_op jit(solution)/shard_map/ppermute | solution.py:277
  8.9 1.8 %prepare.1 = (s32[1024,128]{1,0:T(8,128)S(1)}, s32[1024,128]{1,0:T(8,128)S(1)}, bf16[3,512,256]{2,1,0:T(8,128)(2,1)S(1)}, bf16[3,512,256]{2,1,0:T(8,128)(2,1)S(1)}) custom-call(s32[3]{0:T(128)S(1)} %pad_add_fusion.1.where_ref, s32[2,8]{1,0:T(2,128)S(1)} %pad_add_fusion.refs_0_, s32[2,8]{1,0:T(2,128)S(1)} %collective-permute-done.1.refs_1_, ...), custom_call_target="tpu_custom_call" | custom-call | tf_op jit(solution)/shard_map/prepare/pallas_call | solution.py:101
  11.6 1.7 %fusion = (bf16[256,512]{1,0:T(8,128)(2,1)S(1)}, bf16[256,512]{1,0:T(8,128)(2,1)S(1)}, bf16[256,512]{1,0:T(8,128)(2,1)S(1)}) fusion(bf16[512,4096]{1,0:T(8,128)(2,1)} %param.12, u32[]{:T(128)S(6)} %mul.20, u32[]{:T(128)S(6)} %add.17, u32[]{:T(128)S(6)} %add.15, u32[]{:T(128)S(6)} %add.16), kind=kLoop, calls=%fused_computation.18 | loop fusion | bytes 1572880 | tf_op jit(solution)/shard_map/dynamic_slice | solution.py:312
  13.3 1.6 %collective-permute-start.8 = (bf16[256,512]{1,0:T(8,128)(2,1)S(1)}, bf16[256,512]{1,0:T(8,128)(2,1)S(1)}, u32[]{:S(2)}, u32[]{:S(2)}) collective-permute-start(bf16[256,512]{1,0:T(8,128)(2,1)S(1)} %get-tuple-element.60), channel_id=1, source_target_pairs={{0,1},{1,0},{2,3},{3,2},{4,5},{5,4},{6,7},{7,6},{8,9},{9,8},{10,11... | collective-permute-start | bytes 786440 | tf_op jit(solution)/shard_map/ppermute | solution.py:277
  14.9 1.9 %constant_dynamic-slice_fusion.refs_10_ = bf16[512,1024]{1,0:T(8,128)(2,1)S(1)} fusion(bf16[512,4096]{1,0:T(8,128)(2,1)} %param.12, u32[]{:T(128)S(6)} %mul.21), kind=kLoop, calls=%fused_computation.16 | loop fusion | bytes 2097156 | tf_op jit(solution)/shard_map/dynamic_slice | solution.py:315
  16.8 2.7 %collective-permute-start.9 = (bf16[256,512]{1,0:T(8,128)(2,1)S(1)}, bf16[256,512]{1,0:T(8,128)(2,1)S(1)}, u32[]{:S(2)}, u32[]{:S(2)}) collective-permute-start(bf16[256,512]{1,0:T(8,128)(2,1)S(1)} %get-tuple-element.61), channel_id=1, source_target_pairs={{0,2},{1,3},{2,0},{3,1},{4,6},{5,7},{6,4},{7,5},{8,10},{9,11},{10,... | collective-permute-start | bytes 786440 | tf_op jit(solution)/shard_map/ppermute | solution.py:277
  19.6 1.8 %collective-permute-start.6 = (bf16[1,512,256]{2,1,0:T(8,128)(2,1)S(1)}, bf16[1,512,256]{2,1,0:T(8,128)(2,1)S(1)}, u32[]{:S(2)}, u32[]{:S(2)}) collective-permute-start(bf16[1,512,256]{2,1,0:T(8,128)(2,1)S(1)} %slice.58), channel_id=1, source_target_pairs={{0,16},{4,20},{8,24},{12,28},{16,0},{20,4},{24,8},{28,12},{1,17},{... | collective-permute-start | bytes 786440 | tf_op jit(solution)/shard_map/ppermute | solution.py:277
  21.4 1.6 %collective-permute-start.7 = (bf16[1,512,256]{2,1,0:T(8,128)(2,1)S(1)}, bf16[1,512,256]{2,1,0:T(8,128)(2,1)S(1)}, u32[]{:S(2)}, u32[]{:S(2)}) collective-permute-start(bf16[1,512,256]{2,1,0:T(8,128)(2,1)S(1)} %slice.62), channel_id=1, source_target_pairs={{0,8},{4,12},{8,0},{12,4},{16,24},{20,28},{24,16},{28,20},{1,9},{5... | collective-permute-start | bytes 786440 | tf_op jit(solution)/shard_map/ppermute | solution.py:277
  22.9 2.2 %collective-permute-done.8 = bf16[256,512]{1,0:T(8,128)(2,1)S(1)} collective-permute-done((bf16[256,512]{1,0:T(8,128)(2,1)S(1)}, bf16[256,512]{1,0:T(8,128)(2,1)S(1)}, u32[]{:S(2)}, u32[]{:S(2)}) %collective-permute-start.8) | collective-permute-done | bytes 262176 | tf_op jit(solution)/shard_map/ppermute | solution.py:277
  25.1 6.3 %collective-permute-done.9 = bf16[256,512]{1,0:T(8,128)(2,1)S(1)} collective-permute-done((bf16[256,512]{1,0:T(8,128)(2,1)S(1)}, bf16[256,512]{1,0:T(8,128)(2,1)S(1)}, u32[]{:S(2)}, u32[]{:S(2)}) %collective-permute-start.9) | collective-permute-done | bytes 262176 | tf_op jit(solution)/shard_map/ppermute | solution.py:277
  32.5 2.4 %collective-permute-start.12 = (bf16[256,512]{1,0:T(8,128)(2,1)S(1)}, bf16[256,512]{1,0:T(8,128)(2,1)S(1)}, u32[]{:S(2)}, u32[]{:S(2)}) collective-permute-start(bf16[256,512]{1,0:T(8,128)(2,1)S(1)} %get-tuple-element.51), channel_id=1, source_target_pairs={{0,3},{1,2},{2,1},{3,0},{4,7},{5,6},{6,5},{7,4},{8,11},{9,10},{10,... | collective-permute-start | bytes 786440 | tf_op jit(solution)/shard_map/ppermute | solution.py:277
  35.0 8.2 %score.1 = (bf16[1024,1024]{1,0:T(8,128)(2,1)S(1)}, bf16[1024,256]{1,0:T(8,128)(2,1)S(1)}, f32[1024,128]{1,0:T(8,128)S(1)}) custom-call(s32[8]{0:T(128)S(1)} %select_reduce_fusion.place_ref, s32[1024,128]{1,0:T(8,128)S(1)} %get-tuple-element.35.first_ref, s32[1024,128]{1,0:T(8,128)S(1)} %get-tuple-element.34.grp_ref, ...), custom_call_target="tpu_custom_call" | custom-call | tf_op jit(solution)/shard_map/score/pallas_call | solution.py:176
  45.0 1.6 %collective-permute-start.14 = (bf16[1,512,256]{2,1,0:T(8,128)(2,1)S(1)}, bf16[1,512,256]{2,1,0:T(8,128)(2,1)S(1)}, u32[]{:S(2)}, u32[]{:S(2)}) collective-permute-start(bf16[1,512,256]{2,1,0:T(8,128)(2,1)S(1)} %slice.64), channel_id=1, source_target_pairs={{0,8},{4,12},{8,0},{12,4},{16,24},{20,28},{24,16},{28,20},{1,9},{5... | collective-permute-start | bytes 786440 | tf_op jit(solution)/shard_map/ppermute | solution.py:277
  46.6 4.1 %collective-permute-done.13.rest_5_ = bf16[1,512,256]{2,1,0:T(8,128)(2,1)S(1)} collective-permute-done((bf16[1,512,256]{2,1,0:T(8,128)(2,1)S(1)}, bf16[1,512,256]{2,1,0:T(8,128)(2,1)S(1)}, u32[]{:S(2)}, u32[]{:S(2)}) %collective-permute-start.13) | collective-permute-done | bytes 262176 | tf_op jit(solution)/shard_map/ppermute | solution.py:277
  50.7 1.2 %collective-permute-done.14.rest_6_ = bf16[1,512,256]{2,1,0:T(8,128)(2,1)S(1)} collective-permute-done((bf16[1,512,256]{2,1,0:T(8,128)(2,1)S(1)}, bf16[1,512,256]{2,1,0:T(8,128)(2,1)S(1)}, u32[]{:S(2)}, u32[]{:S(2)}) %collective-permute-start.14) | collective-permute-done | bytes 262176 | tf_op jit(solution)/shard_map/ppermute | solution.py:277
  51.8 1.5 %collective-permute-start.24 = (bf16[3,256,512]{2,1,0:T(8,128)(2,1)S(1)}, bf16[3,256,512]{2,1,0:T(8,128)(2,1)S(1)}, u32[]{:S(2)}, u32[]{:S(2)}) collective-permute-start(bf16[3,256,512]{2,1,0:T(8,128)(2,1)S(1)} %pad_maximum_fusion.refs_11_), channel_id=1, source_target_pairs={{0,8},{4,12},{8,0},{12,4},{16,24},{20,28},{24,16},{28,20},{1,9},{5... | collective-permute-start | bytes 2359304 | tf_op jit(solution)/shard_map/ppermute | solution.py:277
  53.3 3.5 %mix.1 = (bf16[512,256]{1,0:T(8,128)(2,1)S(1)}, bf16[512,256]{1,0:T(8,128)(2,1)S(1)}) custom-call(s32[8]{0:T(128)S(1)} %select_reduce_fusion.place_ref, s32[1024,128]{1,0:T(8,128)S(1)} %get-tuple-element.34.grp_ref, bf16[1024,1024]{1,0:T(8,128)(2,1)S(1)} %get-tuple-element.42.p_ref, bf16[1024,256]{1,0:T(8,128)(2,1)S(1)} %get-tuple-element.43.near_ref, ...), custom_call_target="tpu_custom_call" | custom-call | tf_op jit(solution)/shard_map/mix/pallas_call | solution.py:225
  57.4 3.4 %collective-permute-start.16 = (bf16[512,256]{1,0:T(8,128)(2,1)S(1)}, bf16[512,256]{1,0:T(8,128)(2,1)S(1)}, u32[]{:S(2)}, u32[]{:S(2)}) collective-permute-start(bf16[512,256]{1,0:T(8,128)(2,1)S(1)} %get-tuple-element.55.refs_0_), channel_id=1, source_target_pairs={{0,2},{1,3},{2,0},{3,1},{4,6},{5,7},{6,4},{7,5},{8,10},{9,11},{10,... | collective-permute-start | bytes 786440 | tf_op jit(solution)/shard_map/ppermute | solution.py:277
  60.8 7.5 %collective-permute-done.24.refs_12_ = bf16[3,256,512]{2,1,0:T(8,128)(2,1)S(1)} collective-permute-done((bf16[3,256,512]{2,1,0:T(8,128)(2,1)S(1)}, bf16[3,256,512]{2,1,0:T(8,128)(2,1)S(1)}, u32[]{:S(2)}, u32[]{:S(2)}) %collective-permute-start.24) | collective-permute-done | bytes 786464 | tf_op jit(solution)/shard_map/ppermute | solution.py:277
  69.3 1.8 %collective-permute-start.15 = (bf16[512,256]{1,0:T(8,128)(2,1)S(1)}, bf16[512,256]{1,0:T(8,128)(2,1)S(1)}, u32[]{:S(2)}, u32[]{:S(2)}) collective-permute-start(bf16[512,256]{1,0:T(8,128)(2,1)S(1)} %get-tuple-element.55.refs_0_), channel_id=1, source_target_pairs={{0,1},{1,0},{2,3},{3,2},{4,5},{5,4},{6,7},{7,6},{8,9},{9,8},{10,11... | collective-permute-start | bytes 786440 | tf_op jit(solution)/shard_map/ppermute | solution.py:277
  71.1 7.9 %collective-permute-done.16.refs_2_ = bf16[512,256]{1,0:T(8,128)(2,1)S(1)} collective-permute-done((bf16[512,256]{1,0:T(8,128)(2,1)S(1)}, bf16[512,256]{1,0:T(8,128)(2,1)S(1)}, u32[]{:S(2)}, u32[]{:S(2)}) %collective-permute-start.16) | collective-permute-done | bytes 262176 | tf_op jit(solution)/shard_map/ppermute | solution.py:277
  79.7 4.9 %collective-permute-done.21.refs_7_ = bf16[512,256]{1,0:T(8,128)(2,1)S(1)} collective-permute-done((bf16[512,256]{1,0:T(8,128)(2,1)S(1)}, bf16[512,256]{1,0:T(8,128)(2,1)S(1)}, u32[]{:S(2)}, u32[]{:S(2)}) %collective-permute-start.21) | collective-permute-done | bytes 262176 | tf_op jit(solution)/shard_map/ppermute | solution.py:277
  84.6 1.3 %collective-permute-start.18 = (bf16[512,256]{1,0:T(8,128)(2,1)S(1)}, bf16[512,256]{1,0:T(8,128)(2,1)S(1)}, u32[]{:S(2)}, u32[]{:S(2)}) collective-permute-start(bf16[512,256]{1,0:T(8,128)(2,1)S(1)} %collective-permute-done.16.refs_2_), channel_id=1, source_target_pairs={{2,3},{1,0},{6,7},{5,4},{10,11},{9,8},{14,15},{13,12},{18,19},{17,... | collective-permute-start | bytes 786440 | tf_op jit(solution)/shard_map/ppermute | solution.py:360
  85.9 2.7 %collective-permute-start.20 = (bf16[512,256]{1,0:T(8,128)(2,1)S(1)}, bf16[512,256]{1,0:T(8,128)(2,1)S(1)}, u32[]{:S(2)}, u32[]{:S(2)}) collective-permute-start(bf16[512,256]{1,0:T(8,128)(2,1)S(1)} %collective-permute-done.19.refs_5_), channel_id=1, source_target_pairs={{0,1},{1,0},{2,3},{3,2},{4,5},{5,4},{6,7},{7,6},{8,9},{9,8},{10,11... | collective-permute-start | bytes 786440 | tf_op jit(solution)/shard_map/ppermute | solution.py:277
  89.3 1.3 %collective-permute-start.23 = (bf16[512,256]{1,0:T(8,128)(2,1)S(1)}, bf16[512,256]{1,0:T(8,128)(2,1)S(1)}, u32[]{:S(2)}, u32[]{:S(2)}) collective-permute-start(bf16[512,256]{1,0:T(8,128)(2,1)S(1)} %collective-permute-done.21.refs_7_), channel_id=1, source_target_pairs={{2,3},{1,0},{6,7},{5,4},{10,11},{9,8},{14,15},{13,12},{18,19},{17,... | collective-permute-start | bytes 786440 | tf_op jit(solution)/shard_map/ppermute | solution.py:360
  90.6 5.1 %collective-permute-done.18.refs_4_ = bf16[512,256]{1,0:T(8,128)(2,1)S(1)} collective-permute-done((bf16[512,256]{1,0:T(8,128)(2,1)S(1)}, bf16[512,256]{1,0:T(8,128)(2,1)S(1)}, u32[]{:S(2)}, u32[]{:S(2)}) %collective-permute-start.18) | collective-permute-done | bytes 262176 | tf_op jit(solution)/shard_map/ppermute | solution.py:360
  95.7 5.6 %collective-permute-done.20.refs_6_ = bf16[512,256]{1,0:T(8,128)(2,1)S(1)} collective-permute-done((bf16[512,256]{1,0:T(8,128)(2,1)S(1)}, bf16[512,256]{1,0:T(8,128)(2,1)S(1)}, u32[]{:S(2)}, u32[]{:S(2)}) %collective-permute-start.20) | collective-permute-done | bytes 262176 | tf_op jit(solution)/shard_map/ppermute | solution.py:277
  101.3 3.8 %collective-permute-done.23.refs_9_ = bf16[512,256]{1,0:T(8,128)(2,1)S(1)} collective-permute-done((bf16[512,256]{1,0:T(8,128)(2,1)S(1)}, bf16[512,256]{1,0:T(8,128)(2,1)S(1)}, u32[]{:S(2)}, u32[]{:S(2)}) %collective-permute-start.23) | collective-permute-done | bytes 262176 | tf_op jit(solution)/shard_map/ppermute | solution.py:360
  105.2 3.9 %project.1 = bf16[512,1024]{1,0:T(8,128)(2,1)} custom-call(s32[3]{0:T(128)S(1)} %pad_add_fusion.1.where_ref, bf16[512,256]{1,0:T(8,128)(2,1)S(1)} %get-tuple-element.55.refs_0_, bf16[512,256]{1,0:T(8,128)(2,1)S(1)} %collective-permute-done.15.refs_1_, bf16[512,256]{1,0:T(8,128)(2,1)S(1)} %collective-permute-done.16.refs_2_, ...), custom_call_target="tpu_custom_call" | custom-call | tf_op jit(solution)/shard_map/project/pallas_call | solution.py:266
  (52 shorter events, 8.3 us)
Async XLA Ops:
  0.0 8.9 %copy-start = (f32[128,256]{1,0:T(8,128)S(1)}, f32[128,256]{1,0:T(8,128)}, u32[]{:S(2)}) copy-start(f32[128,256]{1,0:T(8,128)} %constant.28.clone.refs_5_) | copy-start | bytes 393220
  0.0 10.8 %copy-start.1 = (bf16[512,2,512]{2,1,0:T(2,128)(2,1)S(1)}, bf16[512,2,512]{2,1,0:T(2,128)(2,1)}, u32[]{:S(2)}) copy-start(bf16[512,2,512]{2,1,0:T(2,128)(2,1)} %param.8) | copy-start | bytes 3145732
  1.5 2.8 %collective-permute-start = (bf16[512,256]{1,0:T(8,128)(2,1)S(1)}, bf16[512,256]{1,0:T(8,128)(2,1)S(1)}, u32[]{:S(2)}, u32[]{:S(2)}) collective-permute-start(bf16[512,256]{1,0:T(8,128)(2,1)S(1)} %get-tuple-element.68), channel_id=1, source_target_pairs={{0,4},{4,0},{8,12},{12,8},{16,20},{20,16},{24,28},{28,24},{1,5},{5... | collective-permute-start | bytes 786440 | tf_op jit(solution)/shard_map/ppermute | solution.py:277
  2.7 6.2 %collective-permute-start.1 = (s32[2,8]{1,0:T(2,128)S(1)}, s32[2,8]{1,0:T(2,128)S(1)}, u32[]{:S(2)}, u32[]{:S(2)}) collective-permute-start(s32[2,8]{1,0:T(2,128)S(1)} %pad_add_fusion.refs_0_), channel_id=1, source_target_pairs={{0,4},{4,0},{8,12},{12,8},{16,20},{20,16},{24,28},{28,24},{1,5},{5... | collective-permute-start | bytes 200 | tf_op jit(solution)/shard_map/ppermute | solution.py:277
  4.4 15.2 %collective-permute-start.3 = (bf16[2,512,256]{2,1,0:T(8,128)(2,1)S(1)}, bf16[2,512,256]{2,1,0:T(8,128)(2,1)S(1)}, u32[]{:S(2)}, u32[]{:S(2)}) collective-permute-start(bf16[2,512,256]{2,1,0:T(8,128)(2,1)S(1)} %pad_maximum_fusion.1.rest_2_), channel_id=1, source_target_pairs={{0,8},{4,12},{8,0},{12,4},{16,24},{20,28},{24,16},{28,20},{1,9},{5... | collective-permute-start | bytes 1572872 | tf_op jit(solution)/shard_map/ppermute | solution.py:277
  7.4 14.0 %collective-permute-start.4 = (bf16[2,512,256]{2,1,0:T(8,128)(2,1)S(1)}, bf16[2,512,256]{2,1,0:T(8,128)(2,1)S(1)}, u32[]{:S(2)}, u32[]{:S(2)}) collective-permute-start(bf16[2,512,256]{2,1,0:T(8,128)(2,1)S(1)} %pad_maximum_fusion.1.rest_2_), channel_id=1, source_target_pairs={{0,16},{4,20},{8,24},{12,28},{16,0},{20,4},{24,8},{28,12},{1,17},{... | collective-permute-start | bytes 1572872 | tf_op jit(solution)/shard_map/ppermute | solution.py:277
  10.7 20.7 %collective-permute-start.2 = (bf16[3,512,256]{2,1,0:T(8,128)(2,1)S(1)}, bf16[3,512,256]{2,1,0:T(8,128)(2,1)S(1)}, u32[]{:S(2)}, u32[]{:S(2)}) collective-permute-start(bf16[3,512,256]{2,1,0:T(8,128)(2,1)S(1)} %get-tuple-element.37), channel_id=1, source_target_pairs={{0,4},{4,0},{8,12},{12,8},{16,20},{20,16},{24,28},{28,24},{1,5},{5... | collective-permute-start | bytes 2359304 | tf_op jit(solution)/shard_map/ppermute | solution.py:277
  10.9 24.0 %copy-start.2 = (s32[4,2]{0,1:T(2,128)S(1)}, s32[4,2]{0,1:T(2,128)}, u32[]{:S(2)}) copy-start(s32[4,2]{0,1:T(2,128)} %param.11) | copy-start | bytes 100
  11.1 5.8 %collective-permute-start.5 = (bf16[512,256]{1,0:T(8,128)(2,1)S(1)}, bf16[512,256]{1,0:T(8,128)(2,1)S(1)}, u32[]{:S(2)}, u32[]{:S(2)}) collective-permute-start(bf16[512,256]{1,0:T(8,128)(2,1)S(1)} %get-tuple-element.66), channel_id=1, source_target_pairs={{0,4},{4,0},{8,12},{12,8},{16,20},{20,16},{24,28},{28,24},{1,5},{5... | collective-permute-start | bytes 786440 | tf_op jit(solution)/shard_map/ppermute | solution.py:277
  13.3 11.8 %collective-permute-start.8 = (bf16[256,512]{1,0:T(8,128)(2,1)S(1)}, bf16[256,512]{1,0:T(8,128)(2,1)S(1)}, u32[]{:S(2)}, u32[]{:S(2)}) collective-permute-start(bf16[256,512]{1,0:T(8,128)(2,1)S(1)} %get-tuple-element.60), channel_id=1, source_target_pairs={{0,1},{1,0},{2,3},{3,2},{4,5},{5,4},{6,7},{7,6},{8,9},{9,8},{10,11... | collective-permute-start | bytes 786440 | tf_op jit(solution)/shard_map/ppermute | solution.py:277
  16.8 14.6 %collective-permute-start.9 = (bf16[256,512]{1,0:T(8,128)(2,1)S(1)}, bf16[256,512]{1,0:T(8,128)(2,1)S(1)}, u32[]{:S(2)}, u32[]{:S(2)}) collective-permute-start(bf16[256,512]{1,0:T(8,128)(2,1)S(1)} %get-tuple-element.61), channel_id=1, source_target_pairs={{0,2},{1,3},{2,0},{3,1},{4,6},{5,7},{6,4},{7,5},{8,10},{9,11},{10,... | collective-permute-start | bytes 786440 | tf_op jit(solution)/shard_map/ppermute | solution.py:277
  19.6 11.8 %collective-permute-start.6 = (bf16[1,512,256]{2,1,0:T(8,128)(2,1)S(1)}, bf16[1,512,256]{2,1,0:T(8,128)(2,1)S(1)}, u32[]{:S(2)}, u32[]{:S(2)}) collective-permute-start(bf16[1,512,256]{2,1,0:T(8,128)(2,1)S(1)} %slice.58), channel_id=1, source_target_pairs={{0,16},{4,20},{8,24},{12,28},{16,0},{20,4},{24,8},{28,12},{1,17},{... | collective-permute-start | bytes 786440 | tf_op jit(solution)/shard_map/ppermute | solution.py:277
  21.4 10.1 %collective-permute-start.7 = (bf16[1,512,256]{2,1,0:T(8,128)(2,1)S(1)}, bf16[1,512,256]{2,1,0:T(8,128)(2,1)S(1)}, u32[]{:S(2)}, u32[]{:S(2)}) collective-permute-start(bf16[1,512,256]{2,1,0:T(8,128)(2,1)S(1)} %slice.62), channel_id=1, source_target_pairs={{0,8},{4,12},{8,0},{12,4},{16,24},{20,28},{24,16},{28,20},{1,9},{5... | collective-permute-start | bytes 786440 | tf_op jit(solution)/shard_map/ppermute | solution.py:277
  31.4 12.8 %collective-permute-start.10 = (bf16[2,512,256]{2,1,0:T(8,128)(2,1)S(1)}, bf16[2,512,256]{2,1,0:T(8,128)(2,1)S(1)}, u32[]{:S(2)}, u32[]{:S(2)}) collective-permute-start(bf16[2,512,256]{2,1,0:T(8,128)(2,1)S(1)} %pad_maximum_fusion.2.rest_2_), channel_id=1, source_target_pairs={{0,8},{4,12},{8,0},{12,4},{16,24},{20,28},{24,16},{28,20},{1,9},{5... | collective-permute-start | bytes 1572872 | tf_op jit(solution)/shard_map/ppermute | solution.py:277
  32.0 13.0 %collective-permute-start.11 = (bf16[2,512,256]{2,1,0:T(8,128)(2,1)S(1)}, bf16[2,512,256]{2,1,0:T(8,128)(2,1)S(1)}, u32[]{:S(2)}, u32[]{:S(2)}) collective-permute-start(bf16[2,512,256]{2,1,0:T(8,128)(2,1)S(1)} %pad_maximum_fusion.2.rest_2_), channel_id=1, source_target_pairs={{0,16},{4,20},{8,24},{12,28},{16,0},{20,4},{24,8},{28,12},{1,17},{... | collective-permute-start | bytes 1572872 | tf_op jit(solution)/shard_map/ppermute | solution.py:277
  32.5 10.7 %collective-permute-start.12 = (bf16[256,512]{1,0:T(8,128)(2,1)S(1)}, bf16[256,512]{1,0:T(8,128)(2,1)S(1)}, u32[]{:S(2)}, u32[]{:S(2)}) collective-permute-start(bf16[256,512]{1,0:T(8,128)(2,1)S(1)} %get-tuple-element.51), channel_id=1, source_target_pairs={{0,3},{1,2},{2,1},{3,0},{4,7},{5,6},{6,5},{7,4},{8,11},{9,10},{10,... | collective-permute-start | bytes 786440 | tf_op jit(solution)/shard_map/ppermute | solution.py:277
  44.2 6.4 %collective-permute-start.13 = (bf16[1,512,256]{2,1,0:T(8,128)(2,1)S(1)}, bf16[1,512,256]{2,1,0:T(8,128)(2,1)S(1)}, u32[]{:S(2)}, u32[]{:S(2)}) collective-permute-start(bf16[1,512,256]{2,1,0:T(8,128)(2,1)S(1)} %slice.63), channel_id=1, source_target_pairs={{0,16},{4,20},{8,24},{12,28},{16,0},{20,4},{24,8},{28,12},{1,17},{... | collective-permute-start | bytes 786440 | tf_op jit(solution)/shard_map/ppermute | solution.py:277
  45.0 6.8 %collective-permute-start.14 = (bf16[1,512,256]{2,1,0:T(8,128)(2,1)S(1)}, bf16[1,512,256]{2,1,0:T(8,128)(2,1)S(1)}, u32[]{:S(2)}, u32[]{:S(2)}) collective-permute-start(bf16[1,512,256]{2,1,0:T(8,128)(2,1)S(1)} %slice.64), channel_id=1, source_target_pairs={{0,8},{4,12},{8,0},{12,4},{16,24},{20,28},{24,16},{28,20},{1,9},{5... | collective-permute-start | bytes 786440 | tf_op jit(solution)/shard_map/ppermute | solution.py:277
  51.8 16.4 %collective-permute-start.24 = (bf16[3,256,512]{2,1,0:T(8,128)(2,1)S(1)}, bf16[3,256,512]{2,1,0:T(8,128)(2,1)S(1)}, u32[]{:S(2)}, u32[]{:S(2)}) collective-permute-start(bf16[3,256,512]{2,1,0:T(8,128)(2,1)S(1)} %pad_maximum_fusion.refs_11_), channel_id=1, source_target_pairs={{0,8},{4,12},{8,0},{12,4},{16,24},{20,28},{24,16},{28,20},{1,9},{5... | collective-permute-start | bytes 2359304 | tf_op jit(solution)/shard_map/ppermute | solution.py:277
  53.3 32.5 %collective-permute-start.25 = (bf16[3,256,512]{2,1,0:T(8,128)(2,1)S(1)}, bf16[3,256,512]{2,1,0:T(8,128)(2,1)S(1)}, u32[]{:S(2)}, u32[]{:S(2)}) collective-permute-start(bf16[3,256,512]{2,1,0:T(8,128)(2,1)S(1)} %pad_maximum_fusion.refs_11_), channel_id=1, source_target_pairs={{0,4},{4,0},{8,12},{12,8},{16,20},{20,16},{24,28},{28,24},{1,5},{5... | collective-permute-start | bytes 2359304 | tf_op jit(solution)/shard_map/ppermute | solution.py:277
  56.9 11.4 %collective-permute-start.19 = (bf16[512,256]{1,0:T(8,128)(2,1)S(1)}, bf16[512,256]{1,0:T(8,128)(2,1)S(1)}, u32[]{:S(2)}, u32[]{:S(2)}) collective-permute-start(bf16[512,256]{1,0:T(8,128)(2,1)S(1)} %get-tuple-element.56), channel_id=1, source_target_pairs={{0,4},{4,0},{8,12},{12,8},{16,20},{20,16},{24,28},{28,24},{1,5},{5... | collective-permute-start | bytes 786440 | tf_op jit(solution)/shard_map/ppermute | solution.py:277
  57.4 21.6 %collective-permute-start.16 = (bf16[512,256]{1,0:T(8,128)(2,1)S(1)}, bf16[512,256]{1,0:T(8,128)(2,1)S(1)}, u32[]{:S(2)}, u32[]{:S(2)}) collective-permute-start(bf16[512,256]{1,0:T(8,128)(2,1)S(1)} %get-tuple-element.55.refs_0_), channel_id=1, source_target_pairs={{0,2},{1,3},{2,0},{3,1},{4,6},{5,7},{6,4},{7,5},{8,10},{9,11},{10,... | collective-permute-start | bytes 786440 | tf_op jit(solution)/shard_map/ppermute | solution.py:277
  68.3 36.9 %collective-permute-start.26 = (bf16[3,256,512]{2,1,0:T(8,128)(2,1)S(1)}, bf16[3,256,512]{2,1,0:T(8,128)(2,1)S(1)}, u32[]{:S(2)}, u32[]{:S(2)}) collective-permute-start(bf16[3,256,512]{2,1,0:T(8,128)(2,1)S(1)} %collective-permute-done.24.refs_12_), channel_id=1, source_target_pairs={{0,4},{4,0},{8,12},{12,8},{16,20},{20,16},{24,28},{28,24},{1,5},{5... | collective-permute-start | bytes 2359304 | tf_op jit(solution)/shard_map/ppermute | solution.py:277
  68.3 16.3 %collective-permute-start.21 = (bf16[512,256]{1,0:T(8,128)(2,1)S(1)}, bf16[512,256]{1,0:T(8,128)(2,1)S(1)}, u32[]{:S(2)}, u32[]{:S(2)}) collective-permute-start(bf16[512,256]{1,0:T(8,128)(2,1)S(1)} %collective-permute-done.19.refs_5_), channel_id=1, source_target_pairs={{0,2},{1,3},{2,0},{3,1},{4,6},{5,7},{6,4},{7,5},{8,10},{9,11},{10,... | collective-permute-start | bytes 786440 | tf_op jit(solution)/shard_map/ppermute | solution.py:277
  69.3 19.3 %collective-permute-start.15 = (bf16[512,256]{1,0:T(8,128)(2,1)S(1)}, bf16[512,256]{1,0:T(8,128)(2,1)S(1)}, u32[]{:S(2)}, u32[]{:S(2)}) collective-permute-start(bf16[512,256]{1,0:T(8,128)(2,1)S(1)} %get-tuple-element.55.refs_0_), channel_id=1, source_target_pairs={{0,1},{1,0},{2,3},{3,2},{4,5},{5,4},{6,7},{7,6},{8,9},{9,8},{10,11... | collective-permute-start | bytes 786440 | tf_op jit(solution)/shard_map/ppermute | solution.py:277
  79.0 10.3 %collective-permute-start.17 = (bf16[512,256]{1,0:T(8,128)(2,1)S(1)}, bf16[512,256]{1,0:T(8,128)(2,1)S(1)}, u32[]{:S(2)}, u32[]{:S(2)}) collective-permute-start(bf16[512,256]{1,0:T(8,128)(2,1)S(1)} %get-tuple-element.55.refs_0_), channel_id=1, source_target_pairs={{1,2},{2,1},{5,6},{6,5},{9,10},{10,9},{13,14},{14,13},{17,18},{18,... | collective-permute-start | bytes 786440 | tf_op jit(solution)/shard_map/ppermute | solution.py:359
  84.6 11.1 %collective-permute-start.18 = (bf16[512,256]{1,0:T(8,128)(2,1)S(1)}, bf16[512,256]{1,0:T(8,128)(2,1)S(1)}, u32[]{:S(2)}, u32[]{:S(2)}) collective-permute-start(bf16[512,256]{1,0:T(8,128)(2,1)S(1)} %collective-permute-done.16.refs_2_), channel_id=1, source_target_pairs={{2,3},{1,0},{6,7},{5,4},{10,11},{9,8},{14,15},{13,12},{18,19},{17,... | collective-permute-start | bytes 786440 | tf_op jit(solution)/shard_map/ppermute | solution.py:360
  85.9 15.4 %collective-permute-start.20 = (bf16[512,256]{1,0:T(8,128)(2,1)S(1)}, bf16[512,256]{1,0:T(8,128)(2,1)S(1)}, u32[]{:S(2)}, u32[]{:S(2)}) collective-permute-start(bf16[512,256]{1,0:T(8,128)(2,1)S(1)} %collective-permute-done.19.refs_5_), channel_id=1, source_target_pairs={{0,1},{1,0},{2,3},{3,2},{4,5},{5,4},{6,7},{7,6},{8,9},{9,8},{10,11... | collective-permute-start | bytes 786440 | tf_op jit(solution)/shard_map/ppermute | solution.py:277
  88.6 12.7 %collective-permute-start.22 = (bf16[512,256]{1,0:T(8,128)(2,1)S(1)}, bf16[512,256]{1,0:T(8,128)(2,1)S(1)}, u32[]{:S(2)}, u32[]{:S(2)}) collective-permute-start(bf16[512,256]{1,0:T(8,128)(2,1)S(1)} %collective-permute-done.19.refs_5_), channel_id=1, source_target_pairs={{1,2},{2,1},{5,6},{6,5},{9,10},{10,9},{13,14},{14,13},{17,18},{18,... | collective-permute-start | bytes 786440 | tf_op jit(solution)/shard_map/ppermute | solution.py:359
  89.3 15.9 %collective-permute-start.23 = (bf16[512,256]{1,0:T(8,128)(2,1)S(1)}, bf16[512,256]{1,0:T(8,128)(2,1)S(1)}, u32[]{:S(2)}, u32[]{:S(2)}) collective-permute-start(bf16[512,256]{1,0:T(8,128)(2,1)S(1)} %collective-permute-done.21.refs_7_), channel_id=1, source_target_pairs={{2,3},{1,0},{6,7},{5,4},{10,11},{9,8},{14,15},{13,12},{18,19},{17,... | collective-permute-start | bytes 786440 | tf_op jit(solution)/shard_map/ppermute | solution.py:360

commit v5 on v0

v5 whole, which is shorter than its diff:
```python
import functools
import jax
import jax.numpy as jnp
import numpy as np
from jax import lax
from jax.experimental import pallas as pl
from jax.experimental.pallas import tpu as pltpu
from jax.sharding import PartitionSpec as P

HD = 256
ROT = 64
BLK = 512
OWNERS = 2
GROUPS = 4
SLOTS = GROUPS * OWNERS
MOST = 128
SEEN = OWNERS * BLK

NEG_FILL = -1e30
ROPE_BASE = 10000.0
FACTOR = HD ** (-0.5) * 1.4426950408889634

RB = 128

VMEM = pl.BlockSpec(memory_space=pltpu.VMEM)
SMEM = pl.BlockSpec(memory_space=pltpu.SMEM)


def from_root(x, axis, root):
    mine = lax.axis_index(axis) == root
    return lax.psum(jnp.where(mine, x, jnp.zeros_like(x)), axis)


def rope_table():
    inverse = np.float32(ROPE_BASE) ** (-2.0 * np.arange(ROT // 2, dtype=np.float32) / ROT)
    inverse = np.concatenate([np.repeat(inverse, 2), np.zeros(128 - ROT)]).astype(np.float32)
    angles = np.arange(SEEN, SEEN + MOST, dtype=np.float32)[:, None] * inverse[None, :]
    angles = angles.astype(np.float64)
    sign = np.where(np.arange(128) % 2 == 0, -1.0, 1.0)
    table = np.concatenate([np.cos(angles), np.sin(angles) * sign[None, :]], axis=1)
    return jnp.asarray(table.astype(np.float32))


def prep_kernel(table_ref, q_ref, k_ref, v_ref, rope_ref, first_ref, grp_ref, *o_refs):
    rows = q_ref.shape[0]
    requests = table_ref.shape[1]
    lane = lax.broadcasted_iota(jnp.int32, (RB, 128), 1)
    even = (lane % 2) == 0
    for r0 in range(0, rows, RB):
        at = slice(r0, r0 + RB)
        row = r0 + lax.broadcasted_iota(jnp.int32, (RB, 128), 0)
        start = jnp.int32(0)
        first = jnp.zeros((RB, 128), jnp.int32)
        grp = jnp.zeros((RB, 128), jnp.int32) + table_ref[1, 0]
        for r in range(1, requests):
            start = start + table_ref[0, r - 1]
            later = row >= start
            first = jnp.where(later, start, first)
            grp = jnp.where(later, table_ref[1, r], grp)
        first_ref[at, :] = first
        grp_ref[at, :] = grp
        chosen = jnp.where(row - first == lane, 1.0, 0.0)
        turn = lax.dot_general(
            chosen,
            rope_ref[...],
            (((1,), (0,)), ((), ())),
            precision=lax.Precision.HIGHEST,
            preferred_element_type=jnp.float32,
        )
        cos = turn[:, :128]
        sin = turn[:, 128:]
        for i, o_ref in enumerate(o_refs):
            c0 = i * HD
            for n, ref in enumerate((q_ref, k_ref)):
                y = ref[at, c0 : c0 + 128].astype(jnp.float32)
                swapped = jnp.where(even, pltpu.roll(y, 127, 1), pltpu.roll(y, 1, 1))
                o_ref[n, at, 0:128] = (y * cos + swapped * sin).astype(jnp.bfloat16)
                o_ref[n, at, 128:HD] = ref[at, c0 + 128 : c0 + HD]
            o_ref[2, at, :] = v_ref[at, c0 : c0 + HD]


def prepare(table, q, k, v):
    rows, feat = q.shape
    heads = feat // HD
    column = jax.ShapeDtypeStruct((rows, 128), jnp.int32)
    return pl.pallas_call(
        prep_kernel,
        out_shape=[column] * 2 + [jax.ShapeDtypeStruct((3, rows, HD), jnp.bfloat16)] * heads,
        in_specs=[SMEM] + [VMEM] * 4,
        out_specs=[VMEM] * (2 + heads),
        compiler_params=pltpu.CompilerParams(vmem_limit_bytes=4 << 20),
        name="prepare",
    )(table, q, k, v, rope_table())


def wide(x, width):
    return x if width == 128 else jnp.concatenate([x] * (width // 128), axis=1)


def attend_kernel(where_k, where_v, place_ref, first_ref, grp_ref, suf, *rest):
    o_ref, sc, p = rest[-3:]
    keys = [rest[i].at[j] for i, j in where_k]
    values = [rest[i].at[j] for i, j in where_v]
    half = 256
    for b in range(o_ref.shape[0] // RB):
        r0 = b * RB
        buf = b % 2
        at = slice(r0, r0 + RB)
        q = suf[0, at, :]
        grp = wide(grp_ref[at, :], half)
        for d in range(SLOTS):
            g = place_ref[d] // OWNERS
            o = place_ref[d] % OWNERS
            for j in range(BLK // half):
                s = lax.dot_general(
                    q,
                    keys[d][j * half : (j + 1) * half, :],
                    (((1,), (1,)), ((), ())),
                    preferred_element_type=jnp.float32,
                )
                c = pl.ds(pl.multiple_of(o * BLK + j * half, half), half)
                sc[buf, :, c] = jnp.where(grp == g, s, sc[buf, :, c])
        lo = max(0, r0 - MOST)
        width = r0 + RB - lo
        local = lax.dot_general(
            q,
            suf[1, lo : r0 + RB, :],
            (((1,), (1,)), ((), ())),
            preferred_element_type=jnp.float32,
        )
        row = r0 + lax.broadcasted_iota(jnp.int32, (RB, width), 0)
        key = lo + lax.broadcasted_iota(jnp.int32, (RB, width), 1)
        start = wide(first_ref[at, :], width)
        local = jnp.where((key <= row) & (key >= start), local, NEG_FILL)
        top = jnp.max(local, axis=1, keepdims=True)
        whole = sc[buf, :, 0:half]
        for c0 in range(half, SEEN, half):
            whole = jnp.maximum(whole, sc[buf, :, c0 : c0 + half])
        top = jnp.maximum(top, jnp.max(whole, axis=1, keepdims=True))
        e = jnp.exp2((local - top) * FACTOR)
        den = jnp.sum(e, axis=1, keepdims=True)
        acc = jnp.dot(
            e.astype(jnp.bfloat16), suf[2, lo : r0 + RB, :], preferred_element_type=jnp.float32
        )
        total = None
        for c0 in range(0, SEEN, half):
            e = jnp.exp2((sc[buf, :, c0 : c0 + half] - top) * FACTOR)
            p[buf, :, c0 : c0 + half] = e.astype(jnp.bfloat16)
            total = e if total is None else total + e
        den = den + jnp.sum(total, axis=1, keepdims=True)
        for d in range(SLOTS):
            g = place_ref[d] // OWNERS
            o = place_ref[d] % OWNERS
            part = jnp.dot(
                p[buf, :, pl.ds(pl.multiple_of(o * BLK, BLK), BLK)],
                values[d][...],
                preferred_element_type=jnp.float32,
            )
            acc = acc + jnp.where(grp == g, part, 0.0)
        o_ref[at, :] = (acc / den).astype(jnp.bfloat16)


def attend(place, first, grp, suf, pieces, where_k, where_v):
    rows = suf.shape[1]
    return pl.pallas_call(
        functools.partial(attend_kernel, where_k, where_v),
        out_shape=jax.ShapeDtypeStruct((rows, HD), jnp.bfloat16),
        in_specs=[SMEM] + [VMEM] * (3 + len(pieces)),
        out_specs=VMEM,
        scratch_shapes=[
            pltpu.VMEM((2, RB, SEEN), jnp.float32),
            pltpu.VMEM((2, RB, SEEN), jnp.bfloat16),
        ],
        compiler_params=pltpu.CompilerParams(vmem_limit_bytes=8 << 20),
        name="attend",
    )(place, first, grp, suf, *pieces)


def proj_kernel(head, where_ref, *refs):
    att = refs[:5]
    own = refs[5]
    far = refs[6:10]
    add_ref = refs[10] if len(refs) == 12 else None
    o_ref = refs[-1]
    cols = o_ref.shape[1] // 2
    rows = o_ref.shape[0]
    mine = where_ref[1] == head
    side = where_ref[2]
    tall = 256
    for x in range(2):
        c0 = pl.multiple_of(lax.bitwise_xor(side, x) * cols, cols)
        w = [own[head * HD : (head + 1) * HD, pl.ds(c0, cols)]]
        w += [jnp.where(mine, far[x][m], far[2 + x][m]) for m in range(3)]
        for r0 in range(0, rows, tall):
            at = slice(r0, r0 + tall)
            acc = jnp.dot(att[0][at, :], w[0], preferred_element_type=jnp.float32)
            for m in range(1, 4):
                a = att[m][at, :]
                if m == 3:
                    a = a + att[4][at, :]
                acc = acc + jnp.dot(a, w[m], preferred_element_type=jnp.float32)
            if add_ref is not None:
                acc = acc + add_ref[at, pl.ds(c0, cols)]
            o_ref[at, pl.ds(c0, cols)] = acc.astype(o_ref.dtype)


def project(head, where, att, own, far, add=None):
    rows = att[0].shape[0]
    cols = own.shape[1]
    extra = [] if add is None else [add]
    return pl.pallas_call(
        functools.partial(proj_kernel, head),
        out_shape=jax.ShapeDtypeStruct((rows, cols), jnp.float32 if add is None else jnp.bfloat16),
        in_specs=[SMEM] + [VMEM] * (len(att) + 1 + len(far) + len(extra)),
        out_specs=VMEM,
        compiler_params=pltpu.CompilerParams(vmem_limit_bytes=6 << 20),
        name="project",
    )(where, *att, own, *far, *extra)


def swap(x, axis, mask, size):
    return lax.ppermute(x, axis, [(i, i ^ mask) for i in range(size)])


def after(x, *deps):
    return lax.optimization_barrier((x,) + deps)[0]


over_x = functools.partial(swap, axis="req", mask=2, size=8)
over_y = functools.partial(swap, axis="req", mask=4, size=8)
over_core = functools.partial(swap, axis="req", mask=1, size=8)


def over_tp(a):
    two = swap(a, "tp", 2, 4)
    one = swap(a, "tp", 1, 4)
    three = lax.ppermute(after(a, two), "tp", [(1, 2), (2, 1)])
    forward = lax.ppermute(two, "tp", [(2, 3), (1, 0)])
    return [a, one, two, three, forward]


WHERE_K = ((0, 0), (5, 0), (1, 0), (6, 0), (2, 0), (7, 0), (3, 0), (8, 0))
WHERE_V = ((0, 1), (5, 1), (1, 1), (6, 1), (2, 1), (7, 1), (4, 0), (9, 0))


def split_heads(suffix_heads, prefix_cache, lengths, groups, owners, out_weight):
    me = lax.axis_index("req")
    z = lax.axis_index("tp")
    core = me & 1
    side = (me >> 1) & 1
    where = jnp.stack([z, core, side]).astype(jnp.int32)
    place = jnp.sum(
        jnp.where(
            owners[None] == (me ^ jnp.arange(SLOTS, dtype=jnp.int32))[:, None, None],
            jnp.arange(SLOTS, dtype=jnp.int32).reshape(1, GROUPS, OWNERS),
            0,
        ),
        axis=(1, 2),
    ).astype(jnp.int32)
    tp_size = 4

    cols = out_weight.shape[1] // tp_size
    z_u, core_u, side_u = (i.astype(jnp.uint32) for i in (z, core, side))
    starts = [core_u * HD, z_u * cols]
    starts += [(z_u ^ m) * cols + side_u * (cols // 2) for m in range(1, tp_size)]
    prefix = jnp.swapaxes(prefix_cache, 0, 1)
    sends = [
        lax.dynamic_slice(out_weight, (starts[0], starts[1 + m]), (HD, cols // 2))
        for m in range(1, tp_size)
    ]
    w_own = lax.dynamic_slice(
        out_weight, (jnp.zeros_like(starts[0]), starts[1]), (out_weight.shape[0], cols)
    )

    kv0 = prefix[:, :, :HD]
    kvx0 = over_x(kv0)
    kvy0 = over_y(kv0)
    w_one, w_two = (swap(sends[m - 1], "tp", m, tp_size) for m in (1, 2))
    table = jnp.concatenate([lengths, groups], axis=0)
    first, grp, suf0, suf1 = prepare(
        after(table, kv0), suffix_heads[:, 0], suffix_heads[:, 1], suffix_heads[:, 2]
    )
    kxy0 = over_y(after(kvx0[0:1], suf0, w_own))
    vyx0 = over_x(after(kvy0[1:2], suf0, w_own))
    kv1 = after(prefix[:, :, HD:], kvx0, kvy0)
    kvx1 = over_x(kv1)
    kvy1 = over_y(kv1)
    pieces0 = [kv0, kvx0, kvy0, kxy0, vyx0]
    pieces0 += [over_core(p) for p in pieces0]
    att0 = attend(after(place, w_one, w_two), first, grp, suf0, pieces0, WHERE_K, WHERE_V)

    w_three = swap(after(sends[2], w_two), "tp", 3, tp_size)
    kxy1 = over_y(after(kvx1[0:1], att0, w_three))
    vyx1 = over_x(after(kvy1[1:2], att0, w_three))
    pieces1 = [kv1, kvx1, kvy1, kxy1, vyx1]
    pieces1 += [over_core(p) for p in pieces1]
    spread0 = over_tp(att0)
    att1 = attend(after(place, spread0[2]), first, grp, suf1, pieces1, WHERE_K, WHERE_V)

    w_far = jnp.stack([after(w_one, att0), w_two, w_three])
    w_core = over_core(w_far)
    w_x = over_x(after(w_far, kxy1, vyx1))
    spread1 = over_tp(after(att1, *spread0[1:]))
    w_core_x = over_core(after(w_x, att1))
    far = [w_far, w_x, w_core, w_core_x]
    half = project(0, where, spread0, w_own, far)
    return project(1, where, spread1, w_own, far, half)


def whole_heads(suffix_heads, prefix_cache, lengths, groups, owners, out_weight):
    heads = suffix_heads.shape[2] // HD
    received = [
        from_root(prefix_cache, "req", owners[i // OWNERS, i % OWNERS]) for i in range(SLOTS)
    ]
    place = jnp.arange(SLOTS, dtype=jnp.int32)
    first, grp, *sufs = prepare(
        jnp.concatenate([lengths, groups], axis=0),
        suffix_heads[:, 0],
        suffix_heads[:, 1],
        suffix_heads[:, 2],
    )
    where_k = tuple((d, 0) for d in range(SLOTS))
    where_v = tuple((d, 1) for d in range(SLOTS))
    attended = []
    for h in range(heads):
        pieces = [jnp.swapaxes(s[:, :, h * HD : (h + 1) * HD], 0, 1) for s in received]
        attended.append(attend(place, first, grp, sufs[h], pieces, where_k, where_v))
    partial_out = jnp.dot(
        jnp.concatenate(attended, axis=1), out_weight, preferred_element_type=jnp.float32
    )
    return lax.psum_scatter(partial_out.astype(jnp.bfloat16), "tp", scatter_dimension=1, tiled=True)


def per_device(req_size, tp_size, *args):
    if req_size == 8 and tp_size == 4 and args[0].shape[2] == 2 * HD:
        return split_heads(*args)
    return whole_heads(*args)


def solution(mesh):
    placed = (
        P("req", None, "tp"),
        P("req", None, "tp"),
        P("req", None),
        P("req", None),
        P(),
        P("tp", None),
    )
    return jax.shard_map(
        functools.partial(per_device, mesh.shape["req"], mesh.shape["tp"]),
        mesh=mesh,
        in_specs=placed,
        out_specs=P("req", "tp"),
        check_vma=False,
    )
```

time: 267 us -> 115 us (0.43)
  waiting for transfers between devices: 205 us -> 62.4 us
  starting transfers between devices: 0.04 us -> 25.1 us
  between operations: 18.7 us -> 0.22 us
  Pallas kernels: 0 us -> 18.4 us
  matrix products: 17.3 us -> 0 us
  local copies, waits for them, and re-layouts: 17.4 us -> 7.29 us
  other arithmetic: 7.3 us -> 1.22 us
    psum x1 -> x0, waiting for transfers between devices: 128 us -> none  [from_root(): return lax.psum(jnp.where(mine, x, jnp.zeros_like(x)), axis)]
    reduce_scatter x1 -> x0, waiting for transfers between devices: 77.2 us -> none  [per_device(): lax.psum_scatter(partial_out.astype(jnp.bfloat16), 'tp', scatter_dimensio...]
    ppermute x0 -> x32, waiting for transfers between devices: none -> 62.4 us  [the longest x28 50.3 us: swap(): return lax.ppermute(x, axis, [(i, i ^ mask) for i in range(size)])]
    ppermute x0 -> x32, starting transfers between devices: none -> 25.1 us  [the longest x28 21 us: swap(): return lax.ppermute(x, axis, [(i, i ^ mask) for i in range(size)])]
    pallas_call x0 -> x5, Pallas kernels: none -> 18.4 us  [the longest x2 12.2 us: attend(): pl.pallas_call(functools.partial(attend_kernel, where_k, where_v), out_sh...]
    dot_general x9 -> x0, matrix products: 17.3 us -> none  [the longest x2 6.51 us: one_head(): lax.dot_general(query_h, pkey_h, (((1,), (1,)), ((), ())), preferred_elem...]
    unnamed x25 -> x11, local copies, waits for them, and re-layouts: 9.15 us -> 1.45 us
    slice x8 -> x5, local copies, waits for them, and re-layouts: 5.62 us -> 1.09 us  [the longest x1 0.97 us: split_heads(): vyx0 = over_x(after(kvy0[1:2], suf0, w_own))]
  transfers between devices with their start and end apart: 2 -> 32, of which waited for: 2 -> 16; matrix products, arithmetic and copies ran while one was open for 1% -> 6% of each run, Pallas kernels for 0% -> 14%
where the time goes in v5:
time: 115 us
  waiting for transfers between devices  62.4 us (54%)
  starting transfers between devices  25.1 us (22%)
  Pallas kernels  18.4 us (16%)
  local copies, waits for them, and re-layouts  7.29 us (6%)
  other arithmetic  1.22 us (1%)
    ppermute x28, waiting for transfers between devices, swap(): return lax.ppermute(x, axis, [(i, i ^ mask) for i in range(size)])  50.3 us
    ppermute x28, starting transfers between devices, swap(): return lax.ppermute(x, axis, [(i, i ^ mask) for i in range(size)])  21 us
    pallas_call x2, Pallas kernels, attend(): pl.pallas_call(functools.partial(attend_kernel, where_k, where_v), out_sh...  12.2 us
    ppermute x2, waiting for transfers between devices, over_tp(): forward = lax.ppermute(two, 'tp', [(2, 3), (1, 0)])  12 us
    pallas_call x2, Pallas kernels, project(): pl.pallas_call(functools.partial(proj_kernel, head), out_shape=jax.ShapeD...  4.66 us
    ppermute x2, starting transfers between devices, over_tp(): forward = lax.ppermute(two, 'tp', [(2, 3), (1, 0)])  2.75 us
  transfers between devices with their start and end apart: 32, of which 16 were waited for; matrix products, arithmetic and copies ran while one was open for 6% of the time, Pallas kernels for 14%

profile of v5, /device:TPU:0, one launch (start us, length us, event | category | flops | bytes accessed | tf_op | source)
XLA Modules:
  0.0 114.7 jit_solution(12668075610779644343)
XLA Ops:
  0.0 1.4 %copy.12 = bf16[512,2,512]{2,0,1:T(8,128)(2,1)S(1)} copy(bf16[512,2,512]{2,1,0:T(2,128)(2,1)} %param.8) | data formatting | bytes 2097152 | tf_op args[1]
  1.5 3.0 %collective-permute-start.2 = (bf16[2,512,256]{2,1,0:T(8,128)(2,1)S(1)}, bf16[2,512,256]{2,1,0:T(8,128)(2,1)S(1)}, u32[]{:S(2)}, u32[]{:S(2)}) collective-permute-start(bf16[2,512,256]{2,1,0:T(8,128)(2,1)S(1)} %get-tuple-element.50.rest_0_), channel_id=1, source_target_pairs={{0,8},{4,12},{8,0},{12,4},{16,24},{20,28},{24,16},{28,20},{1,9},{5... | collective-permute-start | bytes 1572872 | tf_op jit(solution)/shard_map/ppermute | solution.py:222
  4.5 1.5 %collective-permute-start.3 = (bf16[2,512,256]{2,1,0:T(8,128)(2,1)S(1)}, bf16[2,512,256]{2,1,0:T(8,128)(2,1)}, u32[]{:S(2)}, u32[]{:S(2)}) collective-permute-start(bf16[2,512,256]{2,1,0:T(8,128)(2,1)S(1)} %get-tuple-element.50.rest_0_), channel_id=1, source_target_pairs={{0,16},{4,20},{8,24},{12,28},{16,0},{20,4},{24,8},{28,12},{1,17},{... | collective-permute-start | bytes 1572872 | tf_op jit(solution)/shard_map/ppermute | solution.py:222
  6.0 2.0 %fusion = (bf16[256,512]{1,0:T(8,128)(2,1)}, bf16[256,512]{1,0:T(8,128)(2,1)}, bf16[256,512]{1,0:T(8,128)(2,1)}) fusion(bf16[512,4096]{1,0:T(8,128)(2,1)} %param.12, u32[]{:T(128)S(6)} %mul.20, u32[]{:T(128)S(6)} %add.17, u32[]{:T(128)S(6)} %add.16, u32[]{:T(128)S(6)} %add.15), kind=kLoop, calls=%fused_computation.11 | loop fusion | bytes 1572880 | tf_op jit(solution)/shard_map/dynamic_slice | solution.py:268
  8.0 1.6 %collective-permute-start = (bf16[256,512]{1,0:T(8,128)(2,1)}, bf16[256,512]{1,0:T(8,128)(2,1)S(1)}, u32[]{:S(2)}, u32[]{:S(2)}) collective-permute-start(bf16[256,512]{1,0:T(8,128)(2,1)} %get-tuple-element.45), channel_id=1, source_target_pairs={{0,1},{1,0},{2,3},{3,2},{4,5},{5,4},{6,7},{7,6},{8,9},{9,8},{10,11... | collective-permute-start | bytes 786440 | tf_op jit(solution)/shard_map/ppermute | solution.py:222
  9.6 2.6 %collective-permute-start.1 = (bf16[256,512]{1,0:T(8,128)(2,1)}, bf16[256,512]{1,0:T(8,128)(2,1)}, u32[]{:S(2)}, u32[]{:S(2)}) collective-permute-start(bf16[256,512]{1,0:T(8,128)(2,1)} %get-tuple-element.44), channel_id=1, source_target_pairs={{0,2},{1,3},{2,0},{3,1},{4,6},{5,7},{6,4},{7,5},{8,10},{9,11},{10,... | collective-permute-start | bytes 786440 | tf_op jit(solution)/shard_map/ppermute | solution.py:222
  12.2 1.5 %slice_bitcast_fusion = (bf16[512,512]{1,0:T(8,128)(2,1)S(1)}, bf16[512,512]{1,0:T(8,128)(2,1)S(1)}, bf16[512,512]{1,0:T(8,128)(2,1)S(1)}) fusion(bf16[512,3,512]{2,0,1:T(8,128)(2,1)} %param.7), kind=kLoop, calls=%fused_computation.2 | loop fusion | bytes 3145728 | tf_op jit(solution)/shard_map/squeeze | solution.py:281
  13.7 1.6 %prepare.1 = (s32[512,128]{1,0:T(8,128)S(1)}, s32[512,128]{1,0:T(8,128)S(1)}, bf16[3,512,256]{2,1,0:T(8,128)(2,1)S(1)}, bf16[3,512,256]{2,1,0:T(8,128)(2,1)S(1)}) custom-call(s32[2,8]{1,0:T(2,128)S(1)} %pad_add_fusion.table_ref, bf16[512,512]{1,0:T(8,128)(2,1)S(1)} %get-tuple-element.47.q_ref, bf16[512,512]{1,0:T(8,128)(2,1)S(1)} %get-tuple-element.48.k_ref, ...), custom_call_target="tpu_custom_call" | custom-call | tf_op jit(solution)/shard_map/prepare/pallas_call | solution.py:86
  15.3 1.2 %collective-permute-done.2.rest_1_ = bf16[2,512,256]{2,1,0:T(8,128)(2,1)S(1)} collective-permute-done((bf16[2,512,256]{2,1,0:T(8,128)(2,1)S(1)}, bf16[2,512,256]{2,1,0:T(8,128)(2,1)S(1)}, u32[]{:S(2)}, u32[]{:S(2)}) %collective-permute-start.2) | collective-permute-done | bytes 524320 | tf_op jit(solution)/shard_map/ppermute | solution.py:222
  16.4 1.6 %collective-permute-done.3.rest_2_ = bf16[2,512,256]{2,1,0:T(8,128)(2,1)} collective-permute-done((bf16[2,512,256]{2,1,0:T(8,128)(2,1)S(1)}, bf16[2,512,256]{2,1,0:T(8,128)(2,1)}, u32[]{:S(2)}, u32[]{:S(2)}) %collective-permute-start.3) | collective-permute-done | bytes 524320 | tf_op jit(solution)/shard_map/ppermute | solution.py:222
  18.4 1.3 %constant_dynamic-slice_fusion.refs_5_ = bf16[512,1024]{1,0:T(8,128)(2,1)S(1)} fusion(bf16[512,4096]{1,0:T(8,128)(2,1)} %param.12, u32[]{:T(128)S(6)} %mul.24), kind=kLoop, calls=%fused_computation.9 | loop fusion | bytes 2097156 | tf_op jit(solution)/shard_map/dynamic_slice | solution.py:271
  19.7 2.8 %collective-permute-done = bf16[256,512]{1,0:T(8,128)(2,1)S(1)} collective-permute-done((bf16[256,512]{1,0:T(8,128)(2,1)}, bf16[256,512]{1,0:T(8,128)(2,1)S(1)}, u32[]{:S(2)}, u32[]{:S(2)}) %collective-permute-start) | collective-permute-done | bytes 262176 | tf_op jit(solution)/shard_map/ppermute | solution.py:222
  23.0 1.0 slice.38
  24.0 1.0 collective-permute-done.1
  25.5 5.0 %collective-permute-done.4.rest_3_ = bf16[1,512,256]{2,1,0:T(8,128)(2,1)S(1)} collective-permute-done((bf16[1,512,256]{2,1,0:T(8,128)(2,1)S(1)}, bf16[1,512,256]{2,1,0:T(8,128)(2,1)S(1)}, u32[]{:S(2)}, u32[]{:S(2)}) %collective-permute-start.4) | collective-permute-done | bytes 262176 | tf_op jit(solution)/shard_map/ppermute | solution.py:222
  31.0 5.1 %collective-permute-done.5.rest_4_ = bf16[1,512,256]{2,1,0:T(8,128)(2,1)S(1)} collective-permute-done((bf16[1,512,256]{2,1,0:T(8,128)(2,1)S(1)}, bf16[1,512,256]{2,1,0:T(8,128)(2,1)S(1)}, u32[]{:S(2)}, u32[]{:S(2)}) %collective-permute-start.5) | collective-permute-done | bytes 262176 | tf_op jit(solution)/shard_map/ppermute | solution.py:222
  36.1 3.6 %collective-permute-start.14 = (bf16[256,512]{1,0:T(8,128)(2,1)S(1)}, bf16[256,512]{1,0:T(8,128)(2,1)S(1)}, u32[]{:S(2)}, u32[]{:S(2)}) collective-permute-start(bf16[256,512]{1,0:T(8,128)(2,1)S(1)} %copy-done.1), channel_id=1, source_target_pairs={{0,3},{1,2},{2,1},{3,0},{4,7},{5,6},{6,5},{7,4},{8,11},{9,10},{10,... | collective-permute-start | bytes 786440 | tf_op jit(solution)/shard_map/ppermute | solution.py:222
  41.6 6.4 %attend.2.refs_0_ = bf16[512,256]{1,0:T(8,128)(2,1)S(1)} custom-call(s32[8]{0:T(128)S(1)} %select_reduce_fusion.place_ref, s32[512,128]{1,0:T(8,128)S(1)} %get-tuple-element.26.first_ref, s32[512,128]{1,0:T(8,128)S(1)} %get-tuple-element.27.grp_ref, bf16[3,512,256]{2,1,0:T(8,128)(2,1)S(1)} %get-tuple-element.28.suf, ...), custom_call_target="tpu_custom_call" | custom-call | tf_op jit(solution)/shard_map/attend/pallas_call | solution.py:165
  48.1 1.6 %collective-permute-start.15 = (bf16[1,512,256]{2,1,0:T(8,128)(2,1)S(1)}, bf16[1,512,256]{2,1,0:T(8,128)(2,1)S(1)}, u32[]{:S(2)}, u32[]{:S(2)}) collective-permute-start(bf16[1,512,256]{2,1,0:T(8,128)(2,1)S(1)} %slice.40), channel_id=1, source_target_pairs={{0,16},{4,20},{8,24},{12,28},{16,0},{20,4},{24,8},{28,12},{1,17},{... | collective-permute-start | bytes 786440 | tf_op jit(solution)/shard_map/ppermute | solution.py:222
  50.4 1.0 pad_maximum_fusion.refs_6_
  51.4 5.1 %collective-permute-done.15.rest_3_ = bf16[1,512,256]{2,1,0:T(8,128)(2,1)S(1)} collective-permute-done((bf16[1,512,256]{2,1,0:T(8,128)(2,1)S(1)}, bf16[1,512,256]{2,1,0:T(8,128)(2,1)S(1)}, u32[]{:S(2)}, u32[]{:S(2)}) %collective-permute-start.15) | collective-permute-done | bytes 262176 | tf_op jit(solution)/shard_map/ppermute | solution.py:222
  56.5 1.4 %collective-permute-done.16.rest_4_ = bf16[1,512,256]{2,1,0:T(8,128)(2,1)S(1)} collective-permute-done((bf16[1,512,256]{2,1,0:T(8,128)(2,1)S(1)}, bf16[1,512,256]{2,1,0:T(8,128)(2,1)S(1)}, u32[]{:S(2)}, u32[]{:S(2)}) %collective-permute-start.16) | collective-permute-done | bytes 262176 | tf_op jit(solution)/shard_map/ppermute | solution.py:222
  59.9 13.4 %collective-permute-done.11.refs_2_ = bf16[512,256]{1,0:T(8,128)(2,1)S(1)} collective-permute-done((bf16[512,256]{1,0:T(8,128)(2,1)S(1)}, bf16[512,256]{1,0:T(8,128)(2,1)S(1)}, u32[]{:S(2)}, u32[]{:S(2)}) %collective-permute-start.11) | collective-permute-done | bytes 262176 | tf_op jit(solution)/shard_map/ppermute | solution.py:222
  74.8 1.5 %collective-permute-start.24 = (bf16[512,256]{1,0:T(8,128)(2,1)S(1)}, bf16[512,256]{1,0:T(8,128)(2,1)S(1)}, u32[]{:S(2)}, u32[]{:S(2)}) collective-permute-start(bf16[512,256]{1,0:T(8,128)(2,1)S(1)} %collective-permute-done.11.refs_2_), channel_id=1, source_target_pairs={{2,3},{1,0},{6,7},{5,4},{10,11},{9,8},{14,15},{13,12},{18,19},{17,... | collective-permute-start | bytes 786440 | tf_op jit(solution)/shard_map/ppermute | solution.py:238
  76.2 5.8 %attend.3.refs_0_ = bf16[512,256]{1,0:T(8,128)(2,1)S(1)} custom-call(s32[8]{0:T(128)S(1)} %select_reduce_fusion.place_ref, s32[512,128]{1,0:T(8,128)S(1)} %get-tuple-element.26.first_ref, s32[512,128]{1,0:T(8,128)S(1)} %get-tuple-element.27.grp_ref, bf16[3,512,256]{2,1,0:T(8,128)(2,1)S(1)} %get-tuple-element.32.suf, ...), custom_call_target="tpu_custom_call" | custom-call | tf_op jit(solution)/shard_map/attend/pallas_call | solution.py:165
  82.4 5.2 %collective-permute-done.24.refs_4_ = bf16[512,256]{1,0:T(8,128)(2,1)S(1)} collective-permute-done((bf16[512,256]{1,0:T(8,128)(2,1)S(1)}, bf16[512,256]{1,0:T(8,128)(2,1)S(1)}, u32[]{:S(2)}, u32[]{:S(2)}) %collective-permute-start.24) | collective-permute-done | bytes 262176 | tf_op jit(solution)/shard_map/ppermute | solution.py:238
  87.6 1.2 %collective-permute-start.25 = (bf16[512,256]{1,0:T(8,128)(2,1)S(1)}, bf16[512,256]{1,0:T(8,128)(2,1)S(1)}, u32[]{:S(2)}, u32[]{:S(2)}) collective-permute-start(bf16[512,256]{1,0:T(8,128)(2,1)S(1)} %attend.3.refs_0_), channel_id=1, source_target_pairs={{0,1},{1,0},{2,3},{3,2},{4,5},{5,4},{6,7},{7,6},{8,9},{9,8},{10,11... | collective-permute-start | bytes 786440 | tf_op jit(solution)/shard_map/ppermute | solution.py:222
  88.8 12.3 %collective-permute-done.26.refs_2_ = bf16[512,256]{1,0:T(8,128)(2,1)S(1)} collective-permute-done((bf16[512,256]{1,0:T(8,128)(2,1)S(1)}, bf16[512,256]{1,0:T(8,128)(2,1)S(1)}, u32[]{:S(2)}, u32[]{:S(2)}) %collective-permute-start.26) | collective-permute-done | bytes 262176 | tf_op jit(solution)/shard_map/ppermute | solution.py:222
  101.8 1.3 %collective-permute-start.28 = (bf16[512,256]{1,0:T(8,128)(2,1)S(1)}, bf16[512,256]{1,0:T(8,128)(2,1)S(1)}, u32[]{:S(2)}, u32[]{:S(2)}) collective-permute-start(bf16[512,256]{1,0:T(8,128)(2,1)S(1)} %collective-permute-done.26.refs_2_), channel_id=1, source_target_pairs={{2,3},{1,0},{6,7},{5,4},{10,11},{9,8},{14,15},{13,12},{18,19},{17,... | collective-permute-start | bytes 786440 | tf_op jit(solution)/shard_map/ppermute | solution.py:238
  103.2 1.8 %project.2.refs_10_ = f32[512,1024]{1,0:T(8,128)S(1)} custom-call(s32[3]{0:T(128)S(1)} %pad_add_fusion.1.where_ref, bf16[512,256]{1,0:T(8,128)(2,1)S(1)} %attend.2.refs_0_, bf16[512,256]{1,0:T(8,128)(2,1)S(1)} %collective-permute-done.22.refs_1_, bf16[512,256]{1,0:T(8,128)(2,1)S(1)} %collective-permute-done.11.refs_2_, ...), custom_call_target="tpu_custom_call" | custom-call | tf_op jit(solution)/shard_map/project/pallas_call | solution.py:211
  105.0 6.8 %collective-permute-done.28.refs_4_ = bf16[512,256]{1,0:T(8,128)(2,1)S(1)} collective-permute-done((bf16[512,256]{1,0:T(8,128)(2,1)S(1)}, bf16[512,256]{1,0:T(8,128)(2,1)S(1)}, u32[]{:S(2)}, u32[]{:S(2)}) %collective-permute-start.28) | collective-permute-done | bytes 262176 | tf_op jit(solution)/shard_map/ppermute | solution.py:238
  111.8 2.8 %project.3 = bf16[512,1024]{1,0:T(8,128)(2,1)} custom-call(s32[3]{0:T(128)S(1)} %pad_add_fusion.1.where_ref, bf16[512,256]{1,0:T(8,128)(2,1)S(1)} %attend.3.refs_0_, bf16[512,256]{1,0:T(8,128)(2,1)S(1)} %collective-permute-done.25.refs_1_, bf16[512,256]{1,0:T(8,128)(2,1)S(1)} %collective-permute-done.26.refs_2_, ...), custom_call_target="tpu_custom_call" | custom-call | tf_op jit(solution)/shard_map/project/pallas_call | solution.py:211
  (62 shorter events, 9.2 us)
Async XLA Ops:
  1.5 14.9 %collective-permute-start.2 = (bf16[2,512,256]{2,1,0:T(8,128)(2,1)S(1)}, bf16[2,512,256]{2,1,0:T(8,128)(2,1)S(1)}, u32[]{:S(2)}, u32[]{:S(2)}) collective-permute-start(bf16[2,512,256]{2,1,0:T(8,128)(2,1)S(1)} %get-tuple-element.50.rest_0_), channel_id=1, source_target_pairs={{0,8},{4,12},{8,0},{12,4},{16,24},{20,28},{24,16},{28,20},{1,9},{5... | collective-permute-start | bytes 1572872 | tf_op jit(solution)/shard_map/ppermute | solution.py:222
  4.5 13.5 %collective-permute-start.3 = (bf16[2,512,256]{2,1,0:T(8,128)(2,1)S(1)}, bf16[2,512,256]{2,1,0:T(8,128)(2,1)}, u32[]{:S(2)}, u32[]{:S(2)}) collective-permute-start(bf16[2,512,256]{2,1,0:T(8,128)(2,1)S(1)} %get-tuple-element.50.rest_0_), channel_id=1, source_target_pairs={{0,16},{4,20},{8,24},{12,28},{16,0},{20,4},{24,8},{28,12},{1,17},{... | collective-permute-start | bytes 1572872 | tf_op jit(solution)/shard_map/ppermute | solution.py:222
  6.0 19.4 %collective-permute-start.6 = (bf16[2,512,256]{2,1,0:T(8,128)(2,1)S(1)}, bf16[2,512,256]{2,1,0:T(8,128)(2,1)}, u32[]{:S(2)}, u32[]{:S(2)}) collective-permute-start(bf16[2,512,256]{2,1,0:T(8,128)(2,1)S(1)} %get-tuple-element.50.rest_0_), channel_id=1, source_target_pairs={{0,4},{4,0},{8,12},{12,8},{16,20},{20,16},{24,28},{28,24},{1,5},{5... | collective-permute-start | bytes 1572872 | tf_op jit(solution)/shard_map/ppermute | solution.py:222
  8.0 14.4 %collective-permute-start = (bf16[256,512]{1,0:T(8,128)(2,1)}, bf16[256,512]{1,0:T(8,128)(2,1)S(1)}, u32[]{:S(2)}, u32[]{:S(2)}) collective-permute-start(bf16[256,512]{1,0:T(8,128)(2,1)} %get-tuple-element.45), channel_id=1, source_target_pairs={{0,1},{1,0},{2,3},{3,2},{4,5},{5,4},{6,7},{7,6},{8,9},{9,8},{10,11... | collective-permute-start | bytes 786440 | tf_op jit(solution)/shard_map/ppermute | solution.py:222
  9.6 15.3 %collective-permute-start.1 = (bf16[256,512]{1,0:T(8,128)(2,1)}, bf16[256,512]{1,0:T(8,128)(2,1)}, u32[]{:S(2)}, u32[]{:S(2)}) collective-permute-start(bf16[256,512]{1,0:T(8,128)(2,1)} %get-tuple-element.44), channel_id=1, source_target_pairs={{0,2},{1,3},{2,0},{3,1},{4,6},{5,7},{6,4},{7,5},{8,10},{9,11},{10,... | collective-permute-start | bytes 786440 | tf_op jit(solution)/shard_map/ppermute | solution.py:222
  18.0 21.7 %collective-permute-start.12 = (bf16[2,512,256]{2,1,0:T(8,128)(2,1)S(1)}, bf16[2,512,256]{2,1,0:T(8,128)(2,1)S(1)}, u32[]{:S(2)}, u32[]{:S(2)}) collective-permute-start(bf16[2,512,256]{2,1,0:T(8,128)(2,1)S(1)} %get-tuple-element.33.rest_0_), channel_id=1, source_target_pairs={{0,8},{4,12},{8,0},{12,4},{16,24},{20,28},{24,16},{28,20},{1,9},{5... | collective-permute-start | bytes 1572872 | tf_op jit(solution)/shard_map/ppermute | solution.py:222
  18.4 21.3 %collective-permute-start.7 = (bf16[2,512,256]{2,1,0:T(8,128)(2,1)S(1)}, bf16[2,512,256]{2,1,0:T(8,128)(2,1)S(1)}, u32[]{:S(2)}, u32[]{:S(2)}) collective-permute-start(bf16[2,512,256]{2,1,0:T(8,128)(2,1)S(1)} %collective-permute-done.2.rest_1_), channel_id=1, source_target_pairs={{0,4},{4,0},{8,12},{12,8},{16,20},{20,16},{24,28},{28,24},{1,5},{5... | collective-permute-start | bytes 1572872 | tf_op jit(solution)/shard_map/ppermute | solution.py:222
  22.5 8.0 %collective-permute-start.4 = (bf16[1,512,256]{2,1,0:T(8,128)(2,1)S(1)}, bf16[1,512,256]{2,1,0:T(8,128)(2,1)S(1)}, u32[]{:S(2)}, u32[]{:S(2)}) collective-permute-start(bf16[1,512,256]{2,1,0:T(8,128)(2,1)S(1)} %slice.37), channel_id=1, source_target_pairs={{0,16},{4,20},{8,24},{12,28},{16,0},{20,4},{24,8},{28,12},{1,17},{... | collective-permute-start | bytes 786440 | tf_op jit(solution)/shard_map/ppermute | solution.py:222
  24.9 11.2 %collective-permute-start.5 = (bf16[1,512,256]{2,1,0:T(8,128)(2,1)S(1)}, bf16[1,512,256]{2,1,0:T(8,128)(2,1)S(1)}, u32[]{:S(2)}, u32[]{:S(2)}) collective-permute-start(bf16[1,512,256]{2,1,0:T(8,128)(2,1)S(1)} %slice.38), channel_id=1, source_target_pairs={{0,8},{4,12},{8,0},{12,4},{16,24},{20,28},{24,16},{28,20},{1,9},{5... | collective-permute-start | bytes 786440 | tf_op jit(solution)/shard_map/ppermute | solution.py:222
  25.5 14.9 %collective-permute-start.8 = (bf16[2,512,256]{2,1,0:T(8,128)(2,1)}, bf16[2,512,256]{2,1,0:T(8,128)(2,1)S(1)}, u32[]{:S(2)}, u32[]{:S(2)}) collective-permute-start(bf16[2,512,256]{2,1,0:T(8,128)(2,1)} %collective-permute-done.3.rest_2_), channel_id=1, source_target_pairs={{0,4},{4,0},{8,12},{12,8},{16,20},{20,16},{24,28},{28,24},{1,5},{5... | collective-permute-start | bytes 1572872 | tf_op jit(solution)/shard_map/ppermute | solution.py:222
  30.5 19.2 %collective-permute-start.13 = (bf16[2,512,256]{2,1,0:T(8,128)(2,1)S(1)}, bf16[2,512,256]{2,1,0:T(8,128)(2,1)S(1)}, u32[]{:S(2)}, u32[]{:S(2)}) collective-permute-start(bf16[2,512,256]{2,1,0:T(8,128)(2,1)S(1)} %get-tuple-element.33.rest_0_), channel_id=1, source_target_pairs={{0,16},{4,20},{8,24},{12,28},{16,0},{20,4},{24,8},{28,12},{1,17},{... | collective-permute-start | bytes 1572872 | tf_op jit(solution)/shard_map/ppermute | solution.py:222
  36.1 12.0 %collective-permute-start.14 = (bf16[256,512]{1,0:T(8,128)(2,1)S(1)}, bf16[256,512]{1,0:T(8,128)(2,1)S(1)}, u32[]{:S(2)}, u32[]{:S(2)}) collective-permute-start(bf16[256,512]{1,0:T(8,128)(2,1)S(1)} %copy-done.1), channel_id=1, source_target_pairs={{0,3},{1,2},{2,1},{3,0},{4,7},{5,6},{6,5},{7,4},{8,11},{9,10},{10,... | collective-permute-start | bytes 786440 | tf_op jit(solution)/shard_map/ppermute | solution.py:222
  39.7 1.5 %collective-permute-start.9 = (bf16[1,512,256]{2,1,0:T(8,128)(2,1)S(1)}, bf16[1,512,256]{2,1,0:T(8,128)(2,1)S(1)}, u32[]{:S(2)}, u32[]{:S(2)}) collective-permute-start(bf16[1,512,256]{2,1,0:T(8,128)(2,1)S(1)} %collective-permute-done.4.rest_3_), channel_id=1, source_target_pairs={{0,4},{4,0},{8,12},{12,8},{16,20},{20,16},{24,28},{28,24},{1,5},{5... | collective-permute-start | bytes 786440 | tf_op jit(solution)/shard_map/ppermute | solution.py:222
  39.7 1.9 %collective-permute-start.10 = (bf16[1,512,256]{2,1,0:T(8,128)(2,1)S(1)}, bf16[1,512,256]{2,1,0:T(8,128)(2,1)S(1)}, u32[]{:S(2)}, u32[]{:S(2)}) collective-permute-start(bf16[1,512,256]{2,1,0:T(8,128)(2,1)S(1)} %collective-permute-done.5.rest_4_), channel_id=1, source_target_pairs={{0,4},{4,0},{8,12},{12,8},{16,20},{20,16},{24,28},{28,24},{1,5},{5... | collective-permute-start | bytes 786440 | tf_op jit(solution)/shard_map/ppermute | solution.py:222
  48.1 8.4 %collective-permute-start.15 = (bf16[1,512,256]{2,1,0:T(8,128)(2,1)S(1)}, bf16[1,512,256]{2,1,0:T(8,128)(2,1)S(1)}, u32[]{:S(2)}, u32[]{:S(2)}) collective-permute-start(bf16[1,512,256]{2,1,0:T(8,128)(2,1)S(1)} %slice.40), channel_id=1, source_target_pairs={{0,16},{4,20},{8,24},{12,28},{16,0},{20,4},{24,8},{28,12},{1,17},{... | collective-permute-start | bytes 786440 | tf_op jit(solution)/shard_map/ppermute | solution.py:222
  49.7 8.1 %collective-permute-start.16 = (bf16[1,512,256]{2,1,0:T(8,128)(2,1)S(1)}, bf16[1,512,256]{2,1,0:T(8,128)(2,1)S(1)}, u32[]{:S(2)}, u32[]{:S(2)}) collective-permute-start(bf16[1,512,256]{2,1,0:T(8,128)(2,1)S(1)} %slice.41), channel_id=1, source_target_pairs={{0,8},{4,12},{8,0},{12,4},{16,24},{20,28},{24,16},{28,20},{1,9},{5... | collective-permute-start | bytes 786440 | tf_op jit(solution)/shard_map/ppermute | solution.py:222
  50.4 9.5 %collective-permute-start.17 = (bf16[2,512,256]{2,1,0:T(8,128)(2,1)S(1)}, bf16[2,512,256]{2,1,0:T(8,128)(2,1)S(1)}, u32[]{:S(2)}, u32[]{:S(2)}) collective-permute-start(bf16[2,512,256]{2,1,0:T(8,128)(2,1)S(1)} %get-tuple-element.33.rest_0_), channel_id=1, source_target_pairs={{0,4},{4,0},{8,12},{12,8},{16,20},{20,16},{24,28},{28,24},{1,5},{5... | collective-permute-start | bytes 1572872 | tf_op jit(solution)/shard_map/ppermute | solution.py:222
  57.9 24.2 %collective-permute-start.29 = (bf16[3,256,512]{2,1,0:T(8,128)(2,1)S(1)}, bf16[3,256,512]{2,1,0:T(8,128)(2,1)S(1)}, u32[]{:S(2)}, u32[]{:S(2)}) collective-permute-start(bf16[3,256,512]{2,1,0:T(8,128)(2,1)S(1)} %pad_maximum_fusion.refs_6_), channel_id=1, source_target_pairs={{0,8},{4,12},{8,0},{12,4},{16,24},{20,28},{24,16},{28,20},{1,9},{5... | collective-permute-start | bytes 2359304 | tf_op jit(solution)/shard_map/ppermute | solution.py:222
  58.4 14.8 %collective-permute-start.18 = (bf16[2,512,256]{2,1,0:T(8,128)(2,1)S(1)}, bf16[2,512,256]{2,1,0:T(8,128)(2,1)S(1)}, u32[]{:S(2)}, u32[]{:S(2)}) collective-permute-start(bf16[2,512,256]{2,1,0:T(8,128)(2,1)S(1)} %collective-permute-done.12.rest_1_), channel_id=1, source_target_pairs={{0,4},{4,0},{8,12},{12,8},{16,20},{20,16},{24,28},{28,24},{1,5},{5... | collective-permute-start | bytes 1572872 | tf_op jit(solution)/shard_map/ppermute | solution.py:222
  58.4 14.8 %collective-permute-start.19 = (bf16[2,512,256]{2,1,0:T(8,128)(2,1)S(1)}, bf16[2,512,256]{2,1,0:T(8,128)(2,1)S(1)}, u32[]{:S(2)}, u32[]{:S(2)}) collective-permute-start(bf16[2,512,256]{2,1,0:T(8,128)(2,1)S(1)} %collective-permute-done.13.rest_2_), channel_id=1, source_target_pairs={{0,4},{4,0},{8,12},{12,8},{16,20},{20,16},{24,28},{28,24},{1,5},{5... | collective-permute-start | bytes 1572872 | tf_op jit(solution)/shard_map/ppermute | solution.py:222
  59.0 14.3 %collective-permute-start.11 = (bf16[512,256]{1,0:T(8,128)(2,1)S(1)}, bf16[512,256]{1,0:T(8,128)(2,1)S(1)}, u32[]{:S(2)}, u32[]{:S(2)}) collective-permute-start(bf16[512,256]{1,0:T(8,128)(2,1)S(1)} %attend.2.refs_0_), channel_id=1, source_target_pairs={{0,2},{1,3},{2,0},{3,1},{4,6},{5,7},{6,4},{7,5},{8,10},{9,11},{10,... | collective-permute-start | bytes 786440 | tf_op jit(solution)/shard_map/ppermute | solution.py:222
  59.9 14.0 %collective-permute-start.20 = (bf16[1,512,256]{2,1,0:T(8,128)(2,1)S(1)}, bf16[1,512,256]{2,1,0:T(8,128)(2,1)S(1)}, u32[]{:S(2)}, u32[]{:S(2)}) collective-permute-start(bf16[1,512,256]{2,1,0:T(8,128)(2,1)S(1)} %collective-permute-done.15.rest_3_), channel_id=1, source_target_pairs={{0,4},{4,0},{8,12},{12,8},{16,20},{20,16},{24,28},{28,24},{1,5},{5... | collective-permute-start | bytes 786440 | tf_op jit(solution)/shard_map/ppermute | solution.py:222
  73.2 1.5 %collective-permute-start.21 = (bf16[1,512,256]{2,1,0:T(8,128)(2,1)S(1)}, bf16[1,512,256]{2,1,0:T(8,128)(2,1)S(1)}, u32[]{:S(2)}, u32[]{:S(2)}) collective-permute-start(bf16[1,512,256]{2,1,0:T(8,128)(2,1)S(1)} %collective-permute-done.16.rest_4_), channel_id=1, source_target_pairs={{0,4},{4,0},{8,12},{12,8},{16,20},{20,16},{24,28},{28,24},{1,5},{5... | collective-permute-start | bytes 786440 | tf_op jit(solution)/shard_map/ppermute | solution.py:222
  73.2 9.1 %collective-permute-start.22 = (bf16[512,256]{1,0:T(8,128)(2,1)S(1)}, bf16[512,256]{1,0:T(8,128)(2,1)S(1)}, u32[]{:S(2)}, u32[]{:S(2)}) collective-permute-start(bf16[512,256]{1,0:T(8,128)(2,1)S(1)} %attend.2.refs_0_), channel_id=1, source_target_pairs={{0,1},{1,0},{2,3},{3,2},{4,5},{5,4},{6,7},{7,6},{8,9},{9,8},{10,11... | collective-permute-start | bytes 786440 | tf_op jit(solution)/shard_map/ppermute | solution.py:222
  73.3 29.9 %collective-permute-start.30 = (bf16[3,256,512]{2,1,0:T(8,128)(2,1)S(1)}, bf16[3,256,512]{2,1,0:T(8,128)(2,1)S(1)}, u32[]{:S(2)}, u32[]{:S(2)}) collective-permute-start(bf16[3,256,512]{2,1,0:T(8,128)(2,1)S(1)} %pad_maximum_fusion.refs_6_), channel_id=1, source_target_pairs={{0,4},{4,0},{8,12},{12,8},{16,20},{20,16},{24,28},{28,24},{1,5},{5... | collective-permute-start | bytes 2359304 | tf_op jit(solution)/shard_map/ppermute | solution.py:222
  73.8 8.5 %collective-permute-start.23 = (bf16[512,256]{1,0:T(8,128)(2,1)S(1)}, bf16[512,256]{1,0:T(8,128)(2,1)S(1)}, u32[]{:S(2)}, u32[]{:S(2)}) collective-permute-start(bf16[512,256]{1,0:T(8,128)(2,1)S(1)} %attend.2.refs_0_), channel_id=1, source_target_pairs={{1,2},{2,1},{5,6},{6,5},{9,10},{10,9},{13,14},{14,13},{17,18},{18,... | collective-permute-start | bytes 786440 | tf_op jit(solution)/shard_map/ppermute | solution.py:237
  74.8 12.8 %collective-permute-start.24 = (bf16[512,256]{1,0:T(8,128)(2,1)S(1)}, bf16[512,256]{1,0:T(8,128)(2,1)S(1)}, u32[]{:S(2)}, u32[]{:S(2)}) collective-permute-start(bf16[512,256]{1,0:T(8,128)(2,1)S(1)} %collective-permute-done.11.refs_2_), channel_id=1, source_target_pairs={{2,3},{1,0},{6,7},{5,4},{10,11},{9,8},{14,15},{13,12},{18,19},{17,... | collective-permute-start | bytes 786440 | tf_op jit(solution)/shard_map/ppermute | solution.py:238
  82.0 21.1 %collective-permute-start.31 = (bf16[3,256,512]{2,1,0:T(8,128)(2,1)S(1)}, bf16[3,256,512]{2,1,0:T(8,128)(2,1)S(1)}, u32[]{:S(2)}, u32[]{:S(2)}) collective-permute-start(bf16[3,256,512]{2,1,0:T(8,128)(2,1)S(1)} %collective-permute-done.29.refs_7_), channel_id=1, source_target_pairs={{0,4},{4,0},{8,12},{12,8},{16,20},{20,16},{24,28},{28,24},{1,5},{5... | collective-permute-start | bytes 2359304 | tf_op jit(solution)/shard_map/ppermute | solution.py:222
  87.6 13.5 %collective-permute-start.26 = (bf16[512,256]{1,0:T(8,128)(2,1)S(1)}, bf16[512,256]{1,0:T(8,128)(2,1)S(1)}, u32[]{:S(2)}, u32[]{:S(2)}) collective-permute-start(bf16[512,256]{1,0:T(8,128)(2,1)S(1)} %attend.3.refs_0_), channel_id=1, source_target_pairs={{0,2},{1,3},{2,0},{3,1},{4,6},{5,7},{6,4},{7,5},{8,10},{9,11},{10,... | collective-permute-start | bytes 786440 | tf_op jit(solution)/shard_map/ppermute | solution.py:222
  87.6 17.4 %collective-permute-start.25 = (bf16[512,256]{1,0:T(8,128)(2,1)S(1)}, bf16[512,256]{1,0:T(8,128)(2,1)S(1)}, u32[]{:S(2)}, u32[]{:S(2)}) collective-permute-start(bf16[512,256]{1,0:T(8,128)(2,1)S(1)} %attend.3.refs_0_), channel_id=1, source_target_pairs={{0,1},{1,0},{2,3},{3,2},{4,5},{5,4},{6,7},{7,6},{8,9},{9,8},{10,11... | collective-permute-start | bytes 786440 | tf_op jit(solution)/shard_map/ppermute | solution.py:222
  101.1 3.9 %collective-permute-start.27 = (bf16[512,256]{1,0:T(8,128)(2,1)S(1)}, bf16[512,256]{1,0:T(8,128)(2,1)S(1)}, u32[]{:S(2)}, u32[]{:S(2)}) collective-permute-start(bf16[512,256]{1,0:T(8,128)(2,1)S(1)} %attend.3.refs_0_), channel_id=1, source_target_pairs={{1,2},{2,1},{5,6},{6,5},{9,10},{10,9},{13,14},{14,13},{17,18},{18,... | collective-permute-start | bytes 786440 | tf_op jit(solution)/shard_map/ppermute | solution.py:237
  101.8 10.1 %collective-permute-start.28 = (bf16[512,256]{1,0:T(8,128)(2,1)S(1)}, bf16[512,256]{1,0:T(8,128)(2,1)S(1)}, u32[]{:S(2)}, u32[]{:S(2)}) collective-permute-start(bf16[512,256]{1,0:T(8,128)(2,1)S(1)} %collective-permute-done.26.refs_2_), channel_id=1, source_target_pairs={{2,3},{1,0},{6,7},{5,4},{10,11},{9,8},{14,15},{13,12},{18,19},{17,... | collective-permute-start | bytes 786440 | tf_op jit(solution)/shard_map/ppermute | solution.py:238
  (5 other events, 95.7 us)

commit v6 on v5

--- a/solution.py
+++ b/solution.py
@@ -277,25 +277,27 @@
     kvy0 = over_y(kv0)
     w_one, w_two = (swap(sends[m - 1], "tp", m, tp_size) for m in (1, 2))
     table = jnp.concatenate([lengths, groups], axis=0)
+    kvc0 = over_core(kv0)
     first, grp, suf0, suf1 = prepare(
-        after(table, kv0), suffix_heads[:, 0], suffix_heads[:, 1], suffix_heads[:, 2]
-    )
-    kxy0 = over_y(after(kvx0[0:1], suf0, w_own))
-    vyx0 = over_x(after(kvy0[1:2], suf0, w_own))
-    kv1 = after(prefix[:, :, HD:], kvx0, kvy0)
+        after(table, kvc0), suffix_heads[:, 0], suffix_heads[:, 1], suffix_heads[:, 2]
+    )
+    kxy0 = over_y(after(kvx0[0:1], suf0, w_own, w_two))
+    vyx0 = over_x(after(kvy0[1:2], suf0, w_own, w_two))
+    kv1 = after(prefix[:, :, HD:], kxy0, vyx0)
     kvx1 = over_x(kv1)
     kvy1 = over_y(kv1)
     pieces0 = [kv0, kvx0, kvy0, kxy0, vyx0]
-    pieces0 += [over_core(p) for p in pieces0]
-    att0 = attend(after(place, w_one, w_two), first, grp, suf0, pieces0, WHERE_K, WHERE_V)
+    pieces0 += [kvc0] + [over_core(after(p, w_one)) for p in pieces0[1:3]]
+    pieces0 += [over_core(p) for p in pieces0[3:5]]
+    att0 = attend(place, first, grp, suf0, pieces0, WHERE_K, WHERE_V)
 
     w_three = swap(after(sends[2], w_two), "tp", 3, tp_size)
     kxy1 = over_y(after(kvx1[0:1], att0, w_three))
     vyx1 = over_x(after(kvy1[1:2], att0, w_three))
     pieces1 = [kv1, kvx1, kvy1, kxy1, vyx1]
-    pieces1 += [over_core(p) for p in pieces1]
     spread0 = over_tp(att0)
-    att1 = attend(after(place, spread0[2]), first, grp, suf1, pieces1, WHERE_K, WHERE_V)
+    pieces1 += [over_core(after(p, spread0[2])) for p in pieces1]
+    att1 = attend(place, first, grp, suf1, pieces1, WHERE_K, WHERE_V)
 
     w_far = jnp.stack([after(w_one, att0), w_two, w_three])
     w_core = over_core(w_far)

time: 115 us -> 108 us (0.939)
  waiting for transfers between devices: 62.4 us -> 48.1 us
  starting transfers between devices: 25.1 us -> 34.5 us
    ppermute x28, waiting for transfers between devices: 50.3 us -> 37.2 us  [swap(): return lax.ppermute(x, axis, [(i, i ^ mask) for i in range(size)])]
    ppermute x28, starting transfers between devices: 21 us -> 30.4 us  [swap(): return lax.ppermute(x, axis, [(i, i ^ mask) for i in range(size)])]
  transfers between devices with their start and end apart: 32 -> 32, of which waited for: 16 -> 14; matrix products, arithmetic and copies ran while one was open for 6% -> 5% of each run, Pallas kernels for 14% -> 14%
where the time goes in v6:
time: 108 us; the launch traced here: 107 us
  waiting for transfers between devices  48.1 us (45%)
  starting transfers between devices  34.5 us (32%)
  Pallas kernels  18 us (17%)
  local copies, waits for them, and re-layouts  6.21 us (6%)
    ppermute x28, waiting for transfers between devices, swap(): return lax.ppermute(x, axis, [(i, i ^ mask) for i in range(size)])  37.2 us
    ppermute x28, starting transfers between devices, swap(): return lax.ppermute(x, axis, [(i, i ^ mask) for i in range(size)])  30.4 us
    pallas_call x2, Pallas kernels, attend(): pl.pallas_call(functools.partial(attend_kernel, where_k, where_v), out_sh...  11.7 us
    ppermute x2, waiting for transfers between devices, over_tp(): forward = lax.ppermute(two, 'tp', [(2, 3), (1, 0)])  10.9 us
    pallas_call x2, Pallas kernels, project(): pl.pallas_call(functools.partial(proj_kernel, head), out_shape=jax.ShapeD...  4.74 us
    ppermute x2, starting transfers between devices, over_tp(): forward = lax.ppermute(two, 'tp', [(2, 3), (1, 0)])  2.76 us
  transfers between devices with their start and end apart: 32, of which 14 were waited for; matrix products, arithmetic and copies ran while one was open for 5% of the time, Pallas kernels for 14%

profile of v6, /device:TPU:0, one launch (start us, length us, event | category | flops | bytes accessed | tf_op | source)
XLA Modules:
  0.0 107.2 jit_solution(3254713268504063946)
XLA Ops:
  0.0 1.4 %copy.12 = bf16[512,2,512]{2,0,1:T(8,128)(2,1)S(1)} copy(bf16[512,2,512]{2,1,0:T(2,128)(2,1)} %param.8) | data formatting | bytes 2097152 | tf_op args[1]
  2.0 2.6 %collective-permute-start.4 = (bf16[2,512,256]{2,1,0:T(8,128)(2,1)S(1)}, bf16[2,512,256]{2,1,0:T(8,128)(2,1)S(1)}, u32[]{:S(2)}, u32[]{:S(2)}) collective-permute-start(bf16[2,512,256]{2,1,0:T(8,128)(2,1)S(1)} %get-tuple-element.60.rest_0_), channel_id=1, source_target_pairs={{0,16},{4,20},{8,24},{12,28},{16,0},{20,4},{24,8},{28,12},{1,17},{... | collective-permute-start | bytes 1572872 | tf_op jit(solution)/shard_map/ppermute | solution.py:222
  4.6 1.5 %collective-permute-start.1 = (bf16[2,512,256]{2,1,0:T(8,128)(2,1)S(1)}, bf16[2,512,256]{2,1,0:T(8,128)(2,1)S(1)}, u32[]{:S(2)}, u32[]{:S(2)}) collective-permute-start(bf16[2,512,256]{2,1,0:T(8,128)(2,1)S(1)} %get-tuple-element.60.rest_0_), channel_id=1, source_target_pairs={{0,8},{4,12},{8,0},{12,4},{16,24},{20,28},{24,16},{28,20},{1,9},{5... | collective-permute-start | bytes 1572872 | tf_op jit(solution)/shard_map/ppermute | solution.py:222
  6.1 1.9 %fusion = (bf16[256,512]{1,0:T(8,128)(2,1)S(1)}, bf16[256,512]{1,0:T(8,128)(2,1)}, bf16[256,512]{1,0:T(8,128)(2,1)S(1)}) fusion(bf16[512,4096]{1,0:T(8,128)(2,1)} %param.12, u32[]{:T(128)S(6)} %mul.21, u32[]{:T(128)S(6)} %add.17, u32[]{:T(128)S(6)} %add.15, u32[]{:T(128)S(6)} %add.16), kind=kLoop, calls=%fused_computation.11 | loop fusion | bytes 1572880 | tf_op jit(solution)/shard_map/dynamic_slice | solution.py:268
  8.0 2.6 %collective-permute-start.2 = (bf16[256,512]{1,0:T(8,128)(2,1)}, bf16[256,512]{1,0:T(8,128)(2,1)S(1)}, u32[]{:S(2)}, u32[]{:S(2)}) collective-permute-start(bf16[256,512]{1,0:T(8,128)(2,1)} %get-tuple-element.54), channel_id=1, source_target_pairs={{0,2},{1,3},{2,0},{3,1},{4,6},{5,7},{6,4},{7,5},{8,10},{9,11},{10,... | collective-permute-start | bytes 786440 | tf_op jit(solution)/shard_map/ppermute | solution.py:222
  10.6 1.3 %constant_dynamic-slice_fusion.refs_5_ = bf16[512,1024]{1,0:T(8,128)(2,1)S(1)} fusion(bf16[512,4096]{1,0:T(8,128)(2,1)} %param.12, u32[]{:T(128)S(6)} %mul.20), kind=kLoop, calls=%fused_computation.9 | loop fusion | bytes 2097156 | tf_op jit(solution)/shard_map/dynamic_slice | solution.py:271
  11.9 1.5 %slice_bitcast_fusion = (bf16[512,512]{1,0:T(8,128)(2,1)S(1)}, bf16[512,512]{1,0:T(8,128)(2,1)S(1)}, bf16[512,512]{1,0:T(8,128)(2,1)S(1)}) fusion(bf16[512,3,512]{2,0,1:T(8,128)(2,1)} %param.7), kind=kLoop, calls=%fused_computation.2 | loop fusion | bytes 3145728 | tf_op jit(solution)/shard_map/squeeze | solution.py:282
  13.4 1.6 %prepare.1 = (s32[512,128]{1,0:T(8,128)S(1)}, s32[512,128]{1,0:T(8,128)S(1)}, bf16[3,512,256]{2,1,0:T(8,128)(2,1)S(1)}, bf16[3,512,256]{2,1,0:T(8,128)(2,1)S(1)}) custom-call(s32[2,8]{1,0:T(2,128)S(1)} %pad_add_fusion.table_ref, bf16[512,512]{1,0:T(8,128)(2,1)S(1)} %get-tuple-element.57.q_ref, bf16[512,512]{1,0:T(8,128)(2,1)S(1)} %get-tuple-element.58.k_ref, ...), custom_call_target="tpu_custom_call" | custom-call | tf_op jit(solution)/shard_map/prepare/pallas_call | solution.py:86
  15.0 2.2 %collective-permute-done.4.rest_2_ = bf16[2,512,256]{2,1,0:T(8,128)(2,1)S(1)} collective-permute-done((bf16[2,512,256]{2,1,0:T(8,128)(2,1)S(1)}, bf16[2,512,256]{2,1,0:T(8,128)(2,1)S(1)}, u32[]{:S(2)}, u32[]{:S(2)}) %collective-permute-start.4) | collective-permute-done | bytes 524320 | tf_op jit(solution)/shard_map/ppermute | solution.py:222
  17.2 5.7 %collective-permute-done.2 = bf16[256,512]{1,0:T(8,128)(2,1)S(1)} collective-permute-done((bf16[256,512]{1,0:T(8,128)(2,1)}, bf16[256,512]{1,0:T(8,128)(2,1)S(1)}, u32[]{:S(2)}, u32[]{:S(2)}) %collective-permute-start.2) | collective-permute-done | bytes 262176 | tf_op jit(solution)/shard_map/ppermute | solution.py:222
  23.9 0.8 collective-permute-start.8
  24.7 5.3 %collective-permute-done.5.rest_4_ = bf16[1,512,256]{2,1,0:T(8,128)(2,1)S(1)} collective-permute-done((bf16[1,512,256]{2,1,0:T(8,128)(2,1)S(1)}, bf16[1,512,256]{2,1,0:T(8,128)(2,1)S(1)}, u32[]{:S(2)}, u32[]{:S(2)}) %collective-permute-start.5) | collective-permute-done | bytes 262176 | tf_op jit(solution)/shard_map/ppermute | solution.py:222
  31.4 1.3 %collective-permute-start.7 = (bf16[2,512,256]{2,1,0:T(8,128)(2,1)S(1)}, bf16[2,512,256]{2,1,0:T(8,128)(2,1)S(1)}, u32[]{:S(2)}, u32[]{:S(2)}) collective-permute-start(bf16[2,512,256]{2,1,0:T(8,128)(2,1)S(1)} %get-tuple-element.42.rest_0_), channel_id=1, source_target_pairs={{0,16},{4,20},{8,24},{12,28},{16,0},{20,4},{24,8},{28,12},{1,17},{... | collective-permute-start | bytes 1572872 | tf_op jit(solution)/shard_map/ppermute | solution.py:222
  32.7 1.5 %collective-permute-start.6 = (bf16[2,512,256]{2,1,0:T(8,128)(2,1)S(1)}, bf16[2,512,256]{2,1,0:T(8,128)(2,1)S(1)}, u32[]{:S(2)}, u32[]{:S(2)}) collective-permute-start(bf16[2,512,256]{2,1,0:T(8,128)(2,1)S(1)} %get-tuple-element.42.rest_0_), channel_id=1, source_target_pairs={{0,8},{4,12},{8,0},{12,4},{16,24},{20,28},{24,16},{28,20},{1,9},{5... | collective-permute-start | bytes 1572872 | tf_op jit(solution)/shard_map/ppermute | solution.py:222
  34.2 4.5 %collective-permute-start.13 = (bf16[256,512]{1,0:T(8,128)(2,1)S(1)}, bf16[256,512]{1,0:T(8,128)(2,1)S(1)}, u32[]{:S(2)}, u32[]{:S(2)}) collective-permute-start(bf16[256,512]{1,0:T(8,128)(2,1)S(1)} %get-tuple-element.39), channel_id=1, source_target_pairs={{0,3},{1,2},{2,1},{3,0},{4,7},{5,6},{6,5},{7,4},{8,11},{9,10},{10,... | collective-permute-start | bytes 786440 | tf_op jit(solution)/shard_map/ppermute | solution.py:222
  38.8 5.8 %attend.2.refs_0_ = bf16[512,256]{1,0:T(8,128)(2,1)S(1)} custom-call(s32[8]{0:T(128)S(1)} %select_reduce_fusion.place_ref, s32[512,128]{1,0:T(8,128)S(1)} %get-tuple-element.30.first_ref, s32[512,128]{1,0:T(8,128)S(1)} %get-tuple-element.31.grp_ref, bf16[3,512,256]{2,1,0:T(8,128)(2,1)S(1)} %get-tuple-element.33.suf, ...), custom_call_target="tpu_custom_call" | custom-call | tf_op jit(solution)/shard_map/attend/pallas_call | solution.py:165
  45.3 1.6 %collective-permute-start.15 = (bf16[1,512,256]{2,1,0:T(8,128)(2,1)S(1)}, bf16[1,512,256]{2,1,0:T(8,128)(2,1)S(1)}, u32[]{:S(2)}, u32[]{:S(2)}) collective-permute-start(bf16[1,512,256]{2,1,0:T(8,128)(2,1)S(1)} %slice.41), channel_id=1, source_target_pairs={{0,8},{4,12},{8,0},{12,4},{16,24},{20,28},{24,16},{28,20},{1,9},{5... | collective-permute-start | bytes 786440 | tf_op jit(solution)/shard_map/ppermute | solution.py:222
  46.9 1.3 %collective-permute-start.14 = (bf16[1,512,256]{2,1,0:T(8,128)(2,1)S(1)}, bf16[1,512,256]{2,1,0:T(8,128)(2,1)S(1)}, u32[]{:S(2)}, u32[]{:S(2)}) collective-permute-start(bf16[1,512,256]{2,1,0:T(8,128)(2,1)S(1)} %slice.40), channel_id=1, source_target_pairs={{0,16},{4,20},{8,24},{12,28},{16,0},{20,4},{24,8},{28,12},{1,17},{... | collective-permute-start | bytes 786440 | tf_op jit(solution)/shard_map/ppermute | solution.py:222
  48.2 3.7 %collective-permute-start.16 = (bf16[512,256]{1,0:T(8,128)(2,1)S(1)}, bf16[512,256]{1,0:T(8,128)(2,1)S(1)}, u32[]{:S(2)}, u32[]{:S(2)}) collective-permute-start(bf16[512,256]{1,0:T(8,128)(2,1)S(1)} %attend.2.refs_0_), channel_id=1, source_target_pairs={{0,2},{1,3},{2,0},{3,1},{4,6},{5,7},{6,4},{7,5},{8,10},{9,11},{10,... | collective-permute-start | bytes 786440 | tf_op jit(solution)/shard_map/ppermute | solution.py:222
  52.8 1.6 %collective-permute-done.14.rest_3_ = bf16[1,512,256]{2,1,0:T(8,128)(2,1)S(1)} collective-permute-done((bf16[1,512,256]{2,1,0:T(8,128)(2,1)S(1)}, bf16[1,512,256]{2,1,0:T(8,128)(2,1)S(1)}, u32[]{:S(2)}, u32[]{:S(2)}) %collective-permute-start.14) | collective-permute-done | bytes 262176 | tf_op jit(solution)/shard_map/ppermute | solution.py:222
  54.9 7.3 %collective-permute-done.16.refs_2_ = bf16[512,256]{1,0:T(8,128)(2,1)S(1)} collective-permute-done((bf16[512,256]{1,0:T(8,128)(2,1)S(1)}, bf16[512,256]{1,0:T(8,128)(2,1)S(1)}, u32[]{:S(2)}, u32[]{:S(2)}) %collective-permute-start.16) | collective-permute-done | bytes 262176 | tf_op jit(solution)/shard_map/ppermute | solution.py:222
  63.8 2.5 %collective-permute-done.20.rest_8_ = bf16[1,512,256]{2,1,0:T(8,128)(2,1)S(1)} collective-permute-done((bf16[1,512,256]{2,1,0:T(8,128)(2,1)S(1)}, bf16[1,512,256]{2,1,0:T(8,128)(2,1)S(1)}, u32[]{:S(2)}, u32[]{:S(2)}) %collective-permute-start.20) | collective-permute-done | bytes 262176 | tf_op jit(solution)/shard_map/ppermute | solution.py:222
  67.9 1.5 %collective-permute-start.24 = (bf16[512,256]{1,0:T(8,128)(2,1)S(1)}, bf16[512,256]{1,0:T(8,128)(2,1)S(1)}, u32[]{:S(2)}, u32[]{:S(2)}) collective-permute-start(bf16[512,256]{1,0:T(8,128)(2,1)S(1)} %collective-permute-done.16.refs_2_), channel_id=1, source_target_pairs={{2,3},{1,0},{6,7},{5,4},{10,11},{9,8},{14,15},{13,12},{18,19},{17,... | collective-permute-start | bytes 786440 | tf_op jit(solution)/shard_map/ppermute | solution.py:238
  69.4 5.9 %attend.3.refs_0_ = bf16[512,256]{1,0:T(8,128)(2,1)S(1)} custom-call(s32[8]{0:T(128)S(1)} %select_reduce_fusion.place_ref, s32[512,128]{1,0:T(8,128)S(1)} %get-tuple-element.30.first_ref, s32[512,128]{1,0:T(8,128)S(1)} %get-tuple-element.31.grp_ref, bf16[3,512,256]{2,1,0:T(8,128)(2,1)S(1)} %get-tuple-element.32.suf, ...), custom_call_target="tpu_custom_call" | custom-call | tf_op jit(solution)/shard_map/attend/pallas_call | solution.py:165
  75.4 5.3 %collective-permute-done.24.refs_4_ = bf16[512,256]{1,0:T(8,128)(2,1)S(1)} collective-permute-done((bf16[512,256]{1,0:T(8,128)(2,1)S(1)}, bf16[512,256]{1,0:T(8,128)(2,1)S(1)}, u32[]{:S(2)}, u32[]{:S(2)}) %collective-permute-start.24) | collective-permute-done | bytes 262176 | tf_op jit(solution)/shard_map/ppermute | solution.py:238
  80.7 1.6 %collective-permute-start.26 = (bf16[512,256]{1,0:T(8,128)(2,1)S(1)}, bf16[512,256]{1,0:T(8,128)(2,1)S(1)}, u32[]{:S(2)}, u32[]{:S(2)}) collective-permute-start(bf16[512,256]{1,0:T(8,128)(2,1)S(1)} %attend.3.refs_0_), channel_id=1, source_target_pairs={{0,2},{1,3},{2,0},{3,1},{4,6},{5,7},{6,4},{7,5},{8,10},{9,11},{10,... | collective-permute-start | bytes 786440 | tf_op jit(solution)/shard_map/ppermute | solution.py:222
  82.3 2.5 %collective-permute-start.25 = (bf16[512,256]{1,0:T(8,128)(2,1)S(1)}, bf16[512,256]{1,0:T(8,128)(2,1)S(1)}, u32[]{:S(2)}, u32[]{:S(2)}) collective-permute-start(bf16[512,256]{1,0:T(8,128)(2,1)S(1)} %attend.3.refs_0_), channel_id=1, source_target_pairs={{0,1},{1,0},{2,3},{3,2},{4,5},{5,4},{6,7},{7,6},{8,9},{9,8},{10,11... | collective-permute-start | bytes 786440 | tf_op jit(solution)/shard_map/ppermute | solution.py:222
  84.8 10.0 %collective-permute-done.26.refs_2_ = bf16[512,256]{1,0:T(8,128)(2,1)S(1)} collective-permute-done((bf16[512,256]{1,0:T(8,128)(2,1)S(1)}, bf16[512,256]{1,0:T(8,128)(2,1)S(1)}, u32[]{:S(2)}, u32[]{:S(2)}) %collective-permute-start.26) | collective-permute-done | bytes 262176 | tf_op jit(solution)/shard_map/ppermute | solution.py:222
  95.5 1.3 %collective-permute-start.28 = (bf16[512,256]{1,0:T(8,128)(2,1)S(1)}, bf16[512,256]{1,0:T(8,128)(2,1)S(1)}, u32[]{:S(2)}, u32[]{:S(2)}) collective-permute-start(bf16[512,256]{1,0:T(8,128)(2,1)S(1)} %collective-permute-done.26.refs_2_), channel_id=1, source_target_pairs={{2,3},{1,0},{6,7},{5,4},{10,11},{9,8},{14,15},{13,12},{18,19},{17,... | collective-permute-start | bytes 786440 | tf_op jit(solution)/shard_map/ppermute | solution.py:238
  96.8 1.9 %project.2.refs_10_ = f32[512,1024]{1,0:T(8,128)S(1)} custom-call(s32[3]{0:T(128)S(1)} %pad_add_fusion.1.where_ref, bf16[512,256]{1,0:T(8,128)(2,1)S(1)} %attend.2.refs_0_, bf16[512,256]{1,0:T(8,128)(2,1)S(1)} %collective-permute-done.22.refs_1_, bf16[512,256]{1,0:T(8,128)(2,1)S(1)} %collective-permute-done.16.refs_2_, ...), custom_call_target="tpu_custom_call" | custom-call | tf_op jit(solution)/shard_map/project/pallas_call | solution.py:211
  98.7 5.6 %collective-permute-done.28.refs_4_ = bf16[512,256]{1,0:T(8,128)(2,1)S(1)} collective-permute-done((bf16[512,256]{1,0:T(8,128)(2,1)S(1)}, bf16[512,256]{1,0:T(8,128)(2,1)S(1)}, u32[]{:S(2)}, u32[]{:S(2)}) %collective-permute-start.28) | collective-permute-done | bytes 262176 | tf_op jit(solution)/shard_map/ppermute | solution.py:238
  104.4 2.9 %project.3 = bf16[512,1024]{1,0:T(8,128)(2,1)} custom-call(s32[3]{0:T(128)S(1)} %pad_add_fusion.1.where_ref, bf16[512,256]{1,0:T(8,128)(2,1)S(1)} %attend.3.refs_0_, bf16[512,256]{1,0:T(8,128)(2,1)S(1)} %collective-permute-done.25.refs_1_, bf16[512,256]{1,0:T(8,128)(2,1)S(1)} %collective-permute-done.26.refs_2_, ...), custom_call_target="tpu_custom_call" | custom-call | tf_op jit(solution)/shard_map/project/pallas_call | solution.py:211
  (60 shorter events, 9.5 us)
Async XLA Ops:
  1.5 11.9 %collective-permute-start = (bf16[2,512,256]{2,1,0:T(8,128)(2,1)S(1)}, bf16[2,512,256]{2,1,0:T(8,128)(2,1)S(1)}, u32[]{:S(2)}, u32[]{:S(2)}) collective-permute-start(bf16[2,512,256]{2,1,0:T(8,128)(2,1)S(1)} %get-tuple-element.60.rest_0_), channel_id=1, source_target_pairs={{0,4},{4,0},{8,12},{12,8},{16,20},{20,16},{24,28},{28,24},{1,5},{5... | collective-permute-start | bytes 1572872 | tf_op jit(solution)/shard_map/ppermute | solution.py:222
  2.0 15.1 %collective-permute-start.4 = (bf16[2,512,256]{2,1,0:T(8,128)(2,1)S(1)}, bf16[2,512,256]{2,1,0:T(8,128)(2,1)S(1)}, u32[]{:S(2)}, u32[]{:S(2)}) collective-permute-start(bf16[2,512,256]{2,1,0:T(8,128)(2,1)S(1)} %get-tuple-element.60.rest_0_), channel_id=1, source_target_pairs={{0,16},{4,20},{8,24},{12,28},{16,0},{20,4},{24,8},{28,12},{1,17},{... | collective-permute-start | bytes 1572872 | tf_op jit(solution)/shard_map/ppermute | solution.py:222
  4.6 18.7 %collective-permute-start.1 = (bf16[2,512,256]{2,1,0:T(8,128)(2,1)S(1)}, bf16[2,512,256]{2,1,0:T(8,128)(2,1)S(1)}, u32[]{:S(2)}, u32[]{:S(2)}) collective-permute-start(bf16[2,512,256]{2,1,0:T(8,128)(2,1)S(1)} %get-tuple-element.60.rest_0_), channel_id=1, source_target_pairs={{0,8},{4,12},{8,0},{12,4},{16,24},{20,28},{24,16},{28,20},{1,9},{5... | collective-permute-start | bytes 1572872 | tf_op jit(solution)/shard_map/ppermute | solution.py:222
  8.0 14.8 %collective-permute-start.2 = (bf16[256,512]{1,0:T(8,128)(2,1)}, bf16[256,512]{1,0:T(8,128)(2,1)S(1)}, u32[]{:S(2)}, u32[]{:S(2)}) collective-permute-start(bf16[256,512]{1,0:T(8,128)(2,1)} %get-tuple-element.54), channel_id=1, source_target_pairs={{0,2},{1,3},{2,0},{3,1},{4,6},{5,7},{6,4},{7,5},{8,10},{9,11},{10,... | collective-permute-start | bytes 786440 | tf_op jit(solution)/shard_map/ppermute | solution.py:222
  22.8 7.2 %collective-permute-start.5 = (bf16[1,512,256]{2,1,0:T(8,128)(2,1)S(1)}, bf16[1,512,256]{2,1,0:T(8,128)(2,1)S(1)}, u32[]{:S(2)}, u32[]{:S(2)}) collective-permute-start(bf16[1,512,256]{2,1,0:T(8,128)(2,1)S(1)} %slice.39), channel_id=1, source_target_pairs={{0,8},{4,12},{8,0},{12,4},{16,24},{20,28},{24,16},{28,20},{1,9},{5... | collective-permute-start | bytes 786440 | tf_op jit(solution)/shard_map/ppermute | solution.py:222
  23.4 7.0 %collective-permute-start.3 = (bf16[1,512,256]{2,1,0:T(8,128)(2,1)S(1)}, bf16[1,512,256]{2,1,0:T(8,128)(2,1)S(1)}, u32[]{:S(2)}, u32[]{:S(2)}) collective-permute-start(bf16[1,512,256]{2,1,0:T(8,128)(2,1)S(1)} %slice.38), channel_id=1, source_target_pairs={{0,16},{4,20},{8,24},{12,28},{16,0},{20,4},{24,8},{28,12},{1,17},{... | collective-permute-start | bytes 786440 | tf_op jit(solution)/shard_map/ppermute | solution.py:222
  23.9 7.0 %collective-permute-start.8 = (bf16[256,512]{1,0:T(8,128)(2,1)S(1)}, bf16[256,512]{1,0:T(8,128)(2,1)S(1)}, u32[]{:S(2)}, u32[]{:S(2)}) collective-permute-start(bf16[256,512]{1,0:T(8,128)(2,1)S(1)} %get-tuple-element.55), channel_id=1, source_target_pairs={{0,1},{1,0},{2,3},{3,2},{4,5},{5,4},{6,7},{7,6},{8,9},{9,8},{10,11... | collective-permute-start | bytes 786440 | tf_op jit(solution)/shard_map/ppermute | solution.py:222
  30.1 2.6 %collective-permute-start.12 = (bf16[1,512,256]{2,1,0:T(8,128)(2,1)S(1)}, bf16[1,512,256]{2,1,0:T(8,128)(2,1)S(1)}, u32[]{:S(2)}, u32[]{:S(2)}) collective-permute-start(bf16[1,512,256]{2,1,0:T(8,128)(2,1)S(1)} %collective-permute-done.5.rest_4_), channel_id=1, source_target_pairs={{0,4},{4,0},{8,12},{12,8},{16,20},{20,16},{24,28},{28,24},{1,5},{5... | collective-permute-start | bytes 786440 | tf_op jit(solution)/shard_map/ppermute | solution.py:222
  30.4 3.8 %collective-permute-start.11 = (bf16[1,512,256]{2,1,0:T(8,128)(2,1)S(1)}, bf16[1,512,256]{2,1,0:T(8,128)(2,1)S(1)}, u32[]{:S(2)}, u32[]{:S(2)}) collective-permute-start(bf16[1,512,256]{2,1,0:T(8,128)(2,1)S(1)} %collective-permute-done.3.rest_3_), channel_id=1, source_target_pairs={{0,4},{4,0},{8,12},{12,8},{16,20},{20,16},{24,28},{28,24},{1,5},{5... | collective-permute-start | bytes 786440 | tf_op jit(solution)/shard_map/ppermute | solution.py:222
  30.9 7.9 %collective-permute-start.10 = (bf16[2,512,256]{2,1,0:T(8,128)(2,1)S(1)}, bf16[2,512,256]{2,1,0:T(8,128)(2,1)S(1)}, u32[]{:S(2)}, u32[]{:S(2)}) collective-permute-start(bf16[2,512,256]{2,1,0:T(8,128)(2,1)S(1)} %collective-permute-done.4.rest_2_), channel_id=1, source_target_pairs={{0,4},{4,0},{8,12},{12,8},{16,20},{20,16},{24,28},{28,24},{1,5},{5... | collective-permute-start | bytes 1572872 | tf_op jit(solution)/shard_map/ppermute | solution.py:222
  30.9 7.8 %collective-permute-start.9 = (bf16[2,512,256]{2,1,0:T(8,128)(2,1)S(1)}, bf16[2,512,256]{2,1,0:T(8,128)(2,1)S(1)}, u32[]{:S(2)}, u32[]{:S(2)}) collective-permute-start(bf16[2,512,256]{2,1,0:T(8,128)(2,1)S(1)} %collective-permute-done.1.rest_1_), channel_id=1, source_target_pairs={{0,4},{4,0},{8,12},{12,8},{16,20},{20,16},{24,28},{28,24},{1,5},{5... | collective-permute-start | bytes 1572872 | tf_op jit(solution)/shard_map/ppermute | solution.py:222
  31.4 13.9 %collective-permute-start.7 = (bf16[2,512,256]{2,1,0:T(8,128)(2,1)S(1)}, bf16[2,512,256]{2,1,0:T(8,128)(2,1)S(1)}, u32[]{:S(2)}, u32[]{:S(2)}) collective-permute-start(bf16[2,512,256]{2,1,0:T(8,128)(2,1)S(1)} %get-tuple-element.42.rest_0_), channel_id=1, source_target_pairs={{0,16},{4,20},{8,24},{12,28},{16,0},{20,4},{24,8},{28,12},{1,17},{... | collective-permute-start | bytes 1572872 | tf_op jit(solution)/shard_map/ppermute | solution.py:222
  32.7 14.2 %collective-permute-start.6 = (bf16[2,512,256]{2,1,0:T(8,128)(2,1)S(1)}, bf16[2,512,256]{2,1,0:T(8,128)(2,1)S(1)}, u32[]{:S(2)}, u32[]{:S(2)}) collective-permute-start(bf16[2,512,256]{2,1,0:T(8,128)(2,1)S(1)} %get-tuple-element.42.rest_0_), channel_id=1, source_target_pairs={{0,8},{4,12},{8,0},{12,4},{16,24},{20,28},{24,16},{28,20},{1,9},{5... | collective-permute-start | bytes 1572872 | tf_op jit(solution)/shard_map/ppermute | solution.py:222
  34.2 11.1 %collective-permute-start.13 = (bf16[256,512]{1,0:T(8,128)(2,1)S(1)}, bf16[256,512]{1,0:T(8,128)(2,1)S(1)}, u32[]{:S(2)}, u32[]{:S(2)}) collective-permute-start(bf16[256,512]{1,0:T(8,128)(2,1)S(1)} %get-tuple-element.39), channel_id=1, source_target_pairs={{0,3},{1,2},{2,1},{3,0},{4,7},{5,6},{6,5},{7,4},{8,11},{9,10},{10,... | collective-permute-start | bytes 786440 | tf_op jit(solution)/shard_map/ppermute | solution.py:222
  45.3 7.5 %collective-permute-start.15 = (bf16[1,512,256]{2,1,0:T(8,128)(2,1)S(1)}, bf16[1,512,256]{2,1,0:T(8,128)(2,1)S(1)}, u32[]{:S(2)}, u32[]{:S(2)}) collective-permute-start(bf16[1,512,256]{2,1,0:T(8,128)(2,1)S(1)} %slice.41), channel_id=1, source_target_pairs={{0,8},{4,12},{8,0},{12,4},{16,24},{20,28},{24,16},{28,20},{1,9},{5... | collective-permute-start | bytes 786440 | tf_op jit(solution)/shard_map/ppermute | solution.py:222
  46.9 7.4 %collective-permute-start.14 = (bf16[1,512,256]{2,1,0:T(8,128)(2,1)S(1)}, bf16[1,512,256]{2,1,0:T(8,128)(2,1)S(1)}, u32[]{:S(2)}, u32[]{:S(2)}) collective-permute-start(bf16[1,512,256]{2,1,0:T(8,128)(2,1)S(1)} %slice.40), channel_id=1, source_target_pairs={{0,16},{4,20},{8,24},{12,28},{16,0},{20,4},{24,8},{28,12},{1,17},{... | collective-permute-start | bytes 786440 | tf_op jit(solution)/shard_map/ppermute | solution.py:222
  48.2 13.9 %collective-permute-start.16 = (bf16[512,256]{1,0:T(8,128)(2,1)S(1)}, bf16[512,256]{1,0:T(8,128)(2,1)S(1)}, u32[]{:S(2)}, u32[]{:S(2)}) collective-permute-start(bf16[512,256]{1,0:T(8,128)(2,1)S(1)} %attend.2.refs_0_), channel_id=1, source_target_pairs={{0,2},{1,3},{2,0},{3,1},{4,6},{5,7},{6,4},{7,5},{8,10},{9,11},{10,... | collective-permute-start | bytes 786440 | tf_op jit(solution)/shard_map/ppermute | solution.py:222
  54.3 20.9 %collective-permute-start.29 = (bf16[3,256,512]{2,1,0:T(8,128)(2,1)S(1)}, bf16[3,256,512]{2,1,0:T(8,128)(2,1)S(1)}, u32[]{:S(2)}, u32[]{:S(2)}) collective-permute-start(bf16[3,256,512]{2,1,0:T(8,128)(2,1)S(1)} %pad_maximum_fusion.refs_6_), channel_id=1, source_target_pairs={{0,8},{4,12},{8,0},{12,4},{16,24},{20,28},{24,16},{28,20},{1,9},{5... | collective-permute-start | bytes 2359304 | tf_op jit(solution)/shard_map/ppermute | solution.py:222
  62.2 1.5 %collective-permute-start.21 = (bf16[1,512,256]{2,1,0:T(8,128)(2,1)S(1)}, bf16[1,512,256]{2,1,0:T(8,128)(2,1)S(1)}, u32[]{:S(2)}, u32[]{:S(2)}) collective-permute-start(bf16[1,512,256]{2,1,0:T(8,128)(2,1)S(1)} %collective-permute-done.15.rest_4_), channel_id=1, source_target_pairs={{0,4},{4,0},{8,12},{12,8},{16,20},{20,16},{24,28},{28,24},{1,5},{5... | collective-permute-start | bytes 786440 | tf_op jit(solution)/shard_map/ppermute | solution.py:222
  62.2 4.3 %collective-permute-start.19 = (bf16[2,512,256]{2,1,0:T(8,128)(2,1)S(1)}, bf16[2,512,256]{2,1,0:T(8,128)(2,1)S(1)}, u32[]{:S(2)}, u32[]{:S(2)}) collective-permute-start(bf16[2,512,256]{2,1,0:T(8,128)(2,1)S(1)} %collective-permute-done.7.rest_2_), channel_id=1, source_target_pairs={{0,4},{4,0},{8,12},{12,8},{16,20},{20,16},{24,28},{28,24},{1,5},{5... | collective-permute-start | bytes 1572872 | tf_op jit(solution)/shard_map/ppermute | solution.py:222
  62.7 4.5 %collective-permute-start.18 = (bf16[2,512,256]{2,1,0:T(8,128)(2,1)S(1)}, bf16[2,512,256]{2,1,0:T(8,128)(2,1)S(1)}, u32[]{:S(2)}, u32[]{:S(2)}) collective-permute-start(bf16[2,512,256]{2,1,0:T(8,128)(2,1)S(1)} %collective-permute-done.6.rest_1_), channel_id=1, source_target_pairs={{0,4},{4,0},{8,12},{12,8},{16,20},{20,16},{24,28},{28,24},{1,5},{5... | collective-permute-start | bytes 1572872 | tf_op jit(solution)/shard_map/ppermute | solution.py:222
  62.7 5.2 %collective-permute-start.17 = (bf16[2,512,256]{2,1,0:T(8,128)(2,1)S(1)}, bf16[2,512,256]{2,1,0:T(8,128)(2,1)S(1)}, u32[]{:S(2)}, u32[]{:S(2)}) collective-permute-start(bf16[2,512,256]{2,1,0:T(8,128)(2,1)S(1)} %get-tuple-element.42.rest_0_), channel_id=1, source_target_pairs={{0,4},{4,0},{8,12},{12,8},{16,20},{20,16},{24,28},{28,24},{1,5},{5... | collective-permute-start | bytes 1572872 | tf_op jit(solution)/shard_map/ppermute | solution.py:222
  63.7 2.6 %collective-permute-start.20 = (bf16[1,512,256]{2,1,0:T(8,128)(2,1)S(1)}, bf16[1,512,256]{2,1,0:T(8,128)(2,1)S(1)}, u32[]{:S(2)}, u32[]{:S(2)}) collective-permute-start(bf16[1,512,256]{2,1,0:T(8,128)(2,1)S(1)} %collective-permute-done.14.rest_3_), channel_id=1, source_target_pairs={{0,4},{4,0},{8,12},{12,8},{16,20},{20,16},{24,28},{28,24},{1,5},{5... | collective-permute-start | bytes 786440 | tf_op jit(solution)/shard_map/ppermute | solution.py:222
  66.3 30.5 %collective-permute-start.30 = (bf16[3,256,512]{2,1,0:T(8,128)(2,1)S(1)}, bf16[3,256,512]{2,1,0:T(8,128)(2,1)S(1)}, u32[]{:S(2)}, u32[]{:S(2)}) collective-permute-start(bf16[3,256,512]{2,1,0:T(8,128)(2,1)S(1)} %pad_maximum_fusion.refs_6_), channel_id=1, source_target_pairs={{0,4},{4,0},{8,12},{12,8},{16,20},{20,16},{24,28},{28,24},{1,5},{5... | collective-permute-start | bytes 2359304 | tf_op jit(solution)/shard_map/ppermute | solution.py:222
  66.5 8.9 %collective-permute-start.22 = (bf16[512,256]{1,0:T(8,128)(2,1)S(1)}, bf16[512,256]{1,0:T(8,128)(2,1)S(1)}, u32[]{:S(2)}, u32[]{:S(2)}) collective-permute-start(bf16[512,256]{1,0:T(8,128)(2,1)S(1)} %attend.2.refs_0_), channel_id=1, source_target_pairs={{0,1},{1,0},{2,3},{3,2},{4,5},{5,4},{6,7},{7,6},{8,9},{9,8},{10,11... | collective-permute-start | bytes 786440 | tf_op jit(solution)/shard_map/ppermute | solution.py:222
  67.2 8.2 %collective-permute-start.23 = (bf16[512,256]{1,0:T(8,128)(2,1)S(1)}, bf16[512,256]{1,0:T(8,128)(2,1)S(1)}, u32[]{:S(2)}, u32[]{:S(2)}) collective-permute-start(bf16[512,256]{1,0:T(8,128)(2,1)S(1)} %attend.2.refs_0_), channel_id=1, source_target_pairs={{1,2},{2,1},{5,6},{6,5},{9,10},{10,9},{13,14},{14,13},{17,18},{18,... | collective-permute-start | bytes 786440 | tf_op jit(solution)/shard_map/ppermute | solution.py:237
  67.9 12.8 %collective-permute-start.24 = (bf16[512,256]{1,0:T(8,128)(2,1)S(1)}, bf16[512,256]{1,0:T(8,128)(2,1)S(1)}, u32[]{:S(2)}, u32[]{:S(2)}) collective-permute-start(bf16[512,256]{1,0:T(8,128)(2,1)S(1)} %collective-permute-done.16.refs_2_), channel_id=1, source_target_pairs={{2,3},{1,0},{6,7},{5,4},{10,11},{9,8},{14,15},{13,12},{18,19},{17,... | collective-permute-start | bytes 786440 | tf_op jit(solution)/shard_map/ppermute | solution.py:238
  75.2 21.6 %collective-permute-start.31 = (bf16[3,256,512]{2,1,0:T(8,128)(2,1)S(1)}, bf16[3,256,512]{2,1,0:T(8,128)(2,1)S(1)}, u32[]{:S(2)}, u32[]{:S(2)}) collective-permute-start(bf16[3,256,512]{2,1,0:T(8,128)(2,1)S(1)} %collective-permute-done.29.refs_7_), channel_id=1, source_target_pairs={{0,4},{4,0},{8,12},{12,8},{16,20},{20,16},{24,28},{28,24},{1,5},{5... | collective-permute-start | bytes 2359304 | tf_op jit(solution)/shard_map/ppermute | solution.py:222
  80.7 14.1 %collective-permute-start.26 = (bf16[512,256]{1,0:T(8,128)(2,1)S(1)}, bf16[512,256]{1,0:T(8,128)(2,1)S(1)}, u32[]{:S(2)}, u32[]{:S(2)}) collective-permute-start(bf16[512,256]{1,0:T(8,128)(2,1)S(1)} %attend.3.refs_0_), channel_id=1, source_target_pairs={{0,2},{1,3},{2,0},{3,1},{4,6},{5,7},{6,4},{7,5},{8,10},{9,11},{10,... | collective-permute-start | bytes 786440 | tf_op jit(solution)/shard_map/ppermute | solution.py:222
  82.3 16.4 %collective-permute-start.25 = (bf16[512,256]{1,0:T(8,128)(2,1)S(1)}, bf16[512,256]{1,0:T(8,128)(2,1)S(1)}, u32[]{:S(2)}, u32[]{:S(2)}) collective-permute-start(bf16[512,256]{1,0:T(8,128)(2,1)S(1)} %attend.3.refs_0_), channel_id=1, source_target_pairs={{0,1},{1,0},{2,3},{3,2},{4,5},{5,4},{6,7},{7,6},{8,9},{9,8},{10,11... | collective-permute-start | bytes 786440 | tf_op jit(solution)/shard_map/ppermute | solution.py:222
  94.8 4.0 %collective-permute-start.27 = (bf16[512,256]{1,0:T(8,128)(2,1)S(1)}, bf16[512,256]{1,0:T(8,128)(2,1)S(1)}, u32[]{:S(2)}, u32[]{:S(2)}) collective-permute-start(bf16[512,256]{1,0:T(8,128)(2,1)S(1)} %attend.3.refs_0_), channel_id=1, source_target_pairs={{1,2},{2,1},{5,6},{6,5},{9,10},{10,9},{13,14},{14,13},{17,18},{18,... | collective-permute-start | bytes 786440 | tf_op jit(solution)/shard_map/ppermute | solution.py:237
  95.5 8.9 %collective-permute-start.28 = (bf16[512,256]{1,0:T(8,128)(2,1)S(1)}, bf16[512,256]{1,0:T(8,128)(2,1)S(1)}, u32[]{:S(2)}, u32[]{:S(2)}) collective-permute-start(bf16[512,256]{1,0:T(8,128)(2,1)S(1)} %collective-permute-done.26.refs_2_), channel_id=1, source_target_pairs={{2,3},{1,0},{6,7},{5,4},{10,11},{9,8},{14,15},{13,12},{18,19},{17,... | collective-permute-start | bytes 786440 | tf_op jit(solution)/shard_map/ppermute | solution.py:238
  (4 other events, 66.4 us)

commit v7 on v6

--- a/solution.py
+++ b/solution.py
@@ -178,44 +178,42 @@
 
 def proj_kernel(head, where_ref, *refs):
     att = refs[:5]
-    own = refs[5]
-    far = refs[6:10]
-    add_ref = refs[10] if len(refs) == 12 else None
+    own, near, other = refs[5:8]
+    add_ref = refs[8] if len(refs) == 10 else None
     o_ref = refs[-1]
-    cols = o_ref.shape[1] // 2
+    cols = o_ref.shape[1] // 4
     rows = o_ref.shape[0]
-    mine = where_ref[1] == head
-    side = where_ref[2]
-    tall = 256
-    for x in range(2):
-        c0 = pl.multiple_of(lax.bitwise_xor(side, x) * cols, cols)
-        w = [own[head * HD : (head + 1) * HD, pl.ds(c0, cols)]]
-        w += [jnp.where(mine, far[x][m], far[2 + x][m]) for m in range(3)]
-        for r0 in range(0, rows, tall):
-            at = slice(r0, r0 + tall)
-            acc = jnp.dot(att[0][at, :], w[0], preferred_element_type=jnp.float32)
-            for m in range(1, 4):
-                a = att[m][at, :]
-                if m == 3:
-                    a = a + att[4][at, :]
-                acc = acc + jnp.dot(a, w[m], preferred_element_type=jnp.float32)
-            if add_ref is not None:
-                acc = acc + add_ref[at, pl.ds(c0, cols)]
-            o_ref[at, pl.ds(c0, cols)] = acc.astype(o_ref.dtype)
-
-
-def project(head, where, att, own, far, add=None):
+    mine = where_ref[0] == head
+    for x in range(4):
+        c0 = pl.multiple_of(lax.bitwise_xor(where_ref[1], x) * cols, cols)
+        acc = jnp.dot(
+            att[0][...],
+            own[head * HD : (head + 1) * HD, pl.ds(c0, cols)],
+            preferred_element_type=jnp.float32,
+        )
+        for m in range(1, 4):
+            w = jnp.where(mine, near[3 * x + m - 1], other[3 * x + m - 1])
+            a = att[m][...]
+            if m == 3:
+                a = a + att[4][...]
+            acc = acc + jnp.dot(a, w, preferred_element_type=jnp.float32)
+        if add_ref is not None:
+            acc = acc + add_ref[:, pl.ds(c0, cols)]
+        o_ref[:, pl.ds(c0, cols)] = acc.astype(o_ref.dtype)
+
+
+def project(head, where, att, own, near, other, add=None):
     rows = att[0].shape[0]
     cols = own.shape[1]
     extra = [] if add is None else [add]
     return pl.pallas_call(
         functools.partial(proj_kernel, head),
         out_shape=jax.ShapeDtypeStruct((rows, cols), jnp.float32 if add is None else jnp.bfloat16),
-        in_specs=[SMEM] + [VMEM] * (len(att) + 1 + len(far) + len(extra)),
+        in_specs=[SMEM] + [VMEM] * (len(att) + 3 + len(extra)),
         out_specs=VMEM,
         compiler_params=pltpu.CompilerParams(vmem_limit_bytes=6 << 20),
         name="project",
-    )(where, *att, own, *far, *extra)
+    )(where, *att, own, near, other, *extra)
 
 
 def swap(x, axis, mask, size):
@@ -234,7 +232,7 @@
 def over_tp(a):
     two = swap(a, "tp", 2, 4)
     one = swap(a, "tp", 1, 4)
-    three = lax.ppermute(after(a, two), "tp", [(1, 2), (2, 1)])
+    three = lax.ppermute(a, "tp", [(1, 2), (2, 1)])
     forward = lax.ppermute(two, "tp", [(2, 3), (1, 0)])
     return [a, one, two, three, forward]
 
@@ -247,8 +245,8 @@
     me = lax.axis_index("req")
     z = lax.axis_index("tp")
     core = me & 1
-    side = (me >> 1) & 1
-    where = jnp.stack([z, core, side]).astype(jnp.int32)
+    chip = me >> 1
+    where = jnp.stack([core, chip]).astype(jnp.int32)
     place = jnp.sum(
         jnp.where(
             owners[None] == (me ^ jnp.arange(SLOTS, dtype=jnp.int32))[:, None, None],
@@ -260,53 +258,56 @@
     tp_size = 4
 
     cols = out_weight.shape[1] // tp_size
-    z_u, core_u, side_u = (i.astype(jnp.uint32) for i in (z, core, side))
+    z_u, core_u, chip_u = (i.astype(jnp.uint32) for i in (z, core, chip))
     starts = [core_u * HD, z_u * cols]
-    starts += [(z_u ^ m) * cols + side_u * (cols // 2) for m in range(1, tp_size)]
+    starts += [(z_u ^ m) * cols + chip_u * (cols // 4) for m in range(1, tp_size)]
     prefix = jnp.swapaxes(prefix_cache, 0, 1)
+    kv0, *starts = lax.optimization_barrier((prefix[:, :, :HD], *starts))
     sends = [
-        lax.dynamic_slice(out_weight, (starts[0], starts[1 + m]), (HD, cols // 2))
+        lax.dynamic_slice(out_weight, (starts[0], starts[1 + m]), (HD, cols // 4))
         for m in range(1, tp_size)
     ]
     w_own = lax.dynamic_slice(
         out_weight, (jnp.zeros_like(starts[0]), starts[1]), (out_weight.shape[0], cols)
     )
 
-    kv0 = prefix[:, :, :HD]
     kvx0 = over_x(kv0)
     kvy0 = over_y(kv0)
-    w_one, w_two = (swap(sends[m - 1], "tp", m, tp_size) for m in (1, 2))
+    kvc0 = over_core(kv0)
+    w_one, w_two, w_three = (
+        swap(after(sends[m - 1], kvc0), "tp", m, tp_size) for m in range(1, tp_size)
+    )
     table = jnp.concatenate([lengths, groups], axis=0)
-    kvc0 = over_core(kv0)
     first, grp, suf0, suf1 = prepare(
         after(table, kvc0), suffix_heads[:, 0], suffix_heads[:, 1], suffix_heads[:, 2]
     )
-    kxy0 = over_y(after(kvx0[0:1], suf0, w_own, w_two))
-    vyx0 = over_x(after(kvy0[1:2], suf0, w_own, w_two))
-    kv1 = after(prefix[:, :, HD:], kxy0, vyx0)
+    kxy0 = over_y(after(kvx0[0:1], suf0, w_one, w_two))
+    vyx0 = over_x(after(kvy0[1:2], suf0, w_one, w_two))
+    kv1 = after(prefix[:, :, HD:], kxy0, vyx0, w_own)
     kvx1 = over_x(kv1)
     kvy1 = over_y(kv1)
     pieces0 = [kv0, kvx0, kvy0, kxy0, vyx0]
-    pieces0 += [kvc0] + [over_core(after(p, w_one)) for p in pieces0[1:3]]
+    pieces0 += [kvc0] + [over_core(after(p, suf0)) for p in pieces0[1:3]]
     pieces0 += [over_core(p) for p in pieces0[3:5]]
-    att0 = attend(place, first, grp, suf0, pieces0, WHERE_K, WHERE_V)
-
-    w_three = swap(after(sends[2], w_two), "tp", 3, tp_size)
-    kxy1 = over_y(after(kvx1[0:1], att0, w_three))
-    vyx1 = over_x(after(kvy1[1:2], att0, w_three))
+    att0 = attend(after(place, w_three), first, grp, suf0, pieces0, WHERE_K, WHERE_V)
+
+    kxy1 = over_y(after(kvx1[0:1], att0))
+    vyx1 = over_x(after(kvy1[1:2], att0))
     pieces1 = [kv1, kvx1, kvy1, kxy1, vyx1]
     spread0 = over_tp(att0)
-    pieces1 += [over_core(after(p, spread0[2])) for p in pieces1]
+    pieces1 += [over_core(p) for p in pieces1[:3]]
+    pieces1 += [over_core(after(p, *spread0[1:4])) for p in pieces1[3:5]]
     att1 = attend(place, first, grp, suf1, pieces1, WHERE_K, WHERE_V)
 
     w_far = jnp.stack([after(w_one, att0), w_two, w_three])
-    w_core = over_core(w_far)
     w_x = over_x(after(w_far, kxy1, vyx1))
-    spread1 = over_tp(after(att1, *spread0[1:]))
-    w_core_x = over_core(after(w_x, att1))
-    far = [w_far, w_x, w_core, w_core_x]
-    half = project(0, where, spread0, w_own, far)
-    return project(1, where, spread1, w_own, far, half)
+    w_y = over_y(after(w_far, kxy1, vyx1))
+    w_xy = over_y(w_x)
+    w_chips = jnp.concatenate([w_far, w_x, w_y, w_xy])
+    spread1 = over_tp(att1)
+    w_core = over_core(after(w_chips, *spread1[1:4]))
+    half = project(0, where, spread0, w_own, w_chips, w_core)
+    return project(1, where, spread1, w_own, w_chips, w_core, half)
 
 
 def whole_heads(suffix_heads, prefix_cache, lengths, groups, owners, out_weight):

time: 108 us -> 126 us (1.17)
  waiting for transfers between devices: 48.1 us -> 65.7 us
  starting transfers between devices: 34.5 us -> 35.8 us
    ppermute x28 -> x29, waiting for transfers between devices: 37.2 us -> 52.2 us  [swap(): return lax.ppermute(x, axis, [(i, i ^ mask) for i in range(size)])]
    ppermute x2, waiting for transfers between devices: 10.9 us -> 13.6 us  [over_tp(): forward = lax.ppermute(two, 'tp', [(2, 3), (1, 0)])]
    ppermute x28 -> x29, starting transfers between devices: 30.4 us -> 31.7 us  [swap(): return lax.ppermute(x, axis, [(i, i ^ mask) for i in range(size)])]
    squeeze x1, local copies, waits for them, and re-layouts: 1.46 us -> 0.1 us  [split_heads(): suffix_heads[:, 2]]
  transfers between devices with their start and end apart: 32 -> 33, of which waited for: 14 -> 14; matrix products, arithmetic and copies ran while one was open for 5% -> 3% of each run, Pallas kernels for 14% -> 12%
where the time goes in v7:
time: 126 us
  waiting for transfers between devices  65.7 us (52%)
  starting transfers between devices  35.8 us (28%)
  Pallas kernels  18.2 us (14%)
  local copies, waits for them, and re-layouts  5.79 us (5%)
    ppermute x29, waiting for transfers between devices, swap(): return lax.ppermute(x, axis, [(i, i ^ mask) for i in range(size)])  52.2 us
    ppermute x29, starting transfers between devices, swap(): return lax.ppermute(x, axis, [(i, i ^ mask) for i in range(size)])  31.7 us
    ppermute x2, waiting for transfers between devices, over_tp(): forward = lax.ppermute(two, 'tp', [(2, 3), (1, 0)])  13.6 us
    pallas_call x2, Pallas kernels, attend(): pl.pallas_call(functools.partial(attend_kernel, where_k, where_v), out_sh...  11.8 us
    pallas_call x2, Pallas kernels, project(): pl.pallas_call(functools.partial(proj_kernel, head), out_shape=jax.ShapeD...  4.84 us
    ppermute x2, starting transfers between devices, over_tp(): forward = lax.ppermute(two, 'tp', [(2, 3), (1, 0)])  2.57 us
  transfers between devices with their start and end apart: 33, of which 14 were waited for; matrix products, arithmetic and copies ran while one was open for 3% of the time, Pallas kernels for 12%

profile of v7, /device:TPU:0, one launch (start us, length us, event | category | flops | bytes accessed | tf_op | source)
XLA Modules:
  0.0 126.2 jit_solution(3893356737200570235)
XLA Ops:
  0.0 1.4 %copy.12 = bf16[512,2,512]{2,0,1:T(8,128)(2,1)S(1)} copy(bf16[512,2,512]{2,1,0:T(2,128)(2,1)} %param.8) | data formatting | bytes 2097152 | tf_op args[1]
  2.0 2.6 %collective-permute-start.1 = (bf16[2,512,256]{2,1,0:T(8,128)(2,1)S(1)}, bf16[2,512,256]{2,1,0:T(8,128)(2,1)S(1)}, u32[]{:S(2)}, u32[]{:S(2)}) collective-permute-start(bf16[2,512,256]{2,1,0:T(8,128)(2,1)S(1)} %get-tuple-element.32.rest_0_), channel_id=1, source_target_pairs={{0,8},{4,12},{8,0},{12,4},{16,24},{20,28},{24,16},{28,20},{1,9},{5... | collective-permute-start | bytes 1572872 | tf_op jit(solution)/shard_map/ppermute | solution.py:220
  4.6 1.5 %collective-permute-start.5 = (bf16[2,512,256]{2,1,0:T(8,128)(2,1)S(1)}, bf16[2,512,256]{2,1,0:T(8,128)(2,1)S(1)}, u32[]{:S(2)}, u32[]{:S(2)}) collective-permute-start(bf16[2,512,256]{2,1,0:T(8,128)(2,1)S(1)} %get-tuple-element.32.rest_0_), channel_id=1, source_target_pairs={{0,16},{4,20},{8,24},{12,28},{16,0},{20,4},{24,8},{28,12},{1,17},{... | collective-permute-start | bytes 1572872 | tf_op jit(solution)/shard_map/ppermute | solution.py:220
  7.0 1.6 %prepare.1 = (s32[512,128]{1,0:T(8,128)S(1)}, s32[512,128]{1,0:T(8,128)S(1)}, bf16[3,512,256]{2,1,0:T(8,128)(2,1)S(1)}, bf16[3,512,256]{2,1,0:T(8,128)(2,1)S(1)}) custom-call(s32[2,8]{1,0:T(2,128)S(1)} %pad_add_fusion.table_ref, bf16[512,512]{1,0:T(8,128)(2,1)S(1)} %get-tuple-element.63.q_ref, bf16[512,512]{1,0:T(8,128)(2,1)S(1)} %get-tuple-element.64.k_ref, ...), custom_call_target="tpu_custom_call" | custom-call | tf_op jit(solution)/shard_map/prepare/pallas_call | solution.py:86
  8.6 8.5 %collective-permute-done.1.rest_1_ = bf16[2,512,256]{2,1,0:T(8,128)(2,1)S(1)} collective-permute-done((bf16[2,512,256]{2,1,0:T(8,128)(2,1)S(1)}, bf16[2,512,256]{2,1,0:T(8,128)(2,1)S(1)}, u32[]{:S(2)}, u32[]{:S(2)}) %collective-permute-start.1) | collective-permute-done | bytes 524320 | tf_op jit(solution)/shard_map/ppermute | solution.py:220
  17.1 1.4 %fusion = (bf16[256,256]{1,0:T(8,128)(2,1)S(1)}, bf16[256,256]{1,0:T(8,128)(2,1)S(1)}, bf16[256,256]{1,0:T(8,128)(2,1)S(1)}) fusion(bf16[512,4096]{1,0:T(8,128)(2,1)} %param.12, u32[]{:T(128)S(6)} %mul.20, u32[]{:T(128)S(6)} %add.17, u32[]{:T(128)S(6)} %add.16, u32[]{:T(128)S(6)} %add.15), kind=kLoop, calls=%fused_computation.17 | loop fusion | bytes 786448 | tf_op jit(solution)/shard_map/dynamic_slice | solution.py:267
  18.5 2.9 %collective-permute-start.3 = (bf16[256,256]{1,0:T(8,128)(2,1)S(1)}, bf16[256,256]{1,0:T(8,128)(2,1)S(1)}, u32[]{:S(2)}, u32[]{:S(2)}) collective-permute-start(bf16[256,256]{1,0:T(8,128)(2,1)S(1)} %get-tuple-element.42), channel_id=1, source_target_pairs={{0,2},{1,3},{2,0},{3,1},{4,6},{5,7},{6,4},{7,5},{8,10},{9,11},{10,... | collective-permute-start | bytes 393224 | tf_op jit(solution)/shard_map/ppermute | solution.py:220
  21.4 1.6 %collective-permute-start.2 = (bf16[256,256]{1,0:T(8,128)(2,1)S(1)}, bf16[256,256]{1,0:T(8,128)(2,1)S(1)}, u32[]{:S(2)}, u32[]{:S(2)}) collective-permute-start(bf16[256,256]{1,0:T(8,128)(2,1)S(1)} %get-tuple-element.40), channel_id=1, source_target_pairs={{0,1},{1,0},{2,3},{3,2},{4,5},{5,4},{6,7},{7,6},{8,9},{9,8},{10,11... | collective-permute-start | bytes 393224 | tf_op jit(solution)/shard_map/ppermute | solution.py:220
  23.0 5.4 %collective-permute-done.3 = bf16[256,256]{1,0:T(8,128)(2,1)S(1)} collective-permute-done((bf16[256,256]{1,0:T(8,128)(2,1)S(1)}, bf16[256,256]{1,0:T(8,128)(2,1)S(1)}, u32[]{:S(2)}, u32[]{:S(2)}) %collective-permute-start.3) | collective-permute-done | bytes 131104 | tf_op jit(solution)/shard_map/ppermute | solution.py:220
  28.7 1.5 %collective-permute-start.6 = (bf16[1,512,256]{2,1,0:T(8,128)(2,1)S(1)}, bf16[1,512,256]{2,1,0:T(8,128)(2,1)S(1)}, u32[]{:S(2)}, u32[]{:S(2)}) collective-permute-start(bf16[1,512,256]{2,1,0:T(8,128)(2,1)S(1)} %slice.39), channel_id=1, source_target_pairs={{0,8},{4,12},{8,0},{12,4},{16,24},{20,28},{24,16},{28,20},{1,9},{5... | collective-permute-start | bytes 786440 | tf_op jit(solution)/shard_map/ppermute | solution.py:220
  30.2 1.5 %collective-permute-start.4 = (bf16[1,512,256]{2,1,0:T(8,128)(2,1)S(1)}, bf16[1,512,256]{2,1,0:T(8,128)(2,1)S(1)}, u32[]{:S(2)}, u32[]{:S(2)}) collective-permute-start(bf16[1,512,256]{2,1,0:T(8,128)(2,1)S(1)} %slice.38), channel_id=1, source_target_pairs={{0,16},{4,20},{8,24},{12,28},{16,0},{20,4},{24,8},{28,12},{1,17},{... | collective-permute-start | bytes 786440 | tf_op jit(solution)/shard_map/ppermute | solution.py:220
  31.7 3.2 %collective-permute-start.9 = (bf16[256,256]{1,0:T(8,128)(2,1)S(1)}, bf16[256,256]{1,0:T(8,128)(2,1)S(1)}, u32[]{:S(2)}, u32[]{:S(2)}) collective-permute-start(bf16[256,256]{1,0:T(8,128)(2,1)S(1)} %get-tuple-element.48), channel_id=1, source_target_pairs={{0,3},{1,2},{2,1},{3,0},{4,7},{5,6},{6,5},{7,4},{8,11},{9,10},{10,... | collective-permute-start | bytes 393224 | tf_op jit(solution)/shard_map/ppermute | solution.py:220
  34.9 1.9 %constant_dynamic-slice_fusion.refs_5_ = bf16[512,1024]{1,0:T(8,128)(2,1)S(1)} fusion(bf16[512,4096]{1,0:T(8,128)(2,1)} %param.12, u32[]{:T(128)S(6)} %mul.21), kind=kLoop, calls=%fused_computation.15 | loop fusion | bytes 2097156 | tf_op jit(solution)/shard_map/dynamic_slice | solution.py:270
  37.6 1.5 %collective-permute-start.8 = (bf16[2,512,256]{2,1,0:T(8,128)(2,1)S(1)}, bf16[2,512,256]{2,1,0:T(8,128)(2,1)S(1)}, u32[]{:S(2)}, u32[]{:S(2)}) collective-permute-start(bf16[2,512,256]{2,1,0:T(8,128)(2,1)S(1)} %get-tuple-element.46.rest_0_), channel_id=1, source_target_pairs={{0,16},{4,20},{8,24},{12,28},{16,0},{20,4},{24,8},{28,12},{1,17},{... | collective-permute-start | bytes 1572872 | tf_op jit(solution)/shard_map/ppermute | solution.py:220
  41.5 5.9 %attend.2.refs_0_ = bf16[512,256]{1,0:T(8,128)(2,1)S(1)} custom-call(s32[8]{0:T(128)S(1)} %select_reduce_fusion.place_ref, s32[512,128]{1,0:T(8,128)S(1)} %get-tuple-element.34.first_ref, s32[512,128]{1,0:T(8,128)S(1)} %get-tuple-element.35.grp_ref, bf16[3,512,256]{2,1,0:T(8,128)(2,1)S(1)} %get-tuple-element.37.suf, ...), custom_call_target="tpu_custom_call" | custom-call | tf_op jit(solution)/shard_map/attend/pallas_call | solution.py:165
  47.4 2.3 %collective-permute-start.19 = (bf16[512,256]{1,0:T(8,128)(2,1)S(1)}, bf16[512,256]{1,0:T(8,128)(2,1)S(1)}, u32[]{:S(2)}, u32[]{:S(2)}) collective-permute-start(bf16[512,256]{1,0:T(8,128)(2,1)S(1)} %attend.2.refs_0_), channel_id=1, source_target_pairs={{0,1},{1,0},{2,3},{3,2},{4,5},{5,4},{6,7},{7,6},{8,9},{9,8},{10,11... | collective-permute-start | bytes 786440 | tf_op jit(solution)/shard_map/ppermute | solution.py:220
  49.7 2.2 %collective-permute-start.20 = (bf16[512,256]{1,0:T(8,128)(2,1)S(1)}, bf16[512,256]{1,0:T(8,128)(2,1)S(1)}, u32[]{:S(2)}, u32[]{:S(2)}) collective-permute-start(bf16[512,256]{1,0:T(8,128)(2,1)S(1)} %attend.2.refs_0_), channel_id=1, source_target_pairs={{0,2},{1,3},{2,0},{3,1},{4,6},{5,7},{6,4},{7,5},{8,10},{9,11},{10,... | collective-permute-start | bytes 786440 | tf_op jit(solution)/shard_map/ppermute | solution.py:220
  52.8 1.5 %collective-permute-start.15 = (bf16[1,512,256]{2,1,0:T(8,128)(2,1)S(1)}, bf16[1,512,256]{2,1,0:T(8,128)(2,1)S(1)}, u32[]{:S(2)}, u32[]{:S(2)}) collective-permute-start(bf16[1,512,256]{2,1,0:T(8,128)(2,1)S(1)} %slice.41), channel_id=1, source_target_pairs={{0,8},{4,12},{8,0},{12,4},{16,24},{20,28},{24,16},{28,20},{1,9},{5... | collective-permute-start | bytes 786440 | tf_op jit(solution)/shard_map/ppermute | solution.py:220
  54.3 6.7 %collective-permute-done.19.refs_1_ = bf16[512,256]{1,0:T(8,128)(2,1)S(1)} collective-permute-done((bf16[512,256]{1,0:T(8,128)(2,1)S(1)}, bf16[512,256]{1,0:T(8,128)(2,1)S(1)}, u32[]{:S(2)}, u32[]{:S(2)}) %collective-permute-start.19) | collective-permute-done | bytes 262176 | tf_op jit(solution)/shard_map/ppermute | solution.py:220
  61.6 3.9 %collective-permute-done.20.refs_2_ = bf16[512,256]{1,0:T(8,128)(2,1)S(1)} collective-permute-done((bf16[512,256]{1,0:T(8,128)(2,1)S(1)}, bf16[512,256]{1,0:T(8,128)(2,1)S(1)}, u32[]{:S(2)}, u32[]{:S(2)}) %collective-permute-start.20) | collective-permute-done | bytes 262176 | tf_op jit(solution)/shard_map/ppermute | solution.py:220
  66.2 2.8 %collective-permute-done.14.rest_3_ = bf16[1,512,256]{2,1,0:T(8,128)(2,1)S(1)} collective-permute-done((bf16[1,512,256]{2,1,0:T(8,128)(2,1)S(1)}, bf16[1,512,256]{2,1,0:T(8,128)(2,1)S(1)}, u32[]{:S(2)}, u32[]{:S(2)}) %collective-permute-start.14) | collective-permute-done | bytes 262176 | tf_op jit(solution)/shard_map/ppermute | solution.py:220
  70.5 8.2 %collective-permute-done.28 = bf16[3,256,256]{2,1,0:T(8,128)(2,1)S(1)} collective-permute-done((bf16[3,256,256]{2,1,0:T(8,128)(2,1)S(1)}, bf16[3,256,256]{2,1,0:T(8,128)(2,1)S(1)}, u32[]{:S(2)}, u32[]{:S(2)}) %collective-permute-start.28) | collective-permute-done | bytes 393248 | tf_op jit(solution)/shard_map/ppermute | solution.py:220
  79.2 5.9 %attend.3.refs_0_ = bf16[512,256]{1,0:T(8,128)(2,1)S(1)} custom-call(s32[8]{0:T(128)S(1)} %select_reduce_fusion.place_ref, s32[512,128]{1,0:T(8,128)S(1)} %get-tuple-element.34.first_ref, s32[512,128]{1,0:T(8,128)S(1)} %get-tuple-element.35.grp_ref, bf16[3,512,256]{2,1,0:T(8,128)(2,1)S(1)} %get-tuple-element.36.suf, ...), custom_call_target="tpu_custom_call" | custom-call | tf_op jit(solution)/shard_map/attend/pallas_call | solution.py:165
  85.2 4.1 %collective-permute-start.24 = (bf16[512,256]{1,0:T(8,128)(2,1)S(1)}, bf16[512,256]{1,0:T(8,128)(2,1)S(1)}, u32[]{:S(2)}, u32[]{:S(2)}) collective-permute-start(bf16[512,256]{1,0:T(8,128)(2,1)S(1)} %attend.3.refs_0_), channel_id=1, source_target_pairs={{0,1},{1,0},{2,3},{3,2},{4,5},{5,4},{6,7},{7,6},{8,9},{9,8},{10,11... | collective-permute-start | bytes 786440 | tf_op jit(solution)/shard_map/ppermute | solution.py:220
  90.7 8.9 %collective-permute-done.24.refs_1_ = bf16[512,256]{1,0:T(8,128)(2,1)S(1)} collective-permute-done((bf16[512,256]{1,0:T(8,128)(2,1)S(1)}, bf16[512,256]{1,0:T(8,128)(2,1)S(1)}, u32[]{:S(2)}, u32[]{:S(2)}) %collective-permute-start.24) | collective-permute-done | bytes 262176 | tf_op jit(solution)/shard_map/ppermute | solution.py:220
  99.5 5.5 %collective-permute-done.25.refs_2_ = bf16[512,256]{1,0:T(8,128)(2,1)S(1)} collective-permute-done((bf16[512,256]{1,0:T(8,128)(2,1)S(1)}, bf16[512,256]{1,0:T(8,128)(2,1)S(1)}, u32[]{:S(2)}, u32[]{:S(2)}) %collective-permute-start.25) | collective-permute-done | bytes 262176 | tf_op jit(solution)/shard_map/ppermute | solution.py:220
  105.1 1.3 %collective-permute-start.32 = (bf16[512,256]{1,0:T(8,128)(2,1)S(1)}, bf16[512,256]{1,0:T(8,128)(2,1)S(1)}, u32[]{:S(2)}, u32[]{:S(2)}) collective-permute-start(bf16[512,256]{1,0:T(8,128)(2,1)S(1)} %collective-permute-done.20.refs_2_), channel_id=1, source_target_pairs={{2,3},{1,0},{6,7},{5,4},{10,11},{9,8},{14,15},{13,12},{18,19},{17,... | collective-permute-start | bytes 786440 | tf_op jit(solution)/shard_map/ppermute | solution.py:236
  106.4 1.3 %collective-permute-start.27 = (bf16[512,256]{1,0:T(8,128)(2,1)S(1)}, bf16[512,256]{1,0:T(8,128)(2,1)S(1)}, u32[]{:S(2)}, u32[]{:S(2)}) collective-permute-start(bf16[512,256]{1,0:T(8,128)(2,1)S(1)} %collective-permute-done.25.refs_2_), channel_id=1, source_target_pairs={{2,3},{1,0},{6,7},{5,4},{10,11},{9,8},{14,15},{13,12},{18,19},{17,... | collective-permute-start | bytes 786440 | tf_op jit(solution)/shard_map/ppermute | solution.py:236
  107.7 10.1 %collective-permute-done.32.refs_4_ = bf16[512,256]{1,0:T(8,128)(2,1)S(1)} collective-permute-done((bf16[512,256]{1,0:T(8,128)(2,1)S(1)}, bf16[512,256]{1,0:T(8,128)(2,1)S(1)}, u32[]{:S(2)}, u32[]{:S(2)}) %collective-permute-start.32) | collective-permute-done | bytes 262176 | tf_op jit(solution)/shard_map/ppermute | solution.py:236
  117.8 1.9 %project.2.refs_8_ = f32[512,1024]{1,0:T(8,128)S(1)} custom-call(s32[2]{0:T(128)S(1)} %pad_add_fusion.1.where_ref, bf16[512,256]{1,0:T(8,128)(2,1)S(1)} %attend.2.refs_0_, bf16[512,256]{1,0:T(8,128)(2,1)S(1)} %collective-permute-done.19.refs_1_, bf16[512,256]{1,0:T(8,128)(2,1)S(1)} %collective-permute-done.20.refs_2_, ...), custom_call_target="tpu_custom_call" | custom-call | tf_op jit(solution)/shard_map/project/pallas_call | solution.py:209
  119.7 3.5 %collective-permute-done.27.refs_4_ = bf16[512,256]{1,0:T(8,128)(2,1)S(1)} collective-permute-done((bf16[512,256]{1,0:T(8,128)(2,1)S(1)}, bf16[512,256]{1,0:T(8,128)(2,1)S(1)}, u32[]{:S(2)}, u32[]{:S(2)}) %collective-permute-start.27) | collective-permute-done | bytes 262176 | tf_op jit(solution)/shard_map/ppermute | solution.py:236
  123.2 2.9 %project.3 = bf16[512,1024]{1,0:T(8,128)(2,1)} custom-call(s32[2]{0:T(128)S(1)} %pad_add_fusion.1.where_ref, bf16[512,256]{1,0:T(8,128)(2,1)S(1)} %attend.3.refs_0_, bf16[512,256]{1,0:T(8,128)(2,1)S(1)} %collective-permute-done.24.refs_1_, bf16[512,256]{1,0:T(8,128)(2,1)S(1)} %collective-permute-done.25.refs_2_, ...), custom_call_target="tpu_custom_call" | custom-call | tf_op jit(solution)/shard_map/project/pallas_call | solution.py:209
  (70 shorter events, 10.5 us)
Async XLA Ops:
  1.5 4.8 %collective-permute-start = (bf16[2,512,256]{2,1,0:T(8,128)(2,1)S(1)}, bf16[2,512,256]{2,1,0:T(8,128)(2,1)S(1)}, u32[]{:S(2)}, u32[]{:S(2)}) collective-permute-start(bf16[2,512,256]{2,1,0:T(8,128)(2,1)S(1)} %get-tuple-element.32.rest_0_), channel_id=1, source_target_pairs={{0,4},{4,0},{8,12},{12,8},{16,20},{20,16},{24,28},{28,24},{1,5},{5... | collective-permute-start | bytes 1572872 | tf_op jit(solution)/shard_map/ppermute | solution.py:220
  2.0 15.1 %collective-permute-start.1 = (bf16[2,512,256]{2,1,0:T(8,128)(2,1)S(1)}, bf16[2,512,256]{2,1,0:T(8,128)(2,1)S(1)}, u32[]{:S(2)}, u32[]{:S(2)}) collective-permute-start(bf16[2,512,256]{2,1,0:T(8,128)(2,1)S(1)} %get-tuple-element.32.rest_0_), channel_id=1, source_target_pairs={{0,8},{4,12},{8,0},{12,4},{16,24},{20,28},{24,16},{28,20},{1,9},{5... | collective-permute-start | bytes 1572872 | tf_op jit(solution)/shard_map/ppermute | solution.py:220
  4.6 18.4 %collective-permute-start.5 = (bf16[2,512,256]{2,1,0:T(8,128)(2,1)S(1)}, bf16[2,512,256]{2,1,0:T(8,128)(2,1)S(1)}, u32[]{:S(2)}, u32[]{:S(2)}) collective-permute-start(bf16[2,512,256]{2,1,0:T(8,128)(2,1)S(1)} %get-tuple-element.32.rest_0_), channel_id=1, source_target_pairs={{0,16},{4,20},{8,24},{12,28},{16,0},{20,4},{24,8},{28,12},{1,17},{... | collective-permute-start | bytes 1572872 | tf_op jit(solution)/shard_map/ppermute | solution.py:220
  17.1 22.5 %collective-permute-start.10 = (bf16[2,512,256]{2,1,0:T(8,128)(2,1)S(1)}, bf16[2,512,256]{2,1,0:T(8,128)(2,1)S(1)}, u32[]{:S(2)}, u32[]{:S(2)}) collective-permute-start(bf16[2,512,256]{2,1,0:T(8,128)(2,1)S(1)} %collective-permute-done.1.rest_1_), channel_id=1, source_target_pairs={{0,4},{4,0},{8,12},{12,8},{16,20},{20,16},{24,28},{28,24},{1,5},{5... | collective-permute-start | bytes 1572872 | tf_op jit(solution)/shard_map/ppermute | solution.py:220
  18.5 10.0 %collective-permute-start.3 = (bf16[256,256]{1,0:T(8,128)(2,1)S(1)}, bf16[256,256]{1,0:T(8,128)(2,1)S(1)}, u32[]{:S(2)}, u32[]{:S(2)}) collective-permute-start(bf16[256,256]{1,0:T(8,128)(2,1)S(1)} %get-tuple-element.42), channel_id=1, source_target_pairs={{0,2},{1,3},{2,0},{3,1},{4,6},{5,7},{6,4},{7,5},{8,10},{9,11},{10,... | collective-permute-start | bytes 393224 | tf_op jit(solution)/shard_map/ppermute | solution.py:220
  21.4 7.3 %collective-permute-start.2 = (bf16[256,256]{1,0:T(8,128)(2,1)S(1)}, bf16[256,256]{1,0:T(8,128)(2,1)S(1)}, u32[]{:S(2)}, u32[]{:S(2)}) collective-permute-start(bf16[256,256]{1,0:T(8,128)(2,1)S(1)} %get-tuple-element.40), channel_id=1, source_target_pairs={{0,1},{1,0},{2,3},{3,2},{4,5},{5,4},{6,7},{7,6},{8,9},{9,8},{10,11... | collective-permute-start | bytes 393224 | tf_op jit(solution)/shard_map/ppermute | solution.py:220
  28.7 8.1 %collective-permute-start.6 = (bf16[1,512,256]{2,1,0:T(8,128)(2,1)S(1)}, bf16[1,512,256]{2,1,0:T(8,128)(2,1)S(1)}, u32[]{:S(2)}, u32[]{:S(2)}) collective-permute-start(bf16[1,512,256]{2,1,0:T(8,128)(2,1)S(1)} %slice.39), channel_id=1, source_target_pairs={{0,8},{4,12},{8,0},{12,4},{16,24},{20,28},{24,16},{28,20},{1,9},{5... | collective-permute-start | bytes 786440 | tf_op jit(solution)/shard_map/ppermute | solution.py:220
  30.2 7.4 %collective-permute-start.4 = (bf16[1,512,256]{2,1,0:T(8,128)(2,1)S(1)}, bf16[1,512,256]{2,1,0:T(8,128)(2,1)S(1)}, u32[]{:S(2)}, u32[]{:S(2)}) collective-permute-start(bf16[1,512,256]{2,1,0:T(8,128)(2,1)S(1)} %slice.38), channel_id=1, source_target_pairs={{0,16},{4,20},{8,24},{12,28},{16,0},{20,4},{24,8},{28,12},{1,17},{... | collective-permute-start | bytes 786440 | tf_op jit(solution)/shard_map/ppermute | solution.py:220
  31.7 8.5 %collective-permute-start.11 = (bf16[2,512,256]{2,1,0:T(8,128)(2,1)S(1)}, bf16[2,512,256]{2,1,0:T(8,128)(2,1)S(1)}, u32[]{:S(2)}, u32[]{:S(2)}) collective-permute-start(bf16[2,512,256]{2,1,0:T(8,128)(2,1)S(1)} %collective-permute-done.5.rest_2_), channel_id=1, source_target_pairs={{0,4},{4,0},{8,12},{12,8},{16,20},{20,16},{24,28},{28,24},{1,5},{5... | collective-permute-start | bytes 1572872 | tf_op jit(solution)/shard_map/ppermute | solution.py:220
  31.7 7.9 %collective-permute-start.9 = (bf16[256,256]{1,0:T(8,128)(2,1)S(1)}, bf16[256,256]{1,0:T(8,128)(2,1)S(1)}, u32[]{:S(2)}, u32[]{:S(2)}) collective-permute-start(bf16[256,256]{1,0:T(8,128)(2,1)S(1)} %get-tuple-element.48), channel_id=1, source_target_pairs={{0,3},{1,2},{2,1},{3,0},{4,7},{5,6},{6,5},{7,4},{8,11},{9,10},{10,... | collective-permute-start | bytes 393224 | tf_op jit(solution)/shard_map/ppermute | solution.py:220
  37.6 15.2 %collective-permute-start.8 = (bf16[2,512,256]{2,1,0:T(8,128)(2,1)S(1)}, bf16[2,512,256]{2,1,0:T(8,128)(2,1)S(1)}, u32[]{:S(2)}, u32[]{:S(2)}) collective-permute-start(bf16[2,512,256]{2,1,0:T(8,128)(2,1)S(1)} %get-tuple-element.46.rest_0_), channel_id=1, source_target_pairs={{0,16},{4,20},{8,24},{12,28},{16,0},{20,4},{24,8},{28,12},{1,17},{... | collective-permute-start | bytes 1572872 | tf_op jit(solution)/shard_map/ppermute | solution.py:220
  39.1 15.3 %collective-permute-start.7 = (bf16[2,512,256]{2,1,0:T(8,128)(2,1)S(1)}, bf16[2,512,256]{2,1,0:T(8,128)(2,1)S(1)}, u32[]{:S(2)}, u32[]{:S(2)}) collective-permute-start(bf16[2,512,256]{2,1,0:T(8,128)(2,1)S(1)} %get-tuple-element.46.rest_0_), channel_id=1, source_target_pairs={{0,8},{4,12},{8,0},{12,4},{16,24},{20,28},{24,16},{28,20},{1,9},{5... | collective-permute-start | bytes 1572872 | tf_op jit(solution)/shard_map/ppermute | solution.py:220
  39.6 1.9 %collective-permute-start.12 = (bf16[1,512,256]{2,1,0:T(8,128)(2,1)S(1)}, bf16[1,512,256]{2,1,0:T(8,128)(2,1)S(1)}, u32[]{:S(2)}, u32[]{:S(2)}) collective-permute-start(bf16[1,512,256]{2,1,0:T(8,128)(2,1)S(1)} %collective-permute-done.4.rest_3_), channel_id=1, source_target_pairs={{0,4},{4,0},{8,12},{12,8},{16,20},{20,16},{24,28},{28,24},{1,5},{5... | collective-permute-start | bytes 786440 | tf_op jit(solution)/shard_map/ppermute | solution.py:220
  47.4 13.6 %collective-permute-start.19 = (bf16[512,256]{1,0:T(8,128)(2,1)S(1)}, bf16[512,256]{1,0:T(8,128)(2,1)S(1)}, u32[]{:S(2)}, u32[]{:S(2)}) collective-permute-start(bf16[512,256]{1,0:T(8,128)(2,1)S(1)} %attend.2.refs_0_), channel_id=1, source_target_pairs={{0,1},{1,0},{2,3},{3,2},{4,5},{5,4},{6,7},{7,6},{8,9},{9,8},{10,11... | collective-permute-start | bytes 786440 | tf_op jit(solution)/shard_map/ppermute | solution.py:220
  49.7 15.7 %collective-permute-start.20 = (bf16[512,256]{1,0:T(8,128)(2,1)S(1)}, bf16[512,256]{1,0:T(8,128)(2,1)S(1)}, u32[]{:S(2)}, u32[]{:S(2)}) collective-permute-start(bf16[512,256]{1,0:T(8,128)(2,1)S(1)} %attend.2.refs_0_), channel_id=1, source_target_pairs={{0,2},{1,3},{2,0},{3,1},{4,6},{5,7},{6,4},{7,5},{8,10},{9,11},{10,... | collective-permute-start | bytes 786440 | tf_op jit(solution)/shard_map/ppermute | solution.py:220
  51.9 13.5 %collective-permute-start.21 = (bf16[512,256]{1,0:T(8,128)(2,1)S(1)}, bf16[512,256]{1,0:T(8,128)(2,1)S(1)}, u32[]{:S(2)}, u32[]{:S(2)}) collective-permute-start(bf16[512,256]{1,0:T(8,128)(2,1)S(1)} %attend.2.refs_0_), channel_id=1, source_target_pairs={{1,2},{2,1},{5,6},{6,5},{9,10},{10,9},{13,14},{14,13},{17,18},{18,... | collective-permute-start | bytes 786440 | tf_op jit(solution)/shard_map/ppermute | solution.py:235
  52.8 12.7 %collective-permute-start.15 = (bf16[1,512,256]{2,1,0:T(8,128)(2,1)S(1)}, bf16[1,512,256]{2,1,0:T(8,128)(2,1)S(1)}, u32[]{:S(2)}, u32[]{:S(2)}) collective-permute-start(bf16[1,512,256]{2,1,0:T(8,128)(2,1)S(1)} %slice.41), channel_id=1, source_target_pairs={{0,8},{4,12},{8,0},{12,4},{16,24},{20,28},{24,16},{28,20},{1,9},{5... | collective-permute-start | bytes 786440 | tf_op jit(solution)/shard_map/ppermute | solution.py:220
  54.3 15.5 %collective-permute-start.16 = (bf16[2,512,256]{2,1,0:T(8,128)(2,1)S(1)}, bf16[2,512,256]{2,1,0:T(8,128)(2,1)S(1)}, u32[]{:S(2)}, u32[]{:S(2)}) collective-permute-start(bf16[2,512,256]{2,1,0:T(8,128)(2,1)S(1)} %get-tuple-element.46.rest_0_), channel_id=1, source_target_pairs={{0,4},{4,0},{8,12},{12,8},{16,20},{20,16},{24,28},{28,24},{1,5},{5... | collective-permute-start | bytes 1572872 | tf_op jit(solution)/shard_map/ppermute | solution.py:220
  61.1 7.8 %collective-permute-start.14 = (bf16[1,512,256]{2,1,0:T(8,128)(2,1)S(1)}, bf16[1,512,256]{2,1,0:T(8,128)(2,1)S(1)}, u32[]{:S(2)}, u32[]{:S(2)}) collective-permute-start(bf16[1,512,256]{2,1,0:T(8,128)(2,1)S(1)} %slice.40), channel_id=1, source_target_pairs={{0,16},{4,20},{8,24},{12,28},{16,0},{20,4},{24,8},{28,12},{1,17},{... | collective-permute-start | bytes 786440 | tf_op jit(solution)/shard_map/ppermute | solution.py:220
  65.4 5.0 %collective-permute-start.23 = (bf16[1,512,256]{2,1,0:T(8,128)(2,1)S(1)}, bf16[1,512,256]{2,1,0:T(8,128)(2,1)S(1)}, u32[]{:S(2)}, u32[]{:S(2)}) collective-permute-start(bf16[1,512,256]{2,1,0:T(8,128)(2,1)S(1)} %collective-permute-done.15.rest_4_), channel_id=1, source_target_pairs={{0,4},{4,0},{8,12},{12,8},{16,20},{20,16},{24,28},{28,24},{1,5},{5... | collective-permute-start | bytes 786440 | tf_op jit(solution)/shard_map/ppermute | solution.py:220
  65.5 13.7 %collective-permute-start.17 = (bf16[2,512,256]{2,1,0:T(8,128)(2,1)S(1)}, bf16[2,512,256]{2,1,0:T(8,128)(2,1)S(1)}, u32[]{:S(2)}, u32[]{:S(2)}) collective-permute-start(bf16[2,512,256]{2,1,0:T(8,128)(2,1)S(1)} %collective-permute-done.7.rest_1_), channel_id=1, source_target_pairs={{0,4},{4,0},{8,12},{12,8},{16,20},{20,16},{24,28},{28,24},{1,5},{5... | collective-permute-start | bytes 1572872 | tf_op jit(solution)/shard_map/ppermute | solution.py:220
  66.1 13.1 %collective-permute-start.18 = (bf16[2,512,256]{2,1,0:T(8,128)(2,1)S(1)}, bf16[2,512,256]{2,1,0:T(8,128)(2,1)S(1)}, u32[]{:S(2)}, u32[]{:S(2)}) collective-permute-start(bf16[2,512,256]{2,1,0:T(8,128)(2,1)S(1)} %collective-permute-done.8.rest_2_), channel_id=1, source_target_pairs={{0,4},{4,0},{8,12},{12,8},{16,20},{20,16},{24,28},{28,24},{1,5},{5... | collective-permute-start | bytes 1572872 | tf_op jit(solution)/shard_map/ppermute | solution.py:220
  68.9 9.7 %collective-permute-start.28 = (bf16[3,256,256]{2,1,0:T(8,128)(2,1)S(1)}, bf16[3,256,256]{2,1,0:T(8,128)(2,1)S(1)}, u32[]{:S(2)}, u32[]{:S(2)}) collective-permute-start(bf16[3,256,256]{2,1,0:T(8,128)(2,1)S(1)} %pad_maximum_fusion), channel_id=1, source_target_pairs={{0,8},{4,12},{8,0},{12,4},{16,24},{20,28},{24,16},{28,20},{1,9},{5... | collective-permute-start | bytes 1179656 | tf_op jit(solution)/shard_map/ppermute | solution.py:220
  69.8 20.7 %collective-permute-start.29 = (bf16[3,256,256]{2,1,0:T(8,128)(2,1)S(1)}, bf16[3,256,256]{2,1,0:T(8,128)(2,1)S(1)}, u32[]{:S(2)}, u32[]{:S(2)}) collective-permute-start(bf16[3,256,256]{2,1,0:T(8,128)(2,1)S(1)} %pad_maximum_fusion), channel_id=1, source_target_pairs={{0,16},{4,20},{8,24},{12,28},{16,0},{20,4},{24,8},{28,12},{1,17},{... | collective-permute-start | bytes 1179656 | tf_op jit(solution)/shard_map/ppermute | solution.py:220
  70.4 8.7 %collective-permute-start.22 = (bf16[1,512,256]{2,1,0:T(8,128)(2,1)S(1)}, bf16[1,512,256]{2,1,0:T(8,128)(2,1)S(1)}, u32[]{:S(2)}, u32[]{:S(2)}) collective-permute-start(bf16[1,512,256]{2,1,0:T(8,128)(2,1)S(1)} %collective-permute-done.14.rest_3_), channel_id=1, source_target_pairs={{0,4},{4,0},{8,12},{12,8},{16,20},{20,16},{24,28},{28,24},{1,5},{5... | collective-permute-start | bytes 786440 | tf_op jit(solution)/shard_map/ppermute | solution.py:220
  78.7 12.0 %collective-permute-start.30 = (bf16[3,256,256]{2,1,0:T(8,128)(2,1)S(1)}, bf16[3,256,256]{2,1,0:T(8,128)(2,1)S(1)}, u32[]{:S(2)}, u32[]{:S(2)}) collective-permute-start(bf16[3,256,256]{2,1,0:T(8,128)(2,1)S(1)} %collective-permute-done.28), channel_id=1, source_target_pairs={{0,16},{4,20},{8,24},{12,28},{16,0},{20,4},{24,8},{28,12},{1,17},{... | collective-permute-start | bytes 1179656 | tf_op jit(solution)/shard_map/ppermute | solution.py:220
  85.2 14.3 %collective-permute-start.24 = (bf16[512,256]{1,0:T(8,128)(2,1)S(1)}, bf16[512,256]{1,0:T(8,128)(2,1)S(1)}, u32[]{:S(2)}, u32[]{:S(2)}) collective-permute-start(bf16[512,256]{1,0:T(8,128)(2,1)S(1)} %attend.3.refs_0_), channel_id=1, source_target_pairs={{0,1},{1,0},{2,3},{3,2},{4,5},{5,4},{6,7},{7,6},{8,9},{9,8},{10,11... | collective-permute-start | bytes 786440 | tf_op jit(solution)/shard_map/ppermute | solution.py:220
  89.3 15.8 %collective-permute-start.25 = (bf16[512,256]{1,0:T(8,128)(2,1)S(1)}, bf16[512,256]{1,0:T(8,128)(2,1)S(1)}, u32[]{:S(2)}, u32[]{:S(2)}) collective-permute-start(bf16[512,256]{1,0:T(8,128)(2,1)S(1)} %attend.3.refs_0_), channel_id=1, source_target_pairs={{0,2},{1,3},{2,0},{3,1},{4,6},{5,7},{6,4},{7,5},{8,10},{9,11},{10,... | collective-permute-start | bytes 786440 | tf_op jit(solution)/shard_map/ppermute | solution.py:220
  89.9 15.2 %collective-permute-start.26 = (bf16[512,256]{1,0:T(8,128)(2,1)S(1)}, bf16[512,256]{1,0:T(8,128)(2,1)S(1)}, u32[]{:S(2)}, u32[]{:S(2)}) collective-permute-start(bf16[512,256]{1,0:T(8,128)(2,1)S(1)} %attend.3.refs_0_), channel_id=1, source_target_pairs={{1,2},{2,1},{5,6},{6,5},{9,10},{10,9},{13,14},{14,13},{17,18},{18,... | collective-permute-start | bytes 786440 | tf_op jit(solution)/shard_map/ppermute | solution.py:235
  105.1 12.7 %collective-permute-start.31 = (bf16[12,256,256]{2,1,0:T(8,128)(2,1)S(1)}, bf16[12,256,256]{2,1,0:T(8,128)(2,1)S(1)}, u32[]{:S(2)}, u32[]{:S(2)}) collective-permute-start(bf16[12,256,256]{2,1,0:T(8,128)(2,1)S(1)} %constant_dynamic-update-slice_fusion.refs_6_), channel_id=1, source_target_pairs={{0,4},{4,0},{8,12},{12,8},{16,20},{20,16},{24,28},{28,24},{1,5},{5... | collective-permute-start | bytes 4718600 | tf_op jit(solution)/shard_map/ppermute | solution.py:220
  105.1 12.7 %collective-permute-start.32 = (bf16[512,256]{1,0:T(8,128)(2,1)S(1)}, bf16[512,256]{1,0:T(8,128)(2,1)S(1)}, u32[]{:S(2)}, u32[]{:S(2)}) collective-permute-start(bf16[512,256]{1,0:T(8,128)(2,1)S(1)} %collective-permute-done.20.refs_2_), channel_id=1, source_target_pairs={{2,3},{1,0},{6,7},{5,4},{10,11},{9,8},{14,15},{13,12},{18,19},{17,... | collective-permute-start | bytes 786440 | tf_op jit(solution)/shard_map/ppermute | solution.py:236
  106.4 16.9 %collective-permute-start.27 = (bf16[512,256]{1,0:T(8,128)(2,1)S(1)}, bf16[512,256]{1,0:T(8,128)(2,1)S(1)}, u32[]{:S(2)}, u32[]{:S(2)}) collective-permute-start(bf16[512,256]{1,0:T(8,128)(2,1)S(1)} %collective-permute-done.25.refs_2_), channel_id=1, source_target_pairs={{2,3},{1,0},{6,7},{5,4},{10,11},{9,8},{14,15},{13,12},{18,19},{17,... | collective-permute-start | bytes 786440 | tf_op jit(solution)/shard_map/ppermute | solution.py:236
  (6 other events, 35.3 us)

commit v8 on v4

--- a/solution.py
+++ b/solution.py
@@ -326,8 +326,9 @@
 
     table = jnp.concatenate([lengths, groups], axis=0)
     table_pair = over_core(table)
+    suffix = after(suffix_heads, k_both)
     first, grp, mine, other = prepare(
-        after(where, k_both), (table, table_pair), suffix_heads[:, 0], suffix_heads[:, 1], suffix_heads[:, 2]
+        after(where, k_both), (table, table_pair), suffix[:, 0], suffix[:, 1], suffix[:, 2]
     )
     sufs = [mine, over_core(other)]
     v = after(prefix_cache, k_both)[:, 1]
@@ -335,28 +336,29 @@
     v_other = jnp.where(first_head, v[:, HD:], v[:, :HD])
     v_both = jnp.stack([v_own, over_core(v_other)])
 
-    kxy = over_y(after(kx[0:1], mine, v_both, w_own))
-    kyx = over_x(after(ky[1:2], mine, v_both, w_own))
+    kxy = over_y(after(kx[0:1], mine, v_both))
+    kyx = over_x(after(ky[1:2], mine, v_both))
     v_both = after(v_both, kxy, kyx, w_one, w_two, sufs[1])
     vx = over_x(v_both)
     vy = over_y(v_both)
     w_three = swap(after(sends[2], w_two), "tp", 3, tp_size)
-    scored = score(place, first, grp, sufs, (k_both, kx, ky, kxy, kyx))
+    scored = score(after(place, w_own), first, grp, sufs, (k_both, kx, ky, kxy, kyx))
     w_far = jnp.stack([after(w_one, scored[0]), w_two, w_three])
     w_core = over_core(w_far)
     vxy = over_y(after(vx[0:1], scored[0], w_far))
     vyx = over_x(after(vy[1:2], scored[0], w_far))
     own, pair = mix(0, HD, place, grp, scored, sufs, (v_both, vx, vy, vxy, vyx))
     w_x = over_x(after(w_far, vxy, vyx))
-    w_core_x = over_core(w_x)
 
     back = over_core(pair)
     two_own = swap(own, "tp", 2, tp_size)
     two_back = swap(back, "tp", 2, tp_size)
+    one_own = swap(own, "tp", 1, tp_size)
+    one_back = swap(back, "tp", 1, tp_size)
+    w_core_x = over_core(after(w_x, two_own, two_back, one_own, one_back))
     att = []
-    for a, two in ((own, two_own), (back, two_back)):
-        one = swap(a, "tp", 1, tp_size)
-        three = lax.ppermute(after(a, two), "tp", [(1, 2), (2, 1)])
+    for a, one, two in ((own, one_own, two_own), (back, one_back, two_back)):
+        three = lax.ppermute(after(a, one, two), "tp", [(1, 2), (2, 1)])
         forward = lax.ppermute(two, "tp", [(2, 3), (1, 0)])
         att += [a, one, two, three, forward]
     return project(where, att, w_own, [w_far, w_x, w_core, w_core_x])

time: 109 us -> 104 us (0.954)
  starting transfers between devices: 34 us -> 29.3 us
  local copies, waits for them, and re-layouts: 6.73 us -> 5.44 us
    ppermute x23, starting transfers between devices: 30.1 us -> 25.3 us  [swap(): return lax.ppermute(x, axis, [(i, i ^ mask) for i in range(size)])]
    ppermute x2, waiting for transfers between devices: 8.97 us -> 12.9 us  [split_heads(): forward = lax.ppermute(two, 'tp', [(2, 3), (1, 0)])]
    ppermute x23, waiting for transfers between devices: 40.6 us -> 37.4 us  [swap(): return lax.ppermute(x, axis, [(i, i ^ mask) for i in range(size)])]
    squeeze x1, local copies, waits for them, and re-layouts: 1.46 us -> 0.1 us  [split_heads(): suffix[:, 2]]
  transfers between devices with their start and end apart: 27 -> 27, of which waited for: 11 -> 12; matrix products, arithmetic and copies ran while one was open for 6% -> 5% of each run, Pallas kernels for 12% -> 13%
where the time goes in v8:
time: 104 us
  waiting for transfers between devices  50.3 us (48%)
  starting transfers between devices  29.3 us (28%)
  Pallas kernels  17.3 us (17%)
  local copies, waits for them, and re-layouts  5.44 us (5%)
  other arithmetic  1.12 us (1%)
    ppermute x23, waiting for transfers between devices, swap(): return lax.ppermute(x, axis, [(i, i ^ mask) for i in range(size)])  37.4 us
    ppermute x23, starting transfers between devices, swap(): return lax.ppermute(x, axis, [(i, i ^ mask) for i in range(size)])  25.3 us
    ppermute x2, waiting for transfers between devices, split_heads(): forward = lax.ppermute(two, 'tp', [(2, 3), (1, 0)])  12.9 us
    pallas_call x1, Pallas kernels, score(): pl.pallas_call(functools.partial(score_kernel, len(sufs), tuple((p.shape[...  8.18 us
    pallas_call x1, Pallas kernels, project(): pl.pallas_call(proj_kernel, out_shape=jax.ShapeDtypeStruct((rows, cols),...  3.86 us
    pallas_call x1, Pallas kernels, mix(): pl.pallas_call(functools.partial(mix_kernel, nb, tuple((p.shape[0] for p...  3.52 us
    ppermute x2, starting transfers between devices, split_heads(): forward = lax.ppermute(two, 'tp', [(2, 3), (1, 0)])  2.58 us
  transfers between devices with their start and end apart: 27, of which 12 were waited for; matrix products, arithmetic and copies ran while one was open for 5% of the time, Pallas kernels for 13%

profile of v8, /device:TPU:0, one launch (start us, length us, event | category | flops | bytes accessed | tf_op | source)
XLA Modules:
  0.0 103.7 jit_solution(4228761618297756887)
XLA Ops:
  0.0 1.5 %copy.15 = bf16[512,1,512]{2,0,1:T(8,128)(2,1)S(1)} copy(bf16[512,1,512]{2,1,0:T(2,128)(2,1)} %bitcast.24) | data formatting | bytes 1048576
  2.1 0.7 pad_add_fusion.refs_0_
  3.3 2.9 %collective-permute-start.3 = (bf16[2,512,256]{2,1,0:T(8,128)(2,1)S(1)}, bf16[2,512,256]{2,1,0:T(8,128)(2,1)S(1)}, u32[]{:S(2)}, u32[]{:S(2)}) collective-permute-start(bf16[2,512,256]{2,1,0:T(8,128)(2,1)S(1)} %pad_maximum_fusion.1.rest_2_), channel_id=1, source_target_pairs={{0,8},{4,12},{8,0},{12,4},{16,24},{20,28},{24,16},{28,20},{1,9},{5... | collective-permute-start | bytes 1572872 | tf_op jit(solution)/shard_map/ppermute | solution.py:277
  6.2 1.5 %collective-permute-start.4 = (bf16[2,512,256]{2,1,0:T(8,128)(2,1)S(1)}, bf16[2,512,256]{2,1,0:T(8,128)(2,1)S(1)}, u32[]{:S(2)}, u32[]{:S(2)}) collective-permute-start(bf16[2,512,256]{2,1,0:T(8,128)(2,1)S(1)} %pad_maximum_fusion.1.rest_2_), channel_id=1, source_target_pairs={{0,16},{4,20},{8,24},{12,28},{16,0},{20,4},{24,8},{28,12},{1,17},{... | collective-permute-start | bytes 1572872 | tf_op jit(solution)/shard_map/ppermute | solution.py:277
  7.9 1.8 %prepare.1 = (s32[1024,128]{1,0:T(8,128)S(1)}, s32[1024,128]{1,0:T(8,128)S(1)}, bf16[3,512,256]{2,1,0:T(8,128)(2,1)S(1)}, bf16[3,512,256]{2,1,0:T(8,128)(2,1)S(1)}) custom-call(s32[3]{0:T(128)S(1)} %pad_add_fusion.1.where_ref, s32[2,8]{1,0:T(2,128)S(1)} %pad_add_fusion.refs_0_, s32[2,8]{1,0:T(2,128)S(1)} %collective-permute-done.1.refs_1_, ...), custom_call_target="tpu_custom_call" | custom-call | tf_op jit(solution)/shard_map/prepare/pallas_call | solution.py:101
  10.6 1.7 %fusion = (bf16[256,512]{1,0:T(8,128)(2,1)S(1)}, bf16[256,512]{1,0:T(8,128)(2,1)S(1)}, bf16[256,512]{1,0:T(8,128)(2,1)S(1)}) fusion(bf16[512,4096]{1,0:T(8,128)(2,1)} %param.12, u32[]{:T(128)S(6)} %mul.20, u32[]{:T(128)S(6)} %add.17, u32[]{:T(128)S(6)} %add.15, u32[]{:T(128)S(6)} %add.16), kind=kLoop, calls=%fused_computation.18 | loop fusion | bytes 1572880 | tf_op jit(solution)/shard_map/dynamic_slice | solution.py:312
  12.3 1.6 %collective-permute-start.8 = (bf16[256,512]{1,0:T(8,128)(2,1)S(1)}, bf16[256,512]{1,0:T(8,128)(2,1)S(1)}, u32[]{:S(2)}, u32[]{:S(2)}) collective-permute-start(bf16[256,512]{1,0:T(8,128)(2,1)S(1)} %get-tuple-element.66), channel_id=1, source_target_pairs={{0,1},{1,0},{2,3},{3,2},{4,5},{5,4},{6,7},{7,6},{8,9},{9,8},{10,11... | collective-permute-start | bytes 786440 | tf_op jit(solution)/shard_map/ppermute | solution.py:277
  13.9 2.6 %collective-permute-start.9 = (bf16[256,512]{1,0:T(8,128)(2,1)S(1)}, bf16[256,512]{1,0:T(8,128)(2,1)S(1)}, u32[]{:S(2)}, u32[]{:S(2)}) collective-permute-start(bf16[256,512]{1,0:T(8,128)(2,1)S(1)} %get-tuple-element.67), channel_id=1, source_target_pairs={{0,2},{1,3},{2,0},{3,1},{4,6},{5,7},{6,4},{7,5},{8,10},{9,11},{10,... | collective-permute-start | bytes 786440 | tf_op jit(solution)/shard_map/ppermute | solution.py:277
  16.5 1.9 %collective-permute-done.3.rest_3_ = bf16[2,512,256]{2,1,0:T(8,128)(2,1)S(1)} collective-permute-done((bf16[2,512,256]{2,1,0:T(8,128)(2,1)S(1)}, bf16[2,512,256]{2,1,0:T(8,128)(2,1)S(1)}, u32[]{:S(2)}, u32[]{:S(2)}) %collective-permute-start.3) | collective-permute-done | bytes 524320 | tf_op jit(solution)/shard_map/ppermute | solution.py:277
  18.5 1.8 %collective-permute-start.6 = (bf16[1,512,256]{2,1,0:T(8,128)(2,1)S(1)}, bf16[1,512,256]{2,1,0:T(8,128)(2,1)S(1)}, u32[]{:S(2)}, u32[]{:S(2)}) collective-permute-start(bf16[1,512,256]{2,1,0:T(8,128)(2,1)S(1)} %slice.58), channel_id=1, source_target_pairs={{0,16},{4,20},{8,24},{12,28},{16,0},{20,4},{24,8},{28,12},{1,17},{... | collective-permute-start | bytes 786440 | tf_op jit(solution)/shard_map/ppermute | solution.py:277
  20.3 1.6 %collective-permute-start.7 = (bf16[1,512,256]{2,1,0:T(8,128)(2,1)S(1)}, bf16[1,512,256]{2,1,0:T(8,128)(2,1)S(1)}, u32[]{:S(2)}, u32[]{:S(2)}) collective-permute-start(bf16[1,512,256]{2,1,0:T(8,128)(2,1)S(1)} %slice.62), channel_id=1, source_target_pairs={{0,8},{4,12},{8,0},{12,4},{16,24},{20,28},{24,16},{28,20},{1,9},{5... | collective-permute-start | bytes 786440 | tf_op jit(solution)/shard_map/ppermute | solution.py:277
  21.9 4.2 %collective-permute-done.8 = bf16[256,512]{1,0:T(8,128)(2,1)S(1)} collective-permute-done((bf16[256,512]{1,0:T(8,128)(2,1)S(1)}, bf16[256,512]{1,0:T(8,128)(2,1)S(1)}, u32[]{:S(2)}, u32[]{:S(2)}) %collective-permute-start.8) | collective-permute-done | bytes 262176 | tf_op jit(solution)/shard_map/ppermute | solution.py:277
  26.1 2.4 %collective-permute-done.9 = bf16[256,512]{1,0:T(8,128)(2,1)S(1)} collective-permute-done((bf16[256,512]{1,0:T(8,128)(2,1)S(1)}, bf16[256,512]{1,0:T(8,128)(2,1)S(1)}, u32[]{:S(2)}, u32[]{:S(2)}) %collective-permute-start.9) | collective-permute-done | bytes 262176 | tf_op jit(solution)/shard_map/ppermute | solution.py:277
  28.4 0.7 collective-permute-start.10
  29.6 3.6 %collective-permute-start.12 = (bf16[256,512]{1,0:T(8,128)(2,1)S(1)}, bf16[256,512]{1,0:T(8,128)(2,1)S(1)}, u32[]{:S(2)}, u32[]{:S(2)}) collective-permute-start(bf16[256,512]{1,0:T(8,128)(2,1)S(1)} %get-tuple-element.56), channel_id=1, source_target_pairs={{0,3},{1,2},{2,1},{3,0},{4,7},{5,6},{6,5},{7,4},{8,11},{9,10},{10,... | collective-permute-start | bytes 786440 | tf_op jit(solution)/shard_map/ppermute | solution.py:277
  33.3 1.9 %constant_dynamic-slice_fusion.refs_10_ = bf16[512,1024]{1,0:T(8,128)(2,1)S(1)} fusion(bf16[512,4096]{1,0:T(8,128)(2,1)} %param.12, u32[]{:T(128)S(6)} %mul.21), kind=kLoop, calls=%fused_computation.16 | loop fusion | bytes 2097156 | tf_op jit(solution)/shard_map/dynamic_slice | solution.py:315
  35.2 8.2 %score.1 = (bf16[1024,1024]{1,0:T(8,128)(2,1)S(1)}, bf16[1024,256]{1,0:T(8,128)(2,1)S(1)}, f32[1024,128]{1,0:T(8,128)S(1)}) custom-call(s32[8]{0:T(128)S(1)} %select_reduce_fusion.place_ref, s32[1024,128]{1,0:T(8,128)S(1)} %get-tuple-element.41.first_ref, s32[1024,128]{1,0:T(8,128)S(1)} %get-tuple-element.38.grp_ref, ...), custom_call_target="tpu_custom_call" | custom-call | tf_op jit(solution)/shard_map/score/pallas_call | solution.py:176
  43.5 1.6 %collective-permute-start.13 = (bf16[1,512,256]{2,1,0:T(8,128)(2,1)S(1)}, bf16[1,512,256]{2,1,0:T(8,128)(2,1)S(1)}, u32[]{:S(2)}, u32[]{:S(2)}) collective-permute-start(bf16[1,512,256]{2,1,0:T(8,128)(2,1)S(1)} %slice.63), channel_id=1, source_target_pairs={{0,16},{4,20},{8,24},{12,28},{16,0},{20,4},{24,8},{28,12},{1,17},{... | collective-permute-start | bytes 786440 | tf_op jit(solution)/shard_map/ppermute | solution.py:277
  45.7 4.2 %collective-permute-done.13.rest_5_ = bf16[1,512,256]{2,1,0:T(8,128)(2,1)S(1)} collective-permute-done((bf16[1,512,256]{2,1,0:T(8,128)(2,1)S(1)}, bf16[1,512,256]{2,1,0:T(8,128)(2,1)S(1)}, u32[]{:S(2)}, u32[]{:S(2)}) %collective-permute-start.13) | collective-permute-done | bytes 262176 | tf_op jit(solution)/shard_map/ppermute | solution.py:277
  50.0 2.8 %collective-permute-done.14.rest_6_ = bf16[1,512,256]{2,1,0:T(8,128)(2,1)S(1)} collective-permute-done((bf16[1,512,256]{2,1,0:T(8,128)(2,1)S(1)}, bf16[1,512,256]{2,1,0:T(8,128)(2,1)S(1)}, u32[]{:S(2)}, u32[]{:S(2)}) %collective-permute-start.14) | collective-permute-done | bytes 262176 | tf_op jit(solution)/shard_map/ppermute | solution.py:277
  52.8 3.5 %mix.1 = (bf16[512,256]{1,0:T(8,128)(2,1)S(1)}, bf16[512,256]{1,0:T(8,128)(2,1)S(1)}) custom-call(s32[8]{0:T(128)S(1)} %select_reduce_fusion.place_ref, s32[1024,128]{1,0:T(8,128)S(1)} %get-tuple-element.38.grp_ref, bf16[1024,1024]{1,0:T(8,128)(2,1)S(1)} %get-tuple-element.47.p_ref, bf16[1024,256]{1,0:T(8,128)(2,1)S(1)} %get-tuple-element.48.near_ref, ...), custom_call_target="tpu_custom_call" | custom-call | tf_op jit(solution)/shard_map/mix/pallas_call | solution.py:225
  56.5 2.3 %collective-permute-start.16 = (bf16[512,256]{1,0:T(8,128)(2,1)S(1)}, bf16[512,256]{1,0:T(8,128)(2,1)S(1)}, u32[]{:S(2)}, u32[]{:S(2)}) collective-permute-start(bf16[512,256]{1,0:T(8,128)(2,1)S(1)} %get-tuple-element.60.refs_0_), channel_id=1, source_target_pairs={{0,2},{1,3},{2,0},{3,1},{4,6},{5,7},{6,4},{7,5},{8,10},{9,11},{10,... | collective-permute-start | bytes 786440 | tf_op jit(solution)/shard_map/ppermute | solution.py:277
  58.9 2.5 %collective-permute-start.21 = (bf16[512,256]{1,0:T(8,128)(2,1)S(1)}, bf16[512,256]{1,0:T(8,128)(2,1)S(1)}, u32[]{:S(2)}, u32[]{:S(2)}) collective-permute-start(bf16[512,256]{1,0:T(8,128)(2,1)S(1)} %collective-permute-done.19.refs_5_), channel_id=1, source_target_pairs={{0,2},{1,3},{2,0},{3,1},{4,6},{5,7},{6,4},{7,5},{8,10},{9,11},{10,... | collective-permute-start | bytes 786440 | tf_op jit(solution)/shard_map/ppermute | solution.py:277
  61.4 9.0 %collective-permute-done.15.refs_1_ = bf16[512,256]{1,0:T(8,128)(2,1)S(1)} collective-permute-done((bf16[512,256]{1,0:T(8,128)(2,1)S(1)}, bf16[512,256]{1,0:T(8,128)(2,1)S(1)}, u32[]{:S(2)}, u32[]{:S(2)}) %collective-permute-start.15) | collective-permute-done | bytes 262176 | tf_op jit(solution)/shard_map/ppermute | solution.py:277
  70.4 1.9 %collective-permute-done.16.refs_2_ = bf16[512,256]{1,0:T(8,128)(2,1)S(1)} collective-permute-done((bf16[512,256]{1,0:T(8,128)(2,1)S(1)}, bf16[512,256]{1,0:T(8,128)(2,1)S(1)}, u32[]{:S(2)}, u32[]{:S(2)}) %collective-permute-start.16) | collective-permute-done | bytes 262176 | tf_op jit(solution)/shard_map/ppermute | solution.py:277
  72.3 8.8 %collective-permute-done.20.refs_6_ = bf16[512,256]{1,0:T(8,128)(2,1)S(1)} collective-permute-done((bf16[512,256]{1,0:T(8,128)(2,1)S(1)}, bf16[512,256]{1,0:T(8,128)(2,1)S(1)}, u32[]{:S(2)}, u32[]{:S(2)}) %collective-permute-start.20) | collective-permute-done | bytes 262176 | tf_op jit(solution)/shard_map/ppermute | solution.py:277
  81.2 1.8 %collective-permute-done.21.refs_7_ = bf16[512,256]{1,0:T(8,128)(2,1)S(1)} collective-permute-done((bf16[512,256]{1,0:T(8,128)(2,1)S(1)}, bf16[512,256]{1,0:T(8,128)(2,1)S(1)}, u32[]{:S(2)}, u32[]{:S(2)}) %collective-permute-start.21) | collective-permute-done | bytes 262176 | tf_op jit(solution)/shard_map/ppermute | solution.py:277
  83.6 1.3 %collective-permute-start.18 = (bf16[512,256]{1,0:T(8,128)(2,1)S(1)}, bf16[512,256]{1,0:T(8,128)(2,1)S(1)}, u32[]{:S(2)}, u32[]{:S(2)}) collective-permute-start(bf16[512,256]{1,0:T(8,128)(2,1)S(1)} %collective-permute-done.16.refs_2_), channel_id=1, source_target_pairs={{2,3},{1,0},{6,7},{5,4},{10,11},{9,8},{14,15},{13,12},{18,19},{17,... | collective-permute-start | bytes 786440 | tf_op jit(solution)/shard_map/ppermute | solution.py:362
  85.6 1.3 %collective-permute-start.23 = (bf16[512,256]{1,0:T(8,128)(2,1)S(1)}, bf16[512,256]{1,0:T(8,128)(2,1)S(1)}, u32[]{:S(2)}, u32[]{:S(2)}) collective-permute-start(bf16[512,256]{1,0:T(8,128)(2,1)S(1)} %collective-permute-done.21.refs_7_), channel_id=1, source_target_pairs={{2,3},{1,0},{6,7},{5,4},{10,11},{9,8},{14,15},{13,12},{18,19},{17,... | collective-permute-start | bytes 786440 | tf_op jit(solution)/shard_map/ppermute | solution.py:362
  86.9 7.7 %collective-permute-done.18.refs_4_ = bf16[512,256]{1,0:T(8,128)(2,1)S(1)} collective-permute-done((bf16[512,256]{1,0:T(8,128)(2,1)S(1)}, bf16[512,256]{1,0:T(8,128)(2,1)S(1)}, u32[]{:S(2)}, u32[]{:S(2)}) %collective-permute-start.18) | collective-permute-done | bytes 262176 | tf_op jit(solution)/shard_map/ppermute | solution.py:362
  94.6 5.2 %collective-permute-done.23.refs_9_ = bf16[512,256]{1,0:T(8,128)(2,1)S(1)} collective-permute-done((bf16[512,256]{1,0:T(8,128)(2,1)S(1)}, bf16[512,256]{1,0:T(8,128)(2,1)S(1)}, u32[]{:S(2)}, u32[]{:S(2)}) %collective-permute-start.23) | collective-permute-done | bytes 262176 | tf_op jit(solution)/shard_map/ppermute | solution.py:362
  99.9 3.9 %project.1 = bf16[512,1024]{1,0:T(8,128)(2,1)} custom-call(s32[3]{0:T(128)S(1)} %pad_add_fusion.1.where_ref, bf16[512,256]{1,0:T(8,128)(2,1)S(1)} %get-tuple-element.60.refs_0_, bf16[512,256]{1,0:T(8,128)(2,1)S(1)} %collective-permute-done.15.refs_1_, bf16[512,256]{1,0:T(8,128)(2,1)S(1)} %collective-permute-done.16.refs_2_, ...), custom_call_target="tpu_custom_call" | custom-call | tf_op jit(solution)/shard_map/project/pallas_call | solution.py:266
  (54 shorter events, 5.2 us)
Async XLA Ops:
  0.0 7.9 %copy-start = (f32[128,256]{1,0:T(8,128)S(1)}, f32[128,256]{1,0:T(8,128)}, u32[]{:S(2)}) copy-start(f32[128,256]{1,0:T(8,128)} %constant.28.clone.refs_5_) | copy-start | bytes 393220
  0.0 7.7 %copy-start.2 = (bf16[512,3,512]{2,0,1:T(8,128)(2,1)S(1)}, bf16[512,3,512]{2,0,1:T(8,128)(2,1)}, u32[]{:S(2)}) copy-start(bf16[512,3,512]{2,0,1:T(8,128)(2,1)} %param.7) | copy-start | bytes 4718596
  0.0 9.8 %copy-start.1 = (bf16[512,2,512]{2,1,0:T(2,128)(2,1)S(1)}, bf16[512,2,512]{2,1,0:T(2,128)(2,1)}, u32[]{:S(2)}) copy-start(bf16[512,2,512]{2,1,0:T(2,128)(2,1)} %param.8) | copy-start | bytes 3145732
  1.6 1.7 %collective-permute-start = (bf16[512,256]{1,0:T(8,128)(2,1)S(1)}, bf16[512,256]{1,0:T(8,128)(2,1)S(1)}, u32[]{:S(2)}, u32[]{:S(2)}) collective-permute-start(bf16[512,256]{1,0:T(8,128)(2,1)S(1)} %get-tuple-element.74), channel_id=1, source_target_pairs={{0,4},{4,0},{8,12},{12,8},{16,20},{20,16},{24,28},{28,24},{1,5},{5... | collective-permute-start | bytes 786440 | tf_op jit(solution)/shard_map/ppermute | solution.py:277
  2.8 5.1 %collective-permute-start.1 = (s32[2,8]{1,0:T(2,128)S(1)}, s32[2,8]{1,0:T(2,128)S(1)}, u32[]{:S(2)}, u32[]{:S(2)}) collective-permute-start(s32[2,8]{1,0:T(2,128)S(1)} %pad_add_fusion.refs_0_), channel_id=1, source_target_pairs={{0,4},{4,0},{8,12},{12,8},{16,20},{20,16},{24,28},{28,24},{1,5},{5... | collective-permute-start | bytes 200 | tf_op jit(solution)/shard_map/ppermute | solution.py:277
  3.3 15.2 %collective-permute-start.3 = (bf16[2,512,256]{2,1,0:T(8,128)(2,1)S(1)}, bf16[2,512,256]{2,1,0:T(8,128)(2,1)S(1)}, u32[]{:S(2)}, u32[]{:S(2)}) collective-permute-start(bf16[2,512,256]{2,1,0:T(8,128)(2,1)S(1)} %pad_maximum_fusion.1.rest_2_), channel_id=1, source_target_pairs={{0,8},{4,12},{8,0},{12,4},{16,24},{20,28},{24,16},{28,20},{1,9},{5... | collective-permute-start | bytes 1572872 | tf_op jit(solution)/shard_map/ppermute | solution.py:277
  6.2 14.1 %collective-permute-start.4 = (bf16[2,512,256]{2,1,0:T(8,128)(2,1)S(1)}, bf16[2,512,256]{2,1,0:T(8,128)(2,1)S(1)}, u32[]{:S(2)}, u32[]{:S(2)}) collective-permute-start(bf16[2,512,256]{2,1,0:T(8,128)(2,1)S(1)} %pad_maximum_fusion.1.rest_2_), channel_id=1, source_target_pairs={{0,16},{4,20},{8,24},{12,28},{16,0},{20,4},{24,8},{28,12},{1,17},{... | collective-permute-start | bytes 1572872 | tf_op jit(solution)/shard_map/ppermute | solution.py:277
  9.7 23.6 %copy-start.3 = (s32[4,2]{0,1:T(2,128)S(1)}, s32[4,2]{0,1:T(2,128)}, u32[]{:S(2)}) copy-start(s32[4,2]{0,1:T(2,128)} %param.11) | copy-start | bytes 100
  9.7 18.7 %collective-permute-start.2 = (bf16[3,512,256]{2,1,0:T(8,128)(2,1)S(1)}, bf16[3,512,256]{2,1,0:T(8,128)(2,1)S(1)}, u32[]{:S(2)}, u32[]{:S(2)}) collective-permute-start(bf16[3,512,256]{2,1,0:T(8,128)(2,1)S(1)} %get-tuple-element.43), channel_id=1, source_target_pairs={{0,4},{4,0},{8,12},{12,8},{16,20},{20,16},{24,28},{28,24},{1,5},{5... | collective-permute-start | bytes 2359304 | tf_op jit(solution)/shard_map/ppermute | solution.py:277
  10.0 3.9 %collective-permute-start.5 = (bf16[512,256]{1,0:T(8,128)(2,1)S(1)}, bf16[512,256]{1,0:T(8,128)(2,1)S(1)}, u32[]{:S(2)}, u32[]{:S(2)}) collective-permute-start(bf16[512,256]{1,0:T(8,128)(2,1)S(1)} %get-tuple-element.72), channel_id=1, source_target_pairs={{0,4},{4,0},{8,12},{12,8},{16,20},{20,16},{24,28},{28,24},{1,5},{5... | collective-permute-start | bytes 786440 | tf_op jit(solution)/shard_map/ppermute | solution.py:277
  12.3 13.8 %collective-permute-start.8 = (bf16[256,512]{1,0:T(8,128)(2,1)S(1)}, bf16[256,512]{1,0:T(8,128)(2,1)S(1)}, u32[]{:S(2)}, u32[]{:S(2)}) collective-permute-start(bf16[256,512]{1,0:T(8,128)(2,1)S(1)} %get-tuple-element.66), channel_id=1, source_target_pairs={{0,1},{1,0},{2,3},{3,2},{4,5},{5,4},{6,7},{7,6},{8,9},{9,8},{10,11... | collective-permute-start | bytes 786440 | tf_op jit(solution)/shard_map/ppermute | solution.py:277
  13.9 14.5 %collective-permute-start.9 = (bf16[256,512]{1,0:T(8,128)(2,1)S(1)}, bf16[256,512]{1,0:T(8,128)(2,1)S(1)}, u32[]{:S(2)}, u32[]{:S(2)}) collective-permute-start(bf16[256,512]{1,0:T(8,128)(2,1)S(1)} %get-tuple-element.67), channel_id=1, source_target_pairs={{0,2},{1,3},{2,0},{3,1},{4,6},{5,7},{6,4},{7,5},{8,10},{9,11},{10,... | collective-permute-start | bytes 786440 | tf_op jit(solution)/shard_map/ppermute | solution.py:277
  18.5 10.0 %collective-permute-start.6 = (bf16[1,512,256]{2,1,0:T(8,128)(2,1)S(1)}, bf16[1,512,256]{2,1,0:T(8,128)(2,1)S(1)}, u32[]{:S(2)}, u32[]{:S(2)}) collective-permute-start(bf16[1,512,256]{2,1,0:T(8,128)(2,1)S(1)} %slice.58), channel_id=1, source_target_pairs={{0,16},{4,20},{8,24},{12,28},{16,0},{20,4},{24,8},{28,12},{1,17},{... | collective-permute-start | bytes 786440 | tf_op jit(solution)/shard_map/ppermute | solution.py:277
  20.3 8.1 %collective-permute-start.7 = (bf16[1,512,256]{2,1,0:T(8,128)(2,1)S(1)}, bf16[1,512,256]{2,1,0:T(8,128)(2,1)S(1)}, u32[]{:S(2)}, u32[]{:S(2)}) collective-permute-start(bf16[1,512,256]{2,1,0:T(8,128)(2,1)S(1)} %slice.62), channel_id=1, source_target_pairs={{0,8},{4,12},{8,0},{12,4},{16,24},{20,28},{24,16},{28,20},{1,9},{5... | collective-permute-start | bytes 786440 | tf_op jit(solution)/shard_map/ppermute | solution.py:277
  28.4 15.1 %collective-permute-start.10 = (bf16[2,512,256]{2,1,0:T(8,128)(2,1)S(1)}, bf16[2,512,256]{2,1,0:T(8,128)(2,1)S(1)}, u32[]{:S(2)}, u32[]{:S(2)}) collective-permute-start(bf16[2,512,256]{2,1,0:T(8,128)(2,1)S(1)} %pad_maximum_fusion.2.rest_2_), channel_id=1, source_target_pairs={{0,8},{4,12},{8,0},{12,4},{16,24},{20,28},{24,16},{28,20},{1,9},{5... | collective-permute-start | bytes 1572872 | tf_op jit(solution)/shard_map/ppermute | solution.py:277
  29.1 16.0 %collective-permute-start.11 = (bf16[2,512,256]{2,1,0:T(8,128)(2,1)S(1)}, bf16[2,512,256]{2,1,0:T(8,128)(2,1)S(1)}, u32[]{:S(2)}, u32[]{:S(2)}) collective-permute-start(bf16[2,512,256]{2,1,0:T(8,128)(2,1)S(1)} %pad_maximum_fusion.2.rest_2_), channel_id=1, source_target_pairs={{0,16},{4,20},{8,24},{12,28},{16,0},{20,4},{24,8},{28,12},{1,17},{... | collective-permute-start | bytes 1572872 | tf_op jit(solution)/shard_map/ppermute | solution.py:277
  29.6 13.8 %collective-permute-start.12 = (bf16[256,512]{1,0:T(8,128)(2,1)S(1)}, bf16[256,512]{1,0:T(8,128)(2,1)S(1)}, u32[]{:S(2)}, u32[]{:S(2)}) collective-permute-start(bf16[256,512]{1,0:T(8,128)(2,1)S(1)} %get-tuple-element.56), channel_id=1, source_target_pairs={{0,3},{1,2},{2,1},{3,0},{4,7},{5,6},{6,5},{7,4},{8,11},{9,10},{10,... | collective-permute-start | bytes 786440 | tf_op jit(solution)/shard_map/ppermute | solution.py:277
  43.5 6.4 %collective-permute-start.13 = (bf16[1,512,256]{2,1,0:T(8,128)(2,1)S(1)}, bf16[1,512,256]{2,1,0:T(8,128)(2,1)S(1)}, u32[]{:S(2)}, u32[]{:S(2)}) collective-permute-start(bf16[1,512,256]{2,1,0:T(8,128)(2,1)S(1)} %slice.63), channel_id=1, source_target_pairs={{0,16},{4,20},{8,24},{12,28},{16,0},{20,4},{24,8},{28,12},{1,17},{... | collective-permute-start | bytes 786440 | tf_op jit(solution)/shard_map/ppermute | solution.py:277
  45.1 7.6 %collective-permute-start.14 = (bf16[1,512,256]{2,1,0:T(8,128)(2,1)S(1)}, bf16[1,512,256]{2,1,0:T(8,128)(2,1)S(1)}, u32[]{:S(2)}, u32[]{:S(2)}) collective-permute-start(bf16[1,512,256]{2,1,0:T(8,128)(2,1)S(1)} %slice.64), channel_id=1, source_target_pairs={{0,8},{4,12},{8,0},{12,4},{16,24},{20,28},{24,16},{28,20},{1,9},{5... | collective-permute-start | bytes 786440 | tf_op jit(solution)/shard_map/ppermute | solution.py:277
  52.8 30.2 %collective-permute-start.24 = (bf16[3,256,512]{2,1,0:T(8,128)(2,1)S(1)}, bf16[3,256,512]{2,1,0:T(8,128)(2,1)S(1)}, u32[]{:S(2)}, u32[]{:S(2)}) collective-permute-start(bf16[3,256,512]{2,1,0:T(8,128)(2,1)S(1)} %pad_maximum_fusion.refs_11_), channel_id=1, source_target_pairs={{0,8},{4,12},{8,0},{12,4},{16,24},{20,28},{24,16},{28,20},{1,9},{5... | collective-permute-start | bytes 2359304 | tf_op jit(solution)/shard_map/ppermute | solution.py:277
  56.3 2.5 %collective-permute-start.19 = (bf16[512,256]{1,0:T(8,128)(2,1)S(1)}, bf16[512,256]{1,0:T(8,128)(2,1)S(1)}, u32[]{:S(2)}, u32[]{:S(2)}) collective-permute-start(bf16[512,256]{1,0:T(8,128)(2,1)S(1)} %get-tuple-element.61), channel_id=1, source_target_pairs={{0,4},{4,0},{8,12},{12,8},{16,20},{20,16},{24,28},{28,24},{1,5},{5... | collective-permute-start | bytes 786440 | tf_op jit(solution)/shard_map/ppermute | solution.py:277
  56.4 14.0 %collective-permute-start.15 = (bf16[512,256]{1,0:T(8,128)(2,1)S(1)}, bf16[512,256]{1,0:T(8,128)(2,1)S(1)}, u32[]{:S(2)}, u32[]{:S(2)}) collective-permute-start(bf16[512,256]{1,0:T(8,128)(2,1)S(1)} %get-tuple-element.60.refs_0_), channel_id=1, source_target_pairs={{0,1},{1,0},{2,3},{3,2},{4,5},{5,4},{6,7},{7,6},{8,9},{9,8},{10,11... | collective-permute-start | bytes 786440 | tf_op jit(solution)/shard_map/ppermute | solution.py:277
  56.5 15.8 %collective-permute-start.16 = (bf16[512,256]{1,0:T(8,128)(2,1)S(1)}, bf16[512,256]{1,0:T(8,128)(2,1)S(1)}, u32[]{:S(2)}, u32[]{:S(2)}) collective-permute-start(bf16[512,256]{1,0:T(8,128)(2,1)S(1)} %get-tuple-element.60.refs_0_), channel_id=1, source_target_pairs={{0,2},{1,3},{2,0},{3,1},{4,6},{5,7},{6,4},{7,5},{8,10},{9,11},{10,... | collective-permute-start | bytes 786440 | tf_op jit(solution)/shard_map/ppermute | solution.py:277
  58.8 22.4 %collective-permute-start.20 = (bf16[512,256]{1,0:T(8,128)(2,1)S(1)}, bf16[512,256]{1,0:T(8,128)(2,1)S(1)}, u32[]{:S(2)}, u32[]{:S(2)}) collective-permute-start(bf16[512,256]{1,0:T(8,128)(2,1)S(1)} %collective-permute-done.19.refs_5_), channel_id=1, source_target_pairs={{0,1},{1,0},{2,3},{3,2},{4,5},{5,4},{6,7},{7,6},{8,9},{9,8},{10,11... | collective-permute-start | bytes 786440 | tf_op jit(solution)/shard_map/ppermute | solution.py:277
  58.9 24.0 %collective-permute-start.21 = (bf16[512,256]{1,0:T(8,128)(2,1)S(1)}, bf16[512,256]{1,0:T(8,128)(2,1)S(1)}, u32[]{:S(2)}, u32[]{:S(2)}) collective-permute-start(bf16[512,256]{1,0:T(8,128)(2,1)S(1)} %collective-permute-done.19.refs_5_), channel_id=1, source_target_pairs={{0,2},{1,3},{2,0},{3,1},{4,6},{5,7},{6,4},{7,5},{8,10},{9,11},{10,... | collective-permute-start | bytes 786440 | tf_op jit(solution)/shard_map/ppermute | solution.py:277
  70.4 15.2 %collective-permute-start.25 = (bf16[3,256,512]{2,1,0:T(8,128)(2,1)S(1)}, bf16[3,256,512]{2,1,0:T(8,128)(2,1)S(1)}, u32[]{:S(2)}, u32[]{:S(2)}) collective-permute-start(bf16[3,256,512]{2,1,0:T(8,128)(2,1)S(1)} %pad_maximum_fusion.refs_11_), channel_id=1, source_target_pairs={{0,4},{4,0},{8,12},{12,8},{16,20},{20,16},{24,28},{28,24},{1,5},{5... | collective-permute-start | bytes 2359304 | tf_op jit(solution)/shard_map/ppermute | solution.py:277
  83.0 16.9 %collective-permute-start.26 = (bf16[3,256,512]{2,1,0:T(8,128)(2,1)S(1)}, bf16[3,256,512]{2,1,0:T(8,128)(2,1)S(1)}, u32[]{:S(2)}, u32[]{:S(2)}) collective-permute-start(bf16[3,256,512]{2,1,0:T(8,128)(2,1)S(1)} %collective-permute-done.24.refs_12_), channel_id=1, source_target_pairs={{0,4},{4,0},{8,12},{12,8},{16,20},{20,16},{24,28},{28,24},{1,5},{5... | collective-permute-start | bytes 2359304 | tf_op jit(solution)/shard_map/ppermute | solution.py:277
  83.0 4.0 %collective-permute-start.17 = (bf16[512,256]{1,0:T(8,128)(2,1)S(1)}, bf16[512,256]{1,0:T(8,128)(2,1)S(1)}, u32[]{:S(2)}, u32[]{:S(2)}) collective-permute-start(bf16[512,256]{1,0:T(8,128)(2,1)S(1)} %get-tuple-element.60.refs_0_), channel_id=1, source_target_pairs={{1,2},{2,1},{5,6},{6,5},{9,10},{10,9},{13,14},{14,13},{17,18},{18,... | collective-permute-start | bytes 786440 | tf_op jit(solution)/shard_map/ppermute | solution.py:361
  83.6 11.0 %collective-permute-start.18 = (bf16[512,256]{1,0:T(8,128)(2,1)S(1)}, bf16[512,256]{1,0:T(8,128)(2,1)S(1)}, u32[]{:S(2)}, u32[]{:S(2)}) collective-permute-start(bf16[512,256]{1,0:T(8,128)(2,1)S(1)} %collective-permute-done.16.refs_2_), channel_id=1, source_target_pairs={{2,3},{1,0},{6,7},{5,4},{10,11},{9,8},{14,15},{13,12},{18,19},{17,... | collective-permute-start | bytes 786440 | tf_op jit(solution)/shard_map/ppermute | solution.py:362
  84.9 9.7 %collective-permute-start.22 = (bf16[512,256]{1,0:T(8,128)(2,1)S(1)}, bf16[512,256]{1,0:T(8,128)(2,1)S(1)}, u32[]{:S(2)}, u32[]{:S(2)}) collective-permute-start(bf16[512,256]{1,0:T(8,128)(2,1)S(1)} %collective-permute-done.19.refs_5_), channel_id=1, source_target_pairs={{1,2},{2,1},{5,6},{6,5},{9,10},{10,9},{13,14},{14,13},{17,18},{18,... | collective-permute-start | bytes 786440 | tf_op jit(solution)/shard_map/ppermute | solution.py:361
  85.6 14.2 %collective-permute-start.23 = (bf16[512,256]{1,0:T(8,128)(2,1)S(1)}, bf16[512,256]{1,0:T(8,128)(2,1)S(1)}, u32[]{:S(2)}, u32[]{:S(2)}) collective-permute-start(bf16[512,256]{1,0:T(8,128)(2,1)S(1)} %collective-permute-done.21.refs_7_), channel_id=1, source_target_pairs={{2,3},{1,0},{6,7},{5,4},{10,11},{9,8},{14,15},{13,12},{18,19},{17,... | collective-permute-start | bytes 786440 | tf_op jit(solution)/shard_map/ppermute | solution.py:362

commit v9 on v8

--- a/solution.py
+++ b/solution.py
@@ -188,7 +188,7 @@
     )(place, first, grp, *sufs, *pieces)
 
 
-def mix_kernel(nb, counts, col, place_ref, grp_ref, p_ref, near_ref, den_ref, *rest):
+def mix_kernel(nb, base, counts, col, place_ref, grp_ref, p_ref, near_ref, den_ref, *rest):
     sufs = rest[:nb]
     n_pieces = len(counts)
     pieces = flatten(rest[nb : nb + n_pieces], counts)
@@ -198,7 +198,7 @@
         rows = outs[n].shape[0]
         for b in range(rows // RB):
             r0 = b * RB
-            t0 = n * rows + r0
+            t0 = base + n * rows + r0
             grp = wide(grp_ref[t0 : t0 + RB, :], width)
             lo = max(0, r0 - MOST)
             acc = jnp.dot(
@@ -219,11 +219,11 @@
             outs[n][r0 : r0 + RB, :] = (acc / den).astype(jnp.bfloat16)
 
 
-def mix(col, width, place, grp, scored, sufs, pieces):
+def mix(col, width, place, grp, scored, sufs, pieces, base=0):
     rows = sufs[0].shape[1]
     nb = len(sufs)
     return pl.pallas_call(
-        functools.partial(mix_kernel, nb, tuple(p.shape[0] for p in pieces), col),
+        functools.partial(mix_kernel, nb, base, tuple(p.shape[0] for p in pieces), col),
         out_shape=[jax.ShapeDtypeStruct((rows, width), jnp.bfloat16)] * nb,
         in_specs=[SMEM] + [VMEM] * (4 + nb + len(pieces)),
         out_specs=[VMEM] * nb,
@@ -232,45 +232,48 @@
     )(place, grp, *scored, *sufs, *pieces)
 
 
-def proj_kernel(where_ref, *refs):
-    att = refs[:10]
-    own = refs[10]
-    far = refs[11:15]
-    o_ref = refs[15]
+def proj_kernel(steps, last, where_ref, *refs):
+    att = refs[: 2 * len(steps)]
+    own, *far = refs[2 * len(steps) : 2 * len(steps) + 5]
+    o_ref = refs[-1]
     cols = o_ref.shape[1] // 2
     rows = o_ref.shape[0]
     core = where_ref[1]
     side = where_ref[2]
     tall = 256
     for r0 in range(0, rows, tall):
+        at = slice(r0, r0 + tall)
         for x in range(2):
-            c0 = pl.multiple_of(lax.bitwise_xor(side, x) * cols, cols)
-            acc = jnp.zeros((tall, cols), jnp.float32)
+            c = pl.ds(pl.multiple_of(lax.bitwise_xor(side, x) * cols, cols), cols)
+            acc = refs[-2][at, c] if last else jnp.zeros((tall, cols), jnp.float32)
             for h in range(2):
                 head = lax.bitwise_xor(core, h)
-                for m in range(4):
-                    a = att[h * 5 + m][r0 : r0 + tall, :]
-                    if m == 3:
-                        a = a + att[h * 5 + 4][r0 : r0 + tall, :]
+                lines = []
+                for i, m in enumerate(steps):
+                    lines.append((m, att[h * len(steps) + i][at, :]))
+                if last:
+                    lines = [(3, lines[0][1] + lines[1][1])]
+                for m, a in lines:
                     if m == 0:
-                        w = own[pl.ds(pl.multiple_of(head * HD, HD), HD), pl.ds(c0, cols)]
+                        w = own[pl.ds(pl.multiple_of(head * HD, HD), HD), c]
                     else:
                         w = far[2 * h + x][m - 1]
                     acc = acc + jnp.dot(a, w, preferred_element_type=jnp.float32)
-            o_ref[r0 : r0 + tall, pl.ds(c0, cols)] = acc.astype(jnp.bfloat16)
-
-
-def project(where, att, own, far):
+            o_ref[at, c] = acc.astype(o_ref.dtype)
+
+
+def project(where, steps, att, own, far, add=None):
     rows = att[0].shape[0]
     cols = own.shape[1]
+    extra = [] if add is None else [add]
     return pl.pallas_call(
-        proj_kernel,
-        out_shape=jax.ShapeDtypeStruct((rows, cols), jnp.bfloat16),
-        in_specs=[SMEM] + [VMEM] * (len(att) + 1 + len(far)),
+        functools.partial(proj_kernel, steps, add is not None),
+        out_shape=jax.ShapeDtypeStruct((rows, cols), jnp.float32 if add is None else jnp.bfloat16),
+        in_specs=[SMEM] + [VMEM] * (len(att) + 1 + len(far) + len(extra)),
         out_specs=VMEM,
         compiler_params=pltpu.CompilerParams(vmem_limit_bytes=6 << 20),
         name="project",
-    )(where, *att, own, *far)
+    )(where, *att, own, *far, *extra)
 
 
 def swap(x, axis, mask, size):
@@ -287,6 +290,7 @@
 
 
 def split_heads(suffix_heads, prefix_cache, lengths, groups, owners, out_weight):
+    rows = suffix_heads.shape[0]
     me = lax.axis_index("req")
     z = lax.axis_index("tp")
     core = me & 1
@@ -338,30 +342,34 @@
 
     kxy = over_y(after(kx[0:1], mine, v_both))
     kyx = over_x(after(ky[1:2], mine, v_both))
-    v_both = after(v_both, kxy, kyx, w_one, w_two, sufs[1])
+    v_both = after(v_both, kxy, kyx, w_one, w_two, w_own, sufs[1])
     vx = over_x(v_both)
     vy = over_y(v_both)
     w_three = swap(after(sends[2], w_two), "tp", 3, tp_size)
-    scored = score(after(place, w_own), first, grp, sufs, (k_both, kx, ky, kxy, kyx))
+    scored = score(place, first, grp, sufs, (k_both, kx, ky, kxy, kyx))
     w_far = jnp.stack([after(w_one, scored[0]), w_two, w_three])
     w_core = over_core(w_far)
     vxy = over_y(after(vx[0:1], scored[0], w_far))
     vyx = over_x(after(vy[1:2], scored[0], w_far))
-    own, pair = mix(0, HD, place, grp, scored, sufs, (v_both, vx, vy, vxy, vyx))
+    v_pieces = (v_both, vx, vy, vxy, vyx)
+    (own,) = mix(0, HD, place, grp, scored, sufs[:1], v_pieces)
+    (pair,) = mix(0, HD, place, grp, scored, sufs[1:], v_pieces, rows)
     w_x = over_x(after(w_far, vxy, vyx))
 
     back = over_core(pair)
     two_own = swap(own, "tp", 2, tp_size)
+    one_own = swap(own, "tp", 1, tp_size)
     two_back = swap(back, "tp", 2, tp_size)
-    one_own = swap(own, "tp", 1, tp_size)
     one_back = swap(back, "tp", 1, tp_size)
-    w_core_x = over_core(after(w_x, two_own, two_back, one_own, one_back))
-    att = []
-    for a, one, two in ((own, one_own, two_own), (back, one_back, two_back)):
-        three = lax.ppermute(after(a, one, two), "tp", [(1, 2), (2, 1)])
-        forward = lax.ppermute(two, "tp", [(2, 3), (1, 0)])
-        att += [a, one, two, three, forward]
-    return project(where, att, w_own, [w_far, w_x, w_core, w_core_x])
+    three_own = lax.ppermute(after(own, two_own, one_own, one_back), "tp", [(1, 2), (2, 1)])
+    forward_own = lax.ppermute(after(two_own, one_own, one_back), "tp", [(2, 3), (1, 0)])
+    three_back = lax.ppermute(after(back, two_back, one_back), "tp", [(1, 2), (2, 1)])
+    forward_back = lax.ppermute(two_back, "tp", [(2, 3), (1, 0)])
+    w_core_x = over_core(after(w_x, two_back, one_back, three_own, forward_own))
+    far = [w_far, w_x, w_core, w_core_x]
+    near = project(where, (0, 1, 2), (own, one_own, two_own, back, one_back, two_back), w_own, far)
+    last = (three_own, forward_own, three_back, forward_back)
+    return project(where, (3, 3), last, w_own, far, near)
 
 
 def whole_heads(suffix_heads, prefix_cache, lengths, groups, owners, out_weight):

time: 104 us -> 105 us (level)
  Pallas kernels: 17.3 us -> 18.7 us
  starting transfers between devices: 29.3 us -> 30.6 us
    ppermute x23, waiting for transfers between devices: 37.4 us -> 34.2 us  [swap(): return lax.ppermute(x, axis, [(i, i ^ mask) for i in range(size)])]
    ppermute x4, waiting for transfers between devices: 12.9 us -> 15.4 us  [the longest x1 8.72 us: split_heads(): lax.ppermute(after(two_own, one_own, one_back), 'tp', [(2, 3), (1, 0)])]
    pallas_call x2 -> x4, Pallas kernels: 7.37 us -> 8.76 us  [the longest x2 4.56 us: project(): pl.pallas_call(functools.partial(proj_kernel, steps, add is not None), ou...]
    ppermute x23, starting transfers between devices: 25.3 us -> 26.7 us  [swap(): return lax.ppermute(x, axis, [(i, i ^ mask) for i in range(size)])]
  transfers between devices with their start and end apart: 27 -> 27, of which waited for: 12 -> 11; matrix products, arithmetic and copies ran while one was open for 5% -> 4% of each run, Pallas kernels for 13% -> 14%
where the time goes in v9:
time: 105 us
  waiting for transfers between devices  49.6 us (47%)
  starting transfers between devices  30.6 us (29%)
  Pallas kernels  18.7 us (18%)
  local copies, waits for them, and re-layouts  5.41 us (5%)
    ppermute x23, waiting for transfers between devices, swap(): return lax.ppermute(x, axis, [(i, i ^ mask) for i in range(size)])  34.2 us
    ppermute x23, starting transfers between devices, swap(): return lax.ppermute(x, axis, [(i, i ^ mask) for i in range(size)])  26.7 us
    ppermute x1, waiting for transfers between devices, split_heads(): lax.ppermute(after(two_own, one_own, one_back), 'tp', [(2, 3), (1, 0)])  8.72 us
    pallas_call x1, Pallas kernels, score(): pl.pallas_call(functools.partial(score_kernel, len(sufs), tuple((p.shape[...  8.18 us
    ppermute x1, waiting for transfers between devices, split_heads(): forward_back = lax.ppermute(two_back, 'tp', [(2, 3), (1, 0)])  6.66 us
    pallas_call x2, Pallas kernels, project(): pl.pallas_call(functools.partial(proj_kernel, steps, add is not None), ou...  4.56 us
    pallas_call x2, Pallas kernels, mix(): pl.pallas_call(functools.partial(mix_kernel, nb, base, tuple((p.shape[0]...  4.2 us
  transfers between devices with their start and end apart: 27, of which 11 were waited for; matrix products, arithmetic and copies ran while one was open for 4% of the time, Pallas kernels for 14%

profile of v9, /device:TPU:0, one launch (start us, length us, event | category | flops | bytes accessed | tf_op | source)
XLA Modules:
  0.0 105.1 jit_solution(309145764793640164)
XLA Ops:
  0.0 1.5 %copy.15 = bf16[512,1,512]{2,0,1:T(8,128)(2,1)S(1)} copy(bf16[512,1,512]{2,1,0:T(2,128)(2,1)} %bitcast.24) | data formatting | bytes 1048576
  2.3 1.0 collective-permute-done
  3.3 2.9 %collective-permute-start.3 = (bf16[2,512,256]{2,1,0:T(8,128)(2,1)S(1)}, bf16[2,512,256]{2,1,0:T(8,128)(2,1)S(1)}, u32[]{:S(2)}, u32[]{:S(2)}) collective-permute-start(bf16[2,512,256]{2,1,0:T(8,128)(2,1)S(1)} %pad_maximum_fusion.1.rest_2_), channel_id=1, source_target_pairs={{0,8},{4,12},{8,0},{12,4},{16,24},{20,28},{24,16},{28,20},{1,9},{5... | collective-permute-start | bytes 1572872 | tf_op jit(solution)/shard_map/ppermute | solution.py:280
  6.2 1.5 %collective-permute-start.4 = (bf16[2,512,256]{2,1,0:T(8,128)(2,1)S(1)}, bf16[2,512,256]{2,1,0:T(8,128)(2,1)S(1)}, u32[]{:S(2)}, u32[]{:S(2)}) collective-permute-start(bf16[2,512,256]{2,1,0:T(8,128)(2,1)S(1)} %pad_maximum_fusion.1.rest_2_), channel_id=1, source_target_pairs={{0,16},{4,20},{8,24},{12,28},{16,0},{20,4},{24,8},{28,12},{1,17},{... | collective-permute-start | bytes 1572872 | tf_op jit(solution)/shard_map/ppermute | solution.py:280
  7.9 1.8 %prepare.1 = (s32[1024,128]{1,0:T(8,128)S(1)}, s32[1024,128]{1,0:T(8,128)S(1)}, bf16[3,512,256]{2,1,0:T(8,128)(2,1)S(1)}, bf16[3,512,256]{2,1,0:T(8,128)(2,1)S(1)}) custom-call(s32[3]{0:T(128)S(1)} %pad_add_fusion.1.where_ref, s32[2,8]{1,0:T(2,128)S(1)} %pad_add_fusion.refs_0_, s32[2,8]{1,0:T(2,128)S(1)} %collective-permute-done.1.refs_1_, ...), custom_call_target="tpu_custom_call" | custom-call | tf_op jit(solution)/shard_map/prepare/pallas_call | solution.py:101
  10.6 1.7 %fusion = (bf16[256,512]{1,0:T(8,128)(2,1)S(1)}, bf16[256,512]{1,0:T(8,128)(2,1)S(1)}, bf16[256,512]{1,0:T(8,128)(2,1)S(1)}) fusion(bf16[512,4096]{1,0:T(8,128)(2,1)} %param.12, u32[]{:T(128)S(6)} %mul.20, u32[]{:T(128)S(6)} %add.17, u32[]{:T(128)S(6)} %add.16, u32[]{:T(128)S(6)} %add.15), kind=kLoop, calls=%fused_computation.18 | loop fusion | bytes 1572880 | tf_op jit(solution)/shard_map/dynamic_slice | solution.py:316
  12.2 1.6 %collective-permute-start.8 = (bf16[256,512]{1,0:T(8,128)(2,1)S(1)}, bf16[256,512]{1,0:T(8,128)(2,1)S(1)}, u32[]{:S(2)}, u32[]{:S(2)}) collective-permute-start(bf16[256,512]{1,0:T(8,128)(2,1)S(1)} %get-tuple-element.63), channel_id=1, source_target_pairs={{0,1},{1,0},{2,3},{3,2},{4,5},{5,4},{6,7},{7,6},{8,9},{9,8},{10,11... | collective-permute-start | bytes 786440 | tf_op jit(solution)/shard_map/ppermute | solution.py:280
  13.9 2.6 %collective-permute-start.9 = (bf16[256,512]{1,0:T(8,128)(2,1)S(1)}, bf16[256,512]{1,0:T(8,128)(2,1)S(1)}, u32[]{:S(2)}, u32[]{:S(2)}) collective-permute-start(bf16[256,512]{1,0:T(8,128)(2,1)S(1)} %get-tuple-element.62), channel_id=1, source_target_pairs={{0,2},{1,3},{2,0},{3,1},{4,6},{5,7},{6,4},{7,5},{8,10},{9,11},{10,... | collective-permute-start | bytes 786440 | tf_op jit(solution)/shard_map/ppermute | solution.py:280
  16.5 1.9 %collective-permute-done.3.rest_3_ = bf16[2,512,256]{2,1,0:T(8,128)(2,1)S(1)} collective-permute-done((bf16[2,512,256]{2,1,0:T(8,128)(2,1)S(1)}, bf16[2,512,256]{2,1,0:T(8,128)(2,1)S(1)}, u32[]{:S(2)}, u32[]{:S(2)}) %collective-permute-start.3) | collective-permute-done | bytes 524320 | tf_op jit(solution)/shard_map/ppermute | solution.py:280
  18.5 1.8 %collective-permute-start.6 = (bf16[1,512,256]{2,1,0:T(8,128)(2,1)S(1)}, bf16[1,512,256]{2,1,0:T(8,128)(2,1)S(1)}, u32[]{:S(2)}, u32[]{:S(2)}) collective-permute-start(bf16[1,512,256]{2,1,0:T(8,128)(2,1)S(1)} %slice.58), channel_id=1, source_target_pairs={{0,16},{4,20},{8,24},{12,28},{16,0},{20,4},{24,8},{28,12},{1,17},{... | collective-permute-start | bytes 786440 | tf_op jit(solution)/shard_map/ppermute | solution.py:280
  20.3 1.6 %collective-permute-start.7 = (bf16[1,512,256]{2,1,0:T(8,128)(2,1)S(1)}, bf16[1,512,256]{2,1,0:T(8,128)(2,1)S(1)}, u32[]{:S(2)}, u32[]{:S(2)}) collective-permute-start(bf16[1,512,256]{2,1,0:T(8,128)(2,1)S(1)} %slice.62), channel_id=1, source_target_pairs={{0,8},{4,12},{8,0},{12,4},{16,24},{20,28},{24,16},{28,20},{1,9},{5... | collective-permute-start | bytes 786440 | tf_op jit(solution)/shard_map/ppermute | solution.py:280
  21.9 1.9 %constant_dynamic-slice_fusion.refs_6_.refs_4_ = bf16[512,1024]{1,0:T(8,128)(2,1)S(1)} fusion(bf16[512,4096]{1,0:T(8,128)(2,1)} %param.12, u32[]{:T(128)S(6)} %mul.21), kind=kLoop, calls=%fused_computation.16 | loop fusion | bytes 2097156 | tf_op jit(solution)/shard_map/dynamic_slice | solution.py:319
  23.8 2.3 %collective-permute-done.8 = bf16[256,512]{1,0:T(8,128)(2,1)S(1)} collective-permute-done((bf16[256,512]{1,0:T(8,128)(2,1)S(1)}, bf16[256,512]{1,0:T(8,128)(2,1)S(1)}, u32[]{:S(2)}, u32[]{:S(2)}) %collective-permute-start.8) | collective-permute-done | bytes 262176 | tf_op jit(solution)/shard_map/ppermute | solution.py:280
  26.0 2.4 %collective-permute-done.9 = bf16[256,512]{1,0:T(8,128)(2,1)S(1)} collective-permute-done((bf16[256,512]{1,0:T(8,128)(2,1)S(1)}, bf16[256,512]{1,0:T(8,128)(2,1)S(1)}, u32[]{:S(2)}, u32[]{:S(2)}) %collective-permute-start.9) | collective-permute-done | bytes 262176 | tf_op jit(solution)/shard_map/ppermute | solution.py:280
  29.6 3.6 %collective-permute-start.12 = (bf16[256,512]{1,0:T(8,128)(2,1)S(1)}, bf16[256,512]{1,0:T(8,128)(2,1)S(1)}, u32[]{:S(2)}, u32[]{:S(2)}) collective-permute-start(bf16[256,512]{1,0:T(8,128)(2,1)S(1)} %get-tuple-element.53), channel_id=1, source_target_pairs={{0,3},{1,2},{2,1},{3,0},{4,7},{5,6},{6,5},{7,4},{8,11},{9,10},{10,... | collective-permute-start | bytes 786440 | tf_op jit(solution)/shard_map/ppermute | solution.py:280
  33.3 8.2 %score.1 = (bf16[1024,1024]{1,0:T(8,128)(2,1)S(1)}, bf16[1024,256]{1,0:T(8,128)(2,1)S(1)}, f32[1024,128]{1,0:T(8,128)S(1)}) custom-call(s32[8]{0:T(128)S(1)} %select_reduce_fusion.place_ref, s32[1024,128]{1,0:T(8,128)S(1)} %get-tuple-element.37.first_ref, s32[1024,128]{1,0:T(8,128)S(1)} %get-tuple-element.36.grp_ref, ...), custom_call_target="tpu_custom_call" | custom-call | tf_op jit(solution)/shard_map/score/pallas_call | solution.py:176
  41.7 1.6 %collective-permute-start.13 = (bf16[1,512,256]{2,1,0:T(8,128)(2,1)S(1)}, bf16[1,512,256]{2,1,0:T(8,128)(2,1)S(1)}, u32[]{:S(2)}, u32[]{:S(2)}) collective-permute-start(bf16[1,512,256]{2,1,0:T(8,128)(2,1)S(1)} %slice.63), channel_id=1, source_target_pairs={{0,16},{4,20},{8,24},{12,28},{16,0},{20,4},{24,8},{28,12},{1,17},{... | collective-permute-start | bytes 786440 | tf_op jit(solution)/shard_map/ppermute | solution.py:280
  43.9 4.2 %collective-permute-done.13.rest_4_ = bf16[1,512,256]{2,1,0:T(8,128)(2,1)S(1)} collective-permute-done((bf16[1,512,256]{2,1,0:T(8,128)(2,1)S(1)}, bf16[1,512,256]{2,1,0:T(8,128)(2,1)S(1)}, u32[]{:S(2)}, u32[]{:S(2)}) %collective-permute-start.13) | collective-permute-done | bytes 262176 | tf_op jit(solution)/shard_map/ppermute | solution.py:280
  48.1 1.6 %collective-permute-done.14.rest_5_ = bf16[1,512,256]{2,1,0:T(8,128)(2,1)S(1)} collective-permute-done((bf16[1,512,256]{2,1,0:T(8,128)(2,1)S(1)}, bf16[1,512,256]{2,1,0:T(8,128)(2,1)S(1)}, u32[]{:S(2)}, u32[]{:S(2)}) %collective-permute-start.14) | collective-permute-done | bytes 262176 | tf_op jit(solution)/shard_map/ppermute | solution.py:280
  49.7 2.2 %mix.3 = bf16[512,256]{1,0:T(8,128)(2,1)S(1)} custom-call(s32[8]{0:T(128)S(1)} %select_reduce_fusion.place_ref, s32[1024,128]{1,0:T(8,128)S(1)} %get-tuple-element.36.grp_ref, bf16[1024,1024]{1,0:T(8,128)(2,1)S(1)} %get-tuple-element.43.p_ref, bf16[1024,256]{1,0:T(8,128)(2,1)S(1)} %get-tuple-element.44.near_ref, f32[1024,128]{1,0:T(8,128)S(1)} %get-tuple-element.45.den_ref, ...), custom_call_target="tpu_custom_call" | custom-call | tf_op jit(solution)/shard_map/mix/pallas_call | solution.py:225
  52.6 2.0 %mix.2.refs_0_ = bf16[512,256]{1,0:T(8,128)(2,1)S(1)} custom-call(s32[8]{0:T(128)S(1)} %select_reduce_fusion.place_ref, s32[1024,128]{1,0:T(8,128)S(1)} %get-tuple-element.36.grp_ref, bf16[1024,1024]{1,0:T(8,128)(2,1)S(1)} %get-tuple-element.43.p_ref, bf16[1024,256]{1,0:T(8,128)(2,1)S(1)} %get-tuple-element.44.near_ref, ...), custom_call_target="tpu_custom_call" | custom-call | tf_op jit(solution)/shard_map/mix/pallas_call | solution.py:225
  54.6 2.1 %collective-permute-start.15 = (bf16[512,256]{1,0:T(8,128)(2,1)S(1)}, bf16[512,256]{1,0:T(8,128)(2,1)S(1)}, u32[]{:S(2)}, u32[]{:S(2)}) collective-permute-start(bf16[512,256]{1,0:T(8,128)(2,1)S(1)} %mix.2.refs_0_), channel_id=1, source_target_pairs={{0,2},{1,3},{2,0},{3,1},{4,6},{5,7},{6,4},{7,5},{8,10},{9,11},{10,... | collective-permute-start | bytes 786440 | tf_op jit(solution)/shard_map/ppermute | solution.py:280
  56.7 1.1 %collective-permute-start.16 = (bf16[512,256]{1,0:T(8,128)(2,1)S(1)}, bf16[512,256]{1,0:T(8,128)(2,1)S(1)}, u32[]{:S(2)}, u32[]{:S(2)}) collective-permute-start(bf16[512,256]{1,0:T(8,128)(2,1)S(1)} %mix.2.refs_0_), channel_id=1, source_target_pairs={{0,1},{1,0},{2,3},{3,2},{4,5},{5,4},{6,7},{7,6},{8,9},{9,8},{10,11... | collective-permute-start | bytes 786440 | tf_op jit(solution)/shard_map/ppermute | solution.py:280
  58.7 1.5 %collective-permute-start.21 = (bf16[512,256]{1,0:T(8,128)(2,1)S(1)}, bf16[512,256]{1,0:T(8,128)(2,1)S(1)}, u32[]{:S(2)}, u32[]{:S(2)}) collective-permute-start(bf16[512,256]{1,0:T(8,128)(2,1)S(1)} %collective-permute-done.17.refs_3_), channel_id=1, source_target_pairs={{0,2},{1,3},{2,0},{3,1},{4,6},{5,7},{6,4},{7,5},{8,10},{9,11},{10,... | collective-permute-start | bytes 786440 | tf_op jit(solution)/shard_map/ppermute | solution.py:280
  60.2 10.2 %collective-permute-done.15.refs_2_ = bf16[512,256]{1,0:T(8,128)(2,1)S(1)} collective-permute-done((bf16[512,256]{1,0:T(8,128)(2,1)S(1)}, bf16[512,256]{1,0:T(8,128)(2,1)S(1)}, u32[]{:S(2)}, u32[]{:S(2)}) %collective-permute-start.15) | collective-permute-done | bytes 262176 | tf_op jit(solution)/shard_map/ppermute | solution.py:280
  70.4 10.4 %collective-permute-done.18.refs_4_ = bf16[512,256]{1,0:T(8,128)(2,1)S(1)} collective-permute-done((bf16[512,256]{1,0:T(8,128)(2,1)S(1)}, bf16[512,256]{1,0:T(8,128)(2,1)S(1)}, u32[]{:S(2)}, u32[]{:S(2)}) %collective-permute-start.18) | collective-permute-done | bytes 262176 | tf_op jit(solution)/shard_map/ppermute | solution.py:280
  81.4 1.3 %collective-permute-start.20 = (bf16[512,256]{1,0:T(8,128)(2,1)S(1)}, bf16[512,256]{1,0:T(8,128)(2,1)S(1)}, u32[]{:S(2)}, u32[]{:S(2)}) collective-permute-start(bf16[512,256]{1,0:T(8,128)(2,1)S(1)} %collective-permute-done.15.refs_2_), channel_id=1, source_target_pairs={{2,3},{1,0},{6,7},{5,4},{10,11},{9,8},{14,15},{13,12},{18,19},{17,... | collective-permute-start | bytes 786440 | tf_op jit(solution)/shard_map/ppermute | solution.py:365
  82.8 8.7 %collective-permute-done.20.refs_1_ = bf16[512,256]{1,0:T(8,128)(2,1)S(1)} collective-permute-done((bf16[512,256]{1,0:T(8,128)(2,1)S(1)}, bf16[512,256]{1,0:T(8,128)(2,1)S(1)}, u32[]{:S(2)}, u32[]{:S(2)}) %collective-permute-start.20) | collective-permute-done | bytes 262176 | tf_op jit(solution)/shard_map/ppermute | solution.py:365
  92.2 1.3 %collective-permute-start.23 = (bf16[512,256]{1,0:T(8,128)(2,1)S(1)}, bf16[512,256]{1,0:T(8,128)(2,1)S(1)}, u32[]{:S(2)}, u32[]{:S(2)}) collective-permute-start(bf16[512,256]{1,0:T(8,128)(2,1)S(1)} %collective-permute-done.21.refs_5_), channel_id=1, source_target_pairs={{2,3},{1,0},{6,7},{5,4},{10,11},{9,8},{14,15},{13,12},{18,19},{17,... | collective-permute-start | bytes 786440 | tf_op jit(solution)/shard_map/ppermute | solution.py:367
  93.8 2.3 %project.2.refs_9_ = f32[512,1024]{1,0:T(8,128)S(1)} custom-call(s32[3]{0:T(128)S(1)} %pad_add_fusion.1.where_ref, bf16[512,256]{1,0:T(8,128)(2,1)S(1)} %mix.2.refs_0_, bf16[512,256]{1,0:T(8,128)(2,1)S(1)} %collective-permute-done.16.refs_1_, bf16[512,256]{1,0:T(8,128)(2,1)S(1)} %collective-permute-done.15.refs_2_, ...), custom_call_target="tpu_custom_call" | custom-call | tf_op jit(solution)/shard_map/project/pallas_call | solution.py:269
  96.2 6.7 %collective-permute-done.23.refs_3_ = bf16[512,256]{1,0:T(8,128)(2,1)S(1)} collective-permute-done((bf16[512,256]{1,0:T(8,128)(2,1)S(1)}, bf16[512,256]{1,0:T(8,128)(2,1)S(1)}, u32[]{:S(2)}, u32[]{:S(2)}) %collective-permute-start.23) | collective-permute-done | bytes 262176 | tf_op jit(solution)/shard_map/ppermute | solution.py:367
  102.8 2.2 %project.3 = bf16[512,1024]{1,0:T(8,128)(2,1)} custom-call(s32[3]{0:T(128)S(1)} %pad_add_fusion.1.where_ref, bf16[512,256]{1,0:T(8,128)(2,1)S(1)} %collective-permute-done.19.refs_0_, bf16[512,256]{1,0:T(8,128)(2,1)S(1)} %collective-permute-done.20.refs_1_, bf16[512,256]{1,0:T(8,128)(2,1)S(1)} %collective-permute-done.22.refs_2_, ...), custom_call_target="tpu_custom_call" | custom-call | tf_op jit(solution)/shard_map/project/pallas_call | solution.py:269
  (60 shorter events, 7.2 us)
Async XLA Ops:
  0.0 2.1 %copy-start.5 = (s32[1,8]{1,0:T(1,128)S(1)}, s32[1,8]{1,0:T(1,128)}, u32[]{:S(2)}) copy-start(s32[1,8]{1,0:T(1,128)} %param.9) | copy-start | bytes 100
  0.0 7.7 %copy-start.2 = (bf16[512,3,512]{2,0,1:T(8,128)(2,1)S(1)}, bf16[512,3,512]{2,0,1:T(8,128)(2,1)}, u32[]{:S(2)}) copy-start(bf16[512,3,512]{2,0,1:T(8,128)(2,1)} %param.7) | copy-start | bytes 4718596
  1.5 1.7 %collective-permute-start = (bf16[512,256]{1,0:T(8,128)(2,1)S(1)}, bf16[512,256]{1,0:T(8,128)(2,1)S(1)}, u32[]{:S(2)}, u32[]{:S(2)}) collective-permute-start(bf16[512,256]{1,0:T(8,128)(2,1)S(1)} %get-tuple-element.70), channel_id=1, source_target_pairs={{0,4},{4,0},{8,12},{12,8},{16,20},{20,16},{24,28},{28,24},{1,5},{5... | collective-permute-start | bytes 786440 | tf_op jit(solution)/shard_map/ppermute | solution.py:280
  2.1 5.8 %collective-permute-start.1 = (s32[2,8]{1,0:T(2,128)S(1)}, s32[2,8]{1,0:T(2,128)S(1)}, u32[]{:S(2)}, u32[]{:S(2)}) collective-permute-start(s32[2,8]{1,0:T(2,128)S(1)} %pad_add_fusion.refs_0_), channel_id=1, source_target_pairs={{0,4},{4,0},{8,12},{12,8},{16,20},{20,16},{24,28},{28,24},{1,5},{5... | collective-permute-start | bytes 200 | tf_op jit(solution)/shard_map/ppermute | solution.py:280
  3.2 4.6 %copy-start = (f32[128,256]{1,0:T(8,128)S(1)}, f32[128,256]{1,0:T(8,128)}, u32[]{:S(2)}) copy-start(f32[128,256]{1,0:T(8,128)} %constant.28.clone.refs_5_) | copy-start | bytes 393220
  3.3 6.5 %copy-start.1 = (bf16[512,2,512]{2,1,0:T(2,128)(2,1)S(1)}, bf16[512,2,512]{2,1,0:T(2,128)(2,1)}, u32[]{:S(2)}) copy-start(bf16[512,2,512]{2,1,0:T(2,128)(2,1)} %param.8) | copy-start | bytes 3145732
  3.3 15.2 %collective-permute-start.3 = (bf16[2,512,256]{2,1,0:T(8,128)(2,1)S(1)}, bf16[2,512,256]{2,1,0:T(8,128)(2,1)S(1)}, u32[]{:S(2)}, u32[]{:S(2)}) collective-permute-start(bf16[2,512,256]{2,1,0:T(8,128)(2,1)S(1)} %pad_maximum_fusion.1.rest_2_), channel_id=1, source_target_pairs={{0,8},{4,12},{8,0},{12,4},{16,24},{20,28},{24,16},{28,20},{1,9},{5... | collective-permute-start | bytes 1572872 | tf_op jit(solution)/shard_map/ppermute | solution.py:280
  6.2 14.1 %collective-permute-start.4 = (bf16[2,512,256]{2,1,0:T(8,128)(2,1)S(1)}, bf16[2,512,256]{2,1,0:T(8,128)(2,1)S(1)}, u32[]{:S(2)}, u32[]{:S(2)}) collective-permute-start(bf16[2,512,256]{2,1,0:T(8,128)(2,1)S(1)} %pad_maximum_fusion.1.rest_2_), channel_id=1, source_target_pairs={{0,16},{4,20},{8,24},{12,28},{16,0},{20,4},{24,8},{28,12},{1,17},{... | collective-permute-start | bytes 1572872 | tf_op jit(solution)/shard_map/ppermute | solution.py:280
  9.7 18.7 %collective-permute-start.2 = (bf16[3,512,256]{2,1,0:T(8,128)(2,1)S(1)}, bf16[3,512,256]{2,1,0:T(8,128)(2,1)S(1)}, u32[]{:S(2)}, u32[]{:S(2)}) collective-permute-start(bf16[3,512,256]{2,1,0:T(8,128)(2,1)S(1)} %get-tuple-element.39), channel_id=1, source_target_pairs={{0,4},{4,0},{8,12},{12,8},{16,20},{20,16},{24,28},{28,24},{1,5},{5... | collective-permute-start | bytes 2359304 | tf_op jit(solution)/shard_map/ppermute | solution.py:280
  10.0 3.9 %collective-permute-start.5 = (bf16[512,256]{1,0:T(8,128)(2,1)S(1)}, bf16[512,256]{1,0:T(8,128)(2,1)S(1)}, u32[]{:S(2)}, u32[]{:S(2)}) collective-permute-start(bf16[512,256]{1,0:T(8,128)(2,1)S(1)} %get-tuple-element.68), channel_id=1, source_target_pairs={{0,4},{4,0},{8,12},{12,8},{16,20},{20,16},{24,28},{28,24},{1,5},{5... | collective-permute-start | bytes 786440 | tf_op jit(solution)/shard_map/ppermute | solution.py:280
  12.2 13.8 %collective-permute-start.8 = (bf16[256,512]{1,0:T(8,128)(2,1)S(1)}, bf16[256,512]{1,0:T(8,128)(2,1)S(1)}, u32[]{:S(2)}, u32[]{:S(2)}) collective-permute-start(bf16[256,512]{1,0:T(8,128)(2,1)S(1)} %get-tuple-element.63), channel_id=1, source_target_pairs={{0,1},{1,0},{2,3},{3,2},{4,5},{5,4},{6,7},{7,6},{8,9},{9,8},{10,11... | collective-permute-start | bytes 786440 | tf_op jit(solution)/shard_map/ppermute | solution.py:280
  13.9 14.5 %collective-permute-start.9 = (bf16[256,512]{1,0:T(8,128)(2,1)S(1)}, bf16[256,512]{1,0:T(8,128)(2,1)S(1)}, u32[]{:S(2)}, u32[]{:S(2)}) collective-permute-start(bf16[256,512]{1,0:T(8,128)(2,1)S(1)} %get-tuple-element.62), channel_id=1, source_target_pairs={{0,2},{1,3},{2,0},{3,1},{4,6},{5,7},{6,4},{7,5},{8,10},{9,11},{10,... | collective-permute-start | bytes 786440 | tf_op jit(solution)/shard_map/ppermute | solution.py:280
  16.5 16.8 %copy-start.3 = (s32[4,2]{0,1:T(2,128)S(1)}, s32[4,2]{0,1:T(2,128)}, u32[]{:S(2)}) copy-start(s32[4,2]{0,1:T(2,128)} %param.11) | copy-start | bytes 100
  18.5 9.9 %collective-permute-start.6 = (bf16[1,512,256]{2,1,0:T(8,128)(2,1)S(1)}, bf16[1,512,256]{2,1,0:T(8,128)(2,1)S(1)}, u32[]{:S(2)}, u32[]{:S(2)}) collective-permute-start(bf16[1,512,256]{2,1,0:T(8,128)(2,1)S(1)} %slice.58), channel_id=1, source_target_pairs={{0,16},{4,20},{8,24},{12,28},{16,0},{20,4},{24,8},{28,12},{1,17},{... | collective-permute-start | bytes 786440 | tf_op jit(solution)/shard_map/ppermute | solution.py:280
  20.3 8.1 %collective-permute-start.7 = (bf16[1,512,256]{2,1,0:T(8,128)(2,1)S(1)}, bf16[1,512,256]{2,1,0:T(8,128)(2,1)S(1)}, u32[]{:S(2)}, u32[]{:S(2)}) collective-permute-start(bf16[1,512,256]{2,1,0:T(8,128)(2,1)S(1)} %slice.62), channel_id=1, source_target_pairs={{0,8},{4,12},{8,0},{12,4},{16,24},{20,28},{24,16},{28,20},{1,9},{5... | collective-permute-start | bytes 786440 | tf_op jit(solution)/shard_map/ppermute | solution.py:280
  28.4 13.2 %collective-permute-start.10 = (bf16[2,512,256]{2,1,0:T(8,128)(2,1)S(1)}, bf16[2,512,256]{2,1,0:T(8,128)(2,1)S(1)}, u32[]{:S(2)}, u32[]{:S(2)}) collective-permute-start(bf16[2,512,256]{2,1,0:T(8,128)(2,1)S(1)} %pad_maximum_fusion.2.rest_1_), channel_id=1, source_target_pairs={{0,8},{4,12},{8,0},{12,4},{16,24},{20,28},{24,16},{28,20},{1,9},{5... | collective-permute-start | bytes 1572872 | tf_op jit(solution)/shard_map/ppermute | solution.py:280
  29.1 14.1 %collective-permute-start.11 = (bf16[2,512,256]{2,1,0:T(8,128)(2,1)S(1)}, bf16[2,512,256]{2,1,0:T(8,128)(2,1)S(1)}, u32[]{:S(2)}, u32[]{:S(2)}) collective-permute-start(bf16[2,512,256]{2,1,0:T(8,128)(2,1)S(1)} %pad_maximum_fusion.2.rest_1_), channel_id=1, source_target_pairs={{0,16},{4,20},{8,24},{12,28},{16,0},{20,4},{24,8},{28,12},{1,17},{... | collective-permute-start | bytes 1572872 | tf_op jit(solution)/shard_map/ppermute | solution.py:280
  29.6 11.9 %collective-permute-start.12 = (bf16[256,512]{1,0:T(8,128)(2,1)S(1)}, bf16[256,512]{1,0:T(8,128)(2,1)S(1)}, u32[]{:S(2)}, u32[]{:S(2)}) collective-permute-start(bf16[256,512]{1,0:T(8,128)(2,1)S(1)} %get-tuple-element.53), channel_id=1, source_target_pairs={{0,3},{1,2},{2,1},{3,0},{4,7},{5,6},{6,5},{7,4},{8,11},{9,10},{10,... | collective-permute-start | bytes 786440 | tf_op jit(solution)/shard_map/ppermute | solution.py:280
  41.7 6.4 %collective-permute-start.13 = (bf16[1,512,256]{2,1,0:T(8,128)(2,1)S(1)}, bf16[1,512,256]{2,1,0:T(8,128)(2,1)S(1)}, u32[]{:S(2)}, u32[]{:S(2)}) collective-permute-start(bf16[1,512,256]{2,1,0:T(8,128)(2,1)S(1)} %slice.63), channel_id=1, source_target_pairs={{0,16},{4,20},{8,24},{12,28},{16,0},{20,4},{24,8},{28,12},{1,17},{... | collective-permute-start | bytes 786440 | tf_op jit(solution)/shard_map/ppermute | solution.py:280
  43.3 6.4 %collective-permute-start.14 = (bf16[1,512,256]{2,1,0:T(8,128)(2,1)S(1)}, bf16[1,512,256]{2,1,0:T(8,128)(2,1)S(1)}, u32[]{:S(2)}, u32[]{:S(2)}) collective-permute-start(bf16[1,512,256]{2,1,0:T(8,128)(2,1)S(1)} %slice.64), channel_id=1, source_target_pairs={{0,8},{4,12},{8,0},{12,4},{16,24},{20,28},{24,16},{28,20},{1,9},{5... | collective-permute-start | bytes 786440 | tf_op jit(solution)/shard_map/ppermute | solution.py:280
  51.9 5.9 %collective-permute-start.17 = (bf16[512,256]{1,0:T(8,128)(2,1)S(1)}, bf16[512,256]{1,0:T(8,128)(2,1)S(1)}, u32[]{:S(2)}, u32[]{:S(2)}) collective-permute-start(bf16[512,256]{1,0:T(8,128)(2,1)S(1)} %mix.3), channel_id=1, source_target_pairs={{0,4},{4,0},{8,12},{12,8},{16,20},{20,16},{24,28},{28,24},{1,5},{5... | collective-permute-start | bytes 786440 | tf_op jit(solution)/shard_map/ppermute | solution.py:280
  52.0 39.6 %collective-permute-start.24 = (bf16[3,256,512]{2,1,0:T(8,128)(2,1)S(1)}, bf16[3,256,512]{2,1,0:T(8,128)(2,1)S(1)}, u32[]{:S(2)}, u32[]{:S(2)}) collective-permute-start(bf16[3,256,512]{2,1,0:T(8,128)(2,1)S(1)} %pad_maximum_fusion.refs_7_.refs_5_), channel_id=1, source_target_pairs={{0,8},{4,12},{8,0},{12,4},{16,24},{20,28},{24,16},{28,20},{1,9},{5... | collective-permute-start | bytes 2359304 | tf_op jit(solution)/shard_map/ppermute | solution.py:280
  54.6 15.8 %collective-permute-start.15 = (bf16[512,256]{1,0:T(8,128)(2,1)S(1)}, bf16[512,256]{1,0:T(8,128)(2,1)S(1)}, u32[]{:S(2)}, u32[]{:S(2)}) collective-permute-start(bf16[512,256]{1,0:T(8,128)(2,1)S(1)} %mix.2.refs_0_), channel_id=1, source_target_pairs={{0,2},{1,3},{2,0},{3,1},{4,6},{5,7},{6,4},{7,5},{8,10},{9,11},{10,... | collective-permute-start | bytes 786440 | tf_op jit(solution)/shard_map/ppermute | solution.py:280
  56.7 13.7 %collective-permute-start.16 = (bf16[512,256]{1,0:T(8,128)(2,1)S(1)}, bf16[512,256]{1,0:T(8,128)(2,1)S(1)}, u32[]{:S(2)}, u32[]{:S(2)}) collective-permute-start(bf16[512,256]{1,0:T(8,128)(2,1)S(1)} %mix.2.refs_0_), channel_id=1, source_target_pairs={{0,1},{1,0},{2,3},{3,2},{4,5},{5,4},{6,7},{7,6},{8,9},{9,8},{10,11... | collective-permute-start | bytes 786440 | tf_op jit(solution)/shard_map/ppermute | solution.py:280
  57.8 22.9 %collective-permute-start.18 = (bf16[512,256]{1,0:T(8,128)(2,1)S(1)}, bf16[512,256]{1,0:T(8,128)(2,1)S(1)}, u32[]{:S(2)}, u32[]{:S(2)}) collective-permute-start(bf16[512,256]{1,0:T(8,128)(2,1)S(1)} %collective-permute-done.17.refs_3_), channel_id=1, source_target_pairs={{0,1},{1,0},{2,3},{3,2},{4,5},{5,4},{6,7},{7,6},{8,9},{9,8},{10,11... | collective-permute-start | bytes 786440 | tf_op jit(solution)/shard_map/ppermute | solution.py:280
  58.7 24.1 %collective-permute-start.21 = (bf16[512,256]{1,0:T(8,128)(2,1)S(1)}, bf16[512,256]{1,0:T(8,128)(2,1)S(1)}, u32[]{:S(2)}, u32[]{:S(2)}) collective-permute-start(bf16[512,256]{1,0:T(8,128)(2,1)S(1)} %collective-permute-done.17.refs_3_), channel_id=1, source_target_pairs={{0,2},{1,3},{2,0},{3,1},{4,6},{5,7},{6,4},{7,5},{8,10},{9,11},{10,... | collective-permute-start | bytes 786440 | tf_op jit(solution)/shard_map/ppermute | solution.py:280
  80.8 2.1 %collective-permute-start.19 = (bf16[512,256]{1,0:T(8,128)(2,1)S(1)}, bf16[512,256]{1,0:T(8,128)(2,1)S(1)}, u32[]{:S(2)}, u32[]{:S(2)}) collective-permute-start(bf16[512,256]{1,0:T(8,128)(2,1)S(1)} %mix.2.refs_0_), channel_id=1, source_target_pairs={{1,2},{2,1},{5,6},{6,5},{9,10},{10,9},{13,14},{14,13},{17,18},{18,... | collective-permute-start | bytes 786440 | tf_op jit(solution)/shard_map/ppermute | solution.py:364
  81.4 10.1 %collective-permute-start.20 = (bf16[512,256]{1,0:T(8,128)(2,1)S(1)}, bf16[512,256]{1,0:T(8,128)(2,1)S(1)}, u32[]{:S(2)}, u32[]{:S(2)}) collective-permute-start(bf16[512,256]{1,0:T(8,128)(2,1)S(1)} %collective-permute-done.15.refs_2_), channel_id=1, source_target_pairs={{2,3},{1,0},{6,7},{5,4},{10,11},{9,8},{14,15},{13,12},{18,19},{17,... | collective-permute-start | bytes 786440 | tf_op jit(solution)/shard_map/ppermute | solution.py:365
  82.7 10.8 %collective-permute-start.25 = (bf16[3,256,512]{2,1,0:T(8,128)(2,1)S(1)}, bf16[3,256,512]{2,1,0:T(8,128)(2,1)S(1)}, u32[]{:S(2)}, u32[]{:S(2)}) collective-permute-start(bf16[3,256,512]{2,1,0:T(8,128)(2,1)S(1)} %pad_maximum_fusion.refs_7_.refs_5_), channel_id=1, source_target_pairs={{0,4},{4,0},{8,12},{12,8},{16,20},{20,16},{24,28},{28,24},{1,5},{5... | collective-permute-start | bytes 2359304 | tf_op jit(solution)/shard_map/ppermute | solution.py:280
  91.6 2.3 %collective-permute-start.26 = (bf16[3,256,512]{2,1,0:T(8,128)(2,1)S(1)}, bf16[3,256,512]{2,1,0:T(8,128)(2,1)S(1)}, u32[]{:S(2)}, u32[]{:S(2)}) collective-permute-start(bf16[3,256,512]{2,1,0:T(8,128)(2,1)S(1)} %collective-permute-done.24.refs_8_.refs_6_), channel_id=1, source_target_pairs={{0,4},{4,0},{8,12},{12,8},{16,20},{20,16},{24,28},{28,24},{1,5},{5... | collective-permute-start | bytes 2359304 | tf_op jit(solution)/shard_map/ppermute | solution.py:280
  91.6 4.6 %collective-permute-start.22 = (bf16[512,256]{1,0:T(8,128)(2,1)S(1)}, bf16[512,256]{1,0:T(8,128)(2,1)S(1)}, u32[]{:S(2)}, u32[]{:S(2)}) collective-permute-start(bf16[512,256]{1,0:T(8,128)(2,1)S(1)} %collective-permute-done.17.refs_3_), channel_id=1, source_target_pairs={{1,2},{2,1},{5,6},{6,5},{9,10},{10,9},{13,14},{14,13},{17,18},{18,... | collective-permute-start | bytes 786440 | tf_op jit(solution)/shard_map/ppermute | solution.py:366
  92.2 10.6 %collective-permute-start.23 = (bf16[512,256]{1,0:T(8,128)(2,1)S(1)}, bf16[512,256]{1,0:T(8,128)(2,1)S(1)}, u32[]{:S(2)}, u32[]{:S(2)}) collective-permute-start(bf16[512,256]{1,0:T(8,128)(2,1)S(1)} %collective-permute-done.21.refs_5_), channel_id=1, source_target_pairs={{2,3},{1,0},{6,7},{5,4},{10,11},{9,8},{14,15},{13,12},{18,19},{17,... | collective-permute-start | bytes 786440 | tf_op jit(solution)/shard_map/ppermute | solution.py:367
  (1 other events, 2.1 us)

commit v10 on v9

--- a/solution.py
+++ b/solution.py
@@ -359,11 +359,12 @@
     back = over_core(pair)
     two_own = swap(own, "tp", 2, tp_size)
     one_own = swap(own, "tp", 1, tp_size)
-    two_back = swap(back, "tp", 2, tp_size)
-    one_back = swap(back, "tp", 1, tp_size)
-    three_own = lax.ppermute(after(own, two_own, one_own, one_back), "tp", [(1, 2), (2, 1)])
-    forward_own = lax.ppermute(after(two_own, one_own, one_back), "tp", [(2, 3), (1, 0)])
-    three_back = lax.ppermute(after(back, two_back, one_back), "tp", [(1, 2), (2, 1)])
+    later = after(back, two_own, one_own)
+    two_back = swap(later, "tp", 2, tp_size)
+    one_back = swap(later, "tp", 1, tp_size)
+    three_own = lax.ppermute(after(own, two_own), "tp", [(1, 2), (2, 1)])
+    forward_own = lax.ppermute(two_own, "tp", [(2, 3), (1, 0)])
+    three_back = lax.ppermute(after(later, two_back), "tp", [(1, 2), (2, 1)])
     forward_back = lax.ppermute(two_back, "tp", [(2, 3), (1, 0)])
     w_core_x = over_core(after(w_x, two_back, one_back, three_own, forward_own))
     far = [w_far, w_x, w_core, w_core_x]

time: 105 us -> 104 us (level)
  waiting for transfers between devices: 49.6 us -> 46 us
  starting transfers between devices: 30.6 us -> 32.7 us
    ppermute x23, waiting for transfers between devices: 34.2 us -> 31.5 us  [swap(): return lax.ppermute(x, axis, [(i, i ^ mask) for i in range(size)])]
    ppermute x23, starting transfers between devices: 26.7 us -> 28.8 us  [swap(): return lax.ppermute(x, axis, [(i, i ^ mask) for i in range(size)])]
  transfers between devices with their start and end apart: 27 -> 27, of which waited for: 11 -> 13; matrix products, arithmetic and copies ran while one was open for 4% -> 4% of each run, Pallas kernels for 14% -> 16%
where the time goes in v10:
time: 104 us
  waiting for transfers between devices  46 us (44%)
  starting transfers between devices  32.7 us (31%)
  Pallas kernels  18.8 us (18%)
  local copies, waits for them, and re-layouts  5.41 us (5%)
    ppermute x23, waiting for transfers between devices, swap(): return lax.ppermute(x, axis, [(i, i ^ mask) for i in range(size)])  31.5 us
    ppermute x23, starting transfers between devices, swap(): return lax.ppermute(x, axis, [(i, i ^ mask) for i in range(size)])  28.8 us
    pallas_call x1, Pallas kernels, score(): pl.pallas_call(functools.partial(score_kernel, len(sufs), tuple((p.shape[...  8.18 us
    ppermute x1, waiting for transfers between devices, split_heads(): forward_own = lax.ppermute(two_own, 'tp', [(2, 3), (1, 0)])  7.77 us
    ppermute x1, waiting for transfers between devices, split_heads(): forward_back = lax.ppermute(two_back, 'tp', [(2, 3), (1, 0)])  6.66 us
    pallas_call x2, Pallas kernels, project(): pl.pallas_call(functools.partial(proj_kernel, steps, add is not None), ou...  4.57 us
    pallas_call x2, Pallas kernels, mix(): pl.pallas_call(functools.partial(mix_kernel, nb, base, tuple((p.shape[0]...  4.23 us
  transfers between devices with their start and end apart: 27, of which 13 were waited for; matrix products, arithmetic and copies ran while one was open for 4% of the time, Pallas kernels for 16%

profile of v10, /device:TPU:0, one launch (start us, length us, event | category | flops | bytes accessed | tf_op | source)
XLA Modules:
  0.0 103.6 jit_solution(7565252336813796914)
XLA Ops:
  0.0 1.5 %copy.15 = bf16[512,1,512]{2,0,1:T(8,128)(2,1)S(1)} copy(bf16[512,1,512]{2,1,0:T(2,128)(2,1)} %bitcast.24) | data formatting | bytes 1048576
  3.3 2.9 %collective-permute-start.3 = (bf16[2,512,256]{2,1,0:T(8,128)(2,1)S(1)}, bf16[2,512,256]{2,1,0:T(8,128)(2,1)S(1)}, u32[]{:S(2)}, u32[]{:S(2)}) collective-permute-start(bf16[2,512,256]{2,1,0:T(8,128)(2,1)S(1)} %pad_maximum_fusion.1.rest_2_), channel_id=1, source_target_pairs={{0,8},{4,12},{8,0},{12,4},{16,24},{20,28},{24,16},{28,20},{1,9},{5... | collective-permute-start | bytes 1572872 | tf_op jit(solution)/shard_map/ppermute | solution.py:280
  6.2 1.5 %collective-permute-start.4 = (bf16[2,512,256]{2,1,0:T(8,128)(2,1)S(1)}, bf16[2,512,256]{2,1,0:T(8,128)(2,1)S(1)}, u32[]{:S(2)}, u32[]{:S(2)}) collective-permute-start(bf16[2,512,256]{2,1,0:T(8,128)(2,1)S(1)} %pad_maximum_fusion.1.rest_2_), channel_id=1, source_target_pairs={{0,16},{4,20},{8,24},{12,28},{16,0},{20,4},{24,8},{28,12},{1,17},{... | collective-permute-start | bytes 1572872 | tf_op jit(solution)/shard_map/ppermute | solution.py:280
  7.9 1.8 %prepare.1 = (s32[1024,128]{1,0:T(8,128)S(1)}, s32[1024,128]{1,0:T(8,128)S(1)}, bf16[3,512,256]{2,1,0:T(8,128)(2,1)S(1)}, bf16[3,512,256]{2,1,0:T(8,128)(2,1)S(1)}) custom-call(s32[3]{0:T(128)S(1)} %pad_add_fusion.1.where_ref, s32[2,8]{1,0:T(2,128)S(1)} %pad_add_fusion.refs_0_, s32[2,8]{1,0:T(2,128)S(1)} %collective-permute-done.1.refs_1_, ...), custom_call_target="tpu_custom_call" | custom-call | tf_op jit(solution)/shard_map/prepare/pallas_call | solution.py:101
  10.6 1.7 %fusion = (bf16[256,512]{1,0:T(8,128)(2,1)S(1)}, bf16[256,512]{1,0:T(8,128)(2,1)S(1)}, bf16[256,512]{1,0:T(8,128)(2,1)S(1)}) fusion(bf16[512,4096]{1,0:T(8,128)(2,1)} %param.12, u32[]{:T(128)S(6)} %mul.20, u32[]{:T(128)S(6)} %add.17, u32[]{:T(128)S(6)} %add.16, u32[]{:T(128)S(6)} %add.15), kind=kLoop, calls=%fused_computation.18 | loop fusion | bytes 1572880 | tf_op jit(solution)/shard_map/dynamic_slice | solution.py:316
  12.2 1.6 %collective-permute-start.8 = (bf16[256,512]{1,0:T(8,128)(2,1)S(1)}, bf16[256,512]{1,0:T(8,128)(2,1)S(1)}, u32[]{:S(2)}, u32[]{:S(2)}) collective-permute-start(bf16[256,512]{1,0:T(8,128)(2,1)S(1)} %get-tuple-element.63), channel_id=1, source_target_pairs={{0,1},{1,0},{2,3},{3,2},{4,5},{5,4},{6,7},{7,6},{8,9},{9,8},{10,11... | collective-permute-start | bytes 786440 | tf_op jit(solution)/shard_map/ppermute | solution.py:280
  13.9 2.6 %collective-permute-start.9 = (bf16[256,512]{1,0:T(8,128)(2,1)S(1)}, bf16[256,512]{1,0:T(8,128)(2,1)S(1)}, u32[]{:S(2)}, u32[]{:S(2)}) collective-permute-start(bf16[256,512]{1,0:T(8,128)(2,1)S(1)} %get-tuple-element.62), channel_id=1, source_target_pairs={{0,2},{1,3},{2,0},{3,1},{4,6},{5,7},{6,4},{7,5},{8,10},{9,11},{10,... | collective-permute-start | bytes 786440 | tf_op jit(solution)/shard_map/ppermute | solution.py:280
  16.5 1.9 %collective-permute-done.3.rest_3_ = bf16[2,512,256]{2,1,0:T(8,128)(2,1)S(1)} collective-permute-done((bf16[2,512,256]{2,1,0:T(8,128)(2,1)S(1)}, bf16[2,512,256]{2,1,0:T(8,128)(2,1)S(1)}, u32[]{:S(2)}, u32[]{:S(2)}) %collective-permute-start.3) | collective-permute-done | bytes 524320 | tf_op jit(solution)/shard_map/ppermute | solution.py:280
  18.5 1.8 %collective-permute-start.6 = (bf16[1,512,256]{2,1,0:T(8,128)(2,1)S(1)}, bf16[1,512,256]{2,1,0:T(8,128)(2,1)S(1)}, u32[]{:S(2)}, u32[]{:S(2)}) collective-permute-start(bf16[1,512,256]{2,1,0:T(8,128)(2,1)S(1)} %slice.58), channel_id=1, source_target_pairs={{0,16},{4,20},{8,24},{12,28},{16,0},{20,4},{24,8},{28,12},{1,17},{... | collective-permute-start | bytes 786440 | tf_op jit(solution)/shard_map/ppermute | solution.py:280
  20.3 1.6 %collective-permute-start.7 = (bf16[1,512,256]{2,1,0:T(8,128)(2,1)S(1)}, bf16[1,512,256]{2,1,0:T(8,128)(2,1)S(1)}, u32[]{:S(2)}, u32[]{:S(2)}) collective-permute-start(bf16[1,512,256]{2,1,0:T(8,128)(2,1)S(1)} %slice.62), channel_id=1, source_target_pairs={{0,8},{4,12},{8,0},{12,4},{16,24},{20,28},{24,16},{28,20},{1,9},{5... | collective-permute-start | bytes 786440 | tf_op jit(solution)/shard_map/ppermute | solution.py:280
  21.9 1.9 %constant_dynamic-slice_fusion.refs_6_.refs_4_ = bf16[512,1024]{1,0:T(8,128)(2,1)S(1)} fusion(bf16[512,4096]{1,0:T(8,128)(2,1)} %param.12, u32[]{:T(128)S(6)} %mul.21), kind=kLoop, calls=%fused_computation.16 | loop fusion | bytes 2097156 | tf_op jit(solution)/shard_map/dynamic_slice | solution.py:319
  23.8 2.3 %collective-permute-done.8 = bf16[256,512]{1,0:T(8,128)(2,1)S(1)} collective-permute-done((bf16[256,512]{1,0:T(8,128)(2,1)S(1)}, bf16[256,512]{1,0:T(8,128)(2,1)S(1)}, u32[]{:S(2)}, u32[]{:S(2)}) %collective-permute-start.8) | collective-permute-done | bytes 262176 | tf_op jit(solution)/shard_map/ppermute | solution.py:280
  26.0 2.4 %collective-permute-done.9 = bf16[256,512]{1,0:T(8,128)(2,1)S(1)} collective-permute-done((bf16[256,512]{1,0:T(8,128)(2,1)S(1)}, bf16[256,512]{1,0:T(8,128)(2,1)S(1)}, u32[]{:S(2)}, u32[]{:S(2)}) %collective-permute-start.9) | collective-permute-done | bytes 262176 | tf_op jit(solution)/shard_map/ppermute | solution.py:280
  29.6 3.6 %collective-permute-start.12 = (bf16[256,512]{1,0:T(8,128)(2,1)S(1)}, bf16[256,512]{1,0:T(8,128)(2,1)S(1)}, u32[]{:S(2)}, u32[]{:S(2)}) collective-permute-start(bf16[256,512]{1,0:T(8,128)(2,1)S(1)} %get-tuple-element.53), channel_id=1, source_target_pairs={{0,3},{1,2},{2,1},{3,0},{4,7},{5,6},{6,5},{7,4},{8,11},{9,10},{10,... | collective-permute-start | bytes 786440 | tf_op jit(solution)/shard_map/ppermute | solution.py:280
  33.3 8.2 %score.1 = (bf16[1024,1024]{1,0:T(8,128)(2,1)S(1)}, bf16[1024,256]{1,0:T(8,128)(2,1)S(1)}, f32[1024,128]{1,0:T(8,128)S(1)}) custom-call(s32[8]{0:T(128)S(1)} %select_reduce_fusion.place_ref, s32[1024,128]{1,0:T(8,128)S(1)} %get-tuple-element.37.first_ref, s32[1024,128]{1,0:T(8,128)S(1)} %get-tuple-element.36.grp_ref, ...), custom_call_target="tpu_custom_call" | custom-call | tf_op jit(solution)/shard_map/score/pallas_call | solution.py:176
  41.7 1.6 %collective-permute-start.13 = (bf16[1,512,256]{2,1,0:T(8,128)(2,1)S(1)}, bf16[1,512,256]{2,1,0:T(8,128)(2,1)S(1)}, u32[]{:S(2)}, u32[]{:S(2)}) collective-permute-start(bf16[1,512,256]{2,1,0:T(8,128)(2,1)S(1)} %slice.63), channel_id=1, source_target_pairs={{0,16},{4,20},{8,24},{12,28},{16,0},{20,4},{24,8},{28,12},{1,17},{... | collective-permute-start | bytes 786440 | tf_op jit(solution)/shard_map/ppermute | solution.py:280
  43.9 4.2 %collective-permute-done.13.rest_4_ = bf16[1,512,256]{2,1,0:T(8,128)(2,1)S(1)} collective-permute-done((bf16[1,512,256]{2,1,0:T(8,128)(2,1)S(1)}, bf16[1,512,256]{2,1,0:T(8,128)(2,1)S(1)}, u32[]{:S(2)}, u32[]{:S(2)}) %collective-permute-start.13) | collective-permute-done | bytes 262176 | tf_op jit(solution)/shard_map/ppermute | solution.py:280
  48.1 2.8 %collective-permute-done.14.rest_5_ = bf16[1,512,256]{2,1,0:T(8,128)(2,1)S(1)} collective-permute-done((bf16[1,512,256]{2,1,0:T(8,128)(2,1)S(1)}, bf16[1,512,256]{2,1,0:T(8,128)(2,1)S(1)}, u32[]{:S(2)}, u32[]{:S(2)}) %collective-permute-start.14) | collective-permute-done | bytes 262176 | tf_op jit(solution)/shard_map/ppermute | solution.py:280
  50.9 2.2 %mix.2.refs_0_ = bf16[512,256]{1,0:T(8,128)(2,1)S(1)} custom-call(s32[8]{0:T(128)S(1)} %select_reduce_fusion.place_ref, s32[1024,128]{1,0:T(8,128)S(1)} %get-tuple-element.36.grp_ref, bf16[1024,1024]{1,0:T(8,128)(2,1)S(1)} %get-tuple-element.43.p_ref, bf16[1024,256]{1,0:T(8,128)(2,1)S(1)} %get-tuple-element.44.near_ref, ...), custom_call_target="tpu_custom_call" | custom-call | tf_op jit(solution)/shard_map/mix/pallas_call | solution.py:225
  53.1 2.0 %collective-permute-start.15 = (bf16[512,256]{1,0:T(8,128)(2,1)S(1)}, bf16[512,256]{1,0:T(8,128)(2,1)S(1)}, u32[]{:S(2)}, u32[]{:S(2)}) collective-permute-start(bf16[512,256]{1,0:T(8,128)(2,1)S(1)} %mix.2.refs_0_), channel_id=1, source_target_pairs={{0,2},{1,3},{2,0},{3,1},{4,6},{5,7},{6,4},{7,5},{8,10},{9,11},{10,... | collective-permute-start | bytes 786440 | tf_op jit(solution)/shard_map/ppermute | solution.py:280
  55.1 2.0 %mix.3 = bf16[512,256]{1,0:T(8,128)(2,1)S(1)} custom-call(s32[8]{0:T(128)S(1)} %select_reduce_fusion.place_ref, s32[1024,128]{1,0:T(8,128)S(1)} %get-tuple-element.36.grp_ref, bf16[1024,1024]{1,0:T(8,128)(2,1)S(1)} %get-tuple-element.43.p_ref, bf16[1024,256]{1,0:T(8,128)(2,1)S(1)} %get-tuple-element.44.near_ref, f32[1024,128]{1,0:T(8,128)S(1)} %get-tuple-element.45.den_ref, ...), custom_call_target="tpu_custom_call" | custom-call | tf_op jit(solution)/shard_map/mix/pallas_call | solution.py:225
  57.2 2.3 %collective-permute-start.19 = (bf16[512,256]{1,0:T(8,128)(2,1)S(1)}, bf16[512,256]{1,0:T(8,128)(2,1)S(1)}, u32[]{:S(2)}, u32[]{:S(2)}) collective-permute-start(bf16[512,256]{1,0:T(8,128)(2,1)S(1)} %mix.2.refs_0_), channel_id=1, source_target_pairs={{0,1},{1,0},{2,3},{3,2},{4,5},{5,4},{6,7},{7,6},{8,9},{9,8},{10,11... | collective-permute-start | bytes 786440 | tf_op jit(solution)/shard_map/ppermute | solution.py:280
  59.5 4.8 %collective-permute-done.15.refs_2_ = bf16[512,256]{1,0:T(8,128)(2,1)S(1)} collective-permute-done((bf16[512,256]{1,0:T(8,128)(2,1)S(1)}, bf16[512,256]{1,0:T(8,128)(2,1)S(1)}, u32[]{:S(2)}, u32[]{:S(2)}) %collective-permute-start.15) | collective-permute-done | bytes 262176 | tf_op jit(solution)/shard_map/ppermute | solution.py:280
  65.0 3.8 %collective-permute-done.19.refs_1_ = bf16[512,256]{1,0:T(8,128)(2,1)S(1)} collective-permute-done((bf16[512,256]{1,0:T(8,128)(2,1)S(1)}, bf16[512,256]{1,0:T(8,128)(2,1)S(1)}, u32[]{:S(2)}, u32[]{:S(2)}) %collective-permute-start.19) | collective-permute-done | bytes 262176 | tf_op jit(solution)/shard_map/ppermute | solution.py:280
  70.1 4.1 %collective-permute-start.20 = (bf16[512,256]{1,0:T(8,128)(2,1)S(1)}, bf16[512,256]{1,0:T(8,128)(2,1)S(1)}, u32[]{:S(2)}, u32[]{:S(2)}) collective-permute-start(bf16[512,256]{1,0:T(8,128)(2,1)S(1)} %collective-permute-done.18.refs_3_), channel_id=1, source_target_pairs={{0,2},{1,3},{2,0},{3,1},{4,6},{5,7},{6,4},{7,5},{8,10},{9,11},{10,... | collective-permute-start | bytes 786440 | tf_op jit(solution)/shard_map/ppermute | solution.py:280
  74.3 7.8 %collective-permute-done.17.refs_1_ = bf16[512,256]{1,0:T(8,128)(2,1)S(1)} collective-permute-done((bf16[512,256]{1,0:T(8,128)(2,1)S(1)}, bf16[512,256]{1,0:T(8,128)(2,1)S(1)}, u32[]{:S(2)}, u32[]{:S(2)}) %collective-permute-start.17) | collective-permute-done | bytes 262176 | tf_op jit(solution)/shard_map/ppermute | solution.py:366
  82.0 3.8 %collective-permute-done.20.refs_5_ = bf16[512,256]{1,0:T(8,128)(2,1)S(1)} collective-permute-done((bf16[512,256]{1,0:T(8,128)(2,1)S(1)}, bf16[512,256]{1,0:T(8,128)(2,1)S(1)}, u32[]{:S(2)}, u32[]{:S(2)}) %collective-permute-start.20) | collective-permute-done | bytes 262176 | tf_op jit(solution)/shard_map/ppermute | solution.py:280
  85.8 4.2 %collective-permute-done.25.refs_4_ = bf16[512,256]{1,0:T(8,128)(2,1)S(1)} collective-permute-done((bf16[512,256]{1,0:T(8,128)(2,1)S(1)}, bf16[512,256]{1,0:T(8,128)(2,1)S(1)}, u32[]{:S(2)}, u32[]{:S(2)}) %collective-permute-start.25) | collective-permute-done | bytes 262176 | tf_op jit(solution)/shard_map/ppermute | solution.py:280
  90.7 1.3 %collective-permute-start.22 = (bf16[512,256]{1,0:T(8,128)(2,1)S(1)}, bf16[512,256]{1,0:T(8,128)(2,1)S(1)}, u32[]{:S(2)}, u32[]{:S(2)}) collective-permute-start(bf16[512,256]{1,0:T(8,128)(2,1)S(1)} %collective-permute-done.20.refs_5_), channel_id=1, source_target_pairs={{2,3},{1,0},{6,7},{5,4},{10,11},{9,8},{14,15},{13,12},{18,19},{17,... | collective-permute-start | bytes 786440 | tf_op jit(solution)/shard_map/ppermute | solution.py:368
  92.3 2.3 %project.2.refs_9_ = f32[512,1024]{1,0:T(8,128)S(1)} custom-call(s32[3]{0:T(128)S(1)} %pad_add_fusion.1.where_ref, bf16[512,256]{1,0:T(8,128)(2,1)S(1)} %mix.2.refs_0_, bf16[512,256]{1,0:T(8,128)(2,1)S(1)} %collective-permute-done.19.refs_1_, bf16[512,256]{1,0:T(8,128)(2,1)S(1)} %collective-permute-done.15.refs_2_, ...), custom_call_target="tpu_custom_call" | custom-call | tf_op jit(solution)/shard_map/project/pallas_call | solution.py:269
  94.7 6.7 %collective-permute-done.22.refs_3_ = bf16[512,256]{1,0:T(8,128)(2,1)S(1)} collective-permute-done((bf16[512,256]{1,0:T(8,128)(2,1)S(1)}, bf16[512,256]{1,0:T(8,128)(2,1)S(1)}, u32[]{:S(2)}, u32[]{:S(2)}) %collective-permute-start.22) | collective-permute-done | bytes 262176 | tf_op jit(solution)/shard_map/ppermute | solution.py:368
  101.3 2.2 %project.3 = bf16[512,1024]{1,0:T(8,128)(2,1)} custom-call(s32[3]{0:T(128)S(1)} %pad_add_fusion.1.where_ref, bf16[512,256]{1,0:T(8,128)(2,1)S(1)} %collective-permute-done.16.refs_0_, bf16[512,256]{1,0:T(8,128)(2,1)S(1)} %collective-permute-done.17.refs_1_, bf16[512,256]{1,0:T(8,128)(2,1)S(1)} %collective-permute-done.21.refs_2_, ...), custom_call_target="tpu_custom_call" | custom-call | tf_op jit(solution)/shard_map/project/pallas_call | solution.py:269
  (60 shorter events, 7.9 us)
Async XLA Ops:
  0.0 2.1 %copy-start.5 = (s32[1,8]{1,0:T(1,128)S(1)}, s32[1,8]{1,0:T(1,128)}, u32[]{:S(2)}) copy-start(s32[1,8]{1,0:T(1,128)} %param.9) | copy-start | bytes 100
  0.0 7.7 %copy-start.2 = (bf16[512,3,512]{2,0,1:T(8,128)(2,1)S(1)}, bf16[512,3,512]{2,0,1:T(8,128)(2,1)}, u32[]{:S(2)}) copy-start(bf16[512,3,512]{2,0,1:T(8,128)(2,1)} %param.7) | copy-start | bytes 4718596
  1.5 1.7 %collective-permute-start = (bf16[512,256]{1,0:T(8,128)(2,1)S(1)}, bf16[512,256]{1,0:T(8,128)(2,1)S(1)}, u32[]{:S(2)}, u32[]{:S(2)}) collective-permute-start(bf16[512,256]{1,0:T(8,128)(2,1)S(1)} %get-tuple-element.70), channel_id=1, source_target_pairs={{0,4},{4,0},{8,12},{12,8},{16,20},{20,16},{24,28},{28,24},{1,5},{5... | collective-permute-start | bytes 786440 | tf_op jit(solution)/shard_map/ppermute | solution.py:280
  2.1 5.8 %collective-permute-start.1 = (s32[2,8]{1,0:T(2,128)S(1)}, s32[2,8]{1,0:T(2,128)S(1)}, u32[]{:S(2)}, u32[]{:S(2)}) collective-permute-start(s32[2,8]{1,0:T(2,128)S(1)} %pad_add_fusion.refs_0_), channel_id=1, source_target_pairs={{0,4},{4,0},{8,12},{12,8},{16,20},{20,16},{24,28},{28,24},{1,5},{5... | collective-permute-start | bytes 200 | tf_op jit(solution)/shard_map/ppermute | solution.py:280
  3.2 4.6 %copy-start = (f32[128,256]{1,0:T(8,128)S(1)}, f32[128,256]{1,0:T(8,128)}, u32[]{:S(2)}) copy-start(f32[128,256]{1,0:T(8,128)} %constant.28.clone.refs_5_) | copy-start | bytes 393220
  3.3 6.5 %copy-start.1 = (bf16[512,2,512]{2,1,0:T(2,128)(2,1)S(1)}, bf16[512,2,512]{2,1,0:T(2,128)(2,1)}, u32[]{:S(2)}) copy-start(bf16[512,2,512]{2,1,0:T(2,128)(2,1)} %param.8) | copy-start | bytes 3145732
  3.3 15.2 %collective-permute-start.3 = (bf16[2,512,256]{2,1,0:T(8,128)(2,1)S(1)}, bf16[2,512,256]{2,1,0:T(8,128)(2,1)S(1)}, u32[]{:S(2)}, u32[]{:S(2)}) collective-permute-start(bf16[2,512,256]{2,1,0:T(8,128)(2,1)S(1)} %pad_maximum_fusion.1.rest_2_), channel_id=1, source_target_pairs={{0,8},{4,12},{8,0},{12,4},{16,24},{20,28},{24,16},{28,20},{1,9},{5... | collective-permute-start | bytes 1572872 | tf_op jit(solution)/shard_map/ppermute | solution.py:280
  6.2 14.1 %collective-permute-start.4 = (bf16[2,512,256]{2,1,0:T(8,128)(2,1)S(1)}, bf16[2,512,256]{2,1,0:T(8,128)(2,1)S(1)}, u32[]{:S(2)}, u32[]{:S(2)}) collective-permute-start(bf16[2,512,256]{2,1,0:T(8,128)(2,1)S(1)} %pad_maximum_fusion.1.rest_2_), channel_id=1, source_target_pairs={{0,16},{4,20},{8,24},{12,28},{16,0},{20,4},{24,8},{28,12},{1,17},{... | collective-permute-start | bytes 1572872 | tf_op jit(solution)/shard_map/ppermute | solution.py:280
  9.7 18.7 %collective-permute-start.2 = (bf16[3,512,256]{2,1,0:T(8,128)(2,1)S(1)}, bf16[3,512,256]{2,1,0:T(8,128)(2,1)S(1)}, u32[]{:S(2)}, u32[]{:S(2)}) collective-permute-start(bf16[3,512,256]{2,1,0:T(8,128)(2,1)S(1)} %get-tuple-element.39), channel_id=1, source_target_pairs={{0,4},{4,0},{8,12},{12,8},{16,20},{20,16},{24,28},{28,24},{1,5},{5... | collective-permute-start | bytes 2359304 | tf_op jit(solution)/shard_map/ppermute | solution.py:280
  10.0 3.9 %collective-permute-start.5 = (bf16[512,256]{1,0:T(8,128)(2,1)S(1)}, bf16[512,256]{1,0:T(8,128)(2,1)S(1)}, u32[]{:S(2)}, u32[]{:S(2)}) collective-permute-start(bf16[512,256]{1,0:T(8,128)(2,1)S(1)} %get-tuple-element.68), channel_id=1, source_target_pairs={{0,4},{4,0},{8,12},{12,8},{16,20},{20,16},{24,28},{28,24},{1,5},{5... | collective-permute-start | bytes 786440 | tf_op jit(solution)/shard_map/ppermute | solution.py:280
  12.2 13.8 %collective-permute-start.8 = (bf16[256,512]{1,0:T(8,128)(2,1)S(1)}, bf16[256,512]{1,0:T(8,128)(2,1)S(1)}, u32[]{:S(2)}, u32[]{:S(2)}) collective-permute-start(bf16[256,512]{1,0:T(8,128)(2,1)S(1)} %get-tuple-element.63), channel_id=1, source_target_pairs={{0,1},{1,0},{2,3},{3,2},{4,5},{5,4},{6,7},{7,6},{8,9},{9,8},{10,11... | collective-permute-start | bytes 786440 | tf_op jit(solution)/shard_map/ppermute | solution.py:280
  13.9 14.5 %collective-permute-start.9 = (bf16[256,512]{1,0:T(8,128)(2,1)S(1)}, bf16[256,512]{1,0:T(8,128)(2,1)S(1)}, u32[]{:S(2)}, u32[]{:S(2)}) collective-permute-start(bf16[256,512]{1,0:T(8,128)(2,1)S(1)} %get-tuple-element.62), channel_id=1, source_target_pairs={{0,2},{1,3},{2,0},{3,1},{4,6},{5,7},{6,4},{7,5},{8,10},{9,11},{10,... | collective-permute-start | bytes 786440 | tf_op jit(solution)/shard_map/ppermute | solution.py:280
  16.5 16.8 %copy-start.3 = (s32[4,2]{0,1:T(2,128)S(1)}, s32[4,2]{0,1:T(2,128)}, u32[]{:S(2)}) copy-start(s32[4,2]{0,1:T(2,128)} %param.11) | copy-start | bytes 100
  18.5 9.9 %collective-permute-start.6 = (bf16[1,512,256]{2,1,0:T(8,128)(2,1)S(1)}, bf16[1,512,256]{2,1,0:T(8,128)(2,1)S(1)}, u32[]{:S(2)}, u32[]{:S(2)}) collective-permute-start(bf16[1,512,256]{2,1,0:T(8,128)(2,1)S(1)} %slice.58), channel_id=1, source_target_pairs={{0,16},{4,20},{8,24},{12,28},{16,0},{20,4},{24,8},{28,12},{1,17},{... | collective-permute-start | bytes 786440 | tf_op jit(solution)/shard_map/ppermute | solution.py:280
  20.3 8.1 %collective-permute-start.7 = (bf16[1,512,256]{2,1,0:T(8,128)(2,1)S(1)}, bf16[1,512,256]{2,1,0:T(8,128)(2,1)S(1)}, u32[]{:S(2)}, u32[]{:S(2)}) collective-permute-start(bf16[1,512,256]{2,1,0:T(8,128)(2,1)S(1)} %slice.62), channel_id=1, source_target_pairs={{0,8},{4,12},{8,0},{12,4},{16,24},{20,28},{24,16},{28,20},{1,9},{5... | collective-permute-start | bytes 786440 | tf_op jit(solution)/shard_map/ppermute | solution.py:280
  28.4 13.2 %collective-permute-start.10 = (bf16[2,512,256]{2,1,0:T(8,128)(2,1)S(1)}, bf16[2,512,256]{2,1,0:T(8,128)(2,1)S(1)}, u32[]{:S(2)}, u32[]{:S(2)}) collective-permute-start(bf16[2,512,256]{2,1,0:T(8,128)(2,1)S(1)} %pad_maximum_fusion.2.rest_1_), channel_id=1, source_target_pairs={{0,8},{4,12},{8,0},{12,4},{16,24},{20,28},{24,16},{28,20},{1,9},{5... | collective-permute-start | bytes 1572872 | tf_op jit(solution)/shard_map/ppermute | solution.py:280
  29.1 14.1 %collective-permute-start.11 = (bf16[2,512,256]{2,1,0:T(8,128)(2,1)S(1)}, bf16[2,512,256]{2,1,0:T(8,128)(2,1)S(1)}, u32[]{:S(2)}, u32[]{:S(2)}) collective-permute-start(bf16[2,512,256]{2,1,0:T(8,128)(2,1)S(1)} %pad_maximum_fusion.2.rest_1_), channel_id=1, source_target_pairs={{0,16},{4,20},{8,24},{12,28},{16,0},{20,4},{24,8},{28,12},{1,17},{... | collective-permute-start | bytes 1572872 | tf_op jit(solution)/shard_map/ppermute | solution.py:280
  29.6 11.9 %collective-permute-start.12 = (bf16[256,512]{1,0:T(8,128)(2,1)S(1)}, bf16[256,512]{1,0:T(8,128)(2,1)S(1)}, u32[]{:S(2)}, u32[]{:S(2)}) collective-permute-start(bf16[256,512]{1,0:T(8,128)(2,1)S(1)} %get-tuple-element.53), channel_id=1, source_target_pairs={{0,3},{1,2},{2,1},{3,0},{4,7},{5,6},{6,5},{7,4},{8,11},{9,10},{10,... | collective-permute-start | bytes 786440 | tf_op jit(solution)/shard_map/ppermute | solution.py:280
  41.7 6.4 %collective-permute-start.13 = (bf16[1,512,256]{2,1,0:T(8,128)(2,1)S(1)}, bf16[1,512,256]{2,1,0:T(8,128)(2,1)S(1)}, u32[]{:S(2)}, u32[]{:S(2)}) collective-permute-start(bf16[1,512,256]{2,1,0:T(8,128)(2,1)S(1)} %slice.63), channel_id=1, source_target_pairs={{0,16},{4,20},{8,24},{12,28},{16,0},{20,4},{24,8},{28,12},{1,17},{... | collective-permute-start | bytes 786440 | tf_op jit(solution)/shard_map/ppermute | solution.py:280
  43.3 7.6 %collective-permute-start.14 = (bf16[1,512,256]{2,1,0:T(8,128)(2,1)S(1)}, bf16[1,512,256]{2,1,0:T(8,128)(2,1)S(1)}, u32[]{:S(2)}, u32[]{:S(2)}) collective-permute-start(bf16[1,512,256]{2,1,0:T(8,128)(2,1)S(1)} %slice.64), channel_id=1, source_target_pairs={{0,8},{4,12},{8,0},{12,4},{16,24},{20,28},{24,16},{28,20},{1,9},{5... | collective-permute-start | bytes 786440 | tf_op jit(solution)/shard_map/ppermute | solution.py:280
  50.9 39.1 %collective-permute-start.23 = (bf16[3,256,512]{2,1,0:T(8,128)(2,1)S(1)}, bf16[3,256,512]{2,1,0:T(8,128)(2,1)S(1)}, u32[]{:S(2)}, u32[]{:S(2)}) collective-permute-start(bf16[3,256,512]{2,1,0:T(8,128)(2,1)S(1)} %pad_maximum_fusion.refs_7_.refs_5_), channel_id=1, source_target_pairs={{0,8},{4,12},{8,0},{12,4},{16,24},{20,28},{24,16},{28,20},{1,9},{5... | collective-permute-start | bytes 2359304 | tf_op jit(solution)/shard_map/ppermute | solution.py:280
  53.1 11.2 %collective-permute-start.15 = (bf16[512,256]{1,0:T(8,128)(2,1)S(1)}, bf16[512,256]{1,0:T(8,128)(2,1)S(1)}, u32[]{:S(2)}, u32[]{:S(2)}) collective-permute-start(bf16[512,256]{1,0:T(8,128)(2,1)S(1)} %mix.2.refs_0_), channel_id=1, source_target_pairs={{0,2},{1,3},{2,0},{3,1},{4,6},{5,7},{6,4},{7,5},{8,10},{9,11},{10,... | collective-permute-start | bytes 786440 | tf_op jit(solution)/shard_map/ppermute | solution.py:280
  57.1 7.9 %collective-permute-start.18 = (bf16[512,256]{1,0:T(8,128)(2,1)S(1)}, bf16[512,256]{1,0:T(8,128)(2,1)S(1)}, u32[]{:S(2)}, u32[]{:S(2)}) collective-permute-start(bf16[512,256]{1,0:T(8,128)(2,1)S(1)} %mix.3), channel_id=1, source_target_pairs={{0,4},{4,0},{8,12},{12,8},{16,20},{20,16},{24,28},{28,24},{1,5},{5... | collective-permute-start | bytes 786440 | tf_op jit(solution)/shard_map/ppermute | solution.py:280
  57.2 11.6 %collective-permute-start.19 = (bf16[512,256]{1,0:T(8,128)(2,1)S(1)}, bf16[512,256]{1,0:T(8,128)(2,1)S(1)}, u32[]{:S(2)}, u32[]{:S(2)}) collective-permute-start(bf16[512,256]{1,0:T(8,128)(2,1)S(1)} %mix.2.refs_0_), channel_id=1, source_target_pairs={{0,1},{1,0},{2,3},{3,2},{4,5},{5,4},{6,7},{7,6},{8,9},{9,8},{10,11... | collective-permute-start | bytes 786440 | tf_op jit(solution)/shard_map/ppermute | solution.py:280
  64.4 9.9 %collective-permute-start.16 = (bf16[512,256]{1,0:T(8,128)(2,1)S(1)}, bf16[512,256]{1,0:T(8,128)(2,1)S(1)}, u32[]{:S(2)}, u32[]{:S(2)}) collective-permute-start(bf16[512,256]{1,0:T(8,128)(2,1)S(1)} %mix.2.refs_0_), channel_id=1, source_target_pairs={{1,2},{2,1},{5,6},{6,5},{9,10},{10,9},{13,14},{14,13},{17,18},{18,... | collective-permute-start | bytes 786440 | tf_op jit(solution)/shard_map/ppermute | solution.py:365
  68.8 13.2 %collective-permute-start.17 = (bf16[512,256]{1,0:T(8,128)(2,1)S(1)}, bf16[512,256]{1,0:T(8,128)(2,1)S(1)}, u32[]{:S(2)}, u32[]{:S(2)}) collective-permute-start(bf16[512,256]{1,0:T(8,128)(2,1)S(1)} %collective-permute-done.15.refs_2_), channel_id=1, source_target_pairs={{2,3},{1,0},{6,7},{5,4},{10,11},{9,8},{14,15},{13,12},{18,19},{17,... | collective-permute-start | bytes 786440 | tf_op jit(solution)/shard_map/ppermute | solution.py:366
  70.1 15.7 %collective-permute-start.20 = (bf16[512,256]{1,0:T(8,128)(2,1)S(1)}, bf16[512,256]{1,0:T(8,128)(2,1)S(1)}, u32[]{:S(2)}, u32[]{:S(2)}) collective-permute-start(bf16[512,256]{1,0:T(8,128)(2,1)S(1)} %collective-permute-done.18.refs_3_), channel_id=1, source_target_pairs={{0,2},{1,3},{2,0},{3,1},{4,6},{5,7},{6,4},{7,5},{8,10},{9,11},{10,... | collective-permute-start | bytes 786440 | tf_op jit(solution)/shard_map/ppermute | solution.py:280
  74.2 15.8 %collective-permute-start.25 = (bf16[512,256]{1,0:T(8,128)(2,1)S(1)}, bf16[512,256]{1,0:T(8,128)(2,1)S(1)}, u32[]{:S(2)}, u32[]{:S(2)}) collective-permute-start(bf16[512,256]{1,0:T(8,128)(2,1)S(1)} %collective-permute-done.18.refs_3_), channel_id=1, source_target_pairs={{0,1},{1,0},{2,3},{3,2},{4,5},{5,4},{6,7},{7,6},{8,9},{9,8},{10,11... | collective-permute-start | bytes 786440 | tf_op jit(solution)/shard_map/ppermute | solution.py:280
  74.3 17.8 %collective-permute-start.24 = (bf16[3,256,512]{2,1,0:T(8,128)(2,1)S(1)}, bf16[3,256,512]{2,1,0:T(8,128)(2,1)S(1)}, u32[]{:S(2)}, u32[]{:S(2)}) collective-permute-start(bf16[3,256,512]{2,1,0:T(8,128)(2,1)S(1)} %pad_maximum_fusion.refs_7_.refs_5_), channel_id=1, source_target_pairs={{0,4},{4,0},{8,12},{12,8},{16,20},{20,16},{24,28},{28,24},{1,5},{5... | collective-permute-start | bytes 2359304 | tf_op jit(solution)/shard_map/ppermute | solution.py:280
  90.1 2.3 %collective-permute-start.26 = (bf16[3,256,512]{2,1,0:T(8,128)(2,1)S(1)}, bf16[3,256,512]{2,1,0:T(8,128)(2,1)S(1)}, u32[]{:S(2)}, u32[]{:S(2)}) collective-permute-start(bf16[3,256,512]{2,1,0:T(8,128)(2,1)S(1)} %collective-permute-done.23.refs_8_.refs_6_), channel_id=1, source_target_pairs={{0,4},{4,0},{8,12},{12,8},{16,20},{20,16},{24,28},{28,24},{1,5},{5... | collective-permute-start | bytes 2359304 | tf_op jit(solution)/shard_map/ppermute | solution.py:280
  90.1 4.6 %collective-permute-start.21 = (bf16[512,256]{1,0:T(8,128)(2,1)S(1)}, bf16[512,256]{1,0:T(8,128)(2,1)S(1)}, u32[]{:S(2)}, u32[]{:S(2)}) collective-permute-start(bf16[512,256]{1,0:T(8,128)(2,1)S(1)} %collective-permute-done.18.refs_3_), channel_id=1, source_target_pairs={{1,2},{2,1},{5,6},{6,5},{9,10},{10,9},{13,14},{14,13},{17,18},{18,... | collective-permute-start | bytes 786440 | tf_op jit(solution)/shard_map/ppermute | solution.py:367
  90.7 10.6 %collective-permute-start.22 = (bf16[512,256]{1,0:T(8,128)(2,1)S(1)}, bf16[512,256]{1,0:T(8,128)(2,1)S(1)}, u32[]{:S(2)}, u32[]{:S(2)}) collective-permute-start(bf16[512,256]{1,0:T(8,128)(2,1)S(1)} %collective-permute-done.20.refs_5_), channel_id=1, source_target_pairs={{2,3},{1,0},{6,7},{5,4},{10,11},{9,8},{14,15},{13,12},{18,19},{17,... | collective-permute-start | bytes 786440 | tf_op jit(solution)/shard_map/ppermute | solution.py:368
  (1 other events, 2.1 us)

commit v11 on v10

--- a/solution.py
+++ b/solution.py
@@ -234,32 +234,25 @@
 
 def proj_kernel(steps, last, where_ref, *refs):
     att = refs[: 2 * len(steps)]
-    own, *far = refs[2 * len(steps) : 2 * len(steps) + 5]
+    own, *far = refs[2 * len(steps) : 2 * len(steps) + 3]
     o_ref = refs[-1]
-    cols = o_ref.shape[1] // 2
-    rows = o_ref.shape[0]
+    cols = o_ref.shape[1] // 4
     core = where_ref[1]
-    side = where_ref[2]
-    tall = 256
-    for r0 in range(0, rows, tall):
-        at = slice(r0, r0 + tall)
-        for x in range(2):
-            c = pl.ds(pl.multiple_of(lax.bitwise_xor(side, x) * cols, cols), cols)
-            acc = refs[-2][at, c] if last else jnp.zeros((tall, cols), jnp.float32)
-            for h in range(2):
-                head = lax.bitwise_xor(core, h)
-                lines = []
-                for i, m in enumerate(steps):
-                    lines.append((m, att[h * len(steps) + i][at, :]))
-                if last:
-                    lines = [(3, lines[0][1] + lines[1][1])]
-                for m, a in lines:
-                    if m == 0:
-                        w = own[pl.ds(pl.multiple_of(head * HD, HD), HD), c]
-                    else:
-                        w = far[2 * h + x][m - 1]
-                    acc = acc + jnp.dot(a, w, preferred_element_type=jnp.float32)
-            o_ref[at, c] = acc.astype(o_ref.dtype)
+    for x in range(4):
+        c = pl.ds(pl.multiple_of(lax.bitwise_xor(where_ref[2], x) * cols, cols), cols)
+        acc = refs[-2][:, c] if last else jnp.zeros((o_ref.shape[0], cols), jnp.float32)
+        for h in range(2):
+            head = lax.bitwise_xor(core, h)
+            lines = [(m, att[h * len(steps) + i][...]) for i, m in enumerate(steps)]
+            if last:
+                lines = [(3, lines[0][1] + lines[1][1])]
+            for m, a in lines:
+                if m == 0:
+                    w = own[pl.ds(pl.multiple_of(head * HD, HD), HD), c]
+                else:
+                    w = far[h][3 * x + m - 1]
+                acc = acc + jnp.dot(a, w, preferred_element_type=jnp.float32)
+        o_ref[:, c] = acc.astype(o_ref.dtype)
 
 
 def project(where, steps, att, own, far, add=None):
@@ -294,8 +287,8 @@
     me = lax.axis_index("req")
     z = lax.axis_index("tp")
     core = me & 1
-    side = (me >> 1) & 1
-    where = jnp.stack([z, core, side]).astype(jnp.int32)
+    chip = me >> 1
+    where = jnp.stack([z, core, chip]).astype(jnp.int32)
     place = jnp.sum(
         jnp.where(
             owners[None] == (me ^ jnp.arange(SLOTS, dtype=jnp.int32))[:, None, None],
@@ -308,12 +301,12 @@
     first_head = core == 0
 
     cols = out_weight.shape[1] // tp_size
-    z_u, core_u, side_u = (i.astype(jnp.uint32) for i in (z, core, side))
+    z_u, core_u, chip_u = (i.astype(jnp.uint32) for i in (z, core, chip))
     starts = [core_u * HD, z_u * cols]
-    starts += [(z_u ^ m) * cols + side_u * (cols // 2) for m in range(1, tp_size)]
+    starts += [(z_u ^ m) * cols + chip_u * (cols // 4) for m in range(1, tp_size)]
     first_head, *starts = lax.optimization_barrier((first_head, *starts))
     sends = [
-        lax.dynamic_slice(out_weight, (starts[0], starts[1 + m]), (HD, cols // 2))
+        lax.dynamic_slice(out_weight, (starts[0], starts[1 + m]), (HD, cols // 4))
         for m in range(1, tp_size)
     ]
     w_own = lax.dynamic_slice(
@@ -326,7 +319,7 @@
     k_both = jnp.stack([k_own, over_core(k_other)])
     kx = over_x(k_both)
     ky = over_y(k_both)
-    w_one, w_two = (swap(sends[m - 1], "tp", m, tp_size) for m in (1, 2))
+    w_one, w_two, w_three = (swap(sends[m - 1], "tp", m, tp_size) for m in (1, 2, 3))
 
     table = jnp.concatenate([lengths, groups], axis=0)
     table_pair = over_core(table)
@@ -342,32 +335,33 @@
 
     kxy = over_y(after(kx[0:1], mine, v_both))
     kyx = over_x(after(ky[1:2], mine, v_both))
-    v_both = after(v_both, kxy, kyx, w_one, w_two, w_own, sufs[1])
+    v_both = after(v_both, kxy, kyx, w_one, w_two, w_three, w_own, sufs[1])
     vx = over_x(v_both)
     vy = over_y(v_both)
-    w_three = swap(after(sends[2], w_two), "tp", 3, tp_size)
     scored = score(place, first, grp, sufs, (k_both, kx, ky, kxy, kyx))
     w_far = jnp.stack([after(w_one, scored[0]), w_two, w_three])
-    w_core = over_core(w_far)
     vxy = over_y(after(vx[0:1], scored[0], w_far))
     vyx = over_x(after(vy[1:2], scored[0], w_far))
     v_pieces = (v_both, vx, vy, vxy, vyx)
     (own,) = mix(0, HD, place, grp, scored, sufs[:1], v_pieces)
     (pair,) = mix(0, HD, place, grp, scored, sufs[1:], v_pieces, rows)
     w_x = over_x(after(w_far, vxy, vyx))
+    w_y = over_y(after(w_far, vxy, vyx))
 
     back = over_core(pair)
     two_own = swap(own, "tp", 2, tp_size)
     one_own = swap(own, "tp", 1, tp_size)
-    later = after(back, two_own, one_own)
+    later = after(back, two_own)
     two_back = swap(later, "tp", 2, tp_size)
     one_back = swap(later, "tp", 1, tp_size)
-    three_own = lax.ppermute(after(own, two_own), "tp", [(1, 2), (2, 1)])
+    three_own = lax.ppermute(after(own, two_own, one_own), "tp", [(1, 2), (2, 1)])
     forward_own = lax.ppermute(two_own, "tp", [(2, 3), (1, 0)])
     three_back = lax.ppermute(after(later, two_back), "tp", [(1, 2), (2, 1)])
     forward_back = lax.ppermute(two_back, "tp", [(2, 3), (1, 0)])
-    w_core_x = over_core(after(w_x, two_back, one_back, three_own, forward_own))
-    far = [w_far, w_x, w_core, w_core_x]
+    w_xy = over_y(after(w_x, two_own, one_own))
+    w_chips = jnp.concatenate([w_far, w_x, w_y, w_xy])
+    w_core = over_core(after(w_chips, two_back, one_back, three_own, forward_own))
+    far = [w_chips, w_core]
     near = project(where, (0, 1, 2), (own, one_own, two_own, back, one_back, two_back), w_own, far)
     last = (three_own, forward_own, three_back, forward_back)
     return project(where, (3, 3), last, w_own, far, near)

time: 104 us -> 107 us (1.029)
  starting transfers between devices: 32.7 us -> 34.1 us
  waiting for transfers between devices: 46 us -> 47.4 us
    ppermute x1, waiting for transfers between devices: 7.77 us -> 9.78 us  [split_heads(): forward_own = lax.ppermute(two_own, 'tp', [(2, 3), (1, 0)])]
    ppermute x23 -> x24, starting transfers between devices: 28.8 us -> 30.2 us  [swap(): return lax.ppermute(x, axis, [(i, i ^ mask) for i in range(size)])]
    ppermute x1, waiting for transfers between devices: 6.66 us -> 5.45 us  [split_heads(): forward_back = lax.ppermute(two_back, 'tp', [(2, 3), (1, 0)])]
    ppermute x23 -> x24, waiting for transfers between devices: 31.5 us -> 32.2 us  [swap(): return lax.ppermute(x, axis, [(i, i ^ mask) for i in range(size)])]
  transfers between devices with their start and end apart: 27 -> 28, of which waited for: 13 -> 13; matrix products, arithmetic and copies ran while one was open for 4% -> 4% of each run, Pallas kernels for 16% -> 14%
where the time goes in v11:
time: 107 us; the launch traced here: 106 us
  waiting for transfers between devices  47.4 us (44%)
  starting transfers between devices  34.1 us (32%)
  Pallas kernels  18.8 us (18%)
  local copies, waits for them, and re-layouts  5.23 us (5%)
    ppermute x24, waiting for transfers between devices, swap(): return lax.ppermute(x, axis, [(i, i ^ mask) for i in range(size)])  32.2 us
    ppermute x24, starting transfers between devices, swap(): return lax.ppermute(x, axis, [(i, i ^ mask) for i in range(size)])  30.2 us
    ppermute x1, waiting for transfers between devices, split_heads(): forward_own = lax.ppermute(two_own, 'tp', [(2, 3), (1, 0)])  9.78 us
    pallas_call x1, Pallas kernels, score(): pl.pallas_call(functools.partial(score_kernel, len(sufs), tuple((p.shape[...  8.18 us
    ppermute x1, waiting for transfers between devices, split_heads(): forward_back = lax.ppermute(two_back, 'tp', [(2, 3), (1, 0)])  5.45 us
    pallas_call x2, Pallas kernels, project(): pl.pallas_call(functools.partial(proj_kernel, steps, add is not None), ou...  4.74 us
    pallas_call x2, Pallas kernels, mix(): pl.pallas_call(functools.partial(mix_kernel, nb, base, tuple((p.shape[0]...  4.06 us
  transfers between devices with their start and end apart: 28, of which 13 were waited for; matrix products, arithmetic and copies ran while one was open for 4% of the time, Pallas kernels for 14%

profile of v11, /device:TPU:0, one launch (start us, length us, event | category | flops | bytes accessed | tf_op | source)
XLA Modules:
  0.0 106.3 jit_solution(4222717812054490916)
XLA Ops:
  0.0 1.5 %copy.15 = bf16[512,1,512]{2,0,1:T(8,128)(2,1)S(1)} copy(bf16[512,1,512]{2,1,0:T(2,128)(2,1)} %bitcast.27) | data formatting | bytes 1048576
  3.3 2.9 %collective-permute-start.3 = (bf16[2,512,256]{2,1,0:T(8,128)(2,1)S(1)}, bf16[2,512,256]{2,1,0:T(8,128)(2,1)S(1)}, u32[]{:S(2)}, u32[]{:S(2)}) collective-permute-start(bf16[2,512,256]{2,1,0:T(8,128)(2,1)S(1)} %pad_maximum_fusion.rest_2_), channel_id=1, source_target_pairs={{0,8},{4,12},{8,0},{12,4},{16,24},{20,28},{24,16},{28,20},{1,9},{5... | collective-permute-start | bytes 1572872 | tf_op jit(solution)/shard_map/ppermute | solution.py:273
  6.2 1.5 %collective-permute-start.4 = (bf16[2,512,256]{2,1,0:T(8,128)(2,1)S(1)}, bf16[2,512,256]{2,1,0:T(8,128)(2,1)S(1)}, u32[]{:S(2)}, u32[]{:S(2)}) collective-permute-start(bf16[2,512,256]{2,1,0:T(8,128)(2,1)S(1)} %pad_maximum_fusion.rest_2_), channel_id=1, source_target_pairs={{0,16},{4,20},{8,24},{12,28},{16,0},{20,4},{24,8},{28,12},{1,17},{... | collective-permute-start | bytes 1572872 | tf_op jit(solution)/shard_map/ppermute | solution.py:273
  7.9 1.8 %prepare.1 = (s32[1024,128]{1,0:T(8,128)S(1)}, s32[1024,128]{1,0:T(8,128)S(1)}, bf16[3,512,256]{2,1,0:T(8,128)(2,1)S(1)}, bf16[3,512,256]{2,1,0:T(8,128)(2,1)S(1)}) custom-call(s32[3]{0:T(128)S(1)} %pad_add_fusion.1.where_ref, s32[2,8]{1,0:T(2,128)S(1)} %pad_add_fusion.refs_0_, s32[2,8]{1,0:T(2,128)S(1)} %collective-permute-done.1.refs_1_, ...), custom_call_target="tpu_custom_call" | custom-call | tf_op jit(solution)/shard_map/prepare/pallas_call | solution.py:101
  10.6 1.4 %fusion = (bf16[256,256]{1,0:T(8,128)(2,1)S(1)}, bf16[256,256]{1,0:T(8,128)(2,1)S(1)}, bf16[256,256]{1,0:T(8,128)(2,1)S(1)}) fusion(bf16[512,4096]{1,0:T(8,128)(2,1)} %param.12, u32[]{:T(128)S(6)} %mul.20, u32[]{:T(128)S(6)} %add.17, u32[]{:T(128)S(6)} %add.16, u32[]{:T(128)S(6)} %add.15), kind=kLoop, calls=%fused_computation.24 | loop fusion | bytes 786448 | tf_op jit(solution)/shard_map/dynamic_slice | solution.py:309
  11.9 1.6 %collective-permute-start.8 = (bf16[256,256]{1,0:T(8,128)(2,1)S(1)}, bf16[256,256]{1,0:T(8,128)(2,1)S(1)}, u32[]{:S(2)}, u32[]{:S(2)}) collective-permute-start(bf16[256,256]{1,0:T(8,128)(2,1)S(1)} %get-tuple-element.63), channel_id=1, source_target_pairs={{0,1},{1,0},{2,3},{3,2},{4,5},{5,4},{6,7},{7,6},{8,9},{9,8},{10,11... | collective-permute-start | bytes 393224 | tf_op jit(solution)/shard_map/ppermute | solution.py:273
  13.7 4.8 %collective-permute-done.3.rest_3_ = bf16[2,512,256]{2,1,0:T(8,128)(2,1)S(1)} collective-permute-done((bf16[2,512,256]{2,1,0:T(8,128)(2,1)S(1)}, bf16[2,512,256]{2,1,0:T(8,128)(2,1)S(1)}, u32[]{:S(2)}, u32[]{:S(2)}) %collective-permute-start.3) | collective-permute-done | bytes 524320 | tf_op jit(solution)/shard_map/ppermute | solution.py:273
  18.4 1.8 %collective-permute-start.6 = (bf16[1,512,256]{2,1,0:T(8,128)(2,1)S(1)}, bf16[1,512,256]{2,1,0:T(8,128)(2,1)S(1)}, u32[]{:S(2)}, u32[]{:S(2)}) collective-permute-start(bf16[1,512,256]{2,1,0:T(8,128)(2,1)S(1)} %slice.58), channel_id=1, source_target_pairs={{0,16},{4,20},{8,24},{12,28},{16,0},{20,4},{24,8},{28,12},{1,17},{... | collective-permute-start | bytes 786440 | tf_op jit(solution)/shard_map/ppermute | solution.py:273
  20.3 1.6 %collective-permute-start.7 = (bf16[1,512,256]{2,1,0:T(8,128)(2,1)S(1)}, bf16[1,512,256]{2,1,0:T(8,128)(2,1)S(1)}, u32[]{:S(2)}, u32[]{:S(2)}) collective-permute-start(bf16[1,512,256]{2,1,0:T(8,128)(2,1)S(1)} %slice.62), channel_id=1, source_target_pairs={{0,8},{4,12},{8,0},{12,4},{16,24},{20,28},{24,16},{28,20},{1,9},{5... | collective-permute-start | bytes 786440 | tf_op jit(solution)/shard_map/ppermute | solution.py:273
  21.9 2.6 %collective-permute-start.9 = (bf16[256,256]{1,0:T(8,128)(2,1)S(1)}, bf16[256,256]{1,0:T(8,128)(2,1)S(1)}, u32[]{:S(2)}, u32[]{:S(2)}) collective-permute-start(bf16[256,256]{1,0:T(8,128)(2,1)S(1)} %get-tuple-element.62), channel_id=1, source_target_pairs={{0,2},{1,3},{2,0},{3,1},{4,6},{5,7},{6,4},{7,5},{8,10},{9,11},{10,... | collective-permute-start | bytes 393224 | tf_op jit(solution)/shard_map/ppermute | solution.py:273
  24.5 1.3 %collective-permute-start.10 = (bf16[256,256]{1,0:T(8,128)(2,1)S(1)}, bf16[256,256]{1,0:T(8,128)(2,1)S(1)}, u32[]{:S(2)}, u32[]{:S(2)}) collective-permute-start(bf16[256,256]{1,0:T(8,128)(2,1)S(1)} %get-tuple-element.61), channel_id=1, source_target_pairs={{0,3},{1,2},{2,1},{3,0},{4,7},{5,6},{6,5},{7,4},{8,11},{9,10},{10,... | collective-permute-start | bytes 393224 | tf_op jit(solution)/shard_map/ppermute | solution.py:273
  25.8 1.9 %constant_dynamic-slice_fusion.refs_6_.refs_4_ = bf16[512,1024]{1,0:T(8,128)(2,1)S(1)} fusion(bf16[512,4096]{1,0:T(8,128)(2,1)} %param.12, u32[]{:T(128)S(6)} %mul.21), kind=kLoop, calls=%fused_computation.22 | loop fusion | bytes 2097156 | tf_op jit(solution)/shard_map/dynamic_slice | solution.py:312
  27.7 6.0 %collective-permute-done.9 = bf16[256,256]{1,0:T(8,128)(2,1)S(1)} collective-permute-done((bf16[256,256]{1,0:T(8,128)(2,1)S(1)}, bf16[256,256]{1,0:T(8,128)(2,1)S(1)}, u32[]{:S(2)}, u32[]{:S(2)}) %collective-permute-start.9) | collective-permute-done | bytes 131104 | tf_op jit(solution)/shard_map/ppermute | solution.py:273
  35.5 8.2 %score.1 = (bf16[1024,1024]{1,0:T(8,128)(2,1)S(1)}, bf16[1024,256]{1,0:T(8,128)(2,1)S(1)}, f32[1024,128]{1,0:T(8,128)S(1)}) custom-call(s32[8]{0:T(128)S(1)} %select_reduce_fusion.place_ref, s32[1024,128]{1,0:T(8,128)S(1)} %get-tuple-element.37.first_ref, s32[1024,128]{1,0:T(8,128)S(1)} %get-tuple-element.36.grp_ref, ...), custom_call_target="tpu_custom_call" | custom-call | tf_op jit(solution)/shard_map/score/pallas_call | solution.py:176
  45.0 1.2 %collective-permute-done.12.rest_3_ = bf16[2,512,256]{2,1,0:T(8,128)(2,1)S(1)} collective-permute-done((bf16[2,512,256]{2,1,0:T(8,128)(2,1)S(1)}, bf16[2,512,256]{2,1,0:T(8,128)(2,1)S(1)}, u32[]{:S(2)}, u32[]{:S(2)}) %collective-permute-start.12) | collective-permute-done | bytes 524320 | tf_op jit(solution)/shard_map/ppermute | solution.py:273
  46.2 2.1 %collective-permute-start.14 = (bf16[1,512,256]{2,1,0:T(8,128)(2,1)S(1)}, bf16[1,512,256]{2,1,0:T(8,128)(2,1)S(1)}, u32[]{:S(2)}, u32[]{:S(2)}) collective-permute-start(bf16[1,512,256]{2,1,0:T(8,128)(2,1)S(1)} %slice.64), channel_id=1, source_target_pairs={{0,8},{4,12},{8,0},{12,4},{16,24},{20,28},{24,16},{28,20},{1,9},{5... | collective-permute-start | bytes 786440 | tf_op jit(solution)/shard_map/ppermute | solution.py:273
  48.3 3.0 %collective-permute-done.13.rest_4_ = bf16[1,512,256]{2,1,0:T(8,128)(2,1)S(1)} collective-permute-done((bf16[1,512,256]{2,1,0:T(8,128)(2,1)S(1)}, bf16[1,512,256]{2,1,0:T(8,128)(2,1)S(1)}, u32[]{:S(2)}, u32[]{:S(2)}) %collective-permute-start.13) | collective-permute-done | bytes 262176 | tf_op jit(solution)/shard_map/ppermute | solution.py:273
  51.3 1.3 %collective-permute-done.14.rest_5_ = bf16[1,512,256]{2,1,0:T(8,128)(2,1)S(1)} collective-permute-done((bf16[1,512,256]{2,1,0:T(8,128)(2,1)S(1)}, bf16[1,512,256]{2,1,0:T(8,128)(2,1)S(1)}, u32[]{:S(2)}, u32[]{:S(2)}) %collective-permute-start.14) | collective-permute-done | bytes 262176 | tf_op jit(solution)/shard_map/ppermute | solution.py:273
  52.6 2.0 %mix.2.refs_0_ = bf16[512,256]{1,0:T(8,128)(2,1)S(1)} custom-call(s32[8]{0:T(128)S(1)} %select_reduce_fusion.place_ref, s32[1024,128]{1,0:T(8,128)S(1)} %get-tuple-element.36.grp_ref, bf16[1024,1024]{1,0:T(8,128)(2,1)S(1)} %get-tuple-element.43.p_ref, bf16[1024,256]{1,0:T(8,128)(2,1)S(1)} %get-tuple-element.44.near_ref, ...), custom_call_target="tpu_custom_call" | custom-call | tf_op jit(solution)/shard_map/mix/pallas_call | solution.py:225
  54.7 7.3 %collective-permute-start.15 = (bf16[512,256]{1,0:T(8,128)(2,1)S(1)}, bf16[512,256]{1,0:T(8,128)(2,1)S(1)}, u32[]{:S(2)}, u32[]{:S(2)}) collective-permute-start(bf16[512,256]{1,0:T(8,128)(2,1)S(1)} %mix.2.refs_0_), channel_id=1, source_target_pairs={{0,2},{1,3},{2,0},{3,1},{4,6},{5,7},{6,4},{7,5},{8,10},{9,11},{10,... | collective-permute-start | bytes 786440 | tf_op jit(solution)/shard_map/ppermute | solution.py:273
  64.1 2.0 %mix.3 = bf16[512,256]{1,0:T(8,128)(2,1)S(1)} custom-call(s32[8]{0:T(128)S(1)} %select_reduce_fusion.place_ref, s32[1024,128]{1,0:T(8,128)S(1)} %get-tuple-element.36.grp_ref, bf16[1024,1024]{1,0:T(8,128)(2,1)S(1)} %get-tuple-element.43.p_ref, bf16[1024,256]{1,0:T(8,128)(2,1)S(1)} %get-tuple-element.44.near_ref, f32[1024,128]{1,0:T(8,128)S(1)} %get-tuple-element.45.den_ref, ...), custom_call_target="tpu_custom_call" | custom-call | tf_op jit(solution)/shard_map/mix/pallas_call | solution.py:225
  66.2 5.8 %collective-permute-done.15.refs_2_ = bf16[512,256]{1,0:T(8,128)(2,1)S(1)} collective-permute-done((bf16[512,256]{1,0:T(8,128)(2,1)S(1)}, bf16[512,256]{1,0:T(8,128)(2,1)S(1)}, u32[]{:S(2)}, u32[]{:S(2)}) %collective-permute-start.15) | collective-permute-done | bytes 262176 | tf_op jit(solution)/shard_map/ppermute | solution.py:273
  72.0 1.1 %collective-permute-done.16.refs_1_ = bf16[512,256]{1,0:T(8,128)(2,1)S(1)} collective-permute-done((bf16[512,256]{1,0:T(8,128)(2,1)S(1)}, bf16[512,256]{1,0:T(8,128)(2,1)S(1)}, u32[]{:S(2)}, u32[]{:S(2)}) %collective-permute-start.16) | collective-permute-done | bytes 262176 | tf_op jit(solution)/shard_map/ppermute | solution.py:273
  73.2 1.5 %collective-permute-start.25 = (bf16[3,256,256]{2,1,0:T(8,128)(2,1)S(1)}, bf16[3,256,256]{2,1,0:T(8,128)(2,1)S(1)}, u32[]{:S(2)}, u32[]{:S(2)}) collective-permute-start(bf16[3,256,256]{2,1,0:T(8,128)(2,1)S(1)} %collective-permute-done.23), channel_id=1, source_target_pairs={{0,16},{4,20},{8,24},{12,28},{16,0},{20,4},{24,8},{28,12},{1,17},{... | collective-permute-start | bytes 1179656 | tf_op jit(solution)/shard_map/ppermute | solution.py:273
  76.1 1.3 %collective-permute-start.18 = (bf16[512,256]{1,0:T(8,128)(2,1)S(1)}, bf16[512,256]{1,0:T(8,128)(2,1)S(1)}, u32[]{:S(2)}, u32[]{:S(2)}) collective-permute-start(bf16[512,256]{1,0:T(8,128)(2,1)S(1)} %collective-permute-done.15.refs_2_), channel_id=1, source_target_pairs={{2,3},{1,0},{6,7},{5,4},{10,11},{9,8},{14,15},{13,12},{18,19},{17,... | collective-permute-start | bytes 786440 | tf_op jit(solution)/shard_map/ppermute | solution.py:358
  77.5 5.4 %collective-permute-done.25 = bf16[3,256,256]{2,1,0:T(8,128)(2,1)S(1)} collective-permute-done((bf16[3,256,256]{2,1,0:T(8,128)(2,1)S(1)}, bf16[3,256,256]{2,1,0:T(8,128)(2,1)S(1)}, u32[]{:S(2)}, u32[]{:S(2)}) %collective-permute-start.25) | collective-permute-done | bytes 393248 | tf_op jit(solution)/shard_map/ppermute | solution.py:273
  82.9 9.8 %collective-permute-done.18.refs_1_ = bf16[512,256]{1,0:T(8,128)(2,1)S(1)} collective-permute-done((bf16[512,256]{1,0:T(8,128)(2,1)S(1)}, bf16[512,256]{1,0:T(8,128)(2,1)S(1)}, u32[]{:S(2)}, u32[]{:S(2)}) %collective-permute-start.18) | collective-permute-done | bytes 262176 | tf_op jit(solution)/shard_map/ppermute | solution.py:358
  93.4 1.3 %collective-permute-start.22 = (bf16[512,256]{1,0:T(8,128)(2,1)S(1)}, bf16[512,256]{1,0:T(8,128)(2,1)S(1)}, u32[]{:S(2)}, u32[]{:S(2)}) collective-permute-start(bf16[512,256]{1,0:T(8,128)(2,1)S(1)} %collective-permute-done.20.refs_5_), channel_id=1, source_target_pairs={{2,3},{1,0},{6,7},{5,4},{10,11},{9,8},{14,15},{13,12},{18,19},{17,... | collective-permute-start | bytes 786440 | tf_op jit(solution)/shard_map/ppermute | solution.py:360
  94.7 1.4 %collective-permute-done.27.refs_8_.refs_6_ = bf16[12,256,256]{2,1,0:T(8,128)(2,1)S(1)} collective-permute-done((bf16[12,256,256]{2,1,0:T(8,128)(2,1)S(1)}, bf16[12,256,256]{2,1,0:T(8,128)(2,1)S(1)}, u32[]{:S(2)}, u32[]{:S(2)}) %collective-permute-start.27) | collective-permute-done | bytes 1572896 | tf_op jit(solution)/shard_map/ppermute | solution.py:273
  96.1 2.4 %project.2.refs_7_ = f32[512,1024]{1,0:T(8,128)S(1)} custom-call(s32[3]{0:T(128)S(1)} %pad_add_fusion.1.where_ref, bf16[512,256]{1,0:T(8,128)(2,1)S(1)} %mix.2.refs_0_, bf16[512,256]{1,0:T(8,128)(2,1)S(1)} %collective-permute-done.16.refs_1_, bf16[512,256]{1,0:T(8,128)(2,1)S(1)} %collective-permute-done.15.refs_2_, ...), custom_call_target="tpu_custom_call" | custom-call | tf_op jit(solution)/shard_map/project/pallas_call | solution.py:262
  98.5 5.4 %collective-permute-done.22.refs_3_ = bf16[512,256]{1,0:T(8,128)(2,1)S(1)} collective-permute-done((bf16[512,256]{1,0:T(8,128)(2,1)S(1)}, bf16[512,256]{1,0:T(8,128)(2,1)S(1)}, u32[]{:S(2)}, u32[]{:S(2)}) %collective-permute-start.22) | collective-permute-done | bytes 262176 | tf_op jit(solution)/shard_map/ppermute | solution.py:360
  104.0 2.3 %project.3 = bf16[512,1024]{1,0:T(8,128)(2,1)} custom-call(s32[3]{0:T(128)S(1)} %pad_add_fusion.1.where_ref, bf16[512,256]{1,0:T(8,128)(2,1)S(1)} %collective-permute-done.17.refs_0_, bf16[512,256]{1,0:T(8,128)(2,1)S(1)} %collective-permute-done.18.refs_1_, bf16[512,256]{1,0:T(8,128)(2,1)S(1)} %collective-permute-done.21.refs_2_, ...), custom_call_target="tpu_custom_call" | custom-call | tf_op jit(solution)/shard_map/project/pallas_call | solution.py:262
  (68 shorter events, 10.3 us)
Async XLA Ops:
  0.0 2.0 %copy-start.5 = (s32[1,8]{1,0:T(1,128)S(1)}, s32[1,8]{1,0:T(1,128)}, u32[]{:S(2)}) copy-start(s32[1,8]{1,0:T(1,128)} %param.9) | copy-start | bytes 100
  0.0 7.7 %copy-start.2 = (bf16[512,3,512]{2,0,1:T(8,128)(2,1)S(1)}, bf16[512,3,512]{2,0,1:T(8,128)(2,1)}, u32[]{:S(2)}) copy-start(bf16[512,3,512]{2,0,1:T(8,128)(2,1)} %param.7) | copy-start | bytes 4718596
  1.5 1.7 %collective-permute-start = (bf16[512,256]{1,0:T(8,128)(2,1)S(1)}, bf16[512,256]{1,0:T(8,128)(2,1)S(1)}, u32[]{:S(2)}, u32[]{:S(2)}) collective-permute-start(bf16[512,256]{1,0:T(8,128)(2,1)S(1)} %get-tuple-element.70), channel_id=1, source_target_pairs={{0,4},{4,0},{8,12},{12,8},{16,20},{20,16},{24,28},{28,24},{1,5},{5... | collective-permute-start | bytes 786440 | tf_op jit(solution)/shard_map/ppermute | solution.py:273
  2.1 5.8 %collective-permute-start.1 = (s32[2,8]{1,0:T(2,128)S(1)}, s32[2,8]{1,0:T(2,128)S(1)}, u32[]{:S(2)}, u32[]{:S(2)}) collective-permute-start(s32[2,8]{1,0:T(2,128)S(1)} %pad_add_fusion.refs_0_), channel_id=1, source_target_pairs={{0,4},{4,0},{8,12},{12,8},{16,20},{20,16},{24,28},{28,24},{1,5},{5... | collective-permute-start | bytes 200 | tf_op jit(solution)/shard_map/ppermute | solution.py:273
  3.3 4.6 %copy-start = (f32[128,256]{1,0:T(8,128)S(1)}, f32[128,256]{1,0:T(8,128)}, u32[]{:S(2)}) copy-start(f32[128,256]{1,0:T(8,128)} %constant.26.clone.refs_5_) | copy-start | bytes 393220
  3.3 15.2 %collective-permute-start.3 = (bf16[2,512,256]{2,1,0:T(8,128)(2,1)S(1)}, bf16[2,512,256]{2,1,0:T(8,128)(2,1)S(1)}, u32[]{:S(2)}, u32[]{:S(2)}) collective-permute-start(bf16[2,512,256]{2,1,0:T(8,128)(2,1)S(1)} %pad_maximum_fusion.rest_2_), channel_id=1, source_target_pairs={{0,8},{4,12},{8,0},{12,4},{16,24},{20,28},{24,16},{28,20},{1,9},{5... | collective-permute-start | bytes 1572872 | tf_op jit(solution)/shard_map/ppermute | solution.py:273
  6.2 14.1 %collective-permute-start.4 = (bf16[2,512,256]{2,1,0:T(8,128)(2,1)S(1)}, bf16[2,512,256]{2,1,0:T(8,128)(2,1)S(1)}, u32[]{:S(2)}, u32[]{:S(2)}) collective-permute-start(bf16[2,512,256]{2,1,0:T(8,128)(2,1)S(1)} %pad_maximum_fusion.rest_2_), channel_id=1, source_target_pairs={{0,16},{4,20},{8,24},{12,28},{16,0},{20,4},{24,8},{28,12},{1,17},{... | collective-permute-start | bytes 1572872 | tf_op jit(solution)/shard_map/ppermute | solution.py:273
  9.7 24.1 %collective-permute-start.2 = (bf16[3,512,256]{2,1,0:T(8,128)(2,1)S(1)}, bf16[3,512,256]{2,1,0:T(8,128)(2,1)S(1)}, u32[]{:S(2)}, u32[]{:S(2)}) collective-permute-start(bf16[3,512,256]{2,1,0:T(8,128)(2,1)S(1)} %get-tuple-element.39), channel_id=1, source_target_pairs={{0,4},{4,0},{8,12},{12,8},{16,20},{20,16},{24,28},{28,24},{1,5},{5... | collective-permute-start | bytes 2359304 | tf_op jit(solution)/shard_map/ppermute | solution.py:273
  10.0 3.6 %collective-permute-start.5 = (bf16[512,256]{1,0:T(8,128)(2,1)S(1)}, bf16[512,256]{1,0:T(8,128)(2,1)S(1)}, u32[]{:S(2)}, u32[]{:S(2)}) collective-permute-start(bf16[512,256]{1,0:T(8,128)(2,1)S(1)} %get-tuple-element.68), channel_id=1, source_target_pairs={{0,4},{4,0},{8,12},{12,8},{16,20},{20,16},{24,28},{28,24},{1,5},{5... | collective-permute-start | bytes 786440 | tf_op jit(solution)/shard_map/ppermute | solution.py:273
  11.9 12.5 %collective-permute-start.8 = (bf16[256,256]{1,0:T(8,128)(2,1)S(1)}, bf16[256,256]{1,0:T(8,128)(2,1)S(1)}, u32[]{:S(2)}, u32[]{:S(2)}) collective-permute-start(bf16[256,256]{1,0:T(8,128)(2,1)S(1)} %get-tuple-element.63), channel_id=1, source_target_pairs={{0,1},{1,0},{2,3},{3,2},{4,5},{5,4},{6,7},{7,6},{8,9},{9,8},{10,11... | collective-permute-start | bytes 393224 | tf_op jit(solution)/shard_map/ppermute | solution.py:273
  13.6 21.8 %copy-start.3 = (s32[4,2]{0,1:T(2,128)S(1)}, s32[4,2]{0,1:T(2,128)}, u32[]{:S(2)}) copy-start(s32[4,2]{0,1:T(2,128)} %param.11) | copy-start | bytes 100
  18.4 15.3 %collective-permute-start.6 = (bf16[1,512,256]{2,1,0:T(8,128)(2,1)S(1)}, bf16[1,512,256]{2,1,0:T(8,128)(2,1)S(1)}, u32[]{:S(2)}, u32[]{:S(2)}) collective-permute-start(bf16[1,512,256]{2,1,0:T(8,128)(2,1)S(1)} %slice.58), channel_id=1, source_target_pairs={{0,16},{4,20},{8,24},{12,28},{16,0},{20,4},{24,8},{28,12},{1,17},{... | collective-permute-start | bytes 786440 | tf_op jit(solution)/shard_map/ppermute | solution.py:273
  20.3 13.4 %collective-permute-start.7 = (bf16[1,512,256]{2,1,0:T(8,128)(2,1)S(1)}, bf16[1,512,256]{2,1,0:T(8,128)(2,1)S(1)}, u32[]{:S(2)}, u32[]{:S(2)}) collective-permute-start(bf16[1,512,256]{2,1,0:T(8,128)(2,1)S(1)} %slice.62), channel_id=1, source_target_pairs={{0,8},{4,12},{8,0},{12,4},{16,24},{20,28},{24,16},{28,20},{1,9},{5... | collective-permute-start | bytes 786440 | tf_op jit(solution)/shard_map/ppermute | solution.py:273
  21.9 11.8 %collective-permute-start.9 = (bf16[256,256]{1,0:T(8,128)(2,1)S(1)}, bf16[256,256]{1,0:T(8,128)(2,1)S(1)}, u32[]{:S(2)}, u32[]{:S(2)}) collective-permute-start(bf16[256,256]{1,0:T(8,128)(2,1)S(1)} %get-tuple-element.62), channel_id=1, source_target_pairs={{0,2},{1,3},{2,0},{3,1},{4,6},{5,7},{6,4},{7,5},{8,10},{9,11},{10,... | collective-permute-start | bytes 393224 | tf_op jit(solution)/shard_map/ppermute | solution.py:273
  24.5 9.3 %collective-permute-start.10 = (bf16[256,256]{1,0:T(8,128)(2,1)S(1)}, bf16[256,256]{1,0:T(8,128)(2,1)S(1)}, u32[]{:S(2)}, u32[]{:S(2)}) collective-permute-start(bf16[256,256]{1,0:T(8,128)(2,1)S(1)} %get-tuple-element.61), channel_id=1, source_target_pairs={{0,3},{1,2},{2,1},{3,0},{4,7},{5,6},{6,5},{7,4},{8,11},{9,10},{10,... | collective-permute-start | bytes 393224 | tf_op jit(solution)/shard_map/ppermute | solution.py:273
  33.7 11.1 %collective-permute-start.11 = (bf16[2,512,256]{2,1,0:T(8,128)(2,1)S(1)}, bf16[2,512,256]{2,1,0:T(8,128)(2,1)S(1)}, u32[]{:S(2)}, u32[]{:S(2)}) collective-permute-start(bf16[2,512,256]{2,1,0:T(8,128)(2,1)S(1)} %pad_maximum_fusion.1.rest_1_), channel_id=1, source_target_pairs={{0,8},{4,12},{8,0},{12,4},{16,24},{20,28},{24,16},{28,20},{1,9},{5... | collective-permute-start | bytes 1572872 | tf_op jit(solution)/shard_map/ppermute | solution.py:273
  34.3 11.8 %collective-permute-start.12 = (bf16[2,512,256]{2,1,0:T(8,128)(2,1)S(1)}, bf16[2,512,256]{2,1,0:T(8,128)(2,1)S(1)}, u32[]{:S(2)}, u32[]{:S(2)}) collective-permute-start(bf16[2,512,256]{2,1,0:T(8,128)(2,1)S(1)} %pad_maximum_fusion.1.rest_1_), channel_id=1, source_target_pairs={{0,16},{4,20},{8,24},{12,28},{16,0},{20,4},{24,8},{28,12},{1,17},{... | collective-permute-start | bytes 1572872 | tf_op jit(solution)/shard_map/ppermute | solution.py:273
  44.9 6.4 %collective-permute-start.13 = (bf16[1,512,256]{2,1,0:T(8,128)(2,1)S(1)}, bf16[1,512,256]{2,1,0:T(8,128)(2,1)S(1)}, u32[]{:S(2)}, u32[]{:S(2)}) collective-permute-start(bf16[1,512,256]{2,1,0:T(8,128)(2,1)S(1)} %slice.63), channel_id=1, source_target_pairs={{0,16},{4,20},{8,24},{12,28},{16,0},{20,4},{24,8},{28,12},{1,17},{... | collective-permute-start | bytes 786440 | tf_op jit(solution)/shard_map/ppermute | solution.py:273
  46.2 6.4 %collective-permute-start.14 = (bf16[1,512,256]{2,1,0:T(8,128)(2,1)S(1)}, bf16[1,512,256]{2,1,0:T(8,128)(2,1)S(1)}, u32[]{:S(2)}, u32[]{:S(2)}) collective-permute-start(bf16[1,512,256]{2,1,0:T(8,128)(2,1)S(1)} %slice.64), channel_id=1, source_target_pairs={{0,8},{4,12},{8,0},{12,4},{16,24},{20,28},{24,16},{28,20},{1,9},{5... | collective-permute-start | bytes 786440 | tf_op jit(solution)/shard_map/ppermute | solution.py:273
  54.7 17.4 %collective-permute-start.15 = (bf16[512,256]{1,0:T(8,128)(2,1)S(1)}, bf16[512,256]{1,0:T(8,128)(2,1)S(1)}, u32[]{:S(2)}, u32[]{:S(2)}) collective-permute-start(bf16[512,256]{1,0:T(8,128)(2,1)S(1)} %mix.2.refs_0_), channel_id=1, source_target_pairs={{0,2},{1,3},{2,0},{3,1},{4,6},{5,7},{6,4},{7,5},{8,10},{9,11},{10,... | collective-permute-start | bytes 786440 | tf_op jit(solution)/shard_map/ppermute | solution.py:273
  61.9 11.3 %collective-permute-start.16 = (bf16[512,256]{1,0:T(8,128)(2,1)S(1)}, bf16[512,256]{1,0:T(8,128)(2,1)S(1)}, u32[]{:S(2)}, u32[]{:S(2)}) collective-permute-start(bf16[512,256]{1,0:T(8,128)(2,1)S(1)} %mix.2.refs_0_), channel_id=1, source_target_pairs={{0,1},{1,0},{2,3},{3,2},{4,5},{5,4},{6,7},{7,6},{8,9},{9,8},{10,11... | collective-permute-start | bytes 786440 | tf_op jit(solution)/shard_map/ppermute | solution.py:273
  61.9 11.3 %collective-permute-start.23 = (bf16[3,256,256]{2,1,0:T(8,128)(2,1)S(1)}, bf16[3,256,256]{2,1,0:T(8,128)(2,1)S(1)}, u32[]{:S(2)}, u32[]{:S(2)}) collective-permute-start(bf16[3,256,256]{2,1,0:T(8,128)(2,1)S(1)} %pad_maximum_fusion.2), channel_id=1, source_target_pairs={{0,8},{4,12},{8,0},{12,4},{16,24},{20,28},{24,16},{28,20},{1,9},{5... | collective-permute-start | bytes 1179656 | tf_op jit(solution)/shard_map/ppermute | solution.py:273
  63.0 13.1 %collective-permute-start.24 = (bf16[3,256,256]{2,1,0:T(8,128)(2,1)S(1)}, bf16[3,256,256]{2,1,0:T(8,128)(2,1)S(1)}, u32[]{:S(2)}, u32[]{:S(2)}) collective-permute-start(bf16[3,256,256]{2,1,0:T(8,128)(2,1)S(1)} %pad_maximum_fusion.2), channel_id=1, source_target_pairs={{0,16},{4,20},{8,24},{12,28},{16,0},{20,4},{24,8},{28,12},{1,17},{... | collective-permute-start | bytes 1179656 | tf_op jit(solution)/shard_map/ppermute | solution.py:273
  66.1 8.6 %collective-permute-start.19 = (bf16[512,256]{1,0:T(8,128)(2,1)S(1)}, bf16[512,256]{1,0:T(8,128)(2,1)S(1)}, u32[]{:S(2)}, u32[]{:S(2)}) collective-permute-start(bf16[512,256]{1,0:T(8,128)(2,1)S(1)} %mix.3), channel_id=1, source_target_pairs={{0,4},{4,0},{8,12},{12,8},{16,20},{20,16},{24,28},{28,24},{1,5},{5... | collective-permute-start | bytes 786440 | tf_op jit(solution)/shard_map/ppermute | solution.py:273
  73.2 9.7 %collective-permute-start.25 = (bf16[3,256,256]{2,1,0:T(8,128)(2,1)S(1)}, bf16[3,256,256]{2,1,0:T(8,128)(2,1)S(1)}, u32[]{:S(2)}, u32[]{:S(2)}) collective-permute-start(bf16[3,256,256]{2,1,0:T(8,128)(2,1)S(1)} %collective-permute-done.23), channel_id=1, source_target_pairs={{0,16},{4,20},{8,24},{12,28},{16,0},{20,4},{24,8},{28,12},{1,17},{... | collective-permute-start | bytes 1179656 | tf_op jit(solution)/shard_map/ppermute | solution.py:273
  74.7 18.0 %collective-permute-start.20 = (bf16[512,256]{1,0:T(8,128)(2,1)S(1)}, bf16[512,256]{1,0:T(8,128)(2,1)S(1)}, u32[]{:S(2)}, u32[]{:S(2)}) collective-permute-start(bf16[512,256]{1,0:T(8,128)(2,1)S(1)} %collective-permute-done.19.refs_3_), channel_id=1, source_target_pairs={{0,2},{1,3},{2,0},{3,1},{4,6},{5,7},{6,4},{7,5},{8,10},{9,11},{10,... | collective-permute-start | bytes 786440 | tf_op jit(solution)/shard_map/ppermute | solution.py:273
  74.8 17.9 %collective-permute-start.26 = (bf16[512,256]{1,0:T(8,128)(2,1)S(1)}, bf16[512,256]{1,0:T(8,128)(2,1)S(1)}, u32[]{:S(2)}, u32[]{:S(2)}) collective-permute-start(bf16[512,256]{1,0:T(8,128)(2,1)S(1)} %collective-permute-done.19.refs_3_), channel_id=1, source_target_pairs={{0,1},{1,0},{2,3},{3,2},{4,5},{5,4},{6,7},{7,6},{8,9},{9,8},{10,11... | collective-permute-start | bytes 786440 | tf_op jit(solution)/shard_map/ppermute | solution.py:273
  75.4 7.5 %collective-permute-start.17 = (bf16[512,256]{1,0:T(8,128)(2,1)S(1)}, bf16[512,256]{1,0:T(8,128)(2,1)S(1)}, u32[]{:S(2)}, u32[]{:S(2)}) collective-permute-start(bf16[512,256]{1,0:T(8,128)(2,1)S(1)} %mix.2.refs_0_), channel_id=1, source_target_pairs={{1,2},{2,1},{5,6},{6,5},{9,10},{10,9},{13,14},{14,13},{17,18},{18,... | collective-permute-start | bytes 786440 | tf_op jit(solution)/shard_map/ppermute | solution.py:357
  76.1 16.6 %collective-permute-start.18 = (bf16[512,256]{1,0:T(8,128)(2,1)S(1)}, bf16[512,256]{1,0:T(8,128)(2,1)S(1)}, u32[]{:S(2)}, u32[]{:S(2)}) collective-permute-start(bf16[512,256]{1,0:T(8,128)(2,1)S(1)} %collective-permute-done.15.refs_2_), channel_id=1, source_target_pairs={{2,3},{1,0},{6,7},{5,4},{10,11},{9,8},{14,15},{13,12},{18,19},{17,... | collective-permute-start | bytes 786440 | tf_op jit(solution)/shard_map/ppermute | solution.py:358
  92.7 3.4 %collective-permute-start.27 = (bf16[12,256,256]{2,1,0:T(8,128)(2,1)S(1)}, bf16[12,256,256]{2,1,0:T(8,128)(2,1)S(1)}, u32[]{:S(2)}, u32[]{:S(2)}) collective-permute-start(bf16[12,256,256]{2,1,0:T(8,128)(2,1)S(1)} %constant_dynamic-update-slice_fusion.refs_7_.refs_5_), channel_id=1, source_target_pairs={{0,4},{4,0},{8,12},{12,8},{16,20},{20,16},{24,28},{28,24},{1,5},{5... | collective-permute-start | bytes 4718600 | tf_op jit(solution)/shard_map/ppermute | solution.py:273
  92.7 5.8 %collective-permute-start.21 = (bf16[512,256]{1,0:T(8,128)(2,1)S(1)}, bf16[512,256]{1,0:T(8,128)(2,1)S(1)}, u32[]{:S(2)}, u32[]{:S(2)}) collective-permute-start(bf16[512,256]{1,0:T(8,128)(2,1)S(1)} %collective-permute-done.19.refs_3_), channel_id=1, source_target_pairs={{1,2},{2,1},{5,6},{6,5},{9,10},{10,9},{13,14},{14,13},{17,18},{18,... | collective-permute-start | bytes 786440 | tf_op jit(solution)/shard_map/ppermute | solution.py:359
  93.4 10.6 %collective-permute-start.22 = (bf16[512,256]{1,0:T(8,128)(2,1)S(1)}, bf16[512,256]{1,0:T(8,128)(2,1)S(1)}, u32[]{:S(2)}, u32[]{:S(2)}) collective-permute-start(bf16[512,256]{1,0:T(8,128)(2,1)S(1)} %collective-permute-done.20.refs_5_), channel_id=1, source_target_pairs={{2,3},{1,0},{6,7},{5,4},{10,11},{9,8},{14,15},{13,12},{18,19},{17,... | collective-permute-start | bytes 786440 | tf_op jit(solution)/shard_map/ppermute | solution.py:360
  (2 other events, 4.0 us)

commit v12 on v10

--- a/solution.py
+++ b/solution.py
@@ -359,10 +359,10 @@
     back = over_core(pair)
     two_own = swap(own, "tp", 2, tp_size)
     one_own = swap(own, "tp", 1, tp_size)
-    later = after(back, two_own, one_own)
+    later = after(back, two_own)
     two_back = swap(later, "tp", 2, tp_size)
     one_back = swap(later, "tp", 1, tp_size)
-    three_own = lax.ppermute(after(own, two_own), "tp", [(1, 2), (2, 1)])
+    three_own = lax.ppermute(after(own, two_own, one_own), "tp", [(1, 2), (2, 1)])
     forward_own = lax.ppermute(two_own, "tp", [(2, 3), (1, 0)])
     three_back = lax.ppermute(after(later, two_back), "tp", [(1, 2), (2, 1)])
     forward_back = lax.ppermute(two_back, "tp", [(2, 3), (1, 0)])

time: 104 us -> 101 us (0.971)
  waiting for transfers between devices: 46 us -> 41.2 us
  starting transfers between devices: 32.7 us -> 34.3 us
    ppermute x23, waiting for transfers between devices: 31.5 us -> 26.4 us  [swap(): return lax.ppermute(x, axis, [(i, i ^ mask) for i in range(size)])]
    ppermute x23, starting transfers between devices: 28.8 us -> 30.3 us  [swap(): return lax.ppermute(x, axis, [(i, i ^ mask) for i in range(size)])]
where the time goes in v12:
time: 101 us; the launch traced here: 100 us
  waiting for transfers between devices  41.2 us (41%)
  starting transfers between devices  34.3 us (34%)
  Pallas kernels  18.8 us (19%)
  local copies, waits for them, and re-layouts  5.41 us (5%)
    ppermute x23, starting transfers between devices, swap(): return lax.ppermute(x, axis, [(i, i ^ mask) for i in range(size)])  30.3 us
    ppermute x23, waiting for transfers between devices, swap(): return lax.ppermute(x, axis, [(i, i ^ mask) for i in range(size)])  26.4 us
    pallas_call x1, Pallas kernels, score(): pl.pallas_call(functools.partial(score_kernel, len(sufs), tuple((p.shape[...  8.18 us
    ppermute x1, waiting for transfers between devices, split_heads(): forward_own = lax.ppermute(two_own, 'tp', [(2, 3), (1, 0)])  8.02 us
    ppermute x1, waiting for transfers between devices, split_heads(): forward_back = lax.ppermute(two_back, 'tp', [(2, 3), (1, 0)])  6.8 us
    pallas_call x2, Pallas kernels, project(): pl.pallas_call(functools.partial(proj_kernel, steps, add is not None), ou...  4.56 us
    pallas_call x2, Pallas kernels, mix(): pl.pallas_call(functools.partial(mix_kernel, nb, base, tuple((p.shape[0]...  4.26 us
  transfers between devices with their start and end apart: 27, of which 13 were waited for; matrix products, arithmetic and copies ran while one was open for 4% of the time, Pallas kernels for 16%

profile of v12, /device:TPU:0, one launch (start us, length us, event | category | flops | bytes accessed | tf_op | source)
XLA Modules:
  0.0 100.4 jit_solution(15503471997435816016)
XLA Ops:
  0.0 1.5 %copy.15 = bf16[512,1,512]{2,0,1:T(8,128)(2,1)S(1)} copy(bf16[512,1,512]{2,1,0:T(2,128)(2,1)} %bitcast.24) | data formatting | bytes 1048576
  3.3 2.9 %collective-permute-start.3 = (bf16[2,512,256]{2,1,0:T(8,128)(2,1)S(1)}, bf16[2,512,256]{2,1,0:T(8,128)(2,1)S(1)}, u32[]{:S(2)}, u32[]{:S(2)}) collective-permute-start(bf16[2,512,256]{2,1,0:T(8,128)(2,1)S(1)} %pad_maximum_fusion.1.rest_2_), channel_id=1, source_target_pairs={{0,8},{4,12},{8,0},{12,4},{16,24},{20,28},{24,16},{28,20},{1,9},{5... | collective-permute-start | bytes 1572872 | tf_op jit(solution)/shard_map/ppermute | solution.py:280
  6.2 1.5 %collective-permute-start.4 = (bf16[2,512,256]{2,1,0:T(8,128)(2,1)S(1)}, bf16[2,512,256]{2,1,0:T(8,128)(2,1)S(1)}, u32[]{:S(2)}, u32[]{:S(2)}) collective-permute-start(bf16[2,512,256]{2,1,0:T(8,128)(2,1)S(1)} %pad_maximum_fusion.1.rest_2_), channel_id=1, source_target_pairs={{0,16},{4,20},{8,24},{12,28},{16,0},{20,4},{24,8},{28,12},{1,17},{... | collective-permute-start | bytes 1572872 | tf_op jit(solution)/shard_map/ppermute | solution.py:280
  7.9 1.8 %prepare.1 = (s32[1024,128]{1,0:T(8,128)S(1)}, s32[1024,128]{1,0:T(8,128)S(1)}, bf16[3,512,256]{2,1,0:T(8,128)(2,1)S(1)}, bf16[3,512,256]{2,1,0:T(8,128)(2,1)S(1)}) custom-call(s32[3]{0:T(128)S(1)} %pad_add_fusion.1.where_ref, s32[2,8]{1,0:T(2,128)S(1)} %pad_add_fusion.refs_0_, s32[2,8]{1,0:T(2,128)S(1)} %collective-permute-done.1.refs_1_, ...), custom_call_target="tpu_custom_call" | custom-call | tf_op jit(solution)/shard_map/prepare/pallas_call | solution.py:101
  10.6 1.7 %fusion = (bf16[256,512]{1,0:T(8,128)(2,1)S(1)}, bf16[256,512]{1,0:T(8,128)(2,1)S(1)}, bf16[256,512]{1,0:T(8,128)(2,1)S(1)}) fusion(bf16[512,4096]{1,0:T(8,128)(2,1)} %param.12, u32[]{:T(128)S(6)} %mul.20, u32[]{:T(128)S(6)} %add.17, u32[]{:T(128)S(6)} %add.16, u32[]{:T(128)S(6)} %add.15), kind=kLoop, calls=%fused_computation.18 | loop fusion | bytes 1572880 | tf_op jit(solution)/shard_map/dynamic_slice | solution.py:316
  12.2 1.6 %collective-permute-start.8 = (bf16[256,512]{1,0:T(8,128)(2,1)S(1)}, bf16[256,512]{1,0:T(8,128)(2,1)S(1)}, u32[]{:S(2)}, u32[]{:S(2)}) collective-permute-start(bf16[256,512]{1,0:T(8,128)(2,1)S(1)} %get-tuple-element.63), channel_id=1, source_target_pairs={{0,1},{1,0},{2,3},{3,2},{4,5},{5,4},{6,7},{7,6},{8,9},{9,8},{10,11... | collective-permute-start | bytes 786440 | tf_op jit(solution)/shard_map/ppermute | solution.py:280
  13.9 2.6 %collective-permute-start.9 = (bf16[256,512]{1,0:T(8,128)(2,1)S(1)}, bf16[256,512]{1,0:T(8,128)(2,1)S(1)}, u32[]{:S(2)}, u32[]{:S(2)}) collective-permute-start(bf16[256,512]{1,0:T(8,128)(2,1)S(1)} %get-tuple-element.62), channel_id=1, source_target_pairs={{0,2},{1,3},{2,0},{3,1},{4,6},{5,7},{6,4},{7,5},{8,10},{9,11},{10,... | collective-permute-start | bytes 786440 | tf_op jit(solution)/shard_map/ppermute | solution.py:280
  16.5 1.9 %collective-permute-done.3.rest_3_ = bf16[2,512,256]{2,1,0:T(8,128)(2,1)S(1)} collective-permute-done((bf16[2,512,256]{2,1,0:T(8,128)(2,1)S(1)}, bf16[2,512,256]{2,1,0:T(8,128)(2,1)S(1)}, u32[]{:S(2)}, u32[]{:S(2)}) %collective-permute-start.3) | collective-permute-done | bytes 524320 | tf_op jit(solution)/shard_map/ppermute | solution.py:280
  18.5 1.8 %collective-permute-start.6 = (bf16[1,512,256]{2,1,0:T(8,128)(2,1)S(1)}, bf16[1,512,256]{2,1,0:T(8,128)(2,1)S(1)}, u32[]{:S(2)}, u32[]{:S(2)}) collective-permute-start(bf16[1,512,256]{2,1,0:T(8,128)(2,1)S(1)} %slice.58), channel_id=1, source_target_pairs={{0,16},{4,20},{8,24},{12,28},{16,0},{20,4},{24,8},{28,12},{1,17},{... | collective-permute-start | bytes 786440 | tf_op jit(solution)/shard_map/ppermute | solution.py:280
  20.3 1.6 %collective-permute-start.7 = (bf16[1,512,256]{2,1,0:T(8,128)(2,1)S(1)}, bf16[1,512,256]{2,1,0:T(8,128)(2,1)S(1)}, u32[]{:S(2)}, u32[]{:S(2)}) collective-permute-start(bf16[1,512,256]{2,1,0:T(8,128)(2,1)S(1)} %slice.62), channel_id=1, source_target_pairs={{0,8},{4,12},{8,0},{12,4},{16,24},{20,28},{24,16},{28,20},{1,9},{5... | collective-permute-start | bytes 786440 | tf_op jit(solution)/shard_map/ppermute | solution.py:280
  21.9 1.9 %constant_dynamic-slice_fusion.refs_6_.refs_4_ = bf16[512,1024]{1,0:T(8,128)(2,1)S(1)} fusion(bf16[512,4096]{1,0:T(8,128)(2,1)} %param.12, u32[]{:T(128)S(6)} %mul.21), kind=kLoop, calls=%fused_computation.16 | loop fusion | bytes 2097156 | tf_op jit(solution)/shard_map/dynamic_slice | solution.py:319
  23.8 2.3 %collective-permute-done.8 = bf16[256,512]{1,0:T(8,128)(2,1)S(1)} collective-permute-done((bf16[256,512]{1,0:T(8,128)(2,1)S(1)}, bf16[256,512]{1,0:T(8,128)(2,1)S(1)}, u32[]{:S(2)}, u32[]{:S(2)}) %collective-permute-start.8) | collective-permute-done | bytes 262176 | tf_op jit(solution)/shard_map/ppermute | solution.py:280
  26.0 2.4 %collective-permute-done.9 = bf16[256,512]{1,0:T(8,128)(2,1)S(1)} collective-permute-done((bf16[256,512]{1,0:T(8,128)(2,1)S(1)}, bf16[256,512]{1,0:T(8,128)(2,1)S(1)}, u32[]{:S(2)}, u32[]{:S(2)}) %collective-permute-start.9) | collective-permute-done | bytes 262176 | tf_op jit(solution)/shard_map/ppermute | solution.py:280
  29.6 3.6 %collective-permute-start.12 = (bf16[256,512]{1,0:T(8,128)(2,1)S(1)}, bf16[256,512]{1,0:T(8,128)(2,1)S(1)}, u32[]{:S(2)}, u32[]{:S(2)}) collective-permute-start(bf16[256,512]{1,0:T(8,128)(2,1)S(1)} %get-tuple-element.53), channel_id=1, source_target_pairs={{0,3},{1,2},{2,1},{3,0},{4,7},{5,6},{6,5},{7,4},{8,11},{9,10},{10,... | collective-permute-start | bytes 786440 | tf_op jit(solution)/shard_map/ppermute | solution.py:280
  33.3 8.2 %score.1 = (bf16[1024,1024]{1,0:T(8,128)(2,1)S(1)}, bf16[1024,256]{1,0:T(8,128)(2,1)S(1)}, f32[1024,128]{1,0:T(8,128)S(1)}) custom-call(s32[8]{0:T(128)S(1)} %select_reduce_fusion.place_ref, s32[1024,128]{1,0:T(8,128)S(1)} %get-tuple-element.37.first_ref, s32[1024,128]{1,0:T(8,128)S(1)} %get-tuple-element.36.grp_ref, ...), custom_call_target="tpu_custom_call" | custom-call | tf_op jit(solution)/shard_map/score/pallas_call | solution.py:176
  41.7 1.6 %collective-permute-start.13 = (bf16[1,512,256]{2,1,0:T(8,128)(2,1)S(1)}, bf16[1,512,256]{2,1,0:T(8,128)(2,1)S(1)}, u32[]{:S(2)}, u32[]{:S(2)}) collective-permute-start(bf16[1,512,256]{2,1,0:T(8,128)(2,1)S(1)} %slice.63), channel_id=1, source_target_pairs={{0,16},{4,20},{8,24},{12,28},{16,0},{20,4},{24,8},{28,12},{1,17},{... | collective-permute-start | bytes 786440 | tf_op jit(solution)/shard_map/ppermute | solution.py:280
  43.9 4.2 %collective-permute-done.13.rest_4_ = bf16[1,512,256]{2,1,0:T(8,128)(2,1)S(1)} collective-permute-done((bf16[1,512,256]{2,1,0:T(8,128)(2,1)S(1)}, bf16[1,512,256]{2,1,0:T(8,128)(2,1)S(1)}, u32[]{:S(2)}, u32[]{:S(2)}) %collective-permute-start.13) | collective-permute-done | bytes 262176 | tf_op jit(solution)/shard_map/ppermute | solution.py:280
  48.1 2.8 %collective-permute-done.14.rest_5_ = bf16[1,512,256]{2,1,0:T(8,128)(2,1)S(1)} collective-permute-done((bf16[1,512,256]{2,1,0:T(8,128)(2,1)S(1)}, bf16[1,512,256]{2,1,0:T(8,128)(2,1)S(1)}, u32[]{:S(2)}, u32[]{:S(2)}) %collective-permute-start.14) | collective-permute-done | bytes 262176 | tf_op jit(solution)/shard_map/ppermute | solution.py:280
  50.9 2.2 %mix.2.refs_0_ = bf16[512,256]{1,0:T(8,128)(2,1)S(1)} custom-call(s32[8]{0:T(128)S(1)} %select_reduce_fusion.place_ref, s32[1024,128]{1,0:T(8,128)S(1)} %get-tuple-element.36.grp_ref, bf16[1024,1024]{1,0:T(8,128)(2,1)S(1)} %get-tuple-element.43.p_ref, bf16[1024,256]{1,0:T(8,128)(2,1)S(1)} %get-tuple-element.44.near_ref, ...), custom_call_target="tpu_custom_call" | custom-call | tf_op jit(solution)/shard_map/mix/pallas_call | solution.py:225
  53.1 2.0 %collective-permute-start.15 = (bf16[512,256]{1,0:T(8,128)(2,1)S(1)}, bf16[512,256]{1,0:T(8,128)(2,1)S(1)}, u32[]{:S(2)}, u32[]{:S(2)}) collective-permute-start(bf16[512,256]{1,0:T(8,128)(2,1)S(1)} %mix.2.refs_0_), channel_id=1, source_target_pairs={{0,2},{1,3},{2,0},{3,1},{4,6},{5,7},{6,4},{7,5},{8,10},{9,11},{10,... | collective-permute-start | bytes 786440 | tf_op jit(solution)/shard_map/ppermute | solution.py:280
  55.1 2.2 %collective-permute-start.16 = (bf16[512,256]{1,0:T(8,128)(2,1)S(1)}, bf16[512,256]{1,0:T(8,128)(2,1)S(1)}, u32[]{:S(2)}, u32[]{:S(2)}) collective-permute-start(bf16[512,256]{1,0:T(8,128)(2,1)S(1)} %mix.2.refs_0_), channel_id=1, source_target_pairs={{0,1},{1,0},{2,3},{3,2},{4,5},{5,4},{6,7},{7,6},{8,9},{9,8},{10,11... | collective-permute-start | bytes 786440 | tf_op jit(solution)/shard_map/ppermute | solution.py:280
  57.4 2.0 %mix.3 = bf16[512,256]{1,0:T(8,128)(2,1)S(1)} custom-call(s32[8]{0:T(128)S(1)} %select_reduce_fusion.place_ref, s32[1024,128]{1,0:T(8,128)S(1)} %get-tuple-element.36.grp_ref, bf16[1024,1024]{1,0:T(8,128)(2,1)S(1)} %get-tuple-element.43.p_ref, bf16[1024,256]{1,0:T(8,128)(2,1)S(1)} %get-tuple-element.44.near_ref, f32[1024,128]{1,0:T(8,128)S(1)} %get-tuple-element.45.den_ref, ...), custom_call_target="tpu_custom_call" | custom-call | tf_op jit(solution)/shard_map/mix/pallas_call | solution.py:225
  59.5 4.4 %collective-permute-done.15.refs_2_ = bf16[512,256]{1,0:T(8,128)(2,1)S(1)} collective-permute-done((bf16[512,256]{1,0:T(8,128)(2,1)S(1)}, bf16[512,256]{1,0:T(8,128)(2,1)S(1)}, u32[]{:S(2)}, u32[]{:S(2)}) %collective-permute-start.15) | collective-permute-done | bytes 262176 | tf_op jit(solution)/shard_map/ppermute | solution.py:280
  65.0 1.3 %collective-permute-start.18 = (bf16[512,256]{1,0:T(8,128)(2,1)S(1)}, bf16[512,256]{1,0:T(8,128)(2,1)S(1)}, u32[]{:S(2)}, u32[]{:S(2)}) collective-permute-start(bf16[512,256]{1,0:T(8,128)(2,1)S(1)} %collective-permute-done.15.refs_2_), channel_id=1, source_target_pairs={{2,3},{1,0},{6,7},{5,4},{10,11},{9,8},{14,15},{13,12},{18,19},{17,... | collective-permute-start | bytes 786440 | tf_op jit(solution)/shard_map/ppermute | solution.py:366
  66.3 5.7 %collective-permute-start.20 = (bf16[512,256]{1,0:T(8,128)(2,1)S(1)}, bf16[512,256]{1,0:T(8,128)(2,1)S(1)}, u32[]{:S(2)}, u32[]{:S(2)}) collective-permute-start(bf16[512,256]{1,0:T(8,128)(2,1)S(1)} %collective-permute-done.19.refs_3_), channel_id=1, source_target_pairs={{0,2},{1,3},{2,0},{3,1},{4,6},{5,7},{6,4},{7,5},{8,10},{9,11},{10,... | collective-permute-start | bytes 786440 | tf_op jit(solution)/shard_map/ppermute | solution.py:280
  72.0 8.0 %collective-permute-done.18.refs_1_ = bf16[512,256]{1,0:T(8,128)(2,1)S(1)} collective-permute-done((bf16[512,256]{1,0:T(8,128)(2,1)S(1)}, bf16[512,256]{1,0:T(8,128)(2,1)S(1)}, u32[]{:S(2)}, u32[]{:S(2)}) %collective-permute-start.18) | collective-permute-done | bytes 262176 | tf_op jit(solution)/shard_map/ppermute | solution.py:366
  80.0 5.2 %collective-permute-done.20.refs_5_ = bf16[512,256]{1,0:T(8,128)(2,1)S(1)} collective-permute-done((bf16[512,256]{1,0:T(8,128)(2,1)S(1)}, bf16[512,256]{1,0:T(8,128)(2,1)S(1)}, u32[]{:S(2)}, u32[]{:S(2)}) %collective-permute-start.20) | collective-permute-done | bytes 262176 | tf_op jit(solution)/shard_map/ppermute | solution.py:280
  85.3 1.5 %collective-permute-done.25.refs_4_ = bf16[512,256]{1,0:T(8,128)(2,1)S(1)} collective-permute-done((bf16[512,256]{1,0:T(8,128)(2,1)S(1)}, bf16[512,256]{1,0:T(8,128)(2,1)S(1)}, u32[]{:S(2)}, u32[]{:S(2)}) %collective-permute-start.25) | collective-permute-done | bytes 262176 | tf_op jit(solution)/shard_map/ppermute | solution.py:280
  87.4 1.3 %collective-permute-start.22 = (bf16[512,256]{1,0:T(8,128)(2,1)S(1)}, bf16[512,256]{1,0:T(8,128)(2,1)S(1)}, u32[]{:S(2)}, u32[]{:S(2)}) collective-permute-start(bf16[512,256]{1,0:T(8,128)(2,1)S(1)} %collective-permute-done.20.refs_5_), channel_id=1, source_target_pairs={{2,3},{1,0},{6,7},{5,4},{10,11},{9,8},{14,15},{13,12},{18,19},{17,... | collective-permute-start | bytes 786440 | tf_op jit(solution)/shard_map/ppermute | solution.py:368
  89.0 2.3 %project.2.refs_9_ = f32[512,1024]{1,0:T(8,128)S(1)} custom-call(s32[3]{0:T(128)S(1)} %pad_add_fusion.1.where_ref, bf16[512,256]{1,0:T(8,128)(2,1)S(1)} %mix.2.refs_0_, bf16[512,256]{1,0:T(8,128)(2,1)S(1)} %collective-permute-done.16.refs_1_, bf16[512,256]{1,0:T(8,128)(2,1)S(1)} %collective-permute-done.15.refs_2_, ...), custom_call_target="tpu_custom_call" | custom-call | tf_op jit(solution)/shard_map/project/pallas_call | solution.py:269
  91.4 6.8 %collective-permute-done.22.refs_3_ = bf16[512,256]{1,0:T(8,128)(2,1)S(1)} collective-permute-done((bf16[512,256]{1,0:T(8,128)(2,1)S(1)}, bf16[512,256]{1,0:T(8,128)(2,1)S(1)}, u32[]{:S(2)}, u32[]{:S(2)}) %collective-permute-start.22) | collective-permute-done | bytes 262176 | tf_op jit(solution)/shard_map/ppermute | solution.py:368
  98.2 2.2 %project.3 = bf16[512,1024]{1,0:T(8,128)(2,1)} custom-call(s32[3]{0:T(128)S(1)} %pad_add_fusion.1.where_ref, bf16[512,256]{1,0:T(8,128)(2,1)S(1)} %collective-permute-done.17.refs_0_, bf16[512,256]{1,0:T(8,128)(2,1)S(1)} %collective-permute-done.18.refs_1_, bf16[512,256]{1,0:T(8,128)(2,1)S(1)} %collective-permute-done.21.refs_2_, ...), custom_call_target="tpu_custom_call" | custom-call | tf_op jit(solution)/shard_map/project/pallas_call | solution.py:269
  (60 shorter events, 7.1 us)
Async XLA Ops:
  0.0 2.1 %copy-start.5 = (s32[1,8]{1,0:T(1,128)S(1)}, s32[1,8]{1,0:T(1,128)}, u32[]{:S(2)}) copy-start(s32[1,8]{1,0:T(1,128)} %param.9) | copy-start | bytes 100
  0.0 7.7 %copy-start.2 = (bf16[512,3,512]{2,0,1:T(8,128)(2,1)S(1)}, bf16[512,3,512]{2,0,1:T(8,128)(2,1)}, u32[]{:S(2)}) copy-start(bf16[512,3,512]{2,0,1:T(8,128)(2,1)} %param.7) | copy-start | bytes 4718596
  1.5 1.7 %collective-permute-start = (bf16[512,256]{1,0:T(8,128)(2,1)S(1)}, bf16[512,256]{1,0:T(8,128)(2,1)S(1)}, u32[]{:S(2)}, u32[]{:S(2)}) collective-permute-start(bf16[512,256]{1,0:T(8,128)(2,1)S(1)} %get-tuple-element.70), channel_id=1, source_target_pairs={{0,4},{4,0},{8,12},{12,8},{16,20},{20,16},{24,28},{28,24},{1,5},{5... | collective-permute-start | bytes 786440 | tf_op jit(solution)/shard_map/ppermute | solution.py:280
  2.1 5.8 %collective-permute-start.1 = (s32[2,8]{1,0:T(2,128)S(1)}, s32[2,8]{1,0:T(2,128)S(1)}, u32[]{:S(2)}, u32[]{:S(2)}) collective-permute-start(s32[2,8]{1,0:T(2,128)S(1)} %pad_add_fusion.refs_0_), channel_id=1, source_target_pairs={{0,4},{4,0},{8,12},{12,8},{16,20},{20,16},{24,28},{28,24},{1,5},{5... | collective-permute-start | bytes 200 | tf_op jit(solution)/shard_map/ppermute | solution.py:280
  3.2 4.6 %copy-start = (f32[128,256]{1,0:T(8,128)S(1)}, f32[128,256]{1,0:T(8,128)}, u32[]{:S(2)}) copy-start(f32[128,256]{1,0:T(8,128)} %constant.28.clone.refs_5_) | copy-start | bytes 393220
  3.3 6.5 %copy-start.1 = (bf16[512,2,512]{2,1,0:T(2,128)(2,1)S(1)}, bf16[512,2,512]{2,1,0:T(2,128)(2,1)}, u32[]{:S(2)}) copy-start(bf16[512,2,512]{2,1,0:T(2,128)(2,1)} %param.8) | copy-start | bytes 3145732
  3.3 15.2 %collective-permute-start.3 = (bf16[2,512,256]{2,1,0:T(8,128)(2,1)S(1)}, bf16[2,512,256]{2,1,0:T(8,128)(2,1)S(1)}, u32[]{:S(2)}, u32[]{:S(2)}) collective-permute-start(bf16[2,512,256]{2,1,0:T(8,128)(2,1)S(1)} %pad_maximum_fusion.1.rest_2_), channel_id=1, source_target_pairs={{0,8},{4,12},{8,0},{12,4},{16,24},{20,28},{24,16},{28,20},{1,9},{5... | collective-permute-start | bytes 1572872 | tf_op jit(solution)/shard_map/ppermute | solution.py:280
  6.2 14.1 %collective-permute-start.4 = (bf16[2,512,256]{2,1,0:T(8,128)(2,1)S(1)}, bf16[2,512,256]{2,1,0:T(8,128)(2,1)S(1)}, u32[]{:S(2)}, u32[]{:S(2)}) collective-permute-start(bf16[2,512,256]{2,1,0:T(8,128)(2,1)S(1)} %pad_maximum_fusion.1.rest_2_), channel_id=1, source_target_pairs={{0,16},{4,20},{8,24},{12,28},{16,0},{20,4},{24,8},{28,12},{1,17},{... | collective-permute-start | bytes 1572872 | tf_op jit(solution)/shard_map/ppermute | solution.py:280
  9.7 18.7 %collective-permute-start.2 = (bf16[3,512,256]{2,1,0:T(8,128)(2,1)S(1)}, bf16[3,512,256]{2,1,0:T(8,128)(2,1)S(1)}, u32[]{:S(2)}, u32[]{:S(2)}) collective-permute-start(bf16[3,512,256]{2,1,0:T(8,128)(2,1)S(1)} %get-tuple-element.39), channel_id=1, source_target_pairs={{0,4},{4,0},{8,12},{12,8},{16,20},{20,16},{24,28},{28,24},{1,5},{5... | collective-permute-start | bytes 2359304 | tf_op jit(solution)/shard_map/ppermute | solution.py:280
  10.0 3.9 %collective-permute-start.5 = (bf16[512,256]{1,0:T(8,128)(2,1)S(1)}, bf16[512,256]{1,0:T(8,128)(2,1)S(1)}, u32[]{:S(2)}, u32[]{:S(2)}) collective-permute-start(bf16[512,256]{1,0:T(8,128)(2,1)S(1)} %get-tuple-element.68), channel_id=1, source_target_pairs={{0,4},{4,0},{8,12},{12,8},{16,20},{20,16},{24,28},{28,24},{1,5},{5... | collective-permute-start | bytes 786440 | tf_op jit(solution)/shard_map/ppermute | solution.py:280
  12.2 13.8 %collective-permute-start.8 = (bf16[256,512]{1,0:T(8,128)(2,1)S(1)}, bf16[256,512]{1,0:T(8,128)(2,1)S(1)}, u32[]{:S(2)}, u32[]{:S(2)}) collective-permute-start(bf16[256,512]{1,0:T(8,128)(2,1)S(1)} %get-tuple-element.63), channel_id=1, source_target_pairs={{0,1},{1,0},{2,3},{3,2},{4,5},{5,4},{6,7},{7,6},{8,9},{9,8},{10,11... | collective-permute-start | bytes 786440 | tf_op jit(solution)/shard_map/ppermute | solution.py:280
  13.9 14.5 %collective-permute-start.9 = (bf16[256,512]{1,0:T(8,128)(2,1)S(1)}, bf16[256,512]{1,0:T(8,128)(2,1)S(1)}, u32[]{:S(2)}, u32[]{:S(2)}) collective-permute-start(bf16[256,512]{1,0:T(8,128)(2,1)S(1)} %get-tuple-element.62), channel_id=1, source_target_pairs={{0,2},{1,3},{2,0},{3,1},{4,6},{5,7},{6,4},{7,5},{8,10},{9,11},{10,... | collective-permute-start | bytes 786440 | tf_op jit(solution)/shard_map/ppermute | solution.py:280
  16.5 16.8 %copy-start.3 = (s32[4,2]{0,1:T(2,128)S(1)}, s32[4,2]{0,1:T(2,128)}, u32[]{:S(2)}) copy-start(s32[4,2]{0,1:T(2,128)} %param.11) | copy-start | bytes 100
  18.5 9.9 %collective-permute-start.6 = (bf16[1,512,256]{2,1,0:T(8,128)(2,1)S(1)}, bf16[1,512,256]{2,1,0:T(8,128)(2,1)S(1)}, u32[]{:S(2)}, u32[]{:S(2)}) collective-permute-start(bf16[1,512,256]{2,1,0:T(8,128)(2,1)S(1)} %slice.58), channel_id=1, source_target_pairs={{0,16},{4,20},{8,24},{12,28},{16,0},{20,4},{24,8},{28,12},{1,17},{... | collective-permute-start | bytes 786440 | tf_op jit(solution)/shard_map/ppermute | solution.py:280
  20.3 8.1 %collective-permute-start.7 = (bf16[1,512,256]{2,1,0:T(8,128)(2,1)S(1)}, bf16[1,512,256]{2,1,0:T(8,128)(2,1)S(1)}, u32[]{:S(2)}, u32[]{:S(2)}) collective-permute-start(bf16[1,512,256]{2,1,0:T(8,128)(2,1)S(1)} %slice.62), channel_id=1, source_target_pairs={{0,8},{4,12},{8,0},{12,4},{16,24},{20,28},{24,16},{28,20},{1,9},{5... | collective-permute-start | bytes 786440 | tf_op jit(solution)/shard_map/ppermute | solution.py:280
  28.4 13.2 %collective-permute-start.10 = (bf16[2,512,256]{2,1,0:T(8,128)(2,1)S(1)}, bf16[2,512,256]{2,1,0:T(8,128)(2,1)S(1)}, u32[]{:S(2)}, u32[]{:S(2)}) collective-permute-start(bf16[2,512,256]{2,1,0:T(8,128)(2,1)S(1)} %pad_maximum_fusion.2.rest_1_), channel_id=1, source_target_pairs={{0,8},{4,12},{8,0},{12,4},{16,24},{20,28},{24,16},{28,20},{1,9},{5... | collective-permute-start | bytes 1572872 | tf_op jit(solution)/shard_map/ppermute | solution.py:280
  29.1 14.1 %collective-permute-start.11 = (bf16[2,512,256]{2,1,0:T(8,128)(2,1)S(1)}, bf16[2,512,256]{2,1,0:T(8,128)(2,1)S(1)}, u32[]{:S(2)}, u32[]{:S(2)}) collective-permute-start(bf16[2,512,256]{2,1,0:T(8,128)(2,1)S(1)} %pad_maximum_fusion.2.rest_1_), channel_id=1, source_target_pairs={{0,16},{4,20},{8,24},{12,28},{16,0},{20,4},{24,8},{28,12},{1,17},{... | collective-permute-start | bytes 1572872 | tf_op jit(solution)/shard_map/ppermute | solution.py:280
  29.6 11.9 %collective-permute-start.12 = (bf16[256,512]{1,0:T(8,128)(2,1)S(1)}, bf16[256,512]{1,0:T(8,128)(2,1)S(1)}, u32[]{:S(2)}, u32[]{:S(2)}) collective-permute-start(bf16[256,512]{1,0:T(8,128)(2,1)S(1)} %get-tuple-element.53), channel_id=1, source_target_pairs={{0,3},{1,2},{2,1},{3,0},{4,7},{5,6},{6,5},{7,4},{8,11},{9,10},{10,... | collective-permute-start | bytes 786440 | tf_op jit(solution)/shard_map/ppermute | solution.py:280
  41.7 6.4 %collective-permute-start.13 = (bf16[1,512,256]{2,1,0:T(8,128)(2,1)S(1)}, bf16[1,512,256]{2,1,0:T(8,128)(2,1)S(1)}, u32[]{:S(2)}, u32[]{:S(2)}) collective-permute-start(bf16[1,512,256]{2,1,0:T(8,128)(2,1)S(1)} %slice.63), channel_id=1, source_target_pairs={{0,16},{4,20},{8,24},{12,28},{16,0},{20,4},{24,8},{28,12},{1,17},{... | collective-permute-start | bytes 786440 | tf_op jit(solution)/shard_map/ppermute | solution.py:280
  43.3 7.6 %collective-permute-start.14 = (bf16[1,512,256]{2,1,0:T(8,128)(2,1)S(1)}, bf16[1,512,256]{2,1,0:T(8,128)(2,1)S(1)}, u32[]{:S(2)}, u32[]{:S(2)}) collective-permute-start(bf16[1,512,256]{2,1,0:T(8,128)(2,1)S(1)} %slice.64), channel_id=1, source_target_pairs={{0,8},{4,12},{8,0},{12,4},{16,24},{20,28},{24,16},{28,20},{1,9},{5... | collective-permute-start | bytes 786440 | tf_op jit(solution)/shard_map/ppermute | solution.py:280
  50.9 35.8 %collective-permute-start.23 = (bf16[3,256,512]{2,1,0:T(8,128)(2,1)S(1)}, bf16[3,256,512]{2,1,0:T(8,128)(2,1)S(1)}, u32[]{:S(2)}, u32[]{:S(2)}) collective-permute-start(bf16[3,256,512]{2,1,0:T(8,128)(2,1)S(1)} %pad_maximum_fusion.refs_7_.refs_5_), channel_id=1, source_target_pairs={{0,8},{4,12},{8,0},{12,4},{16,24},{20,28},{24,16},{28,20},{1,9},{5... | collective-permute-start | bytes 2359304 | tf_op jit(solution)/shard_map/ppermute | solution.py:280
  53.1 10.7 %collective-permute-start.15 = (bf16[512,256]{1,0:T(8,128)(2,1)S(1)}, bf16[512,256]{1,0:T(8,128)(2,1)S(1)}, u32[]{:S(2)}, u32[]{:S(2)}) collective-permute-start(bf16[512,256]{1,0:T(8,128)(2,1)S(1)} %mix.2.refs_0_), channel_id=1, source_target_pairs={{0,2},{1,3},{2,0},{3,1},{4,6},{5,7},{6,4},{7,5},{8,10},{9,11},{10,... | collective-permute-start | bytes 786440 | tf_op jit(solution)/shard_map/ppermute | solution.py:280
  55.1 9.2 %collective-permute-start.16 = (bf16[512,256]{1,0:T(8,128)(2,1)S(1)}, bf16[512,256]{1,0:T(8,128)(2,1)S(1)}, u32[]{:S(2)}, u32[]{:S(2)}) collective-permute-start(bf16[512,256]{1,0:T(8,128)(2,1)S(1)} %mix.2.refs_0_), channel_id=1, source_target_pairs={{0,1},{1,0},{2,3},{3,2},{4,5},{5,4},{6,7},{7,6},{8,9},{9,8},{10,11... | collective-permute-start | bytes 786440 | tf_op jit(solution)/shard_map/ppermute | solution.py:280
  59.4 5.6 %collective-permute-start.19 = (bf16[512,256]{1,0:T(8,128)(2,1)S(1)}, bf16[512,256]{1,0:T(8,128)(2,1)S(1)}, u32[]{:S(2)}, u32[]{:S(2)}) collective-permute-start(bf16[512,256]{1,0:T(8,128)(2,1)S(1)} %mix.3), channel_id=1, source_target_pairs={{0,4},{4,0},{8,12},{12,8},{16,20},{20,16},{24,28},{28,24},{1,5},{5... | collective-permute-start | bytes 786440 | tf_op jit(solution)/shard_map/ppermute | solution.py:280
  64.3 7.7 %collective-permute-start.17 = (bf16[512,256]{1,0:T(8,128)(2,1)S(1)}, bf16[512,256]{1,0:T(8,128)(2,1)S(1)}, u32[]{:S(2)}, u32[]{:S(2)}) collective-permute-start(bf16[512,256]{1,0:T(8,128)(2,1)S(1)} %mix.2.refs_0_), channel_id=1, source_target_pairs={{1,2},{2,1},{5,6},{6,5},{9,10},{10,9},{13,14},{14,13},{17,18},{18,... | collective-permute-start | bytes 786440 | tf_op jit(solution)/shard_map/ppermute | solution.py:365
  65.0 15.1 %collective-permute-start.18 = (bf16[512,256]{1,0:T(8,128)(2,1)S(1)}, bf16[512,256]{1,0:T(8,128)(2,1)S(1)}, u32[]{:S(2)}, u32[]{:S(2)}) collective-permute-start(bf16[512,256]{1,0:T(8,128)(2,1)S(1)} %collective-permute-done.15.refs_2_), channel_id=1, source_target_pairs={{2,3},{1,0},{6,7},{5,4},{10,11},{9,8},{14,15},{13,12},{18,19},{17,... | collective-permute-start | bytes 786440 | tf_op jit(solution)/shard_map/ppermute | solution.py:366
  66.3 19.0 %collective-permute-start.20 = (bf16[512,256]{1,0:T(8,128)(2,1)S(1)}, bf16[512,256]{1,0:T(8,128)(2,1)S(1)}, u32[]{:S(2)}, u32[]{:S(2)}) collective-permute-start(bf16[512,256]{1,0:T(8,128)(2,1)S(1)} %collective-permute-done.19.refs_3_), channel_id=1, source_target_pairs={{0,2},{1,3},{2,0},{3,1},{4,6},{5,7},{6,4},{7,5},{8,10},{9,11},{10,... | collective-permute-start | bytes 786440 | tf_op jit(solution)/shard_map/ppermute | solution.py:280
  72.0 14.8 %collective-permute-start.25 = (bf16[512,256]{1,0:T(8,128)(2,1)S(1)}, bf16[512,256]{1,0:T(8,128)(2,1)S(1)}, u32[]{:S(2)}, u32[]{:S(2)}) collective-permute-start(bf16[512,256]{1,0:T(8,128)(2,1)S(1)} %collective-permute-done.19.refs_3_), channel_id=1, source_target_pairs={{0,1},{1,0},{2,3},{3,2},{4,5},{5,4},{6,7},{7,6},{8,9},{9,8},{10,11... | collective-permute-start | bytes 786440 | tf_op jit(solution)/shard_map/ppermute | solution.py:280
  72.0 16.7 %collective-permute-start.24 = (bf16[3,256,512]{2,1,0:T(8,128)(2,1)S(1)}, bf16[3,256,512]{2,1,0:T(8,128)(2,1)S(1)}, u32[]{:S(2)}, u32[]{:S(2)}) collective-permute-start(bf16[3,256,512]{2,1,0:T(8,128)(2,1)S(1)} %pad_maximum_fusion.refs_7_.refs_5_), channel_id=1, source_target_pairs={{0,4},{4,0},{8,12},{12,8},{16,20},{20,16},{24,28},{28,24},{1,5},{5... | collective-permute-start | bytes 2359304 | tf_op jit(solution)/shard_map/ppermute | solution.py:280
  86.7 2.3 %collective-permute-start.26 = (bf16[3,256,512]{2,1,0:T(8,128)(2,1)S(1)}, bf16[3,256,512]{2,1,0:T(8,128)(2,1)S(1)}, u32[]{:S(2)}, u32[]{:S(2)}) collective-permute-start(bf16[3,256,512]{2,1,0:T(8,128)(2,1)S(1)} %collective-permute-done.23.refs_8_.refs_6_), channel_id=1, source_target_pairs={{0,4},{4,0},{8,12},{12,8},{16,20},{20,16},{24,28},{28,24},{1,5},{5... | collective-permute-start | bytes 2359304 | tf_op jit(solution)/shard_map/ppermute | solution.py:280
  86.8 4.6 %collective-permute-start.21 = (bf16[512,256]{1,0:T(8,128)(2,1)S(1)}, bf16[512,256]{1,0:T(8,128)(2,1)S(1)}, u32[]{:S(2)}, u32[]{:S(2)}) collective-permute-start(bf16[512,256]{1,0:T(8,128)(2,1)S(1)} %collective-permute-done.19.refs_3_), channel_id=1, source_target_pairs={{1,2},{2,1},{5,6},{6,5},{9,10},{10,9},{13,14},{14,13},{17,18},{18,... | collective-permute-start | bytes 786440 | tf_op jit(solution)/shard_map/ppermute | solution.py:367
  87.4 10.8 %collective-permute-start.22 = (bf16[512,256]{1,0:T(8,128)(2,1)S(1)}, bf16[512,256]{1,0:T(8,128)(2,1)S(1)}, u32[]{:S(2)}, u32[]{:S(2)}) collective-permute-start(bf16[512,256]{1,0:T(8,128)(2,1)S(1)} %collective-permute-done.20.refs_5_), channel_id=1, source_target_pairs={{2,3},{1,0},{6,7},{5,4},{10,11},{9,8},{14,15},{13,12},{18,19},{17,... | collective-permute-start | bytes 786440 | tf_op jit(solution)/shard_map/ppermute | solution.py:368
  (1 other events, 2.1 us)

commit v13 on v12

--- a/solution.py
+++ b/solution.py
@@ -232,9 +232,10 @@
     )(place, grp, *scored, *sufs, *pieces)
 
 
-def proj_kernel(steps, last, where_ref, *refs):
-    att = refs[: 2 * len(steps)]
-    own, *far = refs[2 * len(steps) : 2 * len(steps) + 5]
+def proj_kernel(plan, last, where_ref, *refs):
+    n_att = sum(len(steps) for steps in plan)
+    att = list(refs[:n_att])
+    own, *far = refs[n_att : n_att + 5]
     o_ref = refs[-1]
     cols = o_ref.shape[1] // 2
     rows = o_ref.shape[0]
@@ -246,14 +247,15 @@
         for x in range(2):
             c = pl.ds(pl.multiple_of(lax.bitwise_xor(side, x) * cols, cols), cols)
             acc = refs[-2][at, c] if last else jnp.zeros((tall, cols), jnp.float32)
-            for h in range(2):
+            i = 0
+            for h, steps in enumerate(plan):
                 head = lax.bitwise_xor(core, h)
-                lines = []
-                for i, m in enumerate(steps):
-                    lines.append((m, att[h * len(steps) + i][at, :]))
-                if last:
-                    lines = [(3, lines[0][1] + lines[1][1])]
-                for m, a in lines:
+                lines = {}
+                for m in steps:
+                    a = att[i][at, :]
+                    lines[m] = lines[m] + a if m in lines else a
+                    i += 1
+                for m, a in lines.items():
                     if m == 0:
                         w = own[pl.ds(pl.multiple_of(head * HD, HD), HD), c]
                     else:
@@ -262,12 +264,12 @@
             o_ref[at, c] = acc.astype(o_ref.dtype)
 
 
-def project(where, steps, att, own, far, add=None):
+def project(where, plan, att, own, far, add=None):
     rows = att[0].shape[0]
     cols = own.shape[1]
     extra = [] if add is None else [add]
     return pl.pallas_call(
-        functools.partial(proj_kernel, steps, add is not None),
+        functools.partial(proj_kernel, plan, add is not None),
         out_shape=jax.ShapeDtypeStruct((rows, cols), jnp.float32 if add is None else jnp.bfloat16),
         in_specs=[SMEM] + [VMEM] * (len(att) + 1 + len(far) + len(extra)),
         out_specs=VMEM,
@@ -353,7 +355,7 @@
     vyx = over_x(after(vy[1:2], scored[0], w_far))
     v_pieces = (v_both, vx, vy, vxy, vyx)
     (own,) = mix(0, HD, place, grp, scored, sufs[:1], v_pieces)
-    (pair,) = mix(0, HD, place, grp, scored, sufs[1:], v_pieces, rows)
+    (pair,) = mix(0, HD, after(place, own), grp, scored, sufs[1:], v_pieces, rows)
     w_x = over_x(after(w_far, vxy, vyx))
 
     back = over_core(pair)
@@ -368,9 +370,14 @@
     forward_back = lax.ppermute(two_back, "tp", [(2, 3), (1, 0)])
     w_core_x = over_core(after(w_x, two_back, one_back, three_own, forward_own))
     far = [w_far, w_x, w_core, w_core_x]
-    near = project(where, (0, 1, 2), (own, one_own, two_own, back, one_back, two_back), w_own, far)
-    last = (three_own, forward_own, three_back, forward_back)
-    return project(where, (3, 3), last, w_own, far, near)
+    near = project(
+        where,
+        ((0, 1, 2, 3, 3), (0, 1, 2)),
+        (own, one_own, two_own, three_own, forward_own, back, one_back, two_back),
+        w_own,
+        far,
+    )
+    return project(where, ((), (3, 3)), (three_back, forward_back), w_own, far, near)
 
 
 def whole_heads(suffix_heads, prefix_cache, lengths, groups, owners, out_weight):

time: 101 us -> 104 us (1.030)
  waiting for transfers between devices: 41.2 us -> 47.1 us
  starting transfers between devices: 34.3 us -> 32 us
    ppermute x23, waiting for transfers between devices: 26.4 us -> 36 us  [swap(): return lax.ppermute(x, axis, [(i, i ^ mask) for i in range(size)])]
    ppermute x1, waiting for transfers between devices: 8.02 us -> 4.66 us  [split_heads(): forward_own = lax.ppermute(two_own, 'tp', [(2, 3), (1, 0)])]
    ppermute x23, starting transfers between devices: 30.3 us -> 28.1 us  [swap(): return lax.ppermute(x, axis, [(i, i ^ mask) for i in range(size)])]
  transfers between devices with their start and end apart: 27 -> 27, of which waited for: 13 -> 12; matrix products, arithmetic and copies ran while one was open for 4% -> 4% of each run, Pallas kernels for 16% -> 16%
where the time goes in v13:
time: 104 us
  waiting for transfers between devices  47.1 us (45%)
  starting transfers between devices  32 us (31%)
  Pallas kernels  18.7 us (18%)
  local copies, waits for them, and re-layouts  5.41 us (5%)
    ppermute x23, waiting for transfers between devices, swap(): return lax.ppermute(x, axis, [(i, i ^ mask) for i in range(size)])  36 us
    ppermute x23, starting transfers between devices, swap(): return lax.ppermute(x, axis, [(i, i ^ mask) for i in range(size)])  28.1 us
    pallas_call x1, Pallas kernels, score(): pl.pallas_call(functools.partial(score_kernel, len(sufs), tuple((p.shape[...  8.18 us
    ppermute x1, waiting for transfers between devices, split_heads(): forward_back = lax.ppermute(two_back, 'tp', [(2, 3), (1, 0)])  6.38 us
    ppermute x1, waiting for transfers between devices, split_heads(): forward_own = lax.ppermute(two_own, 'tp', [(2, 3), (1, 0)])  4.66 us
    pallas_call x2, Pallas kernels, project(): pl.pallas_call(functools.partial(proj_kernel, plan, add is not None), out...  4.55 us
    pallas_call x2, Pallas kernels, mix(): pl.pallas_call(functools.partial(mix_kernel, nb, base, tuple((p.shape[0]...  4.23 us
  transfers between devices with their start and end apart: 27, of which 12 were waited for; matrix products, arithmetic and copies ran while one was open for 4% of the time, Pallas kernels for 16%

profile of v13, /device:TPU:0, one launch (start us, length us, event | category | flops | bytes accessed | tf_op | source)
XLA Modules:
  0.0 103.9 jit_solution(7112949269207589473)
XLA Ops:
  0.0 1.5 %copy.15 = bf16[512,1,512]{2,0,1:T(8,128)(2,1)S(1)} copy(bf16[512,1,512]{2,1,0:T(2,128)(2,1)} %bitcast.24) | data formatting | bytes 1048576
  2.3 1.0 collective-permute-done
  3.3 2.9 %collective-permute-start.3 = (bf16[2,512,256]{2,1,0:T(8,128)(2,1)S(1)}, bf16[2,512,256]{2,1,0:T(8,128)(2,1)S(1)}, u32[]{:S(2)}, u32[]{:S(2)}) collective-permute-start(bf16[2,512,256]{2,1,0:T(8,128)(2,1)S(1)} %pad_maximum_fusion.1.rest_2_), channel_id=1, source_target_pairs={{0,8},{4,12},{8,0},{12,4},{16,24},{20,28},{24,16},{28,20},{1,9},{5... | collective-permute-start | bytes 1572872 | tf_op jit(solution)/shard_map/ppermute | solution.py:282
  6.2 1.5 %collective-permute-start.4 = (bf16[2,512,256]{2,1,0:T(8,128)(2,1)S(1)}, bf16[2,512,256]{2,1,0:T(8,128)(2,1)S(1)}, u32[]{:S(2)}, u32[]{:S(2)}) collective-permute-start(bf16[2,512,256]{2,1,0:T(8,128)(2,1)S(1)} %pad_maximum_fusion.1.rest_2_), channel_id=1, source_target_pairs={{0,16},{4,20},{8,24},{12,28},{16,0},{20,4},{24,8},{28,12},{1,17},{... | collective-permute-start | bytes 1572872 | tf_op jit(solution)/shard_map/ppermute | solution.py:282
  7.9 1.8 %prepare.1 = (s32[1024,128]{1,0:T(8,128)S(1)}, s32[1024,128]{1,0:T(8,128)S(1)}, bf16[3,512,256]{2,1,0:T(8,128)(2,1)S(1)}, bf16[3,512,256]{2,1,0:T(8,128)(2,1)S(1)}) custom-call(s32[3]{0:T(128)S(1)} %pad_add_fusion.1.where_ref, s32[2,8]{1,0:T(2,128)S(1)} %pad_add_fusion.refs_0_, s32[2,8]{1,0:T(2,128)S(1)} %collective-permute-done.1.refs_1_, ...), custom_call_target="tpu_custom_call" | custom-call | tf_op jit(solution)/shard_map/prepare/pallas_call | solution.py:101
  10.6 1.7 %fusion = (bf16[256,512]{1,0:T(8,128)(2,1)S(1)}, bf16[256,512]{1,0:T(8,128)(2,1)S(1)}, bf16[256,512]{1,0:T(8,128)(2,1)S(1)}) fusion(bf16[512,4096]{1,0:T(8,128)(2,1)} %param.12, u32[]{:T(128)S(6)} %mul.20, u32[]{:T(128)S(6)} %add.17, u32[]{:T(128)S(6)} %add.16, u32[]{:T(128)S(6)} %add.15), kind=kLoop, calls=%fused_computation.18 | loop fusion | bytes 1572880 | tf_op jit(solution)/shard_map/dynamic_slice | solution.py:318
  12.2 1.6 %collective-permute-start.8 = (bf16[256,512]{1,0:T(8,128)(2,1)S(1)}, bf16[256,512]{1,0:T(8,128)(2,1)S(1)}, u32[]{:S(2)}, u32[]{:S(2)}) collective-permute-start(bf16[256,512]{1,0:T(8,128)(2,1)S(1)} %get-tuple-element.65), channel_id=1, source_target_pairs={{0,1},{1,0},{2,3},{3,2},{4,5},{5,4},{6,7},{7,6},{8,9},{9,8},{10,11... | collective-permute-start | bytes 786440 | tf_op jit(solution)/shard_map/ppermute | solution.py:282
  13.9 2.6 %collective-permute-start.9 = (bf16[256,512]{1,0:T(8,128)(2,1)S(1)}, bf16[256,512]{1,0:T(8,128)(2,1)S(1)}, u32[]{:S(2)}, u32[]{:S(2)}) collective-permute-start(bf16[256,512]{1,0:T(8,128)(2,1)S(1)} %get-tuple-element.64), channel_id=1, source_target_pairs={{0,2},{1,3},{2,0},{3,1},{4,6},{5,7},{6,4},{7,5},{8,10},{9,11},{10,... | collective-permute-start | bytes 786440 | tf_op jit(solution)/shard_map/ppermute | solution.py:282
  16.5 1.9 %collective-permute-done.3.rest_3_ = bf16[2,512,256]{2,1,0:T(8,128)(2,1)S(1)} collective-permute-done((bf16[2,512,256]{2,1,0:T(8,128)(2,1)S(1)}, bf16[2,512,256]{2,1,0:T(8,128)(2,1)S(1)}, u32[]{:S(2)}, u32[]{:S(2)}) %collective-permute-start.3) | collective-permute-done | bytes 524320 | tf_op jit(solution)/shard_map/ppermute | solution.py:282
  18.5 1.8 %collective-permute-start.6 = (bf16[1,512,256]{2,1,0:T(8,128)(2,1)S(1)}, bf16[1,512,256]{2,1,0:T(8,128)(2,1)S(1)}, u32[]{:S(2)}, u32[]{:S(2)}) collective-permute-start(bf16[1,512,256]{2,1,0:T(8,128)(2,1)S(1)} %slice.58), channel_id=1, source_target_pairs={{0,16},{4,20},{8,24},{12,28},{16,0},{20,4},{24,8},{28,12},{1,17},{... | collective-permute-start | bytes 786440 | tf_op jit(solution)/shard_map/ppermute | solution.py:282
  20.3 1.6 %collective-permute-start.7 = (bf16[1,512,256]{2,1,0:T(8,128)(2,1)S(1)}, bf16[1,512,256]{2,1,0:T(8,128)(2,1)S(1)}, u32[]{:S(2)}, u32[]{:S(2)}) collective-permute-start(bf16[1,512,256]{2,1,0:T(8,128)(2,1)S(1)} %slice.62), channel_id=1, source_target_pairs={{0,8},{4,12},{8,0},{12,4},{16,24},{20,28},{24,16},{28,20},{1,9},{5... | collective-permute-start | bytes 786440 | tf_op jit(solution)/shard_map/ppermute | solution.py:282
  21.9 1.9 %constant_dynamic-slice_fusion.refs_8_.refs_2_ = bf16[512,1024]{1,0:T(8,128)(2,1)S(1)} fusion(bf16[512,4096]{1,0:T(8,128)(2,1)} %param.12, u32[]{:T(128)S(6)} %mul.21), kind=kLoop, calls=%fused_computation.16 | loop fusion | bytes 2097156 | tf_op jit(solution)/shard_map/dynamic_slice | solution.py:321
  23.8 2.3 %collective-permute-done.8 = bf16[256,512]{1,0:T(8,128)(2,1)S(1)} collective-permute-done((bf16[256,512]{1,0:T(8,128)(2,1)S(1)}, bf16[256,512]{1,0:T(8,128)(2,1)S(1)}, u32[]{:S(2)}, u32[]{:S(2)}) %collective-permute-start.8) | collective-permute-done | bytes 262176 | tf_op jit(solution)/shard_map/ppermute | solution.py:282
  26.0 2.4 %collective-permute-done.9 = bf16[256,512]{1,0:T(8,128)(2,1)S(1)} collective-permute-done((bf16[256,512]{1,0:T(8,128)(2,1)S(1)}, bf16[256,512]{1,0:T(8,128)(2,1)S(1)}, u32[]{:S(2)}, u32[]{:S(2)}) %collective-permute-start.9) | collective-permute-done | bytes 262176 | tf_op jit(solution)/shard_map/ppermute | solution.py:282
  29.6 3.6 %collective-permute-start.12 = (bf16[256,512]{1,0:T(8,128)(2,1)S(1)}, bf16[256,512]{1,0:T(8,128)(2,1)S(1)}, u32[]{:S(2)}, u32[]{:S(2)}) collective-permute-start(bf16[256,512]{1,0:T(8,128)(2,1)S(1)} %get-tuple-element.54), channel_id=1, source_target_pairs={{0,3},{1,2},{2,1},{3,0},{4,7},{5,6},{6,5},{7,4},{8,11},{9,10},{10,... | collective-permute-start | bytes 786440 | tf_op jit(solution)/shard_map/ppermute | solution.py:282
  33.3 8.2 %score.1 = (bf16[1024,1024]{1,0:T(8,128)(2,1)S(1)}, bf16[1024,256]{1,0:T(8,128)(2,1)S(1)}, f32[1024,128]{1,0:T(8,128)S(1)}) custom-call(s32[8]{0:T(128)S(1)} %select_reduce_fusion.place_ref, s32[1024,128]{1,0:T(8,128)S(1)} %get-tuple-element.38.first_ref, s32[1024,128]{1,0:T(8,128)S(1)} %get-tuple-element.37.grp_ref, ...), custom_call_target="tpu_custom_call" | custom-call | tf_op jit(solution)/shard_map/score/pallas_call | solution.py:176
  41.7 1.6 %collective-permute-start.13 = (bf16[1,512,256]{2,1,0:T(8,128)(2,1)S(1)}, bf16[1,512,256]{2,1,0:T(8,128)(2,1)S(1)}, u32[]{:S(2)}, u32[]{:S(2)}) collective-permute-start(bf16[1,512,256]{2,1,0:T(8,128)(2,1)S(1)} %slice.63), channel_id=1, source_target_pairs={{0,16},{4,20},{8,24},{12,28},{16,0},{20,4},{24,8},{28,12},{1,17},{... | collective-permute-start | bytes 786440 | tf_op jit(solution)/shard_map/ppermute | solution.py:282
  43.9 4.2 %collective-permute-done.13.rest_4_ = bf16[1,512,256]{2,1,0:T(8,128)(2,1)S(1)} collective-permute-done((bf16[1,512,256]{2,1,0:T(8,128)(2,1)S(1)}, bf16[1,512,256]{2,1,0:T(8,128)(2,1)S(1)}, u32[]{:S(2)}, u32[]{:S(2)}) %collective-permute-start.13) | collective-permute-done | bytes 262176 | tf_op jit(solution)/shard_map/ppermute | solution.py:282
  48.1 2.8 %collective-permute-done.14.rest_5_ = bf16[1,512,256]{2,1,0:T(8,128)(2,1)S(1)} collective-permute-done((bf16[1,512,256]{2,1,0:T(8,128)(2,1)S(1)}, bf16[1,512,256]{2,1,0:T(8,128)(2,1)S(1)}, u32[]{:S(2)}, u32[]{:S(2)}) %collective-permute-start.14) | collective-permute-done | bytes 262176 | tf_op jit(solution)/shard_map/ppermute | solution.py:282
  50.9 2.2 %mix.2.refs_0_ = bf16[512,256]{1,0:T(8,128)(2,1)S(1)} custom-call(s32[8]{0:T(128)S(1)} %select_reduce_fusion.place_ref, s32[1024,128]{1,0:T(8,128)S(1)} %get-tuple-element.37.grp_ref, bf16[1024,1024]{1,0:T(8,128)(2,1)S(1)} %get-tuple-element.44.p_ref, bf16[1024,256]{1,0:T(8,128)(2,1)S(1)} %get-tuple-element.45.near_ref, ...), custom_call_target="tpu_custom_call" | custom-call | tf_op jit(solution)/shard_map/mix/pallas_call | solution.py:225
  53.1 2.0 %mix.3 = bf16[512,256]{1,0:T(8,128)(2,1)S(1)} custom-call(s32[8]{0:T(128)S(1)} %select_reduce_fusion.place_ref, s32[1024,128]{1,0:T(8,128)S(1)} %get-tuple-element.37.grp_ref, bf16[1024,1024]{1,0:T(8,128)(2,1)S(1)} %get-tuple-element.44.p_ref, bf16[1024,256]{1,0:T(8,128)(2,1)S(1)} %get-tuple-element.45.near_ref, f32[1024,128]{1,0:T(8,128)S(1)} %get-tuple-element.46.den_ref, ...), custom_call_target="tpu_custom_call" | custom-call | tf_op jit(solution)/shard_map/mix/pallas_call | solution.py:225
  55.2 2.0 %collective-permute-start.16 = (bf16[512,256]{1,0:T(8,128)(2,1)S(1)}, bf16[512,256]{1,0:T(8,128)(2,1)S(1)}, u32[]{:S(2)}, u32[]{:S(2)}) collective-permute-start(bf16[512,256]{1,0:T(8,128)(2,1)S(1)} %mix.2.refs_0_), channel_id=1, source_target_pairs={{0,2},{1,3},{2,0},{3,1},{4,6},{5,7},{6,4},{7,5},{8,10},{9,11},{10,... | collective-permute-start | bytes 786440 | tf_op jit(solution)/shard_map/ppermute | solution.py:282
  57.2 2.2 %collective-permute-start.23 = (bf16[512,256]{1,0:T(8,128)(2,1)S(1)}, bf16[512,256]{1,0:T(8,128)(2,1)S(1)}, u32[]{:S(2)}, u32[]{:S(2)}) collective-permute-start(bf16[512,256]{1,0:T(8,128)(2,1)S(1)} %mix.2.refs_0_), channel_id=1, source_target_pairs={{0,1},{1,0},{2,3},{3,2},{4,5},{5,4},{6,7},{7,6},{8,9},{9,8},{10,11... | collective-permute-start | bytes 786440 | tf_op jit(solution)/shard_map/ppermute | solution.py:282
  59.5 11.0 %collective-permute-done.16.refs_2_ = bf16[512,256]{1,0:T(8,128)(2,1)S(1)} collective-permute-done((bf16[512,256]{1,0:T(8,128)(2,1)S(1)}, bf16[512,256]{1,0:T(8,128)(2,1)S(1)}, u32[]{:S(2)}, u32[]{:S(2)}) %collective-permute-start.16) | collective-permute-done | bytes 262176 | tf_op jit(solution)/shard_map/ppermute | solution.py:282
  70.5 3.5 %collective-permute-start.22 = (bf16[512,256]{1,0:T(8,128)(2,1)S(1)}, bf16[512,256]{1,0:T(8,128)(2,1)S(1)}, u32[]{:S(2)}, u32[]{:S(2)}) collective-permute-start(bf16[512,256]{1,0:T(8,128)(2,1)S(1)} %collective-permute-done.15.refs_5_), channel_id=1, source_target_pairs={{0,1},{1,0},{2,3},{3,2},{4,5},{5,4},{6,7},{7,6},{8,9},{9,8},{10,11... | collective-permute-start | bytes 786440 | tf_op jit(solution)/shard_map/ppermute | solution.py:282
  74.6 1.3 %collective-permute-start.25 = (bf16[512,256]{1,0:T(8,128)(2,1)S(1)}, bf16[512,256]{1,0:T(8,128)(2,1)S(1)}, u32[]{:S(2)}, u32[]{:S(2)}) collective-permute-start(bf16[512,256]{1,0:T(8,128)(2,1)S(1)} %collective-permute-done.16.refs_2_), channel_id=1, source_target_pairs={{2,3},{1,0},{6,7},{5,4},{10,11},{9,8},{14,15},{13,12},{18,19},{17,... | collective-permute-start | bytes 786440 | tf_op jit(solution)/shard_map/ppermute | solution.py:368
  75.9 9.7 %collective-permute-done.17.refs_7_ = bf16[512,256]{1,0:T(8,128)(2,1)S(1)} collective-permute-done((bf16[512,256]{1,0:T(8,128)(2,1)S(1)}, bf16[512,256]{1,0:T(8,128)(2,1)S(1)}, u32[]{:S(2)}, u32[]{:S(2)}) %collective-permute-start.17) | collective-permute-done | bytes 262176 | tf_op jit(solution)/shard_map/ppermute | solution.py:282
  86.0 4.7 %collective-permute-done.25.refs_4_ = bf16[512,256]{1,0:T(8,128)(2,1)S(1)} collective-permute-done((bf16[512,256]{1,0:T(8,128)(2,1)S(1)}, bf16[512,256]{1,0:T(8,128)(2,1)S(1)}, u32[]{:S(2)}, u32[]{:S(2)}) %collective-permute-start.25) | collective-permute-done | bytes 262176 | tf_op jit(solution)/shard_map/ppermute | solution.py:368
  91.4 1.3 %collective-permute-start.19 = (bf16[512,256]{1,0:T(8,128)(2,1)S(1)}, bf16[512,256]{1,0:T(8,128)(2,1)S(1)}, u32[]{:S(2)}, u32[]{:S(2)}) collective-permute-start(bf16[512,256]{1,0:T(8,128)(2,1)S(1)} %collective-permute-done.17.refs_7_), channel_id=1, source_target_pairs={{2,3},{1,0},{6,7},{5,4},{10,11},{9,8},{14,15},{13,12},{18,19},{17,... | collective-permute-start | bytes 786440 | tf_op jit(solution)/shard_map/ppermute | solution.py:370
  93.0 2.6 %project.2.refs_7_ = f32[512,1024]{1,0:T(8,128)S(1)} custom-call(s32[3]{0:T(128)S(1)} %pad_add_fusion.1.where_ref, bf16[512,256]{1,0:T(8,128)(2,1)S(1)} %mix.2.refs_0_, bf16[512,256]{1,0:T(8,128)(2,1)S(1)} %collective-permute-done.23.refs_1_, bf16[512,256]{1,0:T(8,128)(2,1)S(1)} %collective-permute-done.16.refs_2_, ...), custom_call_target="tpu_custom_call" | custom-call | tf_op jit(solution)/shard_map/project/pallas_call | solution.py:271
  95.6 6.4 %collective-permute-done.19.refs_1_ = bf16[512,256]{1,0:T(8,128)(2,1)S(1)} collective-permute-done((bf16[512,256]{1,0:T(8,128)(2,1)S(1)}, bf16[512,256]{1,0:T(8,128)(2,1)S(1)}, u32[]{:S(2)}, u32[]{:S(2)}) %collective-permute-start.19) | collective-permute-done | bytes 262176 | tf_op jit(solution)/shard_map/ppermute | solution.py:370
  102.0 1.9 %project.3 = bf16[512,1024]{1,0:T(8,128)(2,1)} custom-call(s32[3]{0:T(128)S(1)} %pad_add_fusion.1.where_ref, bf16[512,256]{1,0:T(8,128)(2,1)S(1)} %collective-permute-done.18.refs_0_, bf16[512,256]{1,0:T(8,128)(2,1)S(1)} %collective-permute-done.19.refs_1_, bf16[512,1024]{1,0:T(8,128)(2,1)S(1)} %constant_dynamic-slice_fusion.refs_8_.refs_2_, ...), custom_call_target="tpu_custom_call" | custom-call | tf_op jit(solution)/shard_map/project/pallas_call | solution.py:271
  (60 shorter events, 6.0 us)
Async XLA Ops:
  0.0 2.1 %copy-start.5 = (s32[1,8]{1,0:T(1,128)S(1)}, s32[1,8]{1,0:T(1,128)}, u32[]{:S(2)}) copy-start(s32[1,8]{1,0:T(1,128)} %param.9) | copy-start | bytes 100
  0.0 7.7 %copy-start.2 = (bf16[512,3,512]{2,0,1:T(8,128)(2,1)S(1)}, bf16[512,3,512]{2,0,1:T(8,128)(2,1)}, u32[]{:S(2)}) copy-start(bf16[512,3,512]{2,0,1:T(8,128)(2,1)} %param.7) | copy-start | bytes 4718596
  1.5 1.7 %collective-permute-start = (bf16[512,256]{1,0:T(8,128)(2,1)S(1)}, bf16[512,256]{1,0:T(8,128)(2,1)S(1)}, u32[]{:S(2)}, u32[]{:S(2)}) collective-permute-start(bf16[512,256]{1,0:T(8,128)(2,1)S(1)} %get-tuple-element.72), channel_id=1, source_target_pairs={{0,4},{4,0},{8,12},{12,8},{16,20},{20,16},{24,28},{28,24},{1,5},{5... | collective-permute-start | bytes 786440 | tf_op jit(solution)/shard_map/ppermute | solution.py:282
  2.1 5.8 %collective-permute-start.1 = (s32[2,8]{1,0:T(2,128)S(1)}, s32[2,8]{1,0:T(2,128)S(1)}, u32[]{:S(2)}, u32[]{:S(2)}) collective-permute-start(s32[2,8]{1,0:T(2,128)S(1)} %pad_add_fusion.refs_0_), channel_id=1, source_target_pairs={{0,4},{4,0},{8,12},{12,8},{16,20},{20,16},{24,28},{28,24},{1,5},{5... | collective-permute-start | bytes 200 | tf_op jit(solution)/shard_map/ppermute | solution.py:282
  3.2 4.6 %copy-start = (f32[128,256]{1,0:T(8,128)S(1)}, f32[128,256]{1,0:T(8,128)}, u32[]{:S(2)}) copy-start(f32[128,256]{1,0:T(8,128)} %constant.28.clone.refs_5_) | copy-start | bytes 393220
  3.3 6.5 %copy-start.1 = (bf16[512,2,512]{2,1,0:T(2,128)(2,1)S(1)}, bf16[512,2,512]{2,1,0:T(2,128)(2,1)}, u32[]{:S(2)}) copy-start(bf16[512,2,512]{2,1,0:T(2,128)(2,1)} %param.8) | copy-start | bytes 3145732
  3.3 15.2 %collective-permute-start.3 = (bf16[2,512,256]{2,1,0:T(8,128)(2,1)S(1)}, bf16[2,512,256]{2,1,0:T(8,128)(2,1)S(1)}, u32[]{:S(2)}, u32[]{:S(2)}) collective-permute-start(bf16[2,512,256]{2,1,0:T(8,128)(2,1)S(1)} %pad_maximum_fusion.1.rest_2_), channel_id=1, source_target_pairs={{0,8},{4,12},{8,0},{12,4},{16,24},{20,28},{24,16},{28,20},{1,9},{5... | collective-permute-start | bytes 1572872 | tf_op jit(solution)/shard_map/ppermute | solution.py:282
  6.2 14.1 %collective-permute-start.4 = (bf16[2,512,256]{2,1,0:T(8,128)(2,1)S(1)}, bf16[2,512,256]{2,1,0:T(8,128)(2,1)S(1)}, u32[]{:S(2)}, u32[]{:S(2)}) collective-permute-start(bf16[2,512,256]{2,1,0:T(8,128)(2,1)S(1)} %pad_maximum_fusion.1.rest_2_), channel_id=1, source_target_pairs={{0,16},{4,20},{8,24},{12,28},{16,0},{20,4},{24,8},{28,12},{1,17},{... | collective-permute-start | bytes 1572872 | tf_op jit(solution)/shard_map/ppermute | solution.py:282
  9.7 18.7 %collective-permute-start.2 = (bf16[3,512,256]{2,1,0:T(8,128)(2,1)S(1)}, bf16[3,512,256]{2,1,0:T(8,128)(2,1)S(1)}, u32[]{:S(2)}, u32[]{:S(2)}) collective-permute-start(bf16[3,512,256]{2,1,0:T(8,128)(2,1)S(1)} %get-tuple-element.40), channel_id=1, source_target_pairs={{0,4},{4,0},{8,12},{12,8},{16,20},{20,16},{24,28},{28,24},{1,5},{5... | collective-permute-start | bytes 2359304 | tf_op jit(solution)/shard_map/ppermute | solution.py:282
  10.0 3.9 %collective-permute-start.5 = (bf16[512,256]{1,0:T(8,128)(2,1)S(1)}, bf16[512,256]{1,0:T(8,128)(2,1)S(1)}, u32[]{:S(2)}, u32[]{:S(2)}) collective-permute-start(bf16[512,256]{1,0:T(8,128)(2,1)S(1)} %get-tuple-element.70), channel_id=1, source_target_pairs={{0,4},{4,0},{8,12},{12,8},{16,20},{20,16},{24,28},{28,24},{1,5},{5... | collective-permute-start | bytes 786440 | tf_op jit(solution)/shard_map/ppermute | solution.py:282
  12.2 13.8 %collective-permute-start.8 = (bf16[256,512]{1,0:T(8,128)(2,1)S(1)}, bf16[256,512]{1,0:T(8,128)(2,1)S(1)}, u32[]{:S(2)}, u32[]{:S(2)}) collective-permute-start(bf16[256,512]{1,0:T(8,128)(2,1)S(1)} %get-tuple-element.65), channel_id=1, source_target_pairs={{0,1},{1,0},{2,3},{3,2},{4,5},{5,4},{6,7},{7,6},{8,9},{9,8},{10,11... | collective-permute-start | bytes 786440 | tf_op jit(solution)/shard_map/ppermute | solution.py:282
  13.9 14.5 %collective-permute-start.9 = (bf16[256,512]{1,0:T(8,128)(2,1)S(1)}, bf16[256,512]{1,0:T(8,128)(2,1)S(1)}, u32[]{:S(2)}, u32[]{:S(2)}) collective-permute-start(bf16[256,512]{1,0:T(8,128)(2,1)S(1)} %get-tuple-element.64), channel_id=1, source_target_pairs={{0,2},{1,3},{2,0},{3,1},{4,6},{5,7},{6,4},{7,5},{8,10},{9,11},{10,... | collective-permute-start | bytes 786440 | tf_op jit(solution)/shard_map/ppermute | solution.py:282
  16.5 16.8 %copy-start.3 = (s32[4,2]{0,1:T(2,128)S(1)}, s32[4,2]{0,1:T(2,128)}, u32[]{:S(2)}) copy-start(s32[4,2]{0,1:T(2,128)} %param.11) | copy-start | bytes 100
  18.5 9.9 %collective-permute-start.6 = (bf16[1,512,256]{2,1,0:T(8,128)(2,1)S(1)}, bf16[1,512,256]{2,1,0:T(8,128)(2,1)S(1)}, u32[]{:S(2)}, u32[]{:S(2)}) collective-permute-start(bf16[1,512,256]{2,1,0:T(8,128)(2,1)S(1)} %slice.58), channel_id=1, source_target_pairs={{0,16},{4,20},{8,24},{12,28},{16,0},{20,4},{24,8},{28,12},{1,17},{... | collective-permute-start | bytes 786440 | tf_op jit(solution)/shard_map/ppermute | solution.py:282
  20.3 8.1 %collective-permute-start.7 = (bf16[1,512,256]{2,1,0:T(8,128)(2,1)S(1)}, bf16[1,512,256]{2,1,0:T(8,128)(2,1)S(1)}, u32[]{:S(2)}, u32[]{:S(2)}) collective-permute-start(bf16[1,512,256]{2,1,0:T(8,128)(2,1)S(1)} %slice.62), channel_id=1, source_target_pairs={{0,8},{4,12},{8,0},{12,4},{16,24},{20,28},{24,16},{28,20},{1,9},{5... | collective-permute-start | bytes 786440 | tf_op jit(solution)/shard_map/ppermute | solution.py:282
  28.4 13.2 %collective-permute-start.10 = (bf16[2,512,256]{2,1,0:T(8,128)(2,1)S(1)}, bf16[2,512,256]{2,1,0:T(8,128)(2,1)S(1)}, u32[]{:S(2)}, u32[]{:S(2)}) collective-permute-start(bf16[2,512,256]{2,1,0:T(8,128)(2,1)S(1)} %pad_maximum_fusion.2.rest_1_), channel_id=1, source_target_pairs={{0,8},{4,12},{8,0},{12,4},{16,24},{20,28},{24,16},{28,20},{1,9},{5... | collective-permute-start | bytes 1572872 | tf_op jit(solution)/shard_map/ppermute | solution.py:282
  29.1 14.1 %collective-permute-start.11 = (bf16[2,512,256]{2,1,0:T(8,128)(2,1)S(1)}, bf16[2,512,256]{2,1,0:T(8,128)(2,1)S(1)}, u32[]{:S(2)}, u32[]{:S(2)}) collective-permute-start(bf16[2,512,256]{2,1,0:T(8,128)(2,1)S(1)} %pad_maximum_fusion.2.rest_1_), channel_id=1, source_target_pairs={{0,16},{4,20},{8,24},{12,28},{16,0},{20,4},{24,8},{28,12},{1,17},{... | collective-permute-start | bytes 1572872 | tf_op jit(solution)/shard_map/ppermute | solution.py:282
  29.6 11.9 %collective-permute-start.12 = (bf16[256,512]{1,0:T(8,128)(2,1)S(1)}, bf16[256,512]{1,0:T(8,128)(2,1)S(1)}, u32[]{:S(2)}, u32[]{:S(2)}) collective-permute-start(bf16[256,512]{1,0:T(8,128)(2,1)S(1)} %get-tuple-element.54), channel_id=1, source_target_pairs={{0,3},{1,2},{2,1},{3,0},{4,7},{5,6},{6,5},{7,4},{8,11},{9,10},{10,... | collective-permute-start | bytes 786440 | tf_op jit(solution)/shard_map/ppermute | solution.py:282
  41.7 6.4 %collective-permute-start.13 = (bf16[1,512,256]{2,1,0:T(8,128)(2,1)S(1)}, bf16[1,512,256]{2,1,0:T(8,128)(2,1)S(1)}, u32[]{:S(2)}, u32[]{:S(2)}) collective-permute-start(bf16[1,512,256]{2,1,0:T(8,128)(2,1)S(1)} %slice.63), channel_id=1, source_target_pairs={{0,16},{4,20},{8,24},{12,28},{16,0},{20,4},{24,8},{28,12},{1,17},{... | collective-permute-start | bytes 786440 | tf_op jit(solution)/shard_map/ppermute | solution.py:282
  43.3 7.7 %collective-permute-start.14 = (bf16[1,512,256]{2,1,0:T(8,128)(2,1)S(1)}, bf16[1,512,256]{2,1,0:T(8,128)(2,1)S(1)}, u32[]{:S(2)}, u32[]{:S(2)}) collective-permute-start(bf16[1,512,256]{2,1,0:T(8,128)(2,1)S(1)} %slice.64), channel_id=1, source_target_pairs={{0,8},{4,12},{8,0},{12,4},{16,24},{20,28},{24,16},{28,20},{1,9},{5... | collective-permute-start | bytes 786440 | tf_op jit(solution)/shard_map/ppermute | solution.py:282
  50.9 39.8 %collective-permute-start.20 = (bf16[3,256,512]{2,1,0:T(8,128)(2,1)S(1)}, bf16[3,256,512]{2,1,0:T(8,128)(2,1)S(1)}, u32[]{:S(2)}, u32[]{:S(2)}) collective-permute-start(bf16[3,256,512]{2,1,0:T(8,128)(2,1)S(1)} %pad_maximum_fusion.refs_9_.refs_3_), channel_id=1, source_target_pairs={{0,8},{4,12},{8,0},{12,4},{16,24},{20,28},{24,16},{28,20},{1,9},{5... | collective-permute-start | bytes 2359304 | tf_op jit(solution)/shard_map/ppermute | solution.py:282
  55.2 4.3 %collective-permute-start.15 = (bf16[512,256]{1,0:T(8,128)(2,1)S(1)}, bf16[512,256]{1,0:T(8,128)(2,1)S(1)}, u32[]{:S(2)}, u32[]{:S(2)}) collective-permute-start(bf16[512,256]{1,0:T(8,128)(2,1)S(1)} %mix.3), channel_id=1, source_target_pairs={{0,4},{4,0},{8,12},{12,8},{16,20},{20,16},{24,28},{28,24},{1,5},{5... | collective-permute-start | bytes 786440 | tf_op jit(solution)/shard_map/ppermute | solution.py:282
  55.2 15.2 %collective-permute-start.16 = (bf16[512,256]{1,0:T(8,128)(2,1)S(1)}, bf16[512,256]{1,0:T(8,128)(2,1)S(1)}, u32[]{:S(2)}, u32[]{:S(2)}) collective-permute-start(bf16[512,256]{1,0:T(8,128)(2,1)S(1)} %mix.2.refs_0_), channel_id=1, source_target_pairs={{0,2},{1,3},{2,0},{3,1},{4,6},{5,7},{6,4},{7,5},{8,10},{9,11},{10,... | collective-permute-start | bytes 786440 | tf_op jit(solution)/shard_map/ppermute | solution.py:282
  57.2 16.7 %collective-permute-start.23 = (bf16[512,256]{1,0:T(8,128)(2,1)S(1)}, bf16[512,256]{1,0:T(8,128)(2,1)S(1)}, u32[]{:S(2)}, u32[]{:S(2)}) collective-permute-start(bf16[512,256]{1,0:T(8,128)(2,1)S(1)} %mix.2.refs_0_), channel_id=1, source_target_pairs={{0,1},{1,0},{2,3},{3,2},{4,5},{5,4},{6,7},{7,6},{8,9},{9,8},{10,11... | collective-permute-start | bytes 786440 | tf_op jit(solution)/shard_map/ppermute | solution.py:282
  70.5 15.2 %collective-permute-start.17 = (bf16[512,256]{1,0:T(8,128)(2,1)S(1)}, bf16[512,256]{1,0:T(8,128)(2,1)S(1)}, u32[]{:S(2)}, u32[]{:S(2)}) collective-permute-start(bf16[512,256]{1,0:T(8,128)(2,1)S(1)} %collective-permute-done.15.refs_5_), channel_id=1, source_target_pairs={{0,2},{1,3},{2,0},{3,1},{4,6},{5,7},{6,4},{7,5},{8,10},{9,11},{10,... | collective-permute-start | bytes 786440 | tf_op jit(solution)/shard_map/ppermute | solution.py:282
  70.5 15.5 %collective-permute-start.22 = (bf16[512,256]{1,0:T(8,128)(2,1)S(1)}, bf16[512,256]{1,0:T(8,128)(2,1)S(1)}, u32[]{:S(2)}, u32[]{:S(2)}) collective-permute-start(bf16[512,256]{1,0:T(8,128)(2,1)S(1)} %collective-permute-done.15.refs_5_), channel_id=1, source_target_pairs={{0,1},{1,0},{2,3},{3,2},{4,5},{5,4},{6,7},{7,6},{8,9},{9,8},{10,11... | collective-permute-start | bytes 786440 | tf_op jit(solution)/shard_map/ppermute | solution.py:282
  74.0 12.1 %collective-permute-start.24 = (bf16[512,256]{1,0:T(8,128)(2,1)S(1)}, bf16[512,256]{1,0:T(8,128)(2,1)S(1)}, u32[]{:S(2)}, u32[]{:S(2)}) collective-permute-start(bf16[512,256]{1,0:T(8,128)(2,1)S(1)} %mix.2.refs_0_), channel_id=1, source_target_pairs={{1,2},{2,1},{5,6},{6,5},{9,10},{10,9},{13,14},{14,13},{17,18},{18,... | collective-permute-start | bytes 786440 | tf_op jit(solution)/shard_map/ppermute | solution.py:367
  74.6 16.0 %collective-permute-start.25 = (bf16[512,256]{1,0:T(8,128)(2,1)S(1)}, bf16[512,256]{1,0:T(8,128)(2,1)S(1)}, u32[]{:S(2)}, u32[]{:S(2)}) collective-permute-start(bf16[512,256]{1,0:T(8,128)(2,1)S(1)} %collective-permute-done.16.refs_2_), channel_id=1, source_target_pairs={{2,3},{1,0},{6,7},{5,4},{10,11},{9,8},{14,15},{13,12},{18,19},{17,... | collective-permute-start | bytes 786440 | tf_op jit(solution)/shard_map/ppermute | solution.py:368
  85.7 7.0 %collective-permute-start.21 = (bf16[3,256,512]{2,1,0:T(8,128)(2,1)S(1)}, bf16[3,256,512]{2,1,0:T(8,128)(2,1)S(1)}, u32[]{:S(2)}, u32[]{:S(2)}) collective-permute-start(bf16[3,256,512]{2,1,0:T(8,128)(2,1)S(1)} %pad_maximum_fusion.refs_9_.refs_3_), channel_id=1, source_target_pairs={{0,4},{4,0},{8,12},{12,8},{16,20},{20,16},{24,28},{28,24},{1,5},{5... | collective-permute-start | bytes 2359304 | tf_op jit(solution)/shard_map/ppermute | solution.py:282
  90.7 2.3 %collective-permute-start.26 = (bf16[3,256,512]{2,1,0:T(8,128)(2,1)S(1)}, bf16[3,256,512]{2,1,0:T(8,128)(2,1)S(1)}, u32[]{:S(2)}, u32[]{:S(2)}) collective-permute-start(bf16[3,256,512]{2,1,0:T(8,128)(2,1)S(1)} %collective-permute-done.20.refs_10_.refs_4_), channel_id=1, source_target_pairs={{0,4},{4,0},{8,12},{12,8},{16,20},{20,16},{24,28},{28,24},{1,5},{5... | collective-permute-start | bytes 2359304 | tf_op jit(solution)/shard_map/ppermute | solution.py:282
  90.7 4.9 %collective-permute-start.18 = (bf16[512,256]{1,0:T(8,128)(2,1)S(1)}, bf16[512,256]{1,0:T(8,128)(2,1)S(1)}, u32[]{:S(2)}, u32[]{:S(2)}) collective-permute-start(bf16[512,256]{1,0:T(8,128)(2,1)S(1)} %collective-permute-done.15.refs_5_), channel_id=1, source_target_pairs={{1,2},{2,1},{5,6},{6,5},{9,10},{10,9},{13,14},{14,13},{17,18},{18,... | collective-permute-start | bytes 786440 | tf_op jit(solution)/shard_map/ppermute | solution.py:369
  91.4 10.6 %collective-permute-start.19 = (bf16[512,256]{1,0:T(8,128)(2,1)S(1)}, bf16[512,256]{1,0:T(8,128)(2,1)S(1)}, u32[]{:S(2)}, u32[]{:S(2)}) collective-permute-start(bf16[512,256]{1,0:T(8,128)(2,1)S(1)} %collective-permute-done.17.refs_7_), channel_id=1, source_target_pairs={{2,3},{1,0},{6,7},{5,4},{10,11},{9,8},{14,15},{13,12},{18,19},{17,... | collective-permute-start | bytes 786440 | tf_op jit(solution)/shard_map/ppermute | solution.py:370
  (1 other events, 2.1 us)
